TPU v7x, 32 devices: a whole 2x2x4 slice. The times are simulated.
32 devices in a mesh: dp: 16 (over z, y, x), tensor: 2 (over core).
Axes of the slice: x: 2, y: 2, z: 4, core: 2. Of those that a mesh axis runs over, the one named last changes fastest.
Arguments:
- tokens: bfloat16 [32, 512, 768], P('dp', 'tensor'), may hold values from -6 to 6
- lengths: int32 [32], P('dp'), may hold values from 1 to 512, 10240 in all
- key_mask: int32 [32, 512], P('dp'), may hold values 0 or 1
- order: int32 [16, 2], P('dp'), may hold values from 0 to 1, each once within a row
- query_key_value_weight: bfloat16 [3, 768, 768], P(None, 'dp', 'tensor'), may hold values from -0.21875 to 0.21875
- output_projection_weight: bfloat16 [768, 768], P('tensor', 'dp'), may hold values from -1.25 to 1.25
- up_projection_weight: bfloat16 [768, 3072], P('dp', 'tensor'), may hold values from -0.21875 to 0.21875
- down_projection_weight: bfloat16 [3072, 768], P('tensor', 'dp'), may hold values from -0.109375 to 0.109375
- embedding_projection_weight: bfloat16 [768, 128], P(('dp', 'tensor')), may hold values from -0.21875 to 0.21875
- gains: float32 [2, 768], P(None, ('dp', 'tensor')), may hold values from 0.5 to 1.5
- biases: float32 [6, 768], P(None, ('dp', 'tensor')), may hold values from -3 to 3
- up_bias_vector: float32 [3072], P(('dp', 'tensor')), may hold values from -3 to 3
- cotangent: float32 [32, 512, 128], P('dp', 'tensor'), may hold values from -6 to 6
Outputs:
- embeddings: float32 [32, 512, 128], P('dp', 'tensor')
- grad_tokens: float32 [32, 512, 768], P('dp', 'tensor')
- query_key_value_gradient: float32 [3, 768, 768], P(None, 'dp', 'tensor')
- output_gradient: float32 [768, 768], P('tensor', 'dp')
- up_gradient: float32 [768, 3072], P('dp', 'tensor')
- down_gradient: float32 [3072, 768], P('tensor', 'dp')
- grad_proj: float32 [768, 128], P(('dp', 'tensor'))
- grad_gains: float32 [2, 768], P(None, ('dp', 'tensor'))
- grad_biases: float32 [6, 768], P(None, ('dp', 'tensor'))
- grad_up_bias: float32 [3072], P(('dp', 'tensor'))
Inputs may be any that keep to these rules, and one draw needn't show every extreme that they name: `lengths`: each sequence has 1 to 512 real tokens, and some sequence has exactly 512. `order`: each row is a permutation of 0 to 1.
All inputs are finite; a program needn't handle non-finite values. No bound on the sum of `lengths` or of `key_mask` on one device may be relied on, other than what follows from the above.
Results may differ from a plain program's by a relative error of at most 0.018.
Values may be sent and summed in bfloat16 or wider, within the bound.
No kernel may reach another device: no remote copies, remote signals or barrier semaphores. Data moves between devices by JAX's collectives and lax.ppermute only.
A program may use at most 192 MiB of HBM per device.

v0:
```python
import jax
import jax.numpy as jnp
import numpy as np
from jax import lax
from jax.experimental import pallas as pl
from jax.experimental.pallas import tpu as pltpu
from jax.sharding import PartitionSpec as P

HD = 64
LANES = 128
STRIP = 128
F32 = jnp.float32
BF16 = jnp.bfloat16
VMEM_LIMIT = 60 * 1024 * 1024


def nn(left, right):
    return lax.dot_general(left, right, (((1,), (0,)), ((), ())), preferred_element_type=F32)


def nt(left, right):
    return lax.dot_general(left, right, (((1,), (1,)), ((), ())), preferred_element_type=F32)


def swap_cores(value):
    return lax.ppermute(value, "tensor", [(0, 1), (1, 0)])


def after(value, *others):
    return lax.optimization_barrier((value, others))[0]


def together(*values):
    return lax.optimization_barrier(values)


def strips(count, size, step):
    def run(i, carry):
        step(pl.ds(pl.multiple_of(i * size, size), size))
        return carry

    lax.fori_loop(0, count // size, run, 0)


def call(body, outs, args, grid=None, in_specs=None, out_specs=None, scratch=(), flops=0):
    whole = pl.BlockSpec(memory_space=pltpu.VMEM)
    return pl.pallas_call(
        body,
        out_shape=outs,
        grid=grid or (),
        in_specs=in_specs or [whole] * len(args),
        out_specs=out_specs or jax.tree.map(lambda _: whole, outs),
        scratch_shapes=scratch,
        compiler_params=pltpu.CompilerParams(vmem_limit_bytes=VMEM_LIMIT),
        cost_estimate=pl.CostEstimate(flops=flops, bytes_accessed=1 << 20, transcendentals=0),
    )(*args)


def shaped(shape, dtype):
    return jax.ShapeDtypeStruct(shape, dtype)


ANY = pl.BlockSpec(memory_space=pl.ANY)
WHOLE = pl.BlockSpec(memory_space=pltpu.VMEM)


def load_weights(pieces, target, sems, first=0, last=None):
    quarter = target.shape[1] // 4
    columns = slice(first, last)
    copies = []
    for side in range(2):
        for place in range(4):
            source = place if side == 0 else (0, 2, 1, 3)[place]
            ref = pieces[2 * side + source // 2]
            copies.append(
                pltpu.make_async_copy(
                    ref.at[pl.ds((source % 2) * quarter, quarter), columns],
                    target.at[side, pl.ds(place * quarter, quarter)],
                    sems.at[side, place],
                )
            )
    for copy in copies:
        copy.start()
    return copies


def attention_kernel(
    x_ref, perm_ref, bias_ref, mask_ref, vec_ref, b0_ref, m0_ref, b1_ref, m1_ref, qkv_ref,
    lse_ref, att_ref, res_ref, first_ref, low_ref, lowt_ref, xt_ref, col_ref, rel_ref, w_ref, sems,
):
    cols = qkv_ref.shape[2] // 3
    tokens = x_ref.shape[0]
    copies = load_weights((b0_ref, m0_ref, b1_ref, m1_ref), w_ref, sems, 0, 4 * cols)
    rel_ref[...] = nn(x_ref[...], perm_ref[...]).astype(BF16)
    xt_ref[...] = rel_ref[...].T
    col_ref[...] = jnp.broadcast_to(mask_ref[...], (LANES, tokens)).T
    for copy in copies:
        copy.wait()
    for half in range(2):
        for part in range(3):
            span = slice(part * cols, (part + 1) * cols)
            made = nn(rel_ref[...], w_ref[half, :, span]) + bias_ref[half : half + 1, span]
            qkv_ref[half, :, span] = made.astype(BF16)
    lane = lax.broadcasted_iota(jnp.int32, (tokens, LANES), 1) < HD
    pairs = cols // LANES

    for half in range(2):

        def pair(i, carry, half=half):
            off = pl.multiple_of(i * LANES, LANES)
            query = qkv_ref[half, :, pl.ds(off, LANES)] * BF16(HD ** (-0.5))
            key = qkv_ref[half, :, pl.ds(pl.multiple_of(cols + off, LANES), LANES)]
            value = qkv_ref[half, :, pl.ds(pl.multiple_of(2 * cols + off, LANES), LANES)]
            value_t = value.T
            outs = []
            for head in range(2):
                kept = jnp.where(lane == (head == 0), key, jnp.zeros_like(key))
                scores = nt(kept, query)
                scores = scores + jnp.concatenate([col_ref[...]] * (tokens // LANES), axis=1)
                top = jnp.max(scores, axis=0, keepdims=True)
                shifted = jnp.exp(scores - top)
                total = jnp.sum(shifted, axis=0, keepdims=True)
                out = nn(value_t[head * HD : (head + 1) * HD], shifted.astype(BF16))
                outs.append(out / total)
                lse_ref[half, pl.ds(i * 2 + head, 1), :] = top + jnp.log(total)
            both = jnp.concatenate(outs, axis=0).T
            att_ref[half, :, pl.ds(off, LANES)] = both.astype(BF16)
            return carry

        lax.fori_loop(0, pairs, pair, 0)
    span = slice(3 * cols, 4 * cols)
    res_ref[...] = nt(att_ref[0], w_ref[0, :, span]) + nt(att_ref[1], w_ref[1, :, span])

    def norm(rows):
        value = res_ref[rows, :] + vec_ref[4:5, :] + rel_ref[rows, :].astype(F32)
        res_ref[rows, :] = value
        average = jnp.mean(value, axis=-1, keepdims=True)
        centred = value - average
        inverse = lax.rsqrt(jnp.mean(centred * centred, axis=-1, keepdims=True) + 1e-12)
        first = centred * inverse * vec_ref[0:1, :] + vec_ref[5:6, :]
        first_ref[rows, :] = first
        low_ref[rows, :] = first.astype(BF16)

    strips(tokens, STRIP, norm)
    lowt_ref[...] = low_ref[...].T


def attention_forward(x, perm, head_bias, mask, vec, pieces, cols):
    tokens, width = x.shape
    heads = cols // HD
    outs = (
        shaped((2, tokens, 3 * cols), BF16),
        shaped((2, heads, tokens), F32),
        shaped((2, tokens, cols), BF16),
        shaped((tokens, width), F32),
        shaped((tokens, width), F32),
        shaped((tokens, width), BF16),
        shaped((width, tokens), BF16),
        shaped((width, tokens), BF16),
    )
    return call(
        attention_kernel,
        outs,
        (x, perm, head_bias, mask, vec, *pieces),
        in_specs=[WHOLE] * 5 + [ANY] * 4,
        scratch=[
            pltpu.VMEM((tokens, LANES), F32),
            pltpu.VMEM((tokens, width), BF16),
            pltpu.VMEM((2, width, 4 * cols), BF16),
            pltpu.SemaphoreType.DMA((2, 4)),
        ],
        flops=8 * tokens * width * width,
    )


ERF = (0.254829592, -0.284496736, 1.421413741, -1.453152027, 1.061405429)


def gelu_pair(value):
    size = jnp.abs(value)
    bell = jnp.exp(-0.5 * value * value)
    t = 1.0 / (1.0 + (0.3275911 * 0.5**0.5) * size)
    poly = ERF[4]
    for term in ERF[3::-1]:
        poly = poly * t + term
    tail = 0.5 * poly * t * bell
    phi = jnp.where(value >= 0, 1.0 - tail, tail)
    return value * phi, phi + value * bell * 0.3989422804014327


def join_rows(both_ref, more_ref, target, swapped):
    quarter = target.shape[0] // 4
    for place in range(4):
        source = (0, 2, 1, 3)[place] if swapped else place
        ref = (both_ref, more_ref)[source // 2]
        rows = slice((source % 2) * quarter, (source % 2 + 1) * quarter)
        target[place * quarter : (place + 1) * quarter, :] = ref[rows, :]


def split_rows(value, keep_ref, send_ref, swapped):
    quarter = value.shape[0] // 4
    for place in range(4):
        source = (0, 2, 1, 3)[place] if swapped else place
        ref = (keep_ref, send_ref)[place // 2]
        rows = slice((place % 2) * quarter, (place % 2 + 1) * quarter)
        ref[rows, :] = value[source * quarter : (source + 1) * quarter, :]


def column_block(hidden):
    return 512 if hidden % 512 == 0 else hidden


def up_forward(low, pieces, bias, swapped):
    tokens, width = low.shape
    hidden = pieces[0].shape[1]
    block = column_block(hidden)

    def kernel(low_ref, both_ref, more_ref, bias_ref, hid_ref, slope_ref, acc_ref, w_ref):
        join_rows(both_ref, more_ref, w_ref, swapped)
        acc_ref[...] = nn(low_ref[...], w_ref[...])

        def act(rows):
            active, slope = gelu_pair(acc_ref[rows, :] + bias_ref[...])
            hid_ref[rows, :] = active.astype(BF16)
            slope_ref[rows, :] = slope.astype(BF16)

        strips(tokens, STRIP, act)

    outs = (shaped((tokens, hidden), BF16), shaped((tokens, hidden), BF16))
    chunk = pl.BlockSpec((tokens, block), lambda i: (0, i))
    piece = pl.BlockSpec((width // 2, block), lambda i: (0, i))
    return call(
        kernel,
        outs,
        (low, *pieces, bias),
        grid=(hidden // block,),
        in_specs=[
            pl.BlockSpec((tokens, width), lambda i: (0, 0)),
            piece,
            piece,
            pl.BlockSpec((1, block), lambda i: (0, i)),
        ],
        out_specs=(chunk, chunk),
        scratch=[pltpu.VMEM((tokens, block), F32), pltpu.VMEM((width, block), BF16)],
        flops=2 * tokens * width * hidden,
    )


def down_kernel(
    len_ref, h0_ref, h1_ref, first_ref, vec_ref, proj_ref, cot_ref, b0_ref, m0_ref, b1_ref, m1_ref, emb_ref,
    low_ref, lowt_ref, res_ref, pgrad_ref, sums_ref, ffn_ref, norm_ref, sec_ref, gp_ref,
    gs_ref, inv_ref, prj_ref, w_ref, sems,
):
    copies = load_weights((b0_ref, m0_ref, b1_ref, m1_ref), w_ref, sems)
    tokens = first_ref.shape[0]
    length = len_ref[0]
    for copy in copies:
        copy.wait()
    ffn_ref[...] = nt(h0_ref[...], w_ref[0]) + nt(h1_ref[...], w_ref[1])

    def norm(rows):
        value = first_ref[rows, :] + ffn_ref[rows, :] + vec_ref[6:7, :]
        average = jnp.mean(value, axis=-1, keepdims=True)
        centred = value - average
        inverse = lax.rsqrt(jnp.mean(centred * centred, axis=-1, keepdims=True) + 1e-12)
        normed = centred * inverse
        norm_ref[rows, :] = normed
        inv_ref[rows, :] = jnp.broadcast_to(inverse, (STRIP, LANES))
        sec_ref[rows, :] = (normed * vec_ref[1:2, :] + vec_ref[7:8, :]).astype(BF16)

    strips(tokens, STRIP, norm)
    prj_ref[...] = nn(sec_ref[...], proj_ref[...])

    def embed(rows):
        projected = prj_ref[rows, :]
        valid = rows.start + lax.broadcasted_iota(jnp.int32, projected.shape, 0) < length
        valid = valid.astype(F32)
        scale = lax.rsqrt(jnp.sum(projected * projected, axis=-1, keepdims=True) + 1e-06)
        unit = projected * scale
        emb_ref[rows, :] = unit * valid
        cot = cot_ref[rows, :] * valid
        back = scale * (cot - unit * jnp.sum(unit * cot, axis=-1, keepdims=True))
        gp_ref[rows, :] = back.astype(BF16)

    strips(tokens, STRIP, embed)
    pgrad_ref[...] = nn(sec_ref[...].T, gp_ref[...])
    gs_ref[...] = nt(gp_ref[...], proj_ref[...])
    sums_ref[...] = jnp.zeros_like(sums_ref)

    def back(rows):
        grad = gs_ref[rows, :]
        normed = norm_ref[rows, :]
        scaled = grad * vec_ref[1:2, :]
        inside = (
            scaled
            - jnp.mean(scaled, axis=-1, keepdims=True)
            - normed * jnp.mean(scaled * normed, axis=-1, keepdims=True)
        )
        value = inside * inv_ref[rows, 0:1]
        low = value.astype(BF16)
        res_ref[rows, :] = value
        low_ref[rows, :] = low
        fold = lambda v: jnp.sum(v.reshape(STRIP // 8, 8, v.shape[1]), axis=0)
        sums_ref[0:8, :] += fold(grad * normed)
        sums_ref[8:16, :] += fold(grad)
        sums_ref[16:24, :] += fold(low.astype(F32))

    strips(tokens, STRIP, back)
    lowt_ref[...] = low_ref[...].T


def down_both(length, hidden, pieces, first, vec, proj, cot):
    tokens, width = first.shape
    embed = proj.shape[1]
    outs = (
        shaped((tokens, embed), F32),
        shaped((tokens, width), BF16),
        shaped((width, tokens), BF16),
        shaped((tokens, width), F32),
        shaped((width, embed), F32),
        shaped((24, width), F32),
    )
    args = (length, *hidden, first, vec, proj, cot, *pieces)
    return call(
        down_kernel,
        outs,
        args,
        in_specs=[pl.BlockSpec(memory_space=pltpu.SMEM)] + [WHOLE] * 6 + [ANY] * 4,
        scratch=[
            pltpu.VMEM((tokens, width), F32),
            pltpu.VMEM((tokens, width), F32),
            pltpu.VMEM((tokens, width), BF16),
            pltpu.VMEM((tokens, embed), BF16),
            pltpu.VMEM((tokens, width), F32),
            pltpu.VMEM((tokens, LANES), F32),
            pltpu.VMEM((tokens, embed), F32),
            pltpu.VMEM((2, width, hidden[0].shape[1]), BF16),
            pltpu.SemaphoreType.DMA((2, 4)),
        ],
        flops=2 * tokens * width * hidden[0].shape[1] * 2,
    )


def down_grad(g_low_t, hid, swapped):
    width, tokens = g_low_t.shape
    hidden = hid.shape[1]
    block = column_block(hidden)

    def kernel(gt_ref, hid_ref, keep_ref, send_ref):
        split_rows(nn(gt_ref[...], hid_ref[...]).astype(BF16), keep_ref, send_ref, swapped)

    piece = pl.BlockSpec((width // 2, block), lambda i: (0, i))
    out = shaped((width // 2, hidden), BF16)
    return call(
        kernel,
        (out, out),
        (g_low_t, hid),
        grid=(hidden // block,),
        in_specs=[
            pl.BlockSpec((width, tokens), lambda i: (0, 0)),
            pl.BlockSpec((tokens, block), lambda i: (0, i)),
        ],
        out_specs=(piece, piece),
        flops=2 * tokens * width * hidden,
    )


def up_grad(g_low, low_t, slope, down, up, start, swapped):
    tokens, width = g_low.shape
    hidden = slope.shape[1]
    block = column_block(hidden)

    def kernel(
        g_ref, lowt_ref, slope_ref, db_ref, dm_ref, ub_ref, um_ref, start_ref, keep_ref, send_ref,
        bias_ref, first_ref, gh_ref, gin_ref, wd_ref, wu_ref,
    ):
        join_rows(db_ref, dm_ref, wd_ref, swapped)
        join_rows(ub_ref, um_ref, wu_ref, swapped)
        gh_ref[...] = nn(g_ref[...], wd_ref[...])
        bias_ref[...] = jnp.zeros_like(bias_ref)

        def act(rows):
            grad = (gh_ref[rows, :] * slope_ref[rows, :].astype(F32)).astype(BF16)
            gin_ref[rows, :] = grad
            wide = grad.astype(F32)
            bias_ref[...] += jnp.sum(wide.reshape(STRIP // 8, 8, wide.shape[1]), axis=0)

        strips(tokens, STRIP, act)
        split_rows(nn(lowt_ref[...], gin_ref[...]).astype(BF16), keep_ref, send_ref, swapped)
        part = nt(gin_ref[...], wu_ref[...])

        @pl.when(pl.program_id(0) == 0)
        def _():
            first_ref[...] = start_ref[...] + part

        @pl.when(pl.program_id(0) > 0)
        def _():
            first_ref[...] += part

    row = pl.BlockSpec((tokens, width), lambda i: (0, 0))
    turned = pl.BlockSpec((width, tokens), lambda i: (0, 0))
    act = pl.BlockSpec((tokens, block), lambda i: (0, i))
    piece = pl.BlockSpec((width // 2, block), lambda i: (0, i))
    out = shaped((width // 2, hidden), BF16)
    return call(
        kernel,
        (out, out, shaped((8, hidden), F32), shaped((tokens, width), F32)),
        (g_low, low_t, slope, *down, *up, start),
        grid=(hidden // block,),
        in_specs=[row, turned, act, piece, piece, piece, piece, row],
        out_specs=(piece, piece, pl.BlockSpec((8, block), lambda i: (0, i)), row),
        scratch=[
            pltpu.VMEM((tokens, block), F32),
            pltpu.VMEM((tokens, block), BF16),
            pltpu.VMEM((width, block), BF16),
            pltpu.VMEM((width, block), BF16),
        ],
        flops=6 * tokens * width * hidden,
    )


def branch_kernel(
    gf_ref, res_ref, vec_ref, att_ref, qkv_ref, lse_ref, mask_ref, b0_ref, m0_ref, b1_ref, m1_ref,
    gres_ref, gqkv_ref, sums_ref, low_ref, gatt_ref, col_ref, w_ref, sems,
):
    copies = load_weights(
        (b0_ref, m0_ref, b1_ref, m1_ref), w_ref, sems, 3 * att_ref.shape[2], 4 * att_ref.shape[2]
    )
    tokens = gf_ref.shape[0]
    cols = att_ref.shape[2]
    sums_ref[...] = jnp.zeros_like(sums_ref)

    def back(rows):
        value = res_ref[rows, :]
        average = jnp.mean(value, axis=-1, keepdims=True)
        centred = value - average
        inverse = lax.rsqrt(jnp.mean(centred * centred, axis=-1, keepdims=True) + 1e-12)
        normed = centred * inverse
        grad = gf_ref[rows, :]
        scaled = grad * vec_ref[0:1, :]
        inside = (
            scaled
            - jnp.mean(scaled, axis=-1, keepdims=True)
            - normed * jnp.mean(scaled * normed, axis=-1, keepdims=True)
        )
        out = inside * inverse
        low = out.astype(BF16)
        gres_ref[rows, :] = out
        low_ref[rows, :] = low
        fold = lambda v: jnp.sum(v.reshape(STRIP // 8, 8, v.shape[1]), axis=0)
        sums_ref[0:8, :] += fold(grad * normed)
        sums_ref[8:16, :] += fold(grad)
        sums_ref[16:24, :] += fold(low.astype(F32))

    strips(tokens, STRIP, back)
    for copy in copies:
        copy.wait()
    for half in range(2):
        gatt_ref[half] = nn(low_ref[...], w_ref[half]).astype(BF16)

    col_ref[...] = jnp.broadcast_to(mask_ref[...], (LANES, tokens)).T
    lane = lax.broadcasted_iota(jnp.int32, (tokens, LANES), 1) < HD
    pairs = cols // LANES
    scale = BF16(HD ** (-0.5))
    for half in range(2):

        def pair(i, carry, half=half):
            off = pl.multiple_of(i * LANES, LANES)
            off_k = pl.multiple_of(cols + off, LANES)
            off_v = pl.multiple_of(2 * cols + off, LANES)
            query = qkv_ref[half, :, pl.ds(off, LANES)] * scale
            key = qkv_ref[half, :, pl.ds(off_k, LANES)]
            value = qkv_ref[half, :, pl.ds(off_v, LANES)]
            grad = gatt_ref[half, :, pl.ds(off, LANES)]
            att = att_ref[half, :, pl.ds(off, LANES)]
            key_t = (key * scale).T
            delta = (grad.astype(F32) * att.astype(F32)).T
            g_query, g_key, g_value = [], [], []
            for head in range(2):
                pick = lane == (head == 0)
                span = slice(head * HD, (head + 1) * HD)
                zero = jnp.zeros_like(key)
                scores = nt(jnp.where(pick, key, zero), query)
                scores = scores + jnp.concatenate([col_ref[...]] * (tokens // LANES), axis=1)
                probs = jnp.exp(scores - lse_ref[half, pl.ds(i * 2 + head, 1), :])
                g_probs = nt(jnp.where(pick, value, zero), grad)
                row_delta = jnp.sum(delta[span], axis=0, keepdims=True)
                g_scores = (probs * (g_probs - row_delta)).astype(BF16)
                g_value.append(nn(probs.astype(BF16), grad))
                g_key.append(nn(g_scores, query))
                g_query.append(nn(key_t[span], g_scores))
            g_q = jnp.concatenate(g_query, axis=0).T
            gqkv_ref[half, :, pl.ds(off, LANES)] = g_q.astype(BF16)
            gqkv_ref[half, :, pl.ds(off_k, LANES)] = jnp.where(lane, *g_key).astype(BF16)
            gqkv_ref[half, :, pl.ds(off_v, LANES)] = jnp.where(lane, *g_value).astype(BF16)
            return carry

        lax.fori_loop(0, pairs, pair, 0)


def branch_back(g_first, res, vec, att, qkv, lse, mask, pieces):
    tokens, width = g_first.shape
    cols = att.shape[2]
    outs = (
        shaped((tokens, width), F32),
        shaped((2, tokens, 3 * cols), BF16),
        shaped((24, width), F32),
        shaped((tokens, width), BF16),
    )
    return call(
        branch_kernel,
        outs,
        (g_first, res, vec, att, qkv, lse, mask, *pieces),
        in_specs=[WHOLE] * 7 + [ANY] * 4,
        scratch=[
            pltpu.VMEM((2, tokens, cols), BF16),
            pltpu.VMEM((tokens, LANES), F32),
            pltpu.VMEM((2, width, cols), BF16),
            pltpu.SemaphoreType.DMA((2, 4)),
        ],
        flops=8 * tokens * width * width,
    )


def project_back(x_t, g_qkv, g_branch, att, extra):
    width, tokens = x_t.shape
    cols = att.shape[2]
    small = [] if extra is None else [extra]
    columns = 4 * cols + (extra.shape[2] if small else 0)

    def kernel(xt_ref, g_ref, gb_ref, att_ref, *refs):
        outs = refs[len(small) :]
        turned = gb_ref[...].T
        for half in range(2):
            keep, send = outs[2 * half], outs[2 * half + 1]
            span = slice(0, 3 * cols)
            made = nn(xt_ref[...], g_ref[half]).astype(BF16)
            split_rows(made, keep.at[:, span], send.at[:, span], half == 1)
            span = slice(3 * cols, 4 * cols)
            made = nn(turned, att_ref[half]).astype(BF16)
            split_rows(made, keep.at[:, span], send.at[:, span], half == 1)
            if small:
                span = slice(4 * cols, columns)
                made = refs[0][half]
                split_rows(made, keep.at[:, span], send.at[:, span], half == 1)

    out = shaped((width // 2, columns), BF16)
    return call(
        kernel,
        (out, out, out, out),
        (x_t, g_qkv, g_branch, att, *small),
        flops=8 * tokens * width * cols * 2,
    )


def token_back(g_qkv, start, perm, pieces):
    tokens, width = start.shape
    cols = g_qkv.shape[2]

    def kernel(g_ref, start_ref, perm_ref, b0_ref, m0_ref, b1_ref, m1_ref, out_ref, w_ref, sems):
        copies = load_weights((b0_ref, m0_ref, b1_ref, m1_ref), w_ref, sems, 0, cols)
        for copy in copies:
            copy.wait()
        out_ref[...] = start_ref[...] + nt(g_ref[0], w_ref[0]) + nt(g_ref[1], w_ref[1])
        high = out_ref[...].astype(BF16)
        rest = (out_ref[...] - high.astype(F32)).astype(BF16)
        out_ref[...] = nt(high, perm_ref[...]) + nt(rest, perm_ref[...])

    return call(
        kernel,
        shaped((tokens, width), F32),
        (g_qkv, start, perm, *pieces),
        in_specs=[WHOLE] * 3 + [ANY] * 4,
        scratch=[pltpu.VMEM((2, width, cols), BF16), pltpu.SemaphoreType.DMA((2, 4))],
        flops=4 * tokens * width * cols,
    )


class Exchange:
    def __init__(self, size):
        self.size = size
        self.depth = size.bit_length() - 1
        self.rank = lax.axis_index("dp")
        self.core = lax.axis_index("tensor")
        outer = list(range(self.depth - 1, 1, -1))
        self.bits = (outer + [1, 0], outer + [0, 1])

    def flip(self, value, step):
        pairs = []
        for i in range(self.size):
            for core in range(2):
                pairs.append((i * 2 + core, (i ^ (1 << self.bits[core][step])) * 2 + core))
        return lax.ppermute(value, ("dp", "tensor"), pairs)

    def blocks(self):
        tables = []
        for bits in self.bits:
            tables.append(
                [
                    sum(((j >> step) & 1) << bit for step, bit in enumerate(bits))
                    for j in range(self.size)
                ]
            )
        table = np.array(tables, np.int32)
        return jnp.where(self.core == 0, table[0], table[1]) ^ self.rank


def join(held, came):
    return jnp.concatenate([held, came], axis=0)


def added(*values):
    total = values[0].astype(F32)
    for value in values[1:]:
        total = total + value.astype(F32)
    return total


def halves(value):
    middle = value.shape[0] // 2
    return value[:middle], value[middle:]


def three_parts(value):
    high = lax.reduce_precision(value, 8, 7)
    rest = value - high
    middle = lax.reduce_precision(rest, 8, 7)
    return (high.astype(BF16), middle.astype(BF16), (rest - middle).astype(BF16))


def body(
    tokens,
    lengths,
    key_mask,
    order,
    query_key_value_weight,
    output_projection_weight,
    up_projection_weight,
    down_projection_weight,
    embedding_projection_weight,
    gains,
    biases,
    up_bias_vector,
    cotangent,
):
    size = lax.axis_size("dp")
    core = lax.axis_index("tensor")
    ways = Exchange(size)
    depth = ways.depth
    half_len = tokens.shape[1]
    full_len = key_mask.shape[1]
    width = tokens.shape[2]
    cols = output_projection_weight.shape[0]
    rows = output_projection_weight.shape[1]
    ff_local = up_projection_weight.shape[1]
    chunk = gains.shape[1]
    emb_size = embedding_projection_weight.size
    sides = (core, 1 - core)

    vector = jnp.concatenate([gains.reshape(-1), biases.reshape(-1), up_bias_vector])
    pad_to = -(-vector.size // 128) * 128
    vector_size = vector.size
    vector = jnp.pad(vector, (0, pad_to - vector_size))
    flat = jnp.concatenate([embedding_projection_weight.reshape(-1), *three_parts(vector)])
    extra = -(-flat.size // (rows * 128)) * 128
    flat = jnp.pad(flat, (0, rows * extra - flat.size)).reshape(rows, extra)
    one = jnp.concatenate(
        [
            query_key_value_weight[0],
            query_key_value_weight[1],
            query_key_value_weight[2],
            output_projection_weight.T,
            flat,
        ],
        axis=1,
    )
    two = up_projection_weight
    three = down_projection_weight.T

    mine = order[0, core]
    theirs = order[0, 1 - core]
    my_half = lax.dynamic_index_in_dim(tokens, mine, 0, keepdims=False)
    their_half = lax.dynamic_index_in_dim(tokens, theirs, 0, keepdims=False)
    for step in range(depth - 2):
        if step == 0:
            one_came, half_came = together(ways.flip(one, step), swap_cores(their_half))
        else:
            one_came = ways.flip(one, step)
        one = join(one, one_came)
    for step in range(depth - 3):
        two = join(two, ways.flip(two, step))
    one_came, two_came = together(ways.flip(one, depth - 2), ways.flip(two, depth - 3))
    one_both = join(one, one_came)
    two = join(two, two_came)
    for step in range(depth - 3):
        three = join(three, ways.flip(three, step))
    one_more, three_came = together(ways.flip(one_both, depth - 1), ways.flip(three, depth - 3))
    three = join(three, three_came)
    one_both_other, one_more_other, two_came = together(
        swap_cores(one_both), swap_cores(one_more), ways.flip(two, depth - 2)
    )
    two_both = join(two, two_came)
    one_pieces = (one_both, one_more, one_both_other, one_more_other)

    def in_order(own, other):
        return jnp.where(
            core == 0, jnp.concatenate([own, other]), jnp.concatenate([other, own])
        )

    def half_of(value, which):
        return lax.dynamic_slice_in_dim(value, which * half_len, half_len)

    here = in_order(my_half, half_came)
    seq_len = lengths[mine]
    marks = lax.dynamic_index_in_dim(key_mask, mine, 0, keepdims=False)
    places = jnp.arange(full_len, dtype=jnp.int32)
    key_ok = (places < seq_len) & ((marks == 1) | (places == 0))
    mask = jnp.where(key_ok, 0.0, -1e30).astype(F32)[None, :]
    blocks = ways.blocks()
    where = (blocks[:, None] * rows + jnp.arange(rows, dtype=jnp.int32)[None]).reshape(-1)
    perm = (jnp.arange(width, dtype=jnp.int32)[:, None] == where[None]).astype(BF16)

    wide = 4 * cols
    quarter = width // 4
    small_own = jnp.concatenate([one_both[:, wide:], one_more[:, wide:]])
    small_other = jnp.concatenate(
        [
            one_both_other[:quarter, wide:],
            one_more_other[:quarter, wide:],
            one_both_other[quarter:, wide:],
            one_more_other[quarter:, wide:],
        ]
    )
    small = [part.reshape(size, rows * extra) for part in (small_own, small_other)]
    small = jnp.where(core == 0, jnp.stack(small, 1), jnp.stack(small[::-1], 1))
    proj = small[:, :, :emb_size].reshape(width, -1)
    thirds = small[:, :, emb_size : emb_size + 3 * pad_to].astype(F32)
    thirds = thirds.reshape(size, 2, 3, pad_to)
    vectors = thirds[:, :, 0] + (thirds[:, :, 1] + thirds[:, :, 2])
    places_of = jnp.argsort(blocks)
    plain = vectors[places_of].reshape(size * 2, pad_to)
    vectors = vectors.reshape(size * 2, pad_to)
    vec = jnp.moveaxis(vectors[:, : 8 * chunk].reshape(-1, 8, chunk), 1, 0).reshape(8, width)
    query_bias = plain[:, 2 * chunk : 3 * chunk].reshape(-1)
    value_bias = plain[:, 3 * chunk : 4 * chunk].reshape(-1)
    up_bias = plain[:, 8 * chunk : vector_size].reshape(-1)
    head_bias, side_bias = [], []
    for side in sides:
        query_part = lax.dynamic_slice_in_dim(query_bias, side * cols, cols)
        value_part = lax.dynamic_slice_in_dim(value_bias, side * cols, cols)
        head_bias.append(jnp.concatenate([query_part, jnp.zeros_like(query_part), value_part]))
        side_bias.append(lax.dynamic_slice_in_dim(up_bias, side * ff_local, ff_local)[None])
    head_bias = jnp.stack(head_bias)

    two_more, three_came = ways.flip(two_both, depth - 1), ways.flip(three, depth - 2)
    qkv, lse, att, res_one, first, first_low, first_low_t, here_t = attention_forward(
        after(here, two_both, three), perm, head_bias, mask, vec, one_pieces, cols
    )
    two_more, three_came = after((two_more, three_came), first_low)
    three_both = join(three, three_came)
    three_more = ways.flip(three_both, depth - 1)
    two_both_other, two_more_other = swap_cores(two_both), swap_cores(two_more)
    hid_own, slope_own = up_forward(
        after(first_low, three_both, two_more), (two_both, two_more), side_bias[0], False
    )
    two_both_other, two_more_other = after((two_both_other, two_more_other), hid_own)
    hid_other, slope_other = up_forward(
        first_low, (two_both_other, two_more_other), side_bias[1], True
    )
    three_more = after(three_more, hid_other)
    cot_mine = lax.dynamic_index_in_dim(cotangent, core, 0, keepdims=False)
    cot_other = lax.dynamic_index_in_dim(cotangent, 1 - core, 0, keepdims=False)
    three_both_other, three_more_other, cot_came = together(
        swap_cores(three_both), swap_cores(three_more), swap_cores(cot_other)
    )
    cot = in_order(cot_mine, cot_came)
    emb, g_ffn, g_ffn_t, g_res_two, proj_grad, sums_two = down_both(
        seq_len[None],
        (hid_own, hid_other),
        (three_both, three_more, three_both_other, three_more_other),
        first,
        vec,
        proj,
        cot,
    )

    def low(*values):
        return added(*values).astype(BF16)

    dk_other, ds_other = down_grad(g_ffn_t, hid_other, True)
    ds_came, dk_came = swap_cores(ds_other), swap_cores(dk_other)
    dk, ds = down_grad(g_ffn_t, after(hid_own, ds_other), False)
    ds_came, dk_came = after((ds_came, dk_came), ds)
    d_sent = low(ds, ds_came)
    d_came = ways.flip(d_sent, depth - 1)
    uk_other, us_other, up_bias_other, part = up_grad(
        after(g_ffn, d_sent),
        first_low_t,
        slope_other,
        (three_both_other, three_more_other),
        (two_both_other, two_more_other),
        g_res_two,
        True,
    )
    us_came, uk_came = swap_cores(us_other), swap_cores(uk_other)
    uk, us, up_bias_own, g_first = up_grad(
        after(g_ffn, us_other),
        first_low_t,
        slope_own,
        (three_both, three_more),
        (two_both, two_more),
        part,
        False,
    )
    d_came, us_came, uk_came = after((d_came, us_came, uk_came), us)
    u_sent = low(us, us_came)
    d_kept, d_sent = halves(dk), low(halves(dk)[1], halves(dk_came)[1], halves(d_came)[1])
    u_came = ways.flip(u_sent, depth - 1)
    d_held = added(halves(dk)[0], halves(dk_came)[0], halves(d_came)[0])
    d_came = ways.flip(d_sent, depth - 2)
    g_res_one, g_qkv, sums_one, g_branch = branch_back(
        after(g_first, u_sent, d_sent), res_one, vec, att, qkv, lse, mask, one_pieces
    )
    d_came, u_came = after((d_came, u_came), g_qkv)
    u_sent = low(halves(uk)[1], halves(uk_came)[1], halves(u_came)[1])
    u_held = added(halves(uk)[0], halves(uk_came)[0], halves(u_came)[0])
    u_came = ways.flip(u_sent, depth - 2)
    d_held = d_held + d_came.astype(F32)
    held, sent = halves(d_held)
    d_sent = sent.astype(BF16)
    d_came = ways.flip(d_sent, depth - 3)

    def fold(value):
        return jnp.sum(value.reshape(-1, 8, value.shape[-1]), axis=1)

    def absolute(own, other):
        return jnp.where(
            core == 0, jnp.concatenate([own, other]), jnp.concatenate([other, own])
        )

    gain_two, shift_two, ffn_bias_grad = fold(sums_two)
    gain_one, shift_one, out_bias_grad = fold(sums_one)
    up_bias_grad = absolute(fold(up_bias_own)[0], fold(up_bias_other)[0])
    qkv_bias_grads = jnp.sum(g_qkv.astype(F32), axis=1)
    query_bias_grad = absolute(qkv_bias_grads[0][:cols], qkv_bias_grads[1][:cols])
    value_bias_grad = absolute(qkv_bias_grads[0][2 * cols :], qkv_bias_grads[1][2 * cols :])

    def relative(value):
        return value.reshape(size, 2, -1)[blocks]

    small_grads = jnp.concatenate(
        [
            proj_grad.reshape(size, 2, emb_size),
            gain_one.reshape(size, 2, chunk),
            gain_two.reshape(size, 2, chunk),
            relative(query_bias_grad),
            relative(value_bias_grad),
            out_bias_grad.reshape(size, 2, chunk),
            shift_one.reshape(size, 2, chunk),
            ffn_bias_grad.reshape(size, 2, chunk),
            shift_two.reshape(size, 2, chunk),
            relative(up_bias_grad),
        ],
        axis=2,
    ).astype(BF16)
    small_grads = jnp.pad(small_grads, ((0, 0), (0, 0), (0, rows * extra - small_grads.shape[2])))
    small_grads = jnp.where(core == 0, small_grads, small_grads[:, ::-1])
    small_grads = jnp.moveaxis(small_grads, 1, 0).reshape(2, width, extra)

    qk, qs, qk_other, qs_other = project_back(
        after(here_t, u_sent, d_sent), g_qkv, g_branch, att, small_grads
    )
    d_came, u_came = after((d_came, u_came), qs)
    d_held = held + d_came.astype(F32)
    u_held = u_held + u_came.astype(F32)
    qs_came, qk_came = swap_cores(qs_other), swap_cores(qk_other)
    g_here = token_back(after(g_qkv, qs_other, d_held), g_res_one, perm, one_pieces)
    qs_came, qk_came = after((qs_came, qk_came), g_here)
    q_sent = low(qs, qs_came)
    q_came = ways.flip(q_sent, depth - 1)

    def outer(value, steps):
        for step in range(steps - 1, -1, -1):
            kept, sent = halves(value)
            value = kept + ways.flip(sent.astype(BF16), step).astype(F32)
        return value

    down_shard = outer(d_held, depth - 3)
    up_shard = outer(u_held, depth - 2)
    q_sent = low(halves(qk)[1], halves(qk_came)[1], halves(q_came)[1])
    q_held = added(halves(qk)[0], halves(qk_came)[0], halves(q_came)[0])
    q_held = q_held + ways.flip(q_sent, depth - 2).astype(F32)
    one_shard = outer(q_held, depth - 2)

    qkv_shard = jnp.stack([one_shard[:, i * cols : (i + 1) * cols] for i in range(3)])
    out_shard = one_shard[:, 3 * cols : wide].T
    tail = one_shard[:, wide:].reshape(-1)
    emb_shard = tail[:emb_size].reshape(embedding_projection_weight.shape)
    tail = tail[emb_size:]
    gain_shard = tail[: 2 * chunk].reshape(2, chunk)
    bias_shard = tail[2 * chunk : 8 * chunk].reshape(6, chunk)
    up_bias_shard = tail[8 * chunk : vector_size]

    def give_back(value, places_of):
        own = half_of(value, core)
        other = swap_cores(half_of(value, 1 - core))
        blank = jnp.zeros((2,) + own.shape, value.dtype)
        blank = lax.dynamic_update_slice(blank, own[None], (places_of[0], 0, 0))
        return lax.dynamic_update_slice(blank, other[None], (places_of[1], 0, 0))

    embeddings = give_back(emb, (core, 1 - core))
    grad_tokens = give_back(g_here, (mine, theirs))
    return (
        embeddings,
        grad_tokens,
        qkv_shard,
        out_shard,
        up_shard,
        down_shard.T,
        emb_shard,
        gain_shard,
        bias_shard,
        up_bias_shard,
    )


def solution(mesh):
    return jax.shard_map(
        body,
        mesh=mesh,
        in_specs=(
            P("dp", "tensor", None),
            P("dp"),
            P("dp", None),
            P("dp", None),
            P(None, "dp", "tensor"),
            P("tensor", "dp"),
            P("dp", "tensor"),
            P("tensor", "dp"),
            P(("dp", "tensor"), None),
            P(None, ("dp", "tensor")),
            P(None, ("dp", "tensor")),
            P(("dp", "tensor")),
            P("dp", "tensor", None),
        ),
        out_specs=(
            P("dp", "tensor", None),
            P("dp", "tensor", None),
            P(None, "dp", "tensor"),
            P("tensor", "dp"),
            P("dp", "tensor"),
            P("tensor", "dp"),
            P(("dp", "tensor"), None),
            P(None, ("dp", "tensor")),
            P(None, ("dp", "tensor")),
            P(("dp", "tensor")),
        ),
        check_vma=False,
    )
```

profile of v0, /device:TPU:0, one launch (start us, length us, event | category | flops | bytes accessed | tf_op | source)
XLA Modules:
  0.0 320.4 jit_solution(18342304459555206972)
XLA Ops:
  8.1 3.7 %collective-permute-start = (bf16[48,1664]{1,0:T(8,128)(2,1)S(1)}, bf16[48,1664]{1,0:T(8,128)(2,1)S(1)}, u32[]{:S(2)}, u32[]{:S(2)}) collective-permute-start(bf16[48,1664]{1,0:T(8,128)(2,1)S(1)} %constant_dynamic-update-slice_fusion), channel_id=1, source_target_pairs={{0,16},{1,17},{2,18},{3,19},{4,20},{5,21},{6,22},{7,23},{8,24},{9,... | collective-permute-start | bytes 479240 | tf_op jit(solution)/shard_map/ppermute | solution.py:593
  11.8 8.2 %collective-permute-done = bf16[48,1664]{1,0:T(8,128)(2,1)S(1)} collective-permute-done((bf16[48,1664]{1,0:T(8,128)(2,1)S(1)}, bf16[48,1664]{1,0:T(8,128)(2,1)S(1)}, u32[]{:S(2)}, u32[]{:S(2)}) %collective-permute-start) | collective-permute-done | bytes 159776 | tf_op jit(solution)/shard_map/ppermute | solution.py:593
  21.4 3.4 %collective-permute-start.2 = (bf16[48,1536]{1,0:T(8,128)(2,1)S(1)}, bf16[48,1536]{1,0:T(8,128)(2,1)S(1)}, u32[]{:S(2)}, u32[]{:S(2)}) collective-permute-start(bf16[48,1536]{1,0:T(8,128)(2,1)S(1)} %copy-done.6), channel_id=1, source_target_pairs={{0,16},{1,17},{2,18},{3,19},{4,20},{5,21},{6,22},{7,23},{8,24},{9,... | collective-permute-start | bytes 442376 | tf_op jit(solution)/shard_map/ppermute | solution.py:593
  24.9 11.5 %collective-permute-done.3 = bf16[96,1664]{1,0:T(8,128)(2,1)S(1)} collective-permute-done((bf16[96,1664]{1,0:T(8,128)(2,1)S(1)}, bf16[96,1664]{1,0:T(8,128)(2,1)S(1)}, u32[]{:S(2)}, u32[]{:S(2)}) %collective-permute-start.3) | collective-permute-done | bytes 319520 | tf_op jit(solution)/shard_map/ppermute | solution.py:593
  36.4 1.4 collective-permute-start.4
  39.7 5.6 %collective-permute-done.5 = bf16[96,1536]{1,0:T(8,128)(2,1)S(1)} collective-permute-done((bf16[96,1536]{1,0:T(8,128)(2,1)S(1)}, bf16[96,1536]{1,0:T(8,128)(2,1)S(1)}, u32[]{:S(2)}, u32[]{:S(2)}) %collective-permute-start.5) | collective-permute-done | bytes 294944 | tf_op jit(solution)/shard_map/ppermute | solution.py:593
  47.0 1.4 collective-permute-start.7
  51.2 1.5 fusion.perm_ref
  52.7 4.2 %collective-permute-done.9 = bf16[96,1536]{1,0:T(8,128)(2,1)} collective-permute-done((bf16[96,1536]{1,0:T(8,128)(2,1)}, bf16[96,1536]{1,0:T(8,128)(2,1)}, u32[]{:S(2)}, u32[]{:S(2)}) %collective-permute-start.9) | collective-permute-done | bytes 294944 | tf_op jit(solution)/shard_map/ppermute | solution.py:593
  56.9 7.4 %collective-permute-done.7.m0_ref = bf16[384,1664]{1,0:T(8,128)(2,1)S(1)} collective-permute-done((bf16[384,1664]{1,0:T(8,128)(2,1)S(1)}, bf16[384,1664]{1,0:T(8,128)(2,1)S(1)}, u32[]{:S(2)}, u32[]{:S(2)}) %collective-permute-start.7) | collective-permute-done | bytes 1277984 | tf_op jit(solution)/shard_map/ppermute | solution.py:593
  64.3 1.9 and_select_fusion.mask_ref
  71.3 1.8 pad_maximum_fusion.4
  73.8 5.5 %collective-permute-done.11 = bf16[192,1536]{1,0:T(8,128)(2,1)} collective-permute-done((bf16[192,1536]{1,0:T(8,128)(2,1)}, bf16[192,1536]{1,0:T(8,128)(2,1)}, u32[]{:S(2)}, u32[]{:S(2)}) %collective-permute-start.11) | collective-permute-done | bytes 589856 | tf_op jit(solution)/shard_map/ppermute | solution.py:593
  79.2 1.9 constant_dynamic-update-slice_fusion.1.both_ref.ub_ref
  87.2 19.5 %shard_map.222 = (bf16[2,512,1152]{2,1,0:T(8,128)(2,1)}, f32[2,6,512]{2,1,0:T(8,128)}, bf16[2,512,384]{2,1,0:T(8,128)(2,1)}, f32[512,768]{1,0:T(8,128)}, f32[512...) custom-call(bf16[512,768]{1,0:T(8,128)(2,1)} %maximum_select_fusion.x_ref, ...), custom_call_target="tpu_custom_call" | custom-call | flops 2415919104 | bytes 1048576 | tf_op jit(solution)/shard_map/pallas_call | solution.py:47
  111.2 7.2 %shard_map.223 = (bf16[512,1536]{1,0:T(8,128)(2,1)}, bf16[512,1536]{1,0:T(8,128)(2,1)}) custom-call(bf16[512,768]{1,0:T(8,128)(2,1)} %get-tuple-element.99.low_ref, bf16[384,1536]{1,0:T(8,128)(2,1)} %constant_dynamic-update-slice_fusion.1.both_ref.ub_ref, bf16[384,1536]{1,0:T(8,128)(2,1)} %collective-permute-done.12.more_ref.um_ref, ...), custom_call_target="tpu_custom_call" | custom-call | flops 1207959552 | bytes 1048576 | tf_op jit(solution)/shard_map/pallas_call | solution.py:47
  118.5 7.3 %shard_map.224 = (bf16[512,1536]{1,0:T(8,128)(2,1)}, bf16[512,1536]{1,0:T(8,128)(2,1)}) custom-call(bf16[512,768]{1,0:T(8,128)(2,1)} %get-tuple-element.99.low_ref, bf16[384,1536]{1,0:T(8,128)(2,1)} %collective-permute-done.14.both_ref.ub_ref, bf16[384,1536]{1,0:T(8,128)(2,1)} %collective-permute-done.15.more_ref.um_ref, f32[1,1536]{1,0:T(1,128)} %broadcast_in_dim.49.bias_ref), custom_call_target="tpu_custom_call" | custom-call | flops 1207959552 | bytes 1048576 | tf_op jit(solution)/shard_map/pallas_call | solution.py:47
  129.8 14.8 %shard_map.225 = (f32[512,128]{1,0:T(8,128)}, bf16[512,768]{1,0:T(8,128)(2,1)}, bf16[768,512]{1,0:T(8,128)(2,1)}, f32[512,768]{1,0:T(8,128)}, f32[768,128]{1,0:T(8,128)}, /*index=5*/f32[24,768]{1,0:T(8,128)}) custom-call(s32[1]{0:T(128)} %dynamic_slice.58.len_ref, bf16[512,1536]{1,0:T(8,128)(2,1)} %get-tuple-element.113.h0_ref.hid_ref, ...), custom_call_target="tpu_custom_call" | custom-call | flops 2415919104 | bytes 1048576 | tf_op jit(solution)/shard_map/pallas_call | solution.py:47
  144.6 4.7 %shard_map.226 = (bf16[384,1536]{1,0:T(8,128)(2,1)}, bf16[384,1536]{1,0:T(8,128)(2,1)}) custom-call(bf16[768,512]{1,0:T(8,128)(2,1)} %get-tuple-element.111.gt_ref, bf16[512,1536]{1,0:T(8,128)(2,1)} %get-tuple-element.103.h1_ref.hid_ref), custom_call_target="tpu_custom_call" | custom-call | flops 1207959552 | bytes 1048576 | tf_op jit(solution)/shard_map/pallas_call | solution.py:47
  149.9 4.5 %shard_map.227 = (bf16[384,1536]{1,0:T(8,128)(2,1)}, bf16[384,1536]{1,0:T(8,128)(2,1)}) custom-call(bf16[768,512]{1,0:T(8,128)(2,1)} %get-tuple-element.111.gt_ref, bf16[512,1536]{1,0:T(8,128)(2,1)} %get-tuple-element.113.h0_ref.hid_ref), custom_call_target="tpu_custom_call" | custom-call | flops 1207959552 | bytes 1048576 | tf_op jit(solution)/shard_map/pallas_call | solution.py:47
  155.4 1.5 add_convert_fusion.2
  157.0 11.0 %shard_map.228 = (bf16[384,1536]{1,0:T(8,128)(2,1)}, bf16[384,1536]{1,0:T(8,128)(2,1)}, f32[8,1536]{1,0:T(8,128)}, f32[512,768]{1,0:T(8,128)}) custom-call(bf16[512,768]{1,0:T(8,128)(2,1)} %get-tuple-element.122.g_ref, bf16[768,512]{1,0:T(8,128)(2,1)} %get-tuple-element.118.lowt_ref, bf16[512,1536]{1,0:T(8,128)(2,1)} %get-tuple-element.119.slope_ref, ...), custom_call_target="tpu_custom_call" | custom-call | flops 3623878656 | bytes 1048576 | tf_op jit(solution)/shard_map/pallas_call | solution.py:47
  170.7 1.7 reshape.168
  172.4 1.6 copy.32
  175.6 1.4 reshape_unstack.28
  180.4 11.0 %shard_map.229 = (bf16[384,1536]{1,0:T(8,128)(2,1)}, bf16[384,1536]{1,0:T(8,128)(2,1)}, f32[8,1536]{1,0:T(8,128)}, f32[512,768]{1,0:T(8,128)}) custom-call(bf16[512,768]{1,0:T(8,128)(2,1)} %get-tuple-element.122.g_ref, bf16[768,512]{1,0:T(8,128)(2,1)} %get-tuple-element.118.lowt_ref, bf16[512,1536]{1,0:T(8,128)(2,1)} %get-tuple-element.123.slope_ref, ...), custom_call_target="tpu_custom_call" | custom-call | flops 3623878656 | bytes 1048576 | tf_op jit(solution)/shard_map/pallas_call | solution.py:47
  191.3 1.4 reduce_sum.48
  194.1 1.4 reduce_sum.49
  196.9 1.4 maximum_select_fusion.5
  198.3 2.0 gather_fusion.3
  201.6 2.0 add_convert_fusion.1
  204.0 2.1 add_convert_fusion.5
  206.1 1.5 collective-permute-start.26
  208.2 17.1 %shard_map.230 = (f32[512,768]{1,0:T(8,128)}, bf16[2,512,1152]{2,1,0:T(8,128)(2,1)}, f32[24,768]{1,0:T(8,128)}, bf16[512,768]{1,0:T(8,128)(2,1)}) custom-call(f32[512,768]{1,0:T(8,128)} %get-tuple-element.132.gf_ref, f32[512,768]{1,0:T(8,128)} %get-tuple-element.133.res_ref, f32[8,768]{1,0:T(8,128)} %reshape.165.vec_ref, ...), custom_call_target="tpu_custom_call" | custom-call | flops 2415919104 | bytes 1048576 | tf_op jit(solution)/shard_map/pallas_call | solution.py:47
  225.4 2.1 convert_reduce_fusion
  231.8 1.9 convert_add_fusion.2
  233.7 2.1 add_convert_fusion.4
  235.8 7.6 %shard_map.231 = (bf16[384,1664]{1,0:T(8,128)(2,1)}, bf16[384,1664]{1,0:T(8,128)(2,1)}, bf16[384,1664]{1,0:T(8,128)(2,1)}, bf16[384,1664]{1,0:T(8,128)(2,1)}) custom-call(bf16[768,512]{1,0:T(8,128)(2,1)} %get-tuple-element.143.xt_ref, bf16[2,512,1152]{2,1,0:T(8,128)(2,1)} %get-tuple-element.153.g_ref, bf16[512,768]{1,0:T(8,128)(2,1)} %get-tuple-element.144.gb_ref, ...), custom_call_target="tpu_custom_call" | custom-call | flops 2415919104 | bytes 1048576 | tf_op jit(solution)/shard_map/pallas_call | solution.py:47
  245.1 9.1 %collective-permute-done.28 = bf16[96,1536]{1,0:T(8,128)(2,1)} collective-permute-done((bf16[96,1536]{1,0:T(8,128)(2,1)S(1)}, bf16[96,1536]{1,0:T(8,128)(2,1)}, u32[]{:S(2)}, u32[]{:S(2)}) %collective-permute-start.28) | collective-permute-done | bytes 294944 | tf_op jit(solution)/shard_map/ppermute | solution.py:593
  256.1 11.3 %shard_map.232 = f32[512,768]{1,0:T(8,128)} custom-call(bf16[2,512,1152]{2,1,0:T(8,128)(2,1)} %get-tuple-element.153.g_ref, f32[512,768]{1,0:T(8,128)} %get-tuple-element.154.start_ref, bf16[768,768]{1,0:T(8,128)(2,1)} %fusion.perm_ref, bf16[384,1664]{1,0:T(8,128)(2,1)} %copy-done, bf16[384,1664]{1,0:T(8,128)(2,1)} %copy-done.2, ...), custom_call_target="tpu_custom_call" | custom-call | flops 1811939328 | bytes 1048576 | tf_op jit(solution)/shard_map/pallas_call | solution.py:47
  267.4 3.2 add_convert_fusion
  274.7 1.7 convert_add_fusion.1
  276.5 2.5 collective-permute-start.37
  279.3 8.8 %collective-permute-done.33 = bf16[384,1664]{1,0:T(8,128)(2,1)} collective-permute-done((bf16[384,1664]{1,0:T(8,128)(2,1)}, bf16[384,1664]{1,0:T(8,128)(2,1)}, u32[]{:S(2)}, u32[]{:S(2)}) %collective-permute-start.33) | collective-permute-done | bytes 1277984 | tf_op jit(solution)/shard_map/ppermute | solution.py:593
  292.3 7.7 %collective-permute-done.34 = bf16[192,1664]{1,0:T(8,128)(2,1)S(1)} collective-permute-done((bf16[192,1664]{1,0:T(8,128)(2,1)S(1)}, bf16[192,1664]{1,0:T(8,128)(2,1)S(1)}, u32[]{:S(2)}, u32[]{:S(2)}) %collective-permute-start.34) | collective-permute-done | bytes 639008 | tf_op jit(solution)/shard_map/ppermute | solution.py:593
  302.5 6.0 %collective-permute-done.35 = bf16[96,1664]{1,0:T(8,128)(2,1)S(1)} collective-permute-done((bf16[96,1664]{1,0:T(8,128)(2,1)S(1)}, bf16[96,1664]{1,0:T(8,128)(2,1)S(1)}, u32[]{:S(2)}, u32[]{:S(2)}) %collective-permute-start.35) | collective-permute-done | bytes 319520 | tf_op jit(solution)/shard_map/ppermute | solution.py:593
  308.6 2.1 collective-permute-start.36
  310.8 5.8 %collective-permute-done.36 = bf16[48,1664]{1,0:T(8,128)(2,1)S(1)} collective-permute-done((bf16[48,1664]{1,0:T(8,128)(2,1)S(1)}, bf16[48,1664]{1,0:T(8,128)(2,1)S(1)}, u32[]{:S(2)}, u32[]{:S(2)}) %collective-permute-start.36) | collective-permute-done | bytes 159776 | tf_op jit(solution)/shard_map/ppermute | solution.py:593
  (277 shorter events, 68.4 us)
Async XLA Ops:
  4.6 16.8 %copy-start.6 = (bf16[48,1536]{1,0:T(8,128)(2,1)S(1)}, bf16[48,1536]{1,0:T(8,128)(2,1)}, u32[]{:S(2)}) copy-start(bf16[48,1536]{1,0:T(8,128)(2,1)} %param.21) | copy-start | bytes 442372
  5.3 19.5 %copy-start.5 = (bf16[1536,48]{0,1:T(8,128)(2,1)S(1)}, bf16[1536,48]{0,1:T(8,128)(2,1)}, u32[]{:S(2)}) copy-start(bf16[1536,48]{0,1:T(8,128)(2,1)} %param.22) | copy-start | bytes 442372
  7.2 12.7 %collective-permute-start.1 = (bf16[256,768]{1,0:T(8,128)(2,1)S(1)}, bf16[256,768]{1,0:T(8,128)(2,1)S(1)}, u32[]{:S(2)}, u32[]{:S(2)}) collective-permute-start(bf16[256,768]{1,0:T(8,128)(2,1)S(1)} %get-tuple-element.177), channel_id=1, source_target_pairs={{0,1},{1,0},{2,3},{3,2},{4,5},{5,4},{6,7},{7,6},{8,9},{9,8},{10,11... | collective-permute-start | bytes 1179656 | tf_op jit(solution)/shard_map/ppermute | solution.py:26
  7.8 30.2 %copy-start.38 = (s32[16]{0:T(128)S(1)}, s32[16]{0:T(128)}, u32[]{:S(2)}) copy-start(s32[16]{0:T(128)} %constant.65.clone) | copy-start | bytes 196
  7.8 30.2 %copy-start.39 = (s32[16]{0:T(128)S(1)}, s32[16]{0:T(128)}, u32[]{:S(2)}) copy-start(s32[16]{0:T(128)} %constant.66.clone) | copy-start | bytes 196
  8.1 11.9 %collective-permute-start = (bf16[48,1664]{1,0:T(8,128)(2,1)S(1)}, bf16[48,1664]{1,0:T(8,128)(2,1)S(1)}, u32[]{:S(2)}, u32[]{:S(2)}) collective-permute-start(bf16[48,1664]{1,0:T(8,128)(2,1)S(1)} %constant_dynamic-update-slice_fusion), channel_id=1, source_target_pairs={{0,16},{1,17},{2,18},{3,19},{4,20},{5,21},{6,22},{7,23},{8,24},{9,... | collective-permute-start | bytes 479240 | tf_op jit(solution)/shard_map/ppermute | solution.py:593
  20.7 15.7 %collective-permute-start.3 = (bf16[96,1664]{1,0:T(8,128)(2,1)S(1)}, bf16[96,1664]{1,0:T(8,128)(2,1)S(1)}, u32[]{:S(2)}, u32[]{:S(2)}) collective-permute-start(bf16[96,1664]{1,0:T(8,128)(2,1)S(1)} %pad_maximum_fusion.5), channel_id=1, source_target_pairs={{0,8},{1,9},{2,10},{3,11},{4,12},{5,13},{6,14},{7,15},{8,0},{9,1},... | collective-permute-start | bytes 958472 | tf_op jit(solution)/shard_map/ppermute | solution.py:593
  21.4 16.4 %collective-permute-start.2 = (bf16[48,1536]{1,0:T(8,128)(2,1)S(1)}, bf16[48,1536]{1,0:T(8,128)(2,1)S(1)}, u32[]{:S(2)}, u32[]{:S(2)}) collective-permute-start(bf16[48,1536]{1,0:T(8,128)(2,1)S(1)} %copy-done.6), channel_id=1, source_target_pairs={{0,16},{1,17},{2,18},{3,19},{4,20},{5,21},{6,22},{7,23},{8,24},{9,... | collective-permute-start | bytes 442376 | tf_op jit(solution)/shard_map/ppermute | solution.py:593
  24.8 24.3 %collective-permute-start.8 = (bf16[48,1536]{1,0:T(8,128)(2,1)S(1)}, bf16[48,1536]{1,0:T(8,128)(2,1)S(1)}, u32[]{:S(2)}, u32[]{:S(2)}) collective-permute-start(bf16[48,1536]{1,0:T(8,128)(2,1)S(1)} %bitcast.57), channel_id=1, source_target_pairs={{0,16},{1,17},{2,18},{3,19},{4,20},{5,21},{6,22},{7,23},{8,24},{9,... | collective-permute-start | bytes 442376 | tf_op jit(solution)/shard_map/ppermute | solution.py:593
  36.4 10.5 %collective-permute-start.4 = (bf16[192,1664]{1,0:T(8,128)(2,1)S(1)}, bf16[192,1664]{1,0:T(8,128)(2,1)S(1)}, u32[]{:S(2)}, u32[]{:S(2)}) collective-permute-start(bf16[192,1664]{1,0:T(8,128)(2,1)S(1)} %pad_maximum_fusion.2), channel_id=1, source_target_pairs={{0,4},{1,3},{2,6},{3,1},{4,0},{5,7},{6,2},{7,5},{8,12},{9,11},{10,... | collective-permute-start | bytes 1916936 | tf_op jit(solution)/shard_map/ppermute | solution.py:593
  37.9 7.5 %collective-permute-start.5 = (bf16[96,1536]{1,0:T(8,128)(2,1)S(1)}, bf16[96,1536]{1,0:T(8,128)(2,1)S(1)}, u32[]{:S(2)}, u32[]{:S(2)}) collective-permute-start(bf16[96,1536]{1,0:T(8,128)(2,1)S(1)} %pad_maximum_fusion.6), channel_id=1, source_target_pairs={{0,8},{1,9},{2,10},{3,11},{4,12},{5,13},{6,14},{7,15},{8,0},{9,1},... | collective-permute-start | bytes 884744 | tf_op jit(solution)/shard_map/ppermute | solution.py:593
  47.0 21.2 %copy-start = (bf16[384,1664]{1,0:T(8,128)(2,1)}, bf16[384,1664]{1,0:T(8,128)(2,1)S(1)}, u32[]{:S(2)}) copy-start(bf16[384,1664]{1,0:T(8,128)(2,1)S(1)} %pad_maximum_fusion.b0_ref) | copy-start | bytes 3833860
  47.0 17.3 %collective-permute-start.7 = (bf16[384,1664]{1,0:T(8,128)(2,1)S(1)}, bf16[384,1664]{1,0:T(8,128)(2,1)S(1)}, u32[]{:S(2)}, u32[]{:S(2)}) collective-permute-start(bf16[384,1664]{1,0:T(8,128)(2,1)S(1)} %pad_maximum_fusion.b0_ref), channel_id=1, source_target_pairs={{0,2},{1,5},{2,0},{3,7},{4,6},{5,1},{6,4},{7,3},{8,10},{9,13},{10,... | collective-permute-start | bytes 3833864 | tf_op jit(solution)/shard_map/ppermute | solution.py:593
  49.9 7.0 %collective-permute-start.9 = (bf16[96,1536]{1,0:T(8,128)(2,1)}, bf16[96,1536]{1,0:T(8,128)(2,1)}, u32[]{:S(2)}, u32[]{:S(2)}) collective-permute-start(bf16[96,1536]{1,0:T(8,128)(2,1)} %pad_maximum_fusion.7), channel_id=1, source_target_pairs={{0,8},{1,9},{2,10},{3,11},{4,12},{5,13},{6,14},{7,15},{8,0},{9,1},... | collective-permute-start | bytes 884744 | tf_op jit(solution)/shard_map/ppermute | solution.py:593
  51.2 15.7 %copy-start.25 = (bf16[256,768]{1,0:T(8,128)(2,1)S(1)}, bf16[256,768]{1,0:T(8,128)(2,1)}, u32[]{:S(2)}) copy-start(bf16[256,768]{1,0:T(8,128)(2,1)} %copy-done.24) | copy-start | bytes 1179652
  52.7 15.5 %copy-start.18 = (bf16[96,1536]{1,0:T(8,128)(2,1)S(1)}, bf16[96,1536]{1,0:T(8,128)(2,1)}, u32[]{:S(2)}) copy-start(bf16[96,1536]{1,0:T(8,128)(2,1)} %copy-done.17) | copy-start | bytes 884740
  52.7 26.5 %collective-permute-start.6 = (bf16[384,1664]{1,0:T(8,128)(2,1)S(1)}, bf16[384,1664]{1,0:T(8,128)(2,1)}, u32[]{:S(2)}, u32[]{:S(2)}) collective-permute-start(bf16[384,1664]{1,0:T(8,128)(2,1)S(1)} %pad_maximum_fusion.b0_ref), channel_id=1, source_target_pairs={{0,1},{1,0},{2,3},{3,2},{4,5},{5,4},{6,7},{7,6},{8,9},{9,8},{10,11... | collective-permute-start | bytes 3833864 | tf_op jit(solution)/shard_map/ppermute | solution.py:26
  64.3 14.9 %collective-permute-start.10 = (bf16[384,1664]{1,0:T(8,128)(2,1)S(1)}, bf16[384,1664]{1,0:T(8,128)(2,1)}, u32[]{:S(2)}, u32[]{:S(2)}) collective-permute-start(bf16[384,1664]{1,0:T(8,128)(2,1)S(1)} %collective-permute-done.7.m0_ref), channel_id=1, source_target_pairs={{0,1},{1,0},{2,3},{3,2},{4,5},{5,4},{6,7},{7,6},{8,9},{9,8},{10,11... | collective-permute-start | bytes 3833864 | tf_op jit(solution)/shard_map/ppermute | solution.py:26
  69.0 10.2 %collective-permute-start.11 = (bf16[192,1536]{1,0:T(8,128)(2,1)}, bf16[192,1536]{1,0:T(8,128)(2,1)}, u32[]{:S(2)}, u32[]{:S(2)}) collective-permute-start(bf16[192,1536]{1,0:T(8,128)(2,1)} %pad_maximum_fusion.3), channel_id=1, source_target_pairs={{0,4},{1,3},{2,6},{3,1},{4,0},{5,7},{6,2},{7,5},{8,12},{9,11},{10,... | collective-permute-start | bytes 1769480 | tf_op jit(solution)/shard_map/ppermute | solution.py:593
  73.1 33.6 %collective-permute-start.13 = (bf16[192,1536]{1,0:T(8,128)(2,1)}, bf16[192,1536]{1,0:T(8,128)(2,1)}, u32[]{:S(2)}, u32[]{:S(2)}) collective-permute-start(bf16[192,1536]{1,0:T(8,128)(2,1)} %pad_maximum_fusion.4), channel_id=1, source_target_pairs={{0,4},{1,3},{2,6},{3,1},{4,0},{5,7},{6,2},{7,5},{8,12},{9,11},{10,... | collective-permute-start | bytes 1769480 | tf_op jit(solution)/shard_map/ppermute | solution.py:593
  81.1 25.5 %collective-permute-start.12 = (bf16[384,1536]{1,0:T(8,128)(2,1)}, bf16[384,1536]{1,0:T(8,128)(2,1)}, u32[]{:S(2)}, u32[]{:S(2)}) collective-permute-start(bf16[384,1536]{1,0:T(8,128)(2,1)} %constant_dynamic-update-slice_fusion.1.both_ref.ub_ref), channel_id=1, source_target_pairs={{0,2},{1,5},{2,0},{3,7},{4,6},{5,1},{6,4},{7,3},{8,10},{9,13},{10,... | collective-permute-start | bytes 3538952 | tf_op jit(solution)/shard_map/ppermute | solution.py:593
  82.5 36.0 %collective-permute-start.14 = (bf16[384,1536]{1,0:T(8,128)(2,1)}, bf16[384,1536]{1,0:T(8,128)(2,1)}, u32[]{:S(2)}, u32[]{:S(2)}) collective-permute-start(bf16[384,1536]{1,0:T(8,128)(2,1)} %constant_dynamic-update-slice_fusion.1.both_ref.ub_ref), channel_id=1, source_target_pairs={{0,1},{1,0},{2,3},{3,2},{4,5},{5,4},{6,7},{7,6},{8,9},{9,8},{10,11... | collective-permute-start | bytes 3538952 | tf_op jit(solution)/shard_map/ppermute | solution.py:26
  106.7 11.8 %collective-permute-start.15 = (bf16[384,1536]{1,0:T(8,128)(2,1)}, bf16[384,1536]{1,0:T(8,128)(2,1)}, u32[]{:S(2)}, u32[]{:S(2)}) collective-permute-start(bf16[384,1536]{1,0:T(8,128)(2,1)} %collective-permute-done.12.more_ref.um_ref), channel_id=1, source_target_pairs={{0,1},{1,0},{2,3},{3,2},{4,5},{5,4},{6,7},{7,6},{8,9},{9,8},{10,11... | collective-permute-start | bytes 3538952 | tf_op jit(solution)/shard_map/ppermute | solution.py:26
  108.5 17.3 %collective-permute-start.17 = (bf16[384,1536]{1,0:T(8,128)(2,1)S(1)}, bf16[384,1536]{1,0:T(8,128)(2,1)S(1)}, u32[]{:S(2)}, u32[]{:S(2)}) collective-permute-start(bf16[384,1536]{1,0:T(8,128)(2,1)S(1)} %pad_maximum_fusion.1.b0_ref.db_ref), channel_id=1, source_target_pairs={{0,2},{1,5},{2,0},{3,7},{4,6},{5,1},{6,4},{7,3},{8,10},{9,13},{10,... | collective-permute-start | bytes 3538952 | tf_op jit(solution)/shard_map/ppermute | solution.py:593
  110.7 18.0 %collective-permute-start.16 = (bf16[384,1536]{1,0:T(8,128)(2,1)S(1)}, bf16[384,1536]{1,0:T(8,128)(2,1)}, u32[]{:S(2)}, u32[]{:S(2)}) collective-permute-start(bf16[384,1536]{1,0:T(8,128)(2,1)S(1)} %pad_maximum_fusion.1.b0_ref.db_ref), channel_id=1, source_target_pairs={{0,1},{1,0},{2,3},{3,2},{4,5},{5,4},{6,7},{7,6},{8,9},{9,8},{10,11... | collective-permute-start | bytes 3538952 | tf_op jit(solution)/shard_map/ppermute | solution.py:26
  125.8 3.2 %collective-permute-start.18 = (bf16[384,1536]{1,0:T(8,128)(2,1)S(1)}, bf16[384,1536]{1,0:T(8,128)(2,1)}, u32[]{:S(2)}, u32[]{:S(2)}) collective-permute-start(bf16[384,1536]{1,0:T(8,128)(2,1)S(1)} %collective-permute-done.17.m0_ref.dm_ref), channel_id=1, source_target_pairs={{0,1},{1,0},{2,3},{3,2},{4,5},{5,4},{6,7},{7,6},{8,9},{9,8},{10,11... | collective-permute-start | bytes 3538952 | tf_op jit(solution)/shard_map/ppermute | solution.py:26
  126.0 2.7 collective-permute-start.19
  149.4 5.0 %collective-permute-start.21 = (bf16[384,1536]{1,0:T(8,128)(2,1)}, bf16[384,1536]{1,0:T(8,128)(2,1)S(1)}, u32[]{:S(2)}, u32[]{:S(2)}) collective-permute-start(bf16[384,1536]{1,0:T(8,128)(2,1)} %get-tuple-element.112), channel_id=1, source_target_pairs={{0,1},{1,0},{2,3},{3,2},{4,5},{5,4},{6,7},{7,6},{8,9},{9,8},{10,11... | collective-permute-start | bytes 3538952 | tf_op jit(solution)/shard_map/ppermute | solution.py:26
  149.5 4.9 %collective-permute-start.22 = (bf16[384,1536]{1,0:T(8,128)(2,1)}, bf16[384,1536]{1,0:T(8,128)(2,1)S(1)}, u32[]{:S(2)}, u32[]{:S(2)}) collective-permute-start(bf16[384,1536]{1,0:T(8,128)(2,1)} %get-tuple-element.115), channel_id=1, source_target_pairs={{0,1},{1,0},{2,3},{3,2},{4,5},{5,4},{6,7},{7,6},{8,9},{9,8},{10,11... | collective-permute-start | bytes 3538952 | tf_op jit(solution)/shard_map/ppermute | solution.py:26
  167.9 33.7 %collective-permute-start.24 = (bf16[384,1536]{1,0:T(8,128)(2,1)}, bf16[384,1536]{1,0:T(8,128)(2,1)S(1)}, u32[]{:S(2)}, u32[]{:S(2)}) collective-permute-start(bf16[384,1536]{1,0:T(8,128)(2,1)} %get-tuple-element.121), channel_id=1, source_target_pairs={{0,1},{1,0},{2,3},{3,2},{4,5},{5,4},{6,7},{7,6},{8,9},{9,8},{10,11... | collective-permute-start | bytes 3538952 | tf_op jit(solution)/shard_map/ppermute | solution.py:26
  168.1 33.5 %collective-permute-start.25 = (bf16[384,1536]{1,0:T(8,128)(2,1)}, bf16[384,1536]{1,0:T(8,128)(2,1)S(1)}, u32[]{:S(2)}, u32[]{:S(2)}) collective-permute-start(bf16[384,1536]{1,0:T(8,128)(2,1)} %get-tuple-element.127), channel_id=1, source_target_pairs={{0,1},{1,0},{2,3},{3,2},{4,5},{5,4},{6,7},{7,6},{8,9},{9,8},{10,11... | collective-permute-start | bytes 3538952 | tf_op jit(solution)/shard_map/ppermute | solution.py:26
  168.5 33.1 %collective-permute-start.23 = (bf16[384,1536]{1,0:T(8,128)(2,1)S(1)}, bf16[384,1536]{1,0:T(8,128)(2,1)}, u32[]{:S(2)}, u32[]{:S(2)}) collective-permute-start(bf16[384,1536]{1,0:T(8,128)(2,1)S(1)} %add_convert_fusion.2), channel_id=1, source_target_pairs={{0,2},{1,5},{2,0},{3,7},{4,6},{5,1},{6,4},{7,3},{8,10},{9,13},{10,... | collective-permute-start | bytes 3538952 | tf_op jit(solution)/shard_map/ppermute | solution.py:593
  201.6 32.1 %copy-start.11 = (bf16[384,1536]{1,0:T(8,128)(2,1)}, bf16[384,1536]{1,0:T(8,128)(2,1)S(1)}, u32[]{:S(2)}) copy-start(bf16[384,1536]{1,0:T(8,128)(2,1)S(1)} %collective-permute-done.25) | copy-start | bytes 3538948
  206.1 24.8 %collective-permute-start.26 = (bf16[192,1536]{1,0:T(8,128)(2,1)}, bf16[192,1536]{1,0:T(8,128)(2,1)S(1)}, u32[]{:S(2)}, u32[]{:S(2)}) collective-permute-start(bf16[192,1536]{1,0:T(8,128)(2,1)} %add_convert_fusion.5), channel_id=1, source_target_pairs={{0,4},{1,3},{2,6},{3,1},{4,0},{5,7},{6,2},{7,5},{8,12},{9,11},{10,... | collective-permute-start | bytes 1769480 | tf_op jit(solution)/shard_map/ppermute | solution.py:593
  207.6 24.1 %collective-permute-start.27 = (bf16[384,1536]{1,0:T(8,128)(2,1)S(1)}, bf16[384,1536]{1,0:T(8,128)(2,1)}, u32[]{:S(2)}, u32[]{:S(2)}) collective-permute-start(bf16[384,1536]{1,0:T(8,128)(2,1)S(1)} %add_convert_fusion.1), channel_id=1, source_target_pairs={{0,2},{1,5},{2,0},{3,7},{4,6},{5,1},{6,4},{7,3},{8,10},{9,13},{10,... | collective-permute-start | bytes 3538952 | tf_op jit(solution)/shard_map/ppermute | solution.py:593
  243.5 23.9 %collective-permute-start.31 = (bf16[384,1664]{1,0:T(8,128)(2,1)}, bf16[384,1664]{1,0:T(8,128)(2,1)}, u32[]{:S(2)}, u32[]{:S(2)}) collective-permute-start(bf16[384,1664]{1,0:T(8,128)(2,1)} %get-tuple-element.150), channel_id=1, source_target_pairs={{0,1},{1,0},{2,3},{3,2},{4,5},{5,4},{6,7},{7,6},{8,9},{9,8},{10,11... | collective-permute-start | bytes 3833864 | tf_op jit(solution)/shard_map/ppermute | solution.py:26
  243.5 23.9 %collective-permute-start.32 = (bf16[384,1664]{1,0:T(8,128)(2,1)}, bf16[384,1664]{1,0:T(8,128)(2,1)S(1)}, u32[]{:S(2)}, u32[]{:S(2)}) collective-permute-start(bf16[384,1664]{1,0:T(8,128)(2,1)} %get-tuple-element.156), channel_id=1, source_target_pairs={{0,1},{1,0},{2,3},{3,2},{4,5},{5,4},{6,7},{7,6},{8,9},{9,8},{10,11... | collective-permute-start | bytes 3833864 | tf_op jit(solution)/shard_map/ppermute | solution.py:26
  244.0 10.2 %collective-permute-start.29 = (bf16[192,1536]{1,0:T(8,128)(2,1)}, bf16[192,1536]{1,0:T(8,128)(2,1)S(1)}, u32[]{:S(2)}, u32[]{:S(2)}) collective-permute-start(bf16[192,1536]{1,0:T(8,128)(2,1)} %add_convert_fusion.4), channel_id=1, source_target_pairs={{0,4},{1,3},{2,6},{3,1},{4,0},{5,7},{6,2},{7,5},{8,12},{9,11},{10,... | collective-permute-start | bytes 1769480 | tf_op jit(solution)/shard_map/ppermute | solution.py:593
  245.1 9.1 %collective-permute-start.28 = (bf16[96,1536]{1,0:T(8,128)(2,1)S(1)}, bf16[96,1536]{1,0:T(8,128)(2,1)}, u32[]{:S(2)}, u32[]{:S(2)}) collective-permute-start(bf16[96,1536]{1,0:T(8,128)(2,1)S(1)} %slice.367), channel_id=1, source_target_pairs={{0,8},{1,9},{2,10},{3,11},{4,12},{5,13},{6,14},{7,15},{8,0},{9,1},... | collective-permute-start | bytes 884744 | tf_op jit(solution)/shard_map/ppermute | solution.py:593
  270.6 17.6 %collective-permute-start.33 = (bf16[384,1664]{1,0:T(8,128)(2,1)}, bf16[384,1664]{1,0:T(8,128)(2,1)}, u32[]{:S(2)}, u32[]{:S(2)}) collective-permute-start(bf16[384,1664]{1,0:T(8,128)(2,1)} %add_convert_fusion), channel_id=1, source_target_pairs={{0,2},{1,5},{2,0},{3,7},{4,6},{5,1},{6,4},{7,3},{8,10},{9,13},{10,... | collective-permute-start | bytes 3833864 | tf_op jit(solution)/shard_map/ppermute | solution.py:593
  272.0 1.4 collective-permute-start.20
  274.1 16.4 %collective-permute-start.39 = (bf16[48,1536]{1,0:T(8,128)(2,1)S(1)}, bf16[48,1536]{1,0:T(8,128)(2,1)S(1)}, u32[]{:S(2)}, u32[]{:S(2)}) collective-permute-start(bf16[48,1536]{1,0:T(8,128)(2,1)S(1)} %slice.369), channel_id=1, source_target_pairs={{0,16},{1,17},{2,18},{3,19},{4,20},{5,21},{6,22},{7,23},{8,24},{9,... | collective-permute-start | bytes 442376 | tf_op jit(solution)/shard_map/ppermute | solution.py:593
  276.5 14.8 %collective-permute-start.37 = (bf16[96,1536]{1,0:T(8,128)(2,1)S(1)}, bf16[96,1536]{1,0:T(8,128)(2,1)S(1)}, u32[]{:S(2)}, u32[]{:S(2)}) collective-permute-start(bf16[96,1536]{1,0:T(8,128)(2,1)S(1)} %slice.366), channel_id=1, source_target_pairs={{0,8},{1,9},{2,10},{3,11},{4,12},{5,13},{6,14},{7,15},{8,0},{9,1},... | collective-permute-start | bytes 884744 | tf_op jit(solution)/shard_map/ppermute | solution.py:593
  279.1 31.6 %collective-permute-start.30 = (f32[256,768]{1,0:T(8,128)S(1)}, f32[256,768]{1,0:T(8,128)S(1)}, u32[]{:S(2)}, u32[]{:S(2)}) collective-permute-start(f32[256,768]{1,0:T(8,128)S(1)} %constant_dynamic-slice_fusion.1), channel_id=1, source_target_pairs={{0,1},{1,0},{2,3},{3,2},{4,5},{5,4},{6,7},{7,6},{8,9},{9,8},{10,11... | collective-permute-start | bytes 2359304 | tf_op jit(solution)/shard_map/ppermute | solution.py:26
  289.5 10.5 %collective-permute-start.34 = (bf16[192,1664]{1,0:T(8,128)(2,1)S(1)}, bf16[192,1664]{1,0:T(8,128)(2,1)S(1)}, u32[]{:S(2)}, u32[]{:S(2)}) collective-permute-start(bf16[192,1664]{1,0:T(8,128)(2,1)S(1)} %add_convert_fusion.3), channel_id=1, source_target_pairs={{0,4},{1,3},{2,6},{3,1},{4,0},{5,7},{6,2},{7,5},{8,12},{9,11},{10,... | collective-permute-start | bytes 1916936 | tf_op jit(solution)/shard_map/ppermute | solution.py:593
  291.4 10.4 %collective-permute-start.38 = (bf16[48,1536]{1,0:T(8,128)(2,1)S(1)}, bf16[48,1536]{1,0:T(8,128)(2,1)S(1)}, u32[]{:S(2)}, u32[]{:S(2)}) collective-permute-start(bf16[48,1536]{1,0:T(8,128)(2,1)S(1)} %slice.370), channel_id=1, source_target_pairs={{0,16},{1,17},{2,18},{3,19},{4,20},{5,21},{6,22},{7,23},{8,24},{9,... | collective-permute-start | bytes 442376 | tf_op jit(solution)/shard_map/ppermute | solution.py:593
  301.4 7.1 %collective-permute-start.35 = (bf16[96,1664]{1,0:T(8,128)(2,1)S(1)}, bf16[96,1664]{1,0:T(8,128)(2,1)S(1)}, u32[]{:S(2)}, u32[]{:S(2)}) collective-permute-start(bf16[96,1664]{1,0:T(8,128)(2,1)S(1)} %slice.365), channel_id=1, source_target_pairs={{0,8},{1,9},{2,10},{3,11},{4,12},{5,13},{6,14},{7,15},{8,0},{9,1},... | collective-permute-start | bytes 958472 | tf_op jit(solution)/shard_map/ppermute | solution.py:593
  308.6 8.0 %collective-permute-start.36 = (bf16[48,1664]{1,0:T(8,128)(2,1)S(1)}, bf16[48,1664]{1,0:T(8,128)(2,1)S(1)}, u32[]{:S(2)}, u32[]{:S(2)}) collective-permute-start(bf16[48,1664]{1,0:T(8,128)(2,1)S(1)} %slice.368), channel_id=1, source_target_pairs={{0,16},{1,17},{2,18},{3,19},{4,20},{5,21},{6,22},{7,23},{8,24},{9,... | collective-permute-start | bytes 479240 | tf_op jit(solution)/shard_map/ppermute | solution.py:593
  (33 other events, 182.4 us)
where the time goes:
time: 322 us; the launch traced here: 320 us
  Pallas kernels  116 us (36%)
  waiting for transfers between devices  83.5 us (26%)
  other arithmetic  42.1 us (13%)
  local copies, waits for them, and re-layouts  41.3 us (13%)
  starting transfers between devices  31.9 us (10%)
  between operations  5.59 us (2%)
    pallas_call x11, Pallas kernels, call(): pl.pallas_call(body, out_shape=outs, grid=grid or (), in_specs=in_specs o...  116 us
    ppermute x24, waiting for transfers between devices, flip(): return lax.ppermute(value, ('dp', 'tensor'), pairs)  80.6 us
    ppermute x24, starting transfers between devices, flip(): return lax.ppermute(value, ('dp', 'tensor'), pairs)  27.8 us
    convert_element_type x6, other arithmetic, low(): return added(*values).astype(BF16)  12.3 us
    unnamed x89, local copies, waits for them, and re-layouts  7.43 us
  transfers between devices with their start and end apart: 40, of which 15 were waited for; matrix products, arithmetic and copies ran while one was open for 18% of the time, Pallas kernels for 24%

commit v1 on v0

v1 whole, which is shorter than its diff:
```python
import functools

import jax
import jax.numpy as jnp
import numpy as np
from jax import lax
from jax.experimental import pallas as pl
from jax.experimental.pallas import tpu as pltpu
from jax.sharding import PartitionSpec as P

HD = 64
LANES = 128
STRIP = 128
F32 = jnp.float32
BF16 = jnp.bfloat16
VMEM_LIMIT = 18 * 1024 * 1024


def nn(left, right):
    return lax.dot_general(left, right, (((1,), (0,)), ((), ())), preferred_element_type=F32)


def nt(left, right):
    return lax.dot_general(left, right, (((1,), (1,)), ((), ())), preferred_element_type=F32)


def swap_cores(value):
    return lax.ppermute(value, "tensor", [(0, 1), (1, 0)])


def after(value, *others):
    return lax.optimization_barrier((value, others))[0]


def together(*values):
    return lax.optimization_barrier(values)


def strips(count, size, step):
    def run(i, carry):
        step(pl.ds(pl.multiple_of(i * size, size), size))
        return carry

    lax.fori_loop(0, count // size, run, 0)


def columns_of(width, step):
    block = 256 if width % 256 == 0 else width

    def run(i, carry):
        step(pl.ds(pl.multiple_of(i * block, block), block))
        return carry

    lax.fori_loop(0, width // block, run, 0)


def call(body, outs, args, grid=None, in_specs=None, out_specs=None, scratch=(), flops=0):
    whole = pl.BlockSpec(memory_space=pltpu.VMEM)
    return pl.pallas_call(
        body,
        out_shape=outs,
        grid=grid or (),
        in_specs=in_specs or [whole] * len(args),
        out_specs=out_specs or jax.tree.map(lambda _: whole, outs),
        scratch_shapes=scratch,
        compiler_params=pltpu.CompilerParams(vmem_limit_bytes=VMEM_LIMIT),
        cost_estimate=pl.CostEstimate(flops=flops, bytes_accessed=1 << 20, transcendentals=0),
    )(*args)


def shaped(shape, dtype):
    return jax.ShapeDtypeStruct(shape, dtype)


ANY = pl.BlockSpec(memory_space=pl.ANY)
WHOLE = pl.BlockSpec(memory_space=pltpu.VMEM)


OTHER = (0, 2, 1, 3)


def load_weights(pieces, target, sems, first=0, last=None, at=(0,) * 8):
    quarter = target.shape[1] // 4
    columns = slice(first, last)
    copies = []
    for side in range(2):
        for place in range(4):
            source = place if side == 0 else 4 + OTHER[place]
            rows = pl.ds(at[source] * quarter, quarter)
            copies.append(
                pltpu.make_async_copy(
                    pieces[source].at[rows, columns],
                    target.at[side, pl.ds(place * quarter, quarter)],
                    sems.at[side, place],
                )
            )
    for copy in copies:
        copy.start()
    return copies


def attention_kernel(
    x_ref, perm_ref, bias_ref, mask_ref, vec_ref, *refs
):
    pieces, refs = refs[:8], refs[8:]
    qkv_ref, lse_ref, att_ref, res_ref, first_ref, low_ref, lowt_ref, xt_ref, w_ref = refs[:9]
    col_ref, rel_ref, sems = refs[9:]
    cols = qkv_ref.shape[2] // 3
    tokens = x_ref.shape[0]
    copies = load_weights(pieces, w_ref, sems, 0, 4 * cols)

    def reorder(span):
        rel_ref[:, span] = nn(x_ref[...], perm_ref[:, span]).astype(BF16)

    columns_of(x_ref.shape[1], reorder)
    xt_ref[...] = rel_ref[...].T
    col_ref[...] = jnp.broadcast_to(mask_ref[...], (LANES, tokens)).T
    for copy in copies:
        copy.wait()

    def project(i, carry):
        half, part = i // 3, i % 3
        span = pl.ds(pl.multiple_of(part * cols, cols), cols)
        made = nn(rel_ref[...], w_ref[half, :, span]) + bias_ref[pl.ds(half, 1), span]
        qkv_ref[half, :, span] = made.astype(BF16)
        return carry

    lax.fori_loop(0, 6, project, 0)
    lane = lax.broadcasted_iota(jnp.int32, (tokens, LANES), 1) < HD
    pairs = cols // LANES


    def pair(step, carry):
        half, i = step // pairs, step % pairs
        off = pl.multiple_of(i * LANES, LANES)
        query = qkv_ref[half, :, pl.ds(off, LANES)] * BF16(HD ** (-0.5))
        key = qkv_ref[half, :, pl.ds(pl.multiple_of(cols + off, LANES), LANES)]
        value = qkv_ref[half, :, pl.ds(pl.multiple_of(2 * cols + off, LANES), LANES)]
        value_t = value.T
        outs = []
        for head in range(2):
            kept = jnp.where(lane == (head == 0), key, jnp.zeros_like(key))
            scores = nt(kept, query)
            scores = scores + jnp.concatenate([col_ref[...]] * (tokens // LANES), axis=1)
            top = jnp.max(scores, axis=0, keepdims=True)
            shifted = jnp.exp(scores - top)
            total = jnp.sum(shifted, axis=0, keepdims=True)
            out = nn(value_t[head * HD : (head + 1) * HD], shifted.astype(BF16))
            outs.append(out / total)
            lse_ref[half, pl.ds(i * 2 + head, 1), :] = top + jnp.log(total)
        both = jnp.concatenate(outs, axis=0).T
        att_ref[half, :, pl.ds(off, LANES)] = both.astype(BF16)
        return carry

    lax.fori_loop(0, 2 * pairs, pair, 0)
    out = slice(3 * cols, 4 * cols)

    def branch(span):
        made = nt(att_ref[0], w_ref[0, span, out]) + nt(att_ref[1], w_ref[1, span, out])
        res_ref[:, span] = made

    columns_of(x_ref.shape[1], branch)

    def norm(rows):
        value = res_ref[rows, :] + vec_ref[4:5, :] + rel_ref[rows, :].astype(F32)
        res_ref[rows, :] = value
        average = jnp.mean(value, axis=-1, keepdims=True)
        centred = value - average
        inverse = lax.rsqrt(jnp.mean(centred * centred, axis=-1, keepdims=True) + 1e-12)
        first = centred * inverse * vec_ref[0:1, :] + vec_ref[5:6, :]
        first_ref[rows, :] = first
        low_ref[rows, :] = first.astype(BF16)

    strips(tokens, STRIP, norm)
    lowt_ref[...] = low_ref[...].T


def attention_forward(x, perm, head_bias, mask, vec, pieces, cols):
    tokens, width = x.shape
    heads = cols // HD
    outs = (
        shaped((2, tokens, 3 * cols), BF16),
        shaped((2, heads, tokens), F32),
        shaped((2, tokens, cols), BF16),
        shaped((tokens, width), F32),
        shaped((tokens, width), F32),
        shaped((tokens, width), BF16),
        shaped((width, tokens), BF16),
        shaped((width, tokens), BF16),
        shaped((2, width, 4 * cols), BF16),
    )
    return call(
        attention_kernel,
        outs,
        (x, perm, head_bias, mask, vec, *pieces),
        in_specs=[WHOLE] * 5 + [ANY] * 8,
        scratch=[
            pltpu.VMEM((tokens, LANES), F32),
            pltpu.VMEM((tokens, width), BF16),
            pltpu.SemaphoreType.DMA((2, 4)),
        ],
        flops=8 * tokens * width * width,
    )


ERF = (0.254829592, -0.284496736, 1.421413741, -1.453152027, 1.061405429)


def gelu_pair(value):
    size = jnp.abs(value)
    bell = jnp.exp(-0.5 * value * value)
    t = 1.0 / (1.0 + (0.3275911 * 0.5**0.5) * size)
    poly = ERF[4]
    for term in ERF[3::-1]:
        poly = poly * t + term
    tail = 0.5 * poly * t * bell
    phi = jnp.where(value >= 0, 1.0 - tail, tail)
    return value * phi, phi + value * bell * 0.3989422804014327


def join_rows(refs, target, swapped):
    quarter = target.shape[0] // 4
    for place in range(4):
        source = OTHER[place] if swapped else place
        target[place * quarter : (place + 1) * quarter, :] = refs[source][...]


def split_rows(value, keep_ref, send_ref, swapped):
    quarter = value.shape[0] // 4
    for place in range(4):
        source = OTHER[place] if swapped else place
        ref = (keep_ref, send_ref)[place // 2]
        rows = slice((place % 2) * quarter, (place % 2 + 1) * quarter)
        ref[rows, :] = value[source * quarter : (source + 1) * quarter, :]


def column_block(hidden):
    return 512 if hidden % 512 == 0 else hidden


def up_forward(low, pieces, bias, swapped):
    tokens, width = low.shape
    pieces, at = zip(*pieces)
    hidden = pieces[0].shape[1]
    block = column_block(hidden)

    def kernel(low_ref, a_ref, b_ref, c_ref, d_ref, bias_ref, hid_ref, slope_ref, acc_ref, w_ref):
        join_rows((a_ref, b_ref, c_ref, d_ref), w_ref, swapped)
        acc_ref[...] = nn(low_ref[...], w_ref[...])

        def act(rows):
            active, slope = gelu_pair(acc_ref[rows, :] + bias_ref[...])
            hid_ref[rows, :] = active.astype(BF16)
            slope_ref[rows, :] = slope.astype(BF16)

        strips(tokens, STRIP, act)

    outs = (shaped((tokens, hidden), BF16), shaped((tokens, hidden), BF16))
    chunk = pl.BlockSpec((tokens, block), lambda i: (0, i))
    parts = [pl.BlockSpec((width // 4, block), lambda i, row=row: (row, i)) for row in at]
    return call(
        kernel,
        outs,
        (low, *pieces, bias),
        grid=(hidden // block,),
        in_specs=[
            pl.BlockSpec((tokens, width), lambda i: (0, 0)),
            *parts,
            pl.BlockSpec((1, block), lambda i: (0, i)),
        ],
        out_specs=(chunk, chunk),
        scratch=[pltpu.VMEM((tokens, block), F32), pltpu.VMEM((width, block), BF16)],
        flops=2 * tokens * width * hidden,
    )


def down_kernel(
    at, len_ref, h0_ref, h1_ref, first_ref, vec_ref, proj_ref, cot_ref, *refs
):
    pieces, refs = refs[:8], refs[8:]
    emb_ref, low_ref, lowt_ref, res_ref, pgrad_ref, sums_ref = refs[:6]
    ffn_ref, norm_ref, sec_ref, gp_ref, gs_ref, inv_ref, prj_ref, w_ref, sems = refs[6:]
    copies = load_weights(pieces, w_ref, sems, at=at)
    tokens = first_ref.shape[0]
    length = len_ref[0]
    for copy in copies:
        copy.wait()

    def matmul(span):
        ffn_ref[:, span] = nt(h0_ref[...], w_ref[0, span]) + nt(h1_ref[...], w_ref[1, span])

    columns_of(ffn_ref.shape[1], matmul)

    def norm(rows):
        value = first_ref[rows, :] + ffn_ref[rows, :] + vec_ref[6:7, :]
        average = jnp.mean(value, axis=-1, keepdims=True)
        centred = value - average
        inverse = lax.rsqrt(jnp.mean(centred * centred, axis=-1, keepdims=True) + 1e-12)
        normed = centred * inverse
        norm_ref[rows, :] = normed
        inv_ref[rows, :] = jnp.broadcast_to(inverse, (STRIP, LANES))
        sec_ref[rows, :] = (normed * vec_ref[1:2, :] + vec_ref[7:8, :]).astype(BF16)

    strips(tokens, STRIP, norm)
    prj_ref[...] = nn(sec_ref[...], proj_ref[...])

    def embed(rows):
        projected = prj_ref[rows, :]
        valid = rows.start + lax.broadcasted_iota(jnp.int32, projected.shape, 0) < length
        valid = valid.astype(F32)
        scale = lax.rsqrt(jnp.sum(projected * projected, axis=-1, keepdims=True) + 1e-06)
        unit = projected * scale
        emb_ref[rows, :] = unit * valid
        cot = cot_ref[rows, :] * valid
        back = scale * (cot - unit * jnp.sum(unit * cot, axis=-1, keepdims=True))
        gp_ref[rows, :] = back.astype(BF16)

    strips(tokens, STRIP, embed)
    pgrad_ref[...] = nn(sec_ref[...].T, gp_ref[...])
    gs_ref[...] = nt(gp_ref[...], proj_ref[...])
    sums_ref[...] = jnp.zeros_like(sums_ref)

    def back(rows):
        grad = gs_ref[rows, :]
        normed = norm_ref[rows, :]
        scaled = grad * vec_ref[1:2, :]
        inside = (
            scaled
            - jnp.mean(scaled, axis=-1, keepdims=True)
            - normed * jnp.mean(scaled * normed, axis=-1, keepdims=True)
        )
        value = inside * inv_ref[rows, 0:1]
        low = value.astype(BF16)
        res_ref[rows, :] = value
        low_ref[rows, :] = low
        fold = lambda v: jnp.sum(v.reshape(STRIP // 8, 8, v.shape[1]), axis=0)
        sums_ref[0:8, :] += fold(grad * normed)
        sums_ref[8:16, :] += fold(grad)
        sums_ref[16:24, :] += fold(low.astype(F32))

    strips(tokens, STRIP, back)
    lowt_ref[...] = low_ref[...].T


def down_both(length, hidden, pieces, first, vec, proj, cot):
    tokens, width = first.shape
    embed = proj.shape[1]
    outs = (
        shaped((tokens, embed), F32),
        shaped((tokens, width), BF16),
        shaped((width, tokens), BF16),
        shaped((tokens, width), F32),
        shaped((width, embed), F32),
        shaped((24, width), F32),
    )
    pieces, at = zip(*pieces)
    args = (length, *hidden, first, vec, proj, cot, *pieces)
    return call(
        functools.partial(down_kernel, at),
        outs,
        args,
        in_specs=[pl.BlockSpec(memory_space=pltpu.SMEM)] + [WHOLE] * 6 + [ANY] * 8,
        scratch=[
            pltpu.VMEM((tokens, width), F32),
            pltpu.VMEM((tokens, width), F32),
            pltpu.VMEM((tokens, width), BF16),
            pltpu.VMEM((tokens, embed), BF16),
            pltpu.VMEM((tokens, width), F32),
            pltpu.VMEM((tokens, LANES), F32),
            pltpu.VMEM((tokens, embed), F32),
            pltpu.VMEM((2, width, hidden[0].shape[1]), BF16),
            pltpu.SemaphoreType.DMA((2, 4)),
        ],
        flops=2 * tokens * width * hidden[0].shape[1] * 2,
    )


def down_grad(g_low_t, hid, swapped):
    width, tokens = g_low_t.shape
    hidden = hid.shape[1]
    block = column_block(hidden)

    def kernel(gt_ref, hid_ref, keep_ref, send_ref):
        split_rows(nn(gt_ref[...], hid_ref[...]).astype(BF16), keep_ref, send_ref, swapped)

    piece = pl.BlockSpec((width // 2, block), lambda i: (0, i))
    out = shaped((width // 2, hidden), BF16)
    return call(
        kernel,
        (out, out),
        (g_low_t, hid),
        grid=(hidden // block,),
        in_specs=[
            pl.BlockSpec((width, tokens), lambda i: (0, 0)),
            pl.BlockSpec((tokens, block), lambda i: (0, i)),
        ],
        out_specs=(piece, piece),
        flops=2 * tokens * width * hidden,
    )


def up_grad(g_low, low_t, slope, down, up, start, swapped):
    tokens, width = g_low.shape
    pieces, at = zip(*down, *up)
    hidden = slope.shape[1]
    block = column_block(hidden)

    def kernel(g_ref, lowt_ref, slope_ref, start_ref, *refs):
        join_rows(refs[:4], wd_ref := refs[-2], swapped)
        join_rows(refs[4:8], wu_ref := refs[-1], swapped)
        keep_ref, send_ref, bias_ref, first_ref, gh_ref, gin_ref = refs[8:-2]
        def matmul(span):
            gh_ref[:, span] = nn(g_ref[...], wd_ref[:, span])

        columns_of(block, matmul)
        bias_ref[...] = jnp.zeros_like(bias_ref)

        def act(rows):
            grad = (gh_ref[rows, :] * slope_ref[rows, :].astype(F32)).astype(BF16)
            gin_ref[rows, :] = grad
            wide = grad.astype(F32)
            bias_ref[...] += jnp.sum(wide.reshape(STRIP // 8, 8, wide.shape[1]), axis=0)

        strips(tokens, STRIP, act)
        split_rows(nn(lowt_ref[...], gin_ref[...]).astype(BF16), keep_ref, send_ref, swapped)
        @pl.when(pl.program_id(0) == 0)
        def _():
            first_ref[...] = start_ref[...]

        def add(span):
            first_ref[:, span] += nt(gin_ref[...], wu_ref[span, :])

        columns_of(width, add)

    row = pl.BlockSpec((tokens, width), lambda i: (0, 0))
    turned = pl.BlockSpec((width, tokens), lambda i: (0, 0))
    act = pl.BlockSpec((tokens, block), lambda i: (0, i))
    piece = pl.BlockSpec((width // 2, block), lambda i: (0, i))
    parts = [pl.BlockSpec((width // 4, block), lambda i, row=row: (row, i)) for row in at]
    out = shaped((width // 2, hidden), BF16)
    return call(
        kernel,
        (out, out, shaped((8, hidden), F32), shaped((tokens, width), F32)),
        (g_low, low_t, slope, start, *pieces),
        grid=(hidden // block,),
        in_specs=[row, turned, act, row] + parts,
        out_specs=(piece, piece, pl.BlockSpec((8, block), lambda i: (0, i)), row),
        scratch=[
            pltpu.VMEM((tokens, block), F32),
            pltpu.VMEM((tokens, block), BF16),
            pltpu.VMEM((width, block), BF16),
            pltpu.VMEM((width, block), BF16),
        ],
        flops=6 * tokens * width * hidden,
    )


def norm_back(g_first, res, vec, weights, cols):
    tokens, width = g_first.shape

    def kernel(
        gf_ref, res_ref, vec_ref, w_ref, gres_ref, turn_ref, gatt_ref, sums_ref, low_ref
    ):
        sums_ref[...] = jnp.zeros_like(sums_ref)

        def back(rows):
            value = res_ref[rows, :]
            average = jnp.mean(value, axis=-1, keepdims=True)
            centred = value - average
            inverse = lax.rsqrt(jnp.mean(centred * centred, axis=-1, keepdims=True) + 1e-12)
            normed = centred * inverse
            grad = gf_ref[rows, :]
            scaled = grad * vec_ref[0:1, :]
            inside = (
                scaled
                - jnp.mean(scaled, axis=-1, keepdims=True)
                - normed * jnp.mean(scaled * normed, axis=-1, keepdims=True)
            )
            out = inside * inverse
            low = out.astype(BF16)
            gres_ref[rows, :] = out
            low_ref[rows, :] = low
            fold = lambda v: jnp.sum(v.reshape(STRIP // 8, 8, v.shape[1]), axis=0)
            sums_ref[0:8, :] += fold(grad * normed)
            sums_ref[8:16, :] += fold(grad)
            sums_ref[16:24, :] += fold(low.astype(F32))

        strips(tokens, STRIP, back)
        turn_ref[...] = low_ref[...].T
        for half in range(2):
            gatt_ref[half] = nn(low_ref[...], w_ref[half, :, 3 * cols :]).astype(BF16)

    outs = (
        shaped((tokens, width), F32),
        shaped((width, tokens), BF16),
        shaped((2, tokens, cols), BF16),
        shaped((24, width), F32),
    )
    return call(
        kernel,
        outs,
        (g_first, res, vec, weights),
        scratch=[pltpu.VMEM((tokens, width), BF16)],
        flops=4 * tokens * width * cols,
    )


def attention_back(pairs, g_att, att, qkv, lse, mask):
    tokens, cols = att.shape[1:]
    wide = len(pairs) * LANES
    scale = HD ** (-0.5)

    def kernel(gatt_ref, att_ref, qkv_ref, lse_ref, mask_ref, gqkv_ref, sums_ref, col_ref):
        col_ref[...] = jnp.broadcast_to(mask_ref[...], (LANES, tokens)).T
        lane = lax.broadcasted_iota(jnp.int32, (tokens, LANES), 1) < HD

        def pair(step, carry):
            half, place = step // len(pairs), step % len(pairs)
            i = pairs[0] + place
            off = pl.multiple_of(i * LANES, LANES)
            off_k = pl.multiple_of(cols + off, LANES)
            off_v = pl.multiple_of(2 * cols + off, LANES)
            query = qkv_ref[half, :, pl.ds(off, LANES)] * BF16(scale)
            key = qkv_ref[half, :, pl.ds(off_k, LANES)]
            value = qkv_ref[half, :, pl.ds(off_v, LANES)]
            grad = gatt_ref[half, :, pl.ds(off, LANES)]
            out = att_ref[half, :, pl.ds(off, LANES)]
            key_t = (key * BF16(scale)).T
            delta = (grad.astype(F32) * out.astype(F32)).T
            g_query, g_key, g_value = [], [], []
            for head in range(2):
                pick = lane == (head == 0)
                span = slice(head * HD, (head + 1) * HD)
                zero = jnp.zeros_like(key)
                scores = nt(jnp.where(pick, key, zero), query)
                scores = scores + jnp.concatenate([col_ref[...]] * (tokens // LANES), axis=1)
                probs = jnp.exp(scores - lse_ref[half, pl.ds(i * 2 + head, 1), :])
                g_probs = nt(jnp.where(pick, value, zero), grad)
                row_delta = jnp.sum(delta[span], axis=0, keepdims=True)
                g_scores = (probs * (g_probs - row_delta)).astype(BF16)
                g_value.append(nn(probs.astype(BF16), grad))
                g_key.append(nn(g_scores, query))
                g_query.append(nn(key_t[span], g_scores))
            g_q = jnp.concatenate(g_query, axis=0).T.astype(BF16)
            g_v = jnp.where(lane, *g_value).astype(BF16)
            to = pl.multiple_of(place * LANES, LANES)
            gqkv_ref[half, :, pl.ds(to, LANES)] = g_q
            to_k = pl.ds(pl.multiple_of(wide + to, LANES), LANES)
            gqkv_ref[half, :, to_k] = jnp.where(lane, *g_key).astype(BF16)
            gqkv_ref[half, :, pl.ds(pl.multiple_of(2 * wide + to, LANES), LANES)] = g_v
            for row, grads in ((0, g_q), (1, g_v)):
                total = jnp.sum(grads.astype(F32).reshape(-1, 8, LANES), axis=0)
                sums_ref[half, row, :, pl.ds(to, LANES)] = total
            return carry

        lax.fori_loop(0, 2 * len(pairs), pair, 0)

    return call(
        kernel,
        (shaped((2, tokens, 3 * wide), BF16), shaped((2, 2, 8, wide), F32)),
        (g_att, att, qkv, lse, mask),
        scratch=[pltpu.VMEM((tokens, LANES), F32)],
        flops=20 * tokens * tokens * wide * 2,
    )


def project_other(x_t, g_qkv, beside):
    width, tokens = x_t.shape
    columns = g_qkv.shape[2]
    extra = beside[1].shape[2] if beside else 0

    def kernel(xt_ref, g_ref, *refs):
        keep_ref, send_ref = refs[len(beside) :]
        span = slice(0, columns)
        made = nn(xt_ref[...], g_ref[1]).astype(BF16)
        split_rows(made, keep_ref.at[:, span], send_ref.at[:, span], True)
        if beside:
            span = slice(columns, columns + extra)
            made = nn(refs[0][...], refs[1][1]).astype(BF16)
            split_rows(made, keep_ref.at[:, span], send_ref.at[:, span], True)

    out = shaped((width // 2, columns + extra), BF16)
    return call(
        kernel,
        (out, out),
        (x_t, g_qkv, *beside),
        flops=2 * tokens * width * (columns + extra),
    )


def project_own(x_t, g_qkv, beside, small, keep_came, send_came):
    width, tokens = x_t.shape
    columns = g_qkv.shape[2]
    extra = beside[1].shape[2] if beside else 0
    tail = small[0].shape[1] if small else 0
    middle = width // 2
    count = len(beside) + len(small)

    def kernel(xt_ref, g_ref, kc_ref, sc_ref, *refs):
        keep_ref, send_ref = refs[count:]
        for out, came, first in ((keep_ref, kc_ref, 0), (send_ref, sc_ref, middle)):
            rows = slice(first, first + middle)
            span = slice(0, columns)
            made = nn(xt_ref[rows, :], g_ref[0])
            out[:, span] = (made + came[:, span].astype(F32)).astype(BF16)
            if beside:
                span = slice(columns, columns + extra)
                made = nn(refs[0][rows, :], refs[1][0])
                out[:, span] = (made + came[:, span].astype(F32)).astype(BF16)
            if small:
                total = refs[count - 2][rows, :].astype(F32) + refs[count - 1][rows, :].astype(F32)
                out[:, columns + extra :] = total.astype(BF16)

    out = shaped((middle, columns + extra + tail), BF16)
    return call(
        kernel,
        (out, out),
        (x_t, g_qkv, keep_came, send_came, *beside, *small),
        flops=2 * tokens * width * (columns + extra),
    )


def token_back(g_parts, start, perm, weights, cols):
    tokens, width = start.shape
    widths = [part.shape[2] // 3 for part in g_parts]

    def kernel(a_ref, b_ref, start_ref, perm_ref, w_ref, out_ref, g_ref, high_ref, rest_ref):
        for half in range(2):
            for kind in range(3):
                to = kind * cols
                for ref, wide in zip((a_ref, b_ref), widths):
                    taken = ref[half, :, kind * wide : (kind + 1) * wide]
                    g_ref[half, :, to : to + wide] = taken
                    to += wide
        used = slice(0, 3 * cols)

        def matmul(span):
            made = nt(g_ref[0], w_ref[0, span, used]) + nt(g_ref[1], w_ref[1, span, used])
            made = start_ref[:, span] + made
            high = made.astype(BF16)
            high_ref[:, span] = high
            rest_ref[:, span] = (made - high.astype(F32)).astype(BF16)

        columns_of(width, matmul)

        def reorder(span):
            turn = perm_ref[span, :]
            out_ref[:, span] = nt(high_ref[...], turn) + nt(rest_ref[...], turn)

        columns_of(width, reorder)

    return call(
        kernel,
        shaped((tokens, width), F32),
        (*g_parts, start, perm, weights),
        scratch=[
            pltpu.VMEM((2, tokens, 3 * cols), BF16),
            pltpu.VMEM((tokens, width), BF16),
            pltpu.VMEM((tokens, width), BF16),
        ],
        flops=16 * tokens * width * cols,
    )


class Exchange:
    def __init__(self, size):
        self.size = size
        self.depth = size.bit_length() - 1
        self.rank = lax.axis_index("dp")
        self.core = lax.axis_index("tensor")
        outer = list(range(self.depth - 1, 1, -1))
        self.bits = (outer + [1, 0], outer + [0, 1])

    def flip(self, value, step):
        pairs = []
        for i in range(self.size):
            for core in range(2):
                pairs.append((i * 2 + core, (i ^ (1 << self.bits[core][step])) * 2 + core))
        return lax.ppermute(value, ("dp", "tensor"), pairs)

    def blocks(self):
        tables = []
        for bits in self.bits:
            tables.append(
                [
                    sum(((j >> step) & 1) << bit for step, bit in enumerate(bits))
                    for j in range(self.size)
                ]
            )
        table = np.array(tables, np.int32)
        return jnp.where(self.core == 0, table[0], table[1]) ^ self.rank


def join(held, came):
    return jnp.concatenate([held, came], axis=0)


def added(*values):
    total = values[0].astype(F32)
    for value in values[1:]:
        total = total + value.astype(F32)
    return total


def halves(value):
    middle = value.shape[0] // 2
    return value[:middle], value[middle:]


def three_parts(value):
    high = lax.reduce_precision(value, 8, 7)
    rest = value - high
    middle = lax.reduce_precision(rest, 8, 7)
    return (high.astype(BF16), middle.astype(BF16), (rest - middle).astype(BF16))


SMALL = 48
UP = 32


def pack(qkv_w, out_w, emb_w, gains, biases, up_bias):
    rows, cols = out_w.shape
    chunk = gains.shape[1]
    args = (qkv_w, out_w, emb_w, gains, biases, up_bias[None])

    def kernel(*refs):
        one_ref, refs, vec_ref, sems = refs[6], (*refs[:6], *refs[7:13]), refs[13], refs[14]
        copies = []
        for place in range(6):
            copies.append(pltpu.make_async_copy(refs[place], refs[6 + place], sems.at[place]))
        for copy in copies:
            copy.start()
        for copy in copies:
            copy.wait()
        q_ref, o_ref, e_ref, g_ref, b_ref, u_ref = refs[6:]
        for part in range(3):
            one_ref[:, part * cols : (part + 1) * cols] = q_ref[part]
        one_ref[:, 3 * cols : 4 * cols] = o_ref[...]
        vec_ref[...] = jnp.zeros_like(vec_ref)
        vec_ref[0:2, 0:chunk] = g_ref[...]
        vec_ref[2:8, 0:chunk] = b_ref[...]
        vec_ref[0:1, UP : UP + u_ref.shape[1]] = u_ref[...]
        value = vec_ref[...]
        high = value.astype(BF16).astype(F32)
        middle = (value - high).astype(BF16).astype(F32)
        block = [e_ref[...].astype(F32), high, middle, value - high - middle]
        one_ref[:, 4 * cols :] = jnp.concatenate(block, axis=0).astype(BF16)

    return call(
        kernel,
        shaped((rows, 4 * cols + LANES), BF16),
        args,
        in_specs=[pl.BlockSpec(memory_space=pltpu.HBM)] * 6,
        scratch=[pltpu.VMEM(arg.shape, arg.dtype) for arg in args]
        + [pltpu.VMEM((8, LANES), F32), pltpu.SemaphoreType.DMA((6,))],
    )


def spreads(sides, width, hidden, chunk, up_chunk):
    lane = jnp.arange(LANES, dtype=jnp.int32)[:, None]
    column = jnp.arange(width, dtype=jnp.int32)[None]
    up_column = jnp.arange(hidden, dtype=jnp.int32)[None]
    thin, broad = [], []
    for side in sides:
        thin.append((lane < chunk) & (column % (2 * chunk) == side * chunk + lane))
        broad.append((lane >= UP) & (up_column % (2 * up_chunk) == side * up_chunk + lane - UP))
    return jnp.stack(thin).astype(BF16), jnp.stack(broad).astype(BF16)


def unpack(core, pieces, thin, broad, rel, absolute, up_rel, cols):
    width, hidden = thin.shape[2], broad.shape[2]
    count = width // SMALL

    def kernel(core_ref, thin_ref, broad_ref, rel_ref, abs_ref, up_ref, *refs):
        vec_ref, head_ref, side_ref, proj_ref, e_ref, sems = refs[8:]
        copies = load_weights(refs[:8], e_ref, sems, 4 * cols, 4 * cols + LANES)
        for copy in copies:
            copy.wait()
        first = core_ref[0] == 0
        blocks = [e_ref[side].astype(F32).reshape(count, SMALL, LANES) for side in range(2)]
        tops = [block[:, : SMALL // 2] for block in blocks]
        halves = [jnp.where(first, tops[0], tops[1]), jnp.where(first, tops[1], tops[0])]
        proj_ref[...] = jnp.concatenate(halves, axis=1).reshape(width, LANES).astype(BF16)
        flat = lax.broadcasted_iota(jnp.int32, (count, count * 8), 1)
        pick = flat == 8 * lax.broadcasted_iota(jnp.int32, (count, count * 8), 0)
        pick = pick.astype(F32).astype(BF16)
        vec = jnp.zeros((8, width), F32)
        plain = jnp.zeros((8, width), F32)
        wide = jnp.zeros((1, hidden), F32)
        index = lax.broadcasted_iota(jnp.int32, (count, hidden), 0)
        for side in range(2):
            placed, up_placed = None, None
            for part in (2, 1, 0):
                start = SMALL // 2 + 8 * part
                rows = blocks[side][:, start : start + 8].reshape(count * 8, LANES).astype(BF16)
                spread = nn(rows, thin_ref[side])
                up_spread = nn(nn(pick, rows).astype(BF16), broad_ref[side])
                placed = spread if placed is None else placed + spread
                up_placed = up_spread if up_placed is None else up_placed + up_spread
            for j in range(count):
                row = placed[8 * j : 8 * j + 8]
                vec = vec + jnp.where(rel_ref[...] == j, row, 0.0)
                plain = plain + jnp.where(abs_ref[...] == j, row, 0.0)
            chosen = jnp.where(up_ref[...] == index, up_placed, 0.0)
            wide = wide + jnp.sum(chosen, axis=0, keepdims=True)
        vec_ref[...] = vec
        for side in range(2):
            low_half = first if side == 0 else jnp.logical_not(first)
            part = jnp.where(low_half, plain[:, :cols], plain[:, cols:])
            head_ref[side : side + 1, :cols] = part[2:3]
            head_ref[side : side + 1, cols : 2 * cols] = jnp.zeros((1, cols), F32)
            head_ref[side : side + 1, 2 * cols :] = part[3:4]
            middle = hidden // 2
            side_ref[side : side + 1, :] = jnp.where(low_half, wide[:, :middle], wide[:, middle:])

    outs = (
        shaped((8, width), F32),
        shaped((2, 3 * cols), F32),
        shaped((2, hidden // 2), F32),
        shaped((width, LANES), BF16),
    )
    return call(
        kernel,
        outs,
        (core[None], thin, broad, rel, absolute, up_rel, *pieces),
        in_specs=[pl.BlockSpec(memory_space=pltpu.SMEM)] + [WHOLE] * 5 + [ANY] * 8,
        scratch=[pltpu.VMEM((2, width, LANES), BF16), pltpu.SemaphoreType.DMA((2, 4))],
    )


def pack_grads(
    core, thin, broad, rel, absolute, up_rel, sums_one, sums_two, up_own, up_other, qkv_a, qkv_b,
    proj_grad,
):
    width, hidden = thin.shape[2], broad.shape[2]
    count = width // SMALL

    def kernel(
        core_ref, thin_ref, broad_ref, rel_ref, abs_ref, up_ref, one_ref, two_ref, uo_ref, ux_ref,
        qa_ref, qb_ref, pg_ref, own_ref, other_ref,
    ):
        first = core_ref[0] == 0
        fold = lambda v: jnp.sum(v, axis=0, keepdims=True)

        def ordered(own, other):
            low, high = jnp.where(first, own, other), jnp.where(first, other, own)
            return jnp.concatenate([low, high], axis=1)

        def heads(half, kind):
            return jnp.concatenate([fold(qa_ref[half, kind]), fold(qb_ref[half, kind])], axis=1)

        rows = [
            fold(one_ref[0:8]),
            fold(two_ref[0:8]),
            ordered(heads(0, 0), heads(1, 0)),
            ordered(heads(0, 1), heads(1, 1)),
            fold(one_ref[16:24]),
            fold(one_ref[8:16]),
            fold(two_ref[16:24]),
            fold(two_ref[8:16]),
        ]
        grads = jnp.concatenate(rows, axis=0)
        row = lax.broadcasted_iota(jnp.int32, (8, width), 0)
        block = jnp.where((row == 2) | (row == 3), abs_ref[...], rel_ref[...])
        spread = [jnp.where(block == j, grads, 0.0) for j in range(count)]
        spread = jnp.concatenate(spread, axis=0)
        high = spread.astype(BF16)
        rest = (spread - high.astype(F32)).astype(BF16)
        up = ordered(fold(uo_ref[...]), fold(ux_ref[...]))
        index = lax.broadcasted_iota(jnp.int32, (count, hidden), 0)
        up = jnp.where(up_ref[...] == index, up, 0.0)
        up_high = up.astype(BF16)
        up_rest = (up - up_high.astype(F32)).astype(BF16)
        flat = lax.broadcasted_iota(jnp.int32, (count * 8, count), 0)
        put = flat == 8 * lax.broadcasted_iota(jnp.int32, (count * 8, count), 1)
        put = put.astype(F32).astype(BF16)
        tops = pg_ref[...].reshape(count, SMALL, LANES)
        for side, out_ref in enumerate((own_ref, other_ref)):
            low_half = first if side == 0 else jnp.logical_not(first)
            top = jnp.where(low_half, tops[:, : SMALL // 2], tops[:, SMALL // 2 :])
            thin_part = nt(high, thin_ref[side]) + nt(rest, thin_ref[side])
            up_part = nt(up_high, broad_ref[side]) + nt(up_rest, broad_ref[side])
            vec = (thin_part + nn(put, up_part.astype(BF16))).reshape(count, 8, LANES)
            blank = jnp.zeros((count, SMALL // 2 - 8, LANES), F32)
            made = jnp.concatenate([top, vec, blank], axis=1).reshape(width, LANES).astype(BF16)
            quarter = width // 4
            for place in range(4):
                source = OTHER[place] if side == 1 else place
                out_ref[place * quarter : (place + 1) * quarter, :] = made[
                    source * quarter : (source + 1) * quarter
                ]

    out = shaped((width, LANES), BF16)
    return call(
        kernel,
        (out, out),
        (
            core[None], thin, broad, rel, absolute, up_rel, sums_one, sums_two, up_own, up_other,
            qkv_a, qkv_b, proj_grad,
        ),
        in_specs=[pl.BlockSpec(memory_space=pltpu.SMEM)] + [WHOLE] * 12,
    )


def finish(a_kept, a_came, b_kept, b_came, cols, chunk, up_chunk, emb_shape):
    rows = a_kept.shape[0]
    a_wide = (a_kept.shape[1] - cols) // 3
    b_wide = cols - a_wide

    def kernel(
        ak_ref, ac_ref, bk_ref, bc_ref, qkv_ref, out_ref, emb_ref, gain_ref, bias_ref, up_ref,
        a_ref, b_ref,
    ):
        a_ref[...] = ak_ref[...] + ac_ref[...].astype(F32)
        b_ref[...] = bk_ref[...] + bc_ref[...].astype(F32)
        for part in range(3):
            qkv_ref[part, :, :a_wide] = a_ref[:, part * a_wide : (part + 1) * a_wide]
            qkv_ref[part, :, a_wide:] = b_ref[:, part * b_wide : (part + 1) * b_wide]
        out_ref[...] = a_ref[:, 3 * a_wide :]
        first = 3 * b_wide
        half = SMALL // 2
        emb_ref[...] = b_ref[0:half, first:]
        gain_ref[...] = b_ref[half : half + 2, first : first + chunk]
        bias_ref[...] = b_ref[half + 2 : half + 8, first : first + chunk]
        up_ref[...] = b_ref[half : half + 1, first + UP : first + UP + up_chunk]

    outs = (
        shaped((3, rows, cols), F32),
        shaped((rows, cols), F32),
        shaped(emb_shape, F32),
        shaped((2, chunk), F32),
        shaped((6, chunk), F32),
        shaped((1, up_chunk), F32),
    )
    return call(
        kernel,
        outs,
        (a_kept, a_came, b_kept, b_came),
        scratch=[pltpu.VMEM(a_kept.shape, F32), pltpu.VMEM(b_kept.shape, F32)],
    )


def pack_plain(qkv_w, out_w, emb_w, gains, biases, up_bias):
    rows = out_w.shape[0]
    vector = jnp.concatenate([gains.reshape(-1), biases.reshape(-1), up_bias])
    pad_to = -(-vector.size // LANES) * LANES
    padded = jnp.pad(vector, (0, pad_to - vector.size))
    flat = jnp.concatenate([emb_w.reshape(-1), *three_parts(padded)])
    extra = -(-flat.size // (rows * LANES)) * LANES
    flat = jnp.pad(flat, (0, rows * extra - flat.size)).reshape(rows, extra)
    one = jnp.concatenate([qkv_w[0], qkv_w[1], qkv_w[2], out_w, flat], axis=1)
    sizes = (rows, extra, emb_w.size, gains.shape[1], up_bias.size, pad_to)
    return one, sizes


def unpack_plain(core, sides, pieces, blocks, sizes):
    rows, extra, emb_size, chunk, up_chunk, pad_to = sizes
    size = blocks.shape[0]
    width = size * rows
    cols = width // 2
    ff_local = size * up_chunk
    pieces = [part[:, 4 * cols :] for part in pieces]
    own = jnp.concatenate(pieces[:4])
    other = jnp.concatenate([pieces[4 + place] for place in OTHER])
    small = [part.reshape(size, rows * extra) for part in (own, other)]
    small = jnp.where(core == 0, jnp.stack(small, 1), jnp.stack(small[::-1], 1))
    proj = small[:, :, :emb_size].reshape(width, -1)
    thirds = small[:, :, emb_size : emb_size + 3 * pad_to].astype(F32)
    thirds = thirds.reshape(size, 2, 3, pad_to)
    vectors = thirds[:, :, 0] + (thirds[:, :, 1] + thirds[:, :, 2])
    plain = vectors[jnp.argsort(blocks)].reshape(size * 2, pad_to)
    vectors = vectors.reshape(size * 2, pad_to)
    vec = jnp.moveaxis(vectors[:, : 8 * chunk].reshape(-1, 8, chunk), 1, 0).reshape(8, width)
    query_bias = plain[:, 2 * chunk : 3 * chunk].reshape(-1)
    value_bias = plain[:, 3 * chunk : 4 * chunk].reshape(-1)
    up_bias = plain[:, 8 * chunk : 8 * chunk + up_chunk].reshape(-1)
    head_bias, side_bias = [], []
    for side in sides:
        query_part = lax.dynamic_slice_in_dim(query_bias, side * cols, cols)
        value_part = lax.dynamic_slice_in_dim(value_bias, side * cols, cols)
        head_bias.append(jnp.concatenate([query_part, jnp.zeros_like(query_part), value_part]))
        side_bias.append(lax.dynamic_slice_in_dim(up_bias, side * ff_local, ff_local))
    return vec, jnp.stack(head_bias), jnp.stack(side_bias), proj


def pack_grads_plain(
    core, blocks, sizes, sums_one, sums_two, up_own, up_other, qkv_a, qkv_b, proj_grad
):
    rows, extra, emb_size, chunk, up_chunk, pad_to = sizes
    size = blocks.shape[0]

    def fold(value):
        return jnp.sum(value.reshape(-1, 8, value.shape[-1]), axis=1)

    def absolute(own, other):
        return jnp.where(
            core == 0, jnp.concatenate([own, other]), jnp.concatenate([other, own])
        )

    def relative(value):
        return value.reshape(size, 2, -1)[blocks]

    gain_two, shift_two, ffn_bias = (row.reshape(size, 2, chunk) for row in fold(sums_two))
    gain_one, shift_one, out_bias = (row.reshape(size, 2, chunk) for row in fold(sums_one))
    own, other = jnp.sum(jnp.concatenate([qkv_a, qkv_b], axis=3), axis=2)
    small = jnp.concatenate(
        [
            proj_grad.reshape(size, 2, emb_size),
            gain_one,
            gain_two,
            relative(absolute(own[0], other[0])),
            relative(absolute(own[1], other[1])),
            out_bias,
            shift_one,
            ffn_bias,
            shift_two,
            relative(absolute(fold(up_own)[0], fold(up_other)[0])),
        ],
        axis=2,
    ).astype(BF16)
    small = jnp.pad(small, ((0, 0), (0, 0), (0, rows * extra - small.shape[2])))
    small = jnp.where(core == 0, small, small[:, ::-1])
    own, other = jnp.moveaxis(small, 1, 0).reshape(2, size * rows, extra)
    first, second, third, fourth = jnp.split(other, 4)
    return own, jnp.concatenate([first, third, second, fourth])


def body(
    tokens,
    lengths,
    key_mask,
    order,
    query_key_value_weight,
    output_projection_weight,
    up_projection_weight,
    down_projection_weight,
    embedding_projection_weight,
    gains,
    biases,
    up_bias_vector,
    cotangent,
):
    size = lax.axis_size("dp")
    core = lax.axis_index("tensor")
    ways = Exchange(size)
    depth = ways.depth
    half_len = tokens.shape[1]
    full_len = key_mask.shape[1]
    width = tokens.shape[2]
    cols = output_projection_weight.shape[0]
    rows = output_projection_weight.shape[1]
    ff_local = up_projection_weight.shape[1]
    chunk = gains.shape[1]
    emb_size = embedding_projection_weight.size
    sides = (core, 1 - core)

    fast = rows == SMALL and emb_size == SMALL // 2 * LANES and up_bias_vector.size <= LANES - UP
    small_args = (
        query_key_value_weight,
        output_projection_weight.T,
        embedding_projection_weight,
        gains,
        biases,
        up_bias_vector,
    )
    if fast:
        one = pack(*small_args)
    else:
        one, small_sizes = pack_plain(*small_args)

    wide = 4 * cols
    seconds, lasts = depth - 2, depth - 1
    for step in range(depth - 3):
        one = join(one, ways.flip(one, step))
    tokens, order, lengths, key_mask = after((tokens, order, lengths, key_mask), one)
    mine = order[0, core]
    theirs = order[0, 1 - core]
    my_half = lax.dynamic_index_in_dim(tokens, mine, 0, keepdims=False)
    their_half = lax.dynamic_index_in_dim(tokens, theirs, 0, keepdims=False)
    blocks = ways.blocks()
    one_came = ways.flip(one, depth - 3)
    if fast:
        thin, broad = spreads(sides, width, 2 * ff_local, chunk, up_bias_vector.size)
        places_of = jnp.argsort(blocks)
        rel = (jnp.arange(width, dtype=jnp.int32) // rows)[None]
        absolute = jnp.repeat(places_of, rows)[None].astype(jnp.int32)
        up_rel = jnp.repeat(places_of, 2 * up_bias_vector.size)[None].astype(jnp.int32)
        one_came, thin, broad, rel, absolute, up_rel = together(
            one_came, thin, broad, rel, absolute, up_rel
        )
        tables = (core, thin, broad, rel, absolute, up_rel)

    def in_order(own, other):
        return jnp.where(
            core == 0, jnp.concatenate([own, other]), jnp.concatenate([other, own])
        )

    def half_of(value, which):
        return lax.dynamic_slice_in_dim(value, which * half_len, half_len)

    seq_len = lengths[mine]
    marks = lax.dynamic_index_in_dim(key_mask, mine, 0, keepdims=False)
    places = jnp.arange(full_len, dtype=jnp.int32)
    key_ok = (places < seq_len) & ((marks == 1) | (places == 0))
    mask = jnp.where(key_ok, 0.0, -1e30).astype(F32)[None, :]
    where = (blocks[:, None] * rows + jnp.arange(rows, dtype=jnp.int32)[None]).reshape(-1)
    perm = (jnp.arange(width, dtype=jnp.int32)[:, None] == where[None]).astype(BF16)
    two, three = after((up_projection_weight, down_projection_weight.T), order)
    for step in range(depth - 4):
        two = join(two, ways.flip(two, step))
        three = join(three, ways.flip(three, step))
    two_came = ways.flip(two, depth - 4)
    one_came, two_came = together(one_came, two_came)
    one = join(one, one_came)
    two = join(two, two_came)
    here = in_order(my_half, swap_cores(after(their_half, one)))
    one_b, one_c, two_came, three_came, here, mask, perm = together(
        ways.flip(one, seconds),
        ways.flip(one, lasts),
        ways.flip(two, depth - 3),
        ways.flip(after(three, two), depth - 4),
        here,
        mask,
        perm,
    )
    two = join(two, two_came)
    three = join(three, three_came)
    one_d, two_b, three_came, *one_other = together(
        ways.flip(one_b, lasts),
        ways.flip(two, seconds),
        ways.flip(three, depth - 3),
        swap_cores(one),
        swap_cores(one_b),
        swap_cores(one_c),
    )
    three = join(three, three_came)
    two_both = join(two, two_b)
    one_pieces = (one, one_b, one_c, one_d, *one_other, swap_cores(one_d))
    two_more, three_b = ways.flip(two_both, lasts), ways.flip(three, seconds)
    one_pieces = together(*one_pieces, two_both, three)[:8]
    if fast:
        vec, head_bias, side_bias, proj = unpack(core, one_pieces, *tables[1:], cols)
    else:
        vec, head_bias, side_bias, proj = unpack_plain(
            core, sides, one_pieces, blocks, small_sizes
        )
    side_bias = (side_bias[0:1], side_bias[1:2])

    qkv, lse, att, res_one, first, first_low, first_low_t, here_t, weights = attention_forward(
        here, perm, head_bias, mask, vec, one_pieces, cols
    )
    two_more, three_b = after((two_more, three_b), first_low)
    three_both = join(three, three_b)
    three_more = ways.flip(three_both, lasts)
    two_other = [swap_cores(part) for part in (two_both, two_more)]

    def quarters(both, more):
        return ((both, 0), (both, 1), (more, 0), (more, 1))

    two_own = quarters(two_both, two_more)
    hid_own, slope_own = up_forward(
        after(first_low, three_both, two_more), two_own, side_bias[0], False
    )
    two_other = quarters(*after(two_other, hid_own))
    three_both_other = swap_cores(three_both)
    hid_other, slope_other = up_forward(first_low, two_other, side_bias[1], True)
    three_more, three_both_other = after((three_more, three_both_other), hid_other)
    cot_mine = lax.dynamic_index_in_dim(cotangent, core, 0, keepdims=False)
    cot_other = lax.dynamic_index_in_dim(cotangent, 1 - core, 0, keepdims=False)
    cot = in_order(cot_mine, after(swap_cores(cot_other), hid_other))
    three_own = quarters(three_both, three_more)
    three_other = quarters(three_both_other, swap_cores(three_more))
    emb, g_ffn, g_ffn_t, g_res_two, proj_grad, sums_two = down_both(
        seq_len[None], (hid_own, hid_other), (*three_own, *three_other), first, vec, proj, cot
    )

    def low(*values):
        return added(*values).astype(BF16)

    def spread(value):
        kept, sent = halves(value)
        return kept, sent.astype(BF16)

    dk_other, ds_other = down_grad(g_ffn_t, hid_other, True)
    ds_came, dk_came = swap_cores(ds_other), swap_cores(dk_other)
    dk, ds = down_grad(g_ffn_t, after(hid_own, ds_other), False)
    ds_came, dk_came = after((ds_came, dk_came), ds)
    d_sent = low(ds, ds_came)
    d_came = ways.flip(d_sent, lasts)
    uk_other, us_other, up_bias_other, part = up_grad(
        after(g_ffn, d_sent),
        first_low_t,
        slope_other,
        three_other,
        two_other,
        g_res_two,
        True,
    )
    us_came, uk_came = swap_cores(us_other), swap_cores(uk_other)
    d_came = after(d_came, us_other)
    d_sent = low(halves(dk)[1], halves(dk_came)[1], halves(d_came)[1])
    d_held = added(halves(dk)[0], halves(dk_came)[0], halves(d_came)[0])
    d_came = ways.flip(d_sent, seconds)
    uk, us, up_bias_own, g_first = up_grad(
        after(g_ffn, us_other, d_sent),
        first_low_t,
        slope_own,
        three_own,
        two_own,
        part,
        False,
    )
    d_came, us_came, uk_came = after((d_came, us_came, uk_came), us)
    u_sent = low(us, us_came)
    u_came = ways.flip(u_sent, lasts)
    d_held, d_sent = spread(d_held + d_came.astype(F32))
    d_came = ways.flip(d_sent, depth - 3)
    g_res_one, g_branch_t, g_att, sums_one = norm_back(
        after(g_first, u_sent, d_sent), res_one, vec, weights, cols
    )
    pairs = list(range(cols // LANES))
    split = (len(pairs) + 1) // 2
    g_a, bias_a = attention_back(pairs[:split], g_att, att, qkv, lse, mask)
    beside = (g_branch_t, att)
    ak_other, as_other = project_other(here_t, g_a, beside)
    as_came, ak_came = swap_cores(as_other), swap_cores(ak_other)
    g_b, bias_b = attention_back(pairs[split:], after(g_att, as_other), att, qkv, lse, mask)
    as_came, ak_came = after((as_came, ak_came), g_b)
    a_keep, a_send = project_own(here_t, g_a, beside, (), ak_came, as_came)
    d_came, u_came = after((d_came, u_came), a_send)
    a_came = ways.flip(a_send, lasts)
    u_sent = low(halves(uk)[1], halves(uk_came)[1], halves(u_came)[1])
    u_held = added(halves(uk)[0], halves(uk_came)[0], halves(u_came)[0])
    u_came = ways.flip(u_sent, seconds)
    d_held, d_sent = spread(d_held + d_came.astype(F32))
    d_came = ways.flip(d_sent, depth - 4)
    bk_other, bs_other = project_other(here_t, after(g_b, a_send, u_sent, d_sent), ())
    bs_came, bk_came = swap_cores(bs_other), swap_cores(bk_other)
    if fast:
        small_own, small_other = pack_grads(
            *tables, sums_one, after(sums_two, bs_other), up_bias_own, up_bias_other, bias_a,
            bias_b, proj_grad,
        )
    else:
        small_own, small_other = pack_grads_plain(
            core, blocks, small_sizes, sums_one, sums_two, up_bias_own, up_bias_other, bias_a,
            bias_b, proj_grad,
        )
    small_came = swap_cores(small_other)
    bs_came, bk_came = after((bs_came, bk_came), small_other)
    b_keep, b_send = project_own(here_t, g_b, (), (small_own, small_came), bk_came, bs_came)
    d_came, u_came, a_came = after((d_came, u_came, a_came), b_send)
    b_came = ways.flip(b_send, lasts)
    a_sent = low(halves(a_keep)[1], halves(a_came)[1])
    a_held = added(halves(a_keep)[0], halves(a_came)[0])
    a_came = ways.flip(a_sent, seconds)
    u_held, u_sent = spread(u_held + u_came.astype(F32))
    u_came = ways.flip(u_sent, depth - 3)
    d_held = d_held + d_came.astype(F32)
    g_here = token_back(
        (after(g_a, b_send, a_sent, u_sent), g_b), g_res_one, perm, weights, cols
    )
    a_came, b_came, u_came = after((a_came, b_came, u_came), g_here)
    b_sent = low(halves(b_keep)[1], halves(b_came)[1])
    b_held = added(halves(b_keep)[0], halves(b_came)[0])
    b_came = ways.flip(b_sent, seconds)
    a_held, a_sent = spread(a_held + a_came.astype(F32))
    a_came = ways.flip(a_sent, depth - 3)
    u_held, u_sent = spread(u_held + u_came.astype(F32))
    u_came = ways.flip(u_sent, depth - 4)
    for step in range(depth - 5, -1, -1):
        d_held, sent = spread(d_held)
        d_held = d_held + ways.flip(sent, step).astype(F32)
        u_held, sent = spread(u_held + u_came.astype(F32))
        u_came = ways.flip(sent, step)
    down_shard, up_shard = d_held, u_held + u_came.astype(F32)
    b_held, b_sent = spread(b_held + b_came.astype(F32))
    b_came = ways.flip(b_sent, depth - 3)
    for step in range(depth - 4, -1, -1):
        a_held, sent = spread(a_held + a_came.astype(F32))
        a_came = ways.flip(sent, step)
        b_held, sent = spread(b_held + b_came.astype(F32))
        b_came = ways.flip(sent, step)
    if fast:
        qkv_shard, out_shard, emb_shard, gain_shard, bias_shard, up_bias_shard = finish(
            a_held,
            a_came,
            b_held,
            b_came,
            cols,
            chunk,
            up_bias_vector.size,
            embedding_projection_weight.shape,
        )
        out_shard, up_bias_shard = out_shard.T, up_bias_shard[0]
    else:
        a_shard = a_held + a_came.astype(F32)
        b_shard = b_held + b_came.astype(F32)
        a_wide, b_wide = split * LANES, (len(pairs) - split) * LANES
        qkv_shard = jnp.stack(
            [
                jnp.concatenate(
                    [
                        a_shard[:, i * a_wide : (i + 1) * a_wide],
                        b_shard[:, i * b_wide : (i + 1) * b_wide],
                    ],
                    axis=1,
                )
                for i in range(3)
            ]
        )
        out_shard = a_shard[:, 3 * a_wide :].T
        tail = b_shard[:, 3 * b_wide :].reshape(-1)
        emb_shard = tail[:emb_size].reshape(embedding_projection_weight.shape)
        tail = tail[emb_size:]
        gain_shard = tail[: 2 * chunk].reshape(2, chunk)
        bias_shard = tail[2 * chunk : 8 * chunk].reshape(6, chunk)
        up_bias_shard = tail[8 * chunk : 8 * chunk + up_bias_vector.size]

    def give_back(value, places_of):
        own = half_of(value, core)
        other = swap_cores(half_of(value, 1 - core))
        blank = jnp.zeros((2,) + own.shape, value.dtype)
        blank = lax.dynamic_update_slice(blank, own[None], (places_of[0], 0, 0))
        return lax.dynamic_update_slice(blank, other[None], (places_of[1], 0, 0))

    embeddings = give_back(emb, (core, 1 - core))
    grad_tokens = give_back(g_here, (mine, theirs))
    return (
        embeddings,
        grad_tokens,
        qkv_shard,
        out_shard,
        up_shard,
        down_shard.T,
        emb_shard,
        gain_shard,
        bias_shard,
        up_bias_shard,
    )


def solution(mesh):
    return jax.shard_map(
        body,
        mesh=mesh,
        in_specs=(
            P("dp", "tensor", None),
            P("dp"),
            P("dp", None),
            P("dp", None),
            P(None, "dp", "tensor"),
            P("tensor", "dp"),
            P("dp", "tensor"),
            P("tensor", "dp"),
            P(("dp", "tensor"), None),
            P(None, ("dp", "tensor")),
            P(None, ("dp", "tensor")),
            P(("dp", "tensor")),
            P("dp", "tensor", None),
        ),
        out_specs=(
            P("dp", "tensor", None),
            P("dp", "tensor", None),
            P(None, "dp", "tensor"),
            P("tensor", "dp"),
            P("dp", "tensor"),
            P("tensor", "dp"),
            P(("dp", "tensor"), None),
            P(None, ("dp", "tensor")),
            P(None, ("dp", "tensor")),
            P(("dp", "tensor")),
        ),
        check_vma=False,
    )
```

time: 322 us -> 237 us (0.74)
  Pallas kernels: 116 us -> 85.3 us
  other arithmetic: 42.1 us -> 16.6 us
  waiting for transfers between devices: 83.5 us -> 61.9 us
  local copies, waits for them, and re-layouts: 41.3 us -> 22.6 us
  starting transfers between devices: 31.9 us -> 44.5 us
    pallas_call x11 -> x20, Pallas kernels: 116 us -> 85.3 us  [call(): pl.pallas_call(body, out_shape=outs, grid=grid or (), in_specs=in_specs o...]
    ppermute x24 -> x29, waiting for transfers between devices: 80.6 us -> 56.8 us  [flip(): return lax.ppermute(value, ('dp', 'tensor'), pairs)]
    ppermute x24 -> x29, starting transfers between devices: 27.8 us -> 40.8 us  [flip(): return lax.ppermute(value, ('dp', 'tensor'), pairs)]
    unnamed x89 -> x114, local copies, waits for them, and re-layouts: 7.43 us -> 16.8 us
    convert_element_type x6, other arithmetic: 12.3 us -> 3.33 us  [low(): return added(*values).astype(BF16)]
    another operation x21 -> x2, local copies, waits for them, and re-layouts: 7.28 us -> 0.17 us  [the longest x1 0.08 us: body(): jnp.repeat(places_of, 2 * up_bias_vector.size)[None].astype(jnp.int32)]
    reshape x13 -> x0, local copies, waits for them, and re-layouts: 6.33 us -> none  [the longest x2 3.29 us: body(): proj_grad.reshape(size, 2, emb_size)]
    reduce_sum x5 -> x0, other arithmetic: 5.88 us -> none  [the longest x4 3.78 us: fold(): return jnp.sum(value.reshape(-1, 8, value.shape[-1]), axis=1)]
  transfers between devices with their start and end apart: 40 -> 50, of which waited for: 15 -> 22; matrix products, arithmetic and copies ran while one was open for 18% -> 9% of each run, Pallas kernels for 24% -> 31%
where the time goes in v1:
time: 237 us; the launch traced here: 236 us
  Pallas kernels  85.3 us (36%)
  waiting for transfers between devices  61.9 us (26%)
  starting transfers between devices  44.5 us (19%)
  local copies, waits for them, and re-layouts  22.6 us (10%)
  other arithmetic  16.6 us (7%)
  between operations  5.65 us (2%)
    pallas_call x20, Pallas kernels, call(): pl.pallas_call(body, out_shape=outs, grid=grid or (), in_specs=in_specs o...  85.3 us
    ppermute x29, waiting for transfers between devices, flip(): return lax.ppermute(value, ('dp', 'tensor'), pairs)  56.8 us
    ppermute x29, starting transfers between devices, flip(): return lax.ppermute(value, ('dp', 'tensor'), pairs)  40.8 us
    unnamed x114, local copies, waits for them, and re-layouts  16.8 us
    ppermute x21, waiting for transfers between devices, swap_cores(): return lax.ppermute(value, 'tensor', [(0, 1), (1, 0)])  5.03 us
  transfers between devices with their start and end apart: 50, of which 22 were waited for; matrix products, arithmetic and copies ran while one was open for 9% of the time, Pallas kernels for 31%

profile of v1, /device:TPU:0, one launch (start us, length us, event | category | flops | bytes accessed | tf_op | source)
XLA Modules:
  0.0 236.5 jit_solution(7781790444923238319)
XLA Ops:
  5.4 4.1 %collective-permute-start = (bf16[48,1664]{1,0:T(8,128)(2,1)S(1)}, bf16[48,1664]{1,0:T(8,128)(2,1)S(1)}, u32[]{:S(2)}, u32[]{:S(2)}) collective-permute-start(bf16[48,1664]{1,0:T(8,128)(2,1)S(1)} %shard_map.222), channel_id=1, source_target_pairs={{0,16},{1,17},{2,18},{3,19},{4,20},{5,21},{6,22},{7,23},{8,24},{9,... | collective-permute-start | bytes 479240 | tf_op jit(solution)/shard_map/ppermute | solution.py:679
  13.0 4.0 %collective-permute-done = bf16[48,1664]{1,0:T(8,128)(2,1)S(1)} collective-permute-done((bf16[48,1664]{1,0:T(8,128)(2,1)S(1)}, bf16[48,1664]{1,0:T(8,128)(2,1)S(1)}, u32[]{:S(2)}, u32[]{:S(2)}) %collective-permute-start) | collective-permute-done | bytes 159776 | tf_op jit(solution)/shard_map/ppermute | solution.py:679
  18.5 3.4 %collective-permute-start.2 = (bf16[48,1536]{1,0:T(8,128)(2,1)}, bf16[48,1536]{1,0:T(8,128)(2,1)}, u32[]{:S(2)}, u32[]{:S(2)}) collective-permute-start(bf16[48,1536]{1,0:T(8,128)(2,1)} %param.21), channel_id=1, source_target_pairs={{0,16},{1,17},{2,18},{3,19},{4,20},{5,21},{6,22},{7,23},{8,24},{9,... | collective-permute-start | bytes 442376 | tf_op jit(solution)/shard_map/ppermute | solution.py:679
  21.8 1.6 constant_dynamic-update-slice_fusion.5
  31.0 1.3 collective-permute-start.3
  32.3 1.5 collective-permute-start.4
  34.7 3.4 %collective-permute-start.5 = (bf16[96,1536]{1,0:T(8,128)(2,1)S(1)}, bf16[96,1536]{1,0:T(8,128)(2,1)S(1)}, u32[]{:S(2)}, u32[]{:S(2)}) collective-permute-start(bf16[96,1536]{1,0:T(8,128)(2,1)S(1)} %get-tuple-element.285), channel_id=1, source_target_pairs={{0,8},{1,9},{2,10},{3,11},{4,12},{5,13},{6,14},{7,15},{8,0},{9,1},... | collective-permute-start | bytes 884744 | tf_op jit(solution)/shard_map/ppermute | solution.py:679
  39.3 1.7 collective-permute-start.6
  42.1 6.1 %collective-permute-done.6 = bf16[48,1536]{1,0:T(8,128)(2,1)S(1)} collective-permute-done((bf16[48,1536]{1,0:T(8,128)(2,1)S(1)}, bf16[48,1536]{1,0:T(8,128)(2,1)S(1)}, u32[]{:S(2)}, u32[]{:S(2)}) %collective-permute-start.6) | collective-permute-done | bytes 147488 | tf_op jit(solution)/shard_map/ppermute | solution.py:679
  50.7 1.6 collective-permute-start.9
  52.4 2.2 collective-permute-start.10
  54.6 7.2 %collective-permute-done.10 = bf16[96,1536]{1,0:T(8,128)(2,1)S(1)} collective-permute-done((bf16[96,1536]{1,0:T(8,128)(2,1)S(1)}, bf16[96,1536]{1,0:T(8,128)(2,1)S(1)}, u32[]{:S(2)}, u32[]{:S(2)}) %collective-permute-start.10) | collective-permute-done | bytes 294944 | tf_op jit(solution)/shard_map/ppermute | solution.py:679
  61.7 3.5 %collective-permute-done.9 = bf16[192,1536]{1,0:T(8,128)(2,1)S(1)} collective-permute-done((bf16[192,1536]{1,0:T(8,128)(2,1)S(1)}, bf16[192,1536]{1,0:T(8,128)(2,1)S(1)}, u32[]{:S(2)}, u32[]{:S(2)}) %collective-permute-start.9) | collective-permute-done | bytes 589856 | tf_op jit(solution)/shard_map/ppermute | solution.py:679
  66.1 1.6 collective-permute-start.16
  68.1 1.7 shard_map.223
  69.8 15.6 %shard_map.224 = (bf16[2,512,1152]{2,1,0:T(8,128)(2,1)S(1)}, f32[2,6,512]{2,1,0:T(8,128)S(1)}, bf16[2,512,384]{2,1,0:T(8,128)(2,1)S(1)}, f32[512,768]{1,0:T(8,12...) custom-call(bf16[512,768]{1,0:T(8,128)(2,1)S(1)} %maximum_select_fus, ...), custom_call_target="tpu_custom_call" | custom-call | flops 2415919104 | bytes 1048576 | tf_op jit(solution)/shard_map/pallas_call | solution.py:59
  85.4 2.5 %collective-permute-done.15.c_ref.d_ref.refs_6_.refs_7_ = bf16[384,1536]{1,0:T(8,128)(2,1)S(1)} collective-permute-done((bf16[384,1536]{1,0:T(8,128)(2,1)S(1)}, bf16[384,1536]{1,0:T(8,128)(2,1)S(1)}, u32[]{:S(2)}, u32[]{:S(2)}) %collective-permute-start.15) | collective-permute-done | bytes 1179680 | tf_op jit(solution)/shard_map/ppermute | solution.py:679
  88.8 5.1 %shard_map.225 = (bf16[512,1536]{1,0:T(8,128)(2,1)S(1)}, bf16[512,1536]{1,0:T(8,128)(2,1)S(1)}) custom-call(bf16[512,768]{1,0:T(8,128)(2,1)S(1)} %get-tuple-element.184.low_ref, bf16[384,1536]{1,0:T(8,128)(2,1)S(1)} %constant_dynamic-update-slice_fusion.2.a_ref.b_ref.refs_4_.refs_5_, ...), custom_call_target="tpu_custom_call" | custom-call | flops 1207959552 | bytes 1048576 | tf_op jit(solution)/shard_map/pallas_call | solution.py:59
  93.9 5.1 %shard_map.226 = (bf16[512,1536]{1,0:T(8,128)(2,1)S(1)}, bf16[512,1536]{1,0:T(8,128)(2,1)S(1)}) custom-call(bf16[512,768]{1,0:T(8,128)(2,1)S(1)} %get-tuple-element.184.low_ref, bf16[384,1536]{1,0:T(8,128)(2,1)S(1)} %collective-permute-done.17.a_ref.b_ref.refs_4_.refs_5_, bf16[384,1536]{1,0:T(8,128)(2,1)S(1)} %collective-permute-done.17.a_ref.b_ref.refs_4_.refs_5_, ...), custom_call_target="tpu_custom_call" | custom-call | flops 1207959552 | bytes 1048576 | tf_op jit(solution)/shard_map/pallas_call | solution.py:59
  99.0 5.2 %collective-permute-done.20.refs_2_.refs_3_ = bf16[384,1536]{1,0:T(8,128)(2,1)S(1)} collective-permute-done((bf16[384,1536]{1,0:T(8,128)(2,1)S(1)}, bf16[384,1536]{1,0:T(8,128)(2,1)S(1)}, u32[]{:S(2)}, u32[]{:S(2)}) %collective-permute-start.20) | collective-permute-done | bytes 1179680 | tf_op jit(solution)/shard_map/ppermute | solution.py:679
  104.8 2.4 %collective-permute-done.19 = f32[256,128]{1,0:T(8,128)S(1)} collective-permute-done((f32[256,128]{1,0:T(8,128)S(1)}, f32[256,128]{1,0:T(8,128)S(1)}, u32[]{:S(2)}, u32[]{:S(2)}) %collective-permute-start.19) | collective-permute-done | bytes 131104 | tf_op jit(solution)/shard_map/ppermute | solution.py:28
  107.3 9.2 %shard_map.227 = (f32[512,128]{1,0:T(8,128)S(1)}, bf16[512,768]{1,0:T(8,128)(2,1)S(1)}, bf16[768,512]{1,0:T(8,128)(2,1)S(1)}, f32[512,768]{1,0:T(8,128)S(1)}, f3...) custom-call(s32[1]{0:T(128)} %dynamic_slice.40.len_ref, bf16[512,1536]{1,0:T(8,128)(2,1)S(1)} %get-tuple-element.199.h0_ref.hid_ref, ...), custom_call_target="tpu_custom_call" | custom-call | flops 2415919104 | bytes 1048576 | tf_op jit(solution)/shard_map/pallas_call | solution.py:59
  116.5 2.0 shard_map.228
  119.1 2.0 shard_map.229
  121.4 1.7 collective-permute-done.25
  124.0 8.6 %shard_map.230 = (bf16[384,1536]{1,0:T(8,128)(2,1)S(1)}, bf16[384,1536]{1,0:T(8,128)(2,1)S(1)}, f32[8,1536]{1,0:T(8,128)S(1)}, f32[512,768]{1,0:T(8,128)S(1)}) custom-call(bf16[512,768]{1,0:T(8,128)(2,1)S(1)} %get-tuple-element.211.g_ref, bf16[768,512]{1,0:T(8,128)(2,1)S(1)} %get-tuple-element.204.lowt_ref, ...), custom_call_target="tpu_custom_call" | custom-call | flops 3623878656 | bytes 1048576 | tf_op jit(solution)/shard_map/pallas_call | solution.py:59
  133.3 6.4 %collective-permute-done.26 = bf16[384,1536]{1,0:T(8,128)(2,1)S(1)} collective-permute-done((bf16[384,1536]{1,0:T(8,128)(2,1)S(1)}, bf16[384,1536]{1,0:T(8,128)(2,1)S(1)}, u32[]{:S(2)}, u32[]{:S(2)}) %collective-permute-start.26) | collective-permute-done | bytes 1179680 | tf_op jit(solution)/shard_map/ppermute | solution.py:679
  140.5 8.6 %shard_map.231 = (bf16[384,1536]{1,0:T(8,128)(2,1)S(1)}, bf16[384,1536]{1,0:T(8,128)(2,1)S(1)}, f32[8,1536]{1,0:T(8,128)S(1)}, f32[512,768]{1,0:T(8,128)S(1)}) custom-call(bf16[512,768]{1,0:T(8,128)(2,1)S(1)} %get-tuple-element.211.g_ref, bf16[768,512]{1,0:T(8,128)(2,1)S(1)} %get-tuple-element.204.lowt_ref, ...), custom_call_target="tpu_custom_call" | custom-call | flops 3623878656 | bytes 1048576 | tf_op jit(solution)/shard_map/pallas_call | solution.py:59
  151.1 2.4 %shard_map.232 = (f32[512,768]{1,0:T(8,128)S(1)}, bf16[768,512]{1,0:T(8,128)(2,1)S(1)}, bf16[2,512,384]{2,1,0:T(8,128)(2,1)S(1)}, f32[24,768]{1,0:T(8,128)S(1)}) custom-call(f32[512,768]{1,0:T(8,128)S(1)} %get-tuple-element.219.gf_ref, f32[512,768]{1,0:T(8,128)S(1)} %get-tuple-element.220.res_ref, f32[8,768]{1,0:T(8,128)S(1)} %get-tuple-element.180.vec_ref, ...), custom_call_target="tpu_custom_call" | custom-call | flops 603979776 | bytes 1048576 | tf_op jit(solution)/shard_map/pallas_call | solution.py:59
  155.3 6.8 %shard_map.233 = (bf16[2,512,768]{2,1,0:T(8,128)(2,1)S(1)}, f32[2,2,8,256]{3,2,1,0:T(8,128)S(1)}) custom-call(bf16[2,512,384]{2,1,0:T(8,128)(2,1)S(1)} %get-tuple-element.230.gatt_ref, bf16[2,512,384]{2,1,0:T(8,128)(2,1)S(1)} %get-tuple-element.223.att_ref.refs_1_, bf16[2,512,1152]{2,1,0:T(8,128)(2,1)S(1)} %get-tuple-element.224.qkv_ref, ...), custom_call_target="tpu_custom_call" | custom-call | flops 2684354560 | bytes 1048576 | tf_op jit(solution)/shard_map/pallas_call | solution.py:59
  164.5 2.7 %collective-permute-start.32 = (bf16[96,1536]{1,0:T(8,128)(2,1)S(1)}, bf16[96,1536]{1,0:T(8,128)(2,1)S(1)}, u32[]{:S(2)}, u32[]{:S(2)}) collective-permute-start(bf16[96,1536]{1,0:T(8,128)(2,1)S(1)} %slice.213), channel_id=1, source_target_pairs={{0,8},{1,9},{2,10},{3,11},{4,12},{5,13},{6,14},{7,15},{8,0},{9,1},... | collective-permute-start | bytes 884744 | tf_op jit(solution)/shard_map/ppermute | solution.py:679
  167.3 3.7 %shard_map.235 = (bf16[2,512,384]{2,1,0:T(8,128)(2,1)S(1)}, f32[2,2,8,128]{3,2,1,0:T(8,128)S(1)}) custom-call(bf16[2,512,384]{2,1,0:T(8,128)(2,1)S(1)} %get-tuple-element.230.gatt_ref, bf16[2,512,384]{2,1,0:T(8,128)(2,1)S(1)} %get-tuple-element.223.att_ref.refs_1_, bf16[2,512,1152]{2,1,0:T(8,128)(2,1)S(1)} %get-tuple-element.224.qkv_ref, ...), custom_call_target="tpu_custom_call" | custom-call | flops 1342177280 | bytes 1048576 | tf_op jit(solution)/shard_map/pallas_call | solution.py:59
  171.0 2.2 shard_map.236
  173.2 1.5 collective-permute-start.39
  187.5 2.4 %shard_map.238 = (bf16[768,128]{1,0:T(8,128)(2,1)S(1)}, bf16[768,128]{1,0:T(8,128)(2,1)S(1)}) custom-call(s32[1]{0:T(128)} %bitcast.8.core_ref, bf16[2,128,768]{2,1,0:T(8,128)(2,1)S(1)} %copy-done.8, bf16[2,128,3072]{2,1,0:T(8,128)(2,1)S(1)} %add_convert_fusion.broad_ref, s32[1,768]{1,0:T(1,128)S(1)} %and_select_fusion.rel_ref, s32[1,768]{1,0:T(1,128)S(1)} %copy-done.32, ...), custom_call_target="tpu_custom_call" | custom-call | bytes 1048576 | tf_op jit(solution)/shard_map/pallas_call | solution.py:59
  189.9 1.8 collective-permute-start.37
  193.2 1.7 shard_map.239
  194.9 1.6 collective-permute-start.42
  196.5 3.8 %collective-permute-done.37 = bf16[48,1536]{1,0:T(8,128)(2,1)S(1)} collective-permute-done((bf16[48,1536]{1,0:T(8,128)(2,1)S(1)}, bf16[48,1536]{1,0:T(8,128)(2,1)S(1)}, u32[]{:S(2)}, u32[]{:S(2)}) %collective-permute-start.37) | collective-permute-done | bytes 147488 | tf_op jit(solution)/shard_map/ppermute | solution.py:679
  200.3 1.8 convert_add_fusion
  204.7 1.7 fusion.1
  206.4 4.7 %shard_map.240 = f32[512,768]{1,0:T(8,128)S(1)} custom-call(bf16[2,512,768]{2,1,0:T(8,128)(2,1)S(1)} %copy-done.2, bf16[2,512,384]{2,1,0:T(8,128)(2,1)S(1)} %copy-done.4, f32[512,768]{1,0:T(8,128)S(1)} %copy-done.10, bf16[768,768]{1,0:T(8,128)(2,1)S(1)} %copy-done.6, bf16[2,768,1536]{2,1,0:T(8,128)(2,1)S(1)} %bitcast.28), custom_call_target="tpu_custom_call" | custom-call | flops 2415919104 | bytes 1048576 | tf_op jit(solution)/shard_map/pallas_call | solution.py:59
  212.0 2.9 %collective-permute-start.49 = (bf16[48,1536]{1,0:T(8,128)(2,1)S(1)}, bf16[48,1536]{1,0:T(8,128)(2,1)S(1)}, u32[]{:S(2)}, u32[]{:S(2)}) collective-permute-start(bf16[48,1536]{1,0:T(8,128)(2,1)S(1)} %slice.215), channel_id=1, source_target_pairs={{0,16},{1,17},{2,18},{3,19},{4,20},{5,21},{6,22},{7,23},{8,24},{9,... | collective-permute-start | bytes 442376 | tf_op jit(solution)/shard_map/ppermute | solution.py:679
  217.5 4.7 %collective-permute-done.49 = bf16[48,1536]{1,0:T(8,128)(2,1)S(1)} collective-permute-done((bf16[48,1536]{1,0:T(8,128)(2,1)S(1)}, bf16[48,1536]{1,0:T(8,128)(2,1)S(1)}, u32[]{:S(2)}, u32[]{:S(2)}) %collective-permute-start.49) | collective-permute-done | bytes 147488 | tf_op jit(solution)/shard_map/ppermute | solution.py:679
  223.2 3.8 %collective-permute-done.44 = bf16[96,1152]{1,0:T(8,128)(2,1)S(1)} collective-permute-done((bf16[96,1152]{1,0:T(8,128)(2,1)S(1)}, bf16[96,1152]{1,0:T(8,128)(2,1)S(1)}, u32[]{:S(2)}, u32[]{:S(2)}) %collective-permute-start.44) | collective-permute-done | bytes 221216 | tf_op jit(solution)/shard_map/ppermute | solution.py:679
  227.2 1.5 collective-permute-done.47
  228.7 1.5 collective-permute-start.48
  230.3 4.9 %collective-permute-done.45.ac_ref = bf16[48,1152]{1,0:T(8,128)(2,1)S(1)} collective-permute-done((bf16[48,1152]{1,0:T(8,128)(2,1)S(1)}, bf16[48,1152]{1,0:T(8,128)(2,1)S(1)}, u32[]{:S(2)}, u32[]{:S(2)}) %collective-permute-start.45) | collective-permute-done | bytes 110624 | tf_op jit(solution)/shard_map/ppermute | solution.py:679
  (256 shorter events, 53.2 us)
Async XLA Ops:
  5.4 11.6 %collective-permute-start = (bf16[48,1664]{1,0:T(8,128)(2,1)S(1)}, bf16[48,1664]{1,0:T(8,128)(2,1)S(1)}, u32[]{:S(2)}, u32[]{:S(2)}) collective-permute-start(bf16[48,1664]{1,0:T(8,128)(2,1)S(1)} %shard_map.222), channel_id=1, source_target_pairs={{0,16},{1,17},{2,18},{3,19},{4,20},{5,21},{6,22},{7,23},{8,24},{9,... | collective-permute-start | bytes 479240 | tf_op jit(solution)/shard_map/ppermute | solution.py:679
  17.7 12.2 %collective-permute-start.1 = (bf16[96,1664]{1,0:T(8,128)(2,1)}, bf16[96,1664]{1,0:T(8,128)(2,1)}, u32[]{:S(2)}, u32[]{:S(2)}) collective-permute-start(bf16[96,1664]{1,0:T(8,128)(2,1)} %pad_maximum_fusion.2), channel_id=1, source_target_pairs={{0,8},{1,9},{2,10},{3,11},{4,12},{5,13},{6,14},{7,15},{8,0},{9,1},... | collective-permute-start | bytes 958472 | tf_op jit(solution)/shard_map/ppermute | solution.py:679
  18.5 11.5 %collective-permute-start.2 = (bf16[48,1536]{1,0:T(8,128)(2,1)}, bf16[48,1536]{1,0:T(8,128)(2,1)}, u32[]{:S(2)}, u32[]{:S(2)}) collective-permute-start(bf16[48,1536]{1,0:T(8,128)(2,1)} %param.21), channel_id=1, source_target_pairs={{0,16},{1,17},{2,18},{3,19},{4,20},{5,21},{6,22},{7,23},{8,24},{9,... | collective-permute-start | bytes 442376 | tf_op jit(solution)/shard_map/ppermute | solution.py:679
  31.0 18.0 %collective-permute-start.3 = (bf16[192,1664]{1,0:T(8,128)(2,1)S(1)}, bf16[192,1664]{1,0:T(8,128)(2,1)S(1)}, u32[]{:S(2)}, u32[]{:S(2)}) collective-permute-start(bf16[192,1664]{1,0:T(8,128)(2,1)S(1)} %pad_maximum_fusion.refs_0_), channel_id=1, source_target_pairs={{0,4},{1,3},{2,6},{3,1},{4,0},{5,7},{6,2},{7,5},{8,12},{9,11},{10,... | collective-permute-start | bytes 1916936 | tf_op jit(solution)/shard_map/ppermute | solution.py:679
  32.3 16.7 %collective-permute-start.4 = (bf16[192,1664]{1,0:T(8,128)(2,1)S(1)}, bf16[192,1664]{1,0:T(8,128)(2,1)S(1)}, u32[]{:S(2)}, u32[]{:S(2)}) collective-permute-start(bf16[192,1664]{1,0:T(8,128)(2,1)S(1)} %pad_maximum_fusion.refs_0_), channel_id=1, source_target_pairs={{0,2},{1,5},{2,0},{3,7},{4,6},{5,1},{6,4},{7,3},{8,10},{9,13},{10,... | collective-permute-start | bytes 1916936 | tf_op jit(solution)/shard_map/ppermute | solution.py:679
  33.8 7.9 %collective-permute-start.7 = (bf16[256,768]{1,0:T(8,128)(2,1)S(1)}, bf16[256,768]{1,0:T(8,128)(2,1)S(1)}, u32[]{:S(2)}, u32[]{:S(2)}) collective-permute-start(bf16[256,768]{1,0:T(8,128)(2,1)S(1)} %get-tuple-element.151), channel_id=1, source_target_pairs={{0,1},{1,0},{2,3},{3,2},{4,5},{5,4},{6,7},{7,6},{8,9},{9,8},{10,11... | collective-permute-start | bytes 1179656 | tf_op jit(solution)/shard_map/ppermute | solution.py:28
  34.7 14.2 %collective-permute-start.5 = (bf16[96,1536]{1,0:T(8,128)(2,1)S(1)}, bf16[96,1536]{1,0:T(8,128)(2,1)S(1)}, u32[]{:S(2)}, u32[]{:S(2)}) collective-permute-start(bf16[96,1536]{1,0:T(8,128)(2,1)S(1)} %get-tuple-element.285), channel_id=1, source_target_pairs={{0,8},{1,9},{2,10},{3,11},{4,12},{5,13},{6,14},{7,15},{8,0},{9,1},... | collective-permute-start | bytes 884744 | tf_op jit(solution)/shard_map/ppermute | solution.py:679
  39.3 9.0 %collective-permute-start.6 = (bf16[48,1536]{1,0:T(8,128)(2,1)S(1)}, bf16[48,1536]{1,0:T(8,128)(2,1)S(1)}, u32[]{:S(2)}, u32[]{:S(2)}) collective-permute-start(bf16[48,1536]{1,0:T(8,128)(2,1)S(1)} %bitcast.31), channel_id=1, source_target_pairs={{0,16},{1,17},{2,18},{3,19},{4,20},{5,21},{6,22},{7,23},{8,24},{9,... | collective-permute-start | bytes 442376 | tf_op jit(solution)/shard_map/ppermute | solution.py:679
  41.7 10.7 %collective-permute-start.11 = (bf16[192,1664]{1,0:T(8,128)(2,1)S(1)}, bf16[192,1664]{1,0:T(8,128)(2,1)S(1)}, u32[]{:S(2)}, u32[]{:S(2)}) collective-permute-start(bf16[192,1664]{1,0:T(8,128)(2,1)S(1)} %pad_maximum_fusion.refs_0_), channel_id=1, source_target_pairs={{0,1},{1,0},{2,3},{3,2},{4,5},{5,4},{6,7},{7,6},{8,9},{9,8},{10,11... | collective-permute-start | bytes 1916936 | tf_op jit(solution)/shard_map/ppermute | solution.py:28
  49.0 16.3 %collective-permute-start.12 = (bf16[192,1664]{1,0:T(8,128)(2,1)S(1)}, bf16[192,1664]{1,0:T(8,128)(2,1)S(1)}, u32[]{:S(2)}, u32[]{:S(2)}) collective-permute-start(bf16[192,1664]{1,0:T(8,128)(2,1)S(1)} %collective-permute-done.3.refs_1_), channel_id=1, source_target_pairs={{0,1},{1,0},{2,3},{3,2},{4,5},{5,4},{6,7},{7,6},{8,9},{9,8},{10,11... | collective-permute-start | bytes 1916936 | tf_op jit(solution)/shard_map/ppermute | solution.py:28
  49.0 16.3 %collective-permute-start.8 = (bf16[192,1664]{1,0:T(8,128)(2,1)S(1)}, bf16[192,1664]{1,0:T(8,128)(2,1)S(1)}, u32[]{:S(2)}, u32[]{:S(2)}) collective-permute-start(bf16[192,1664]{1,0:T(8,128)(2,1)S(1)} %collective-permute-done.3.refs_1_), channel_id=1, source_target_pairs={{0,2},{1,5},{2,0},{3,7},{4,6},{5,1},{6,4},{7,3},{8,10},{9,13},{10,... | collective-permute-start | bytes 1916936 | tf_op jit(solution)/shard_map/ppermute | solution.py:679
  49.6 15.7 %collective-permute-start.13 = (bf16[192,1664]{1,0:T(8,128)(2,1)S(1)}, bf16[192,1664]{1,0:T(8,128)(2,1)S(1)}, u32[]{:S(2)}, u32[]{:S(2)}) collective-permute-start(bf16[192,1664]{1,0:T(8,128)(2,1)S(1)} %collective-permute-done.4.refs_2_), channel_id=1, source_target_pairs={{0,1},{1,0},{2,3},{3,2},{4,5},{5,4},{6,7},{7,6},{8,9},{9,8},{10,11... | collective-permute-start | bytes 1916936 | tf_op jit(solution)/shard_map/ppermute | solution.py:28
  50.7 14.5 %collective-permute-start.9 = (bf16[192,1536]{1,0:T(8,128)(2,1)S(1)}, bf16[192,1536]{1,0:T(8,128)(2,1)S(1)}, u32[]{:S(2)}, u32[]{:S(2)}) collective-permute-start(bf16[192,1536]{1,0:T(8,128)(2,1)S(1)} %pad_maximum_fusion.1), channel_id=1, source_target_pairs={{0,4},{1,3},{2,6},{3,1},{4,0},{5,7},{6,2},{7,5},{8,12},{9,11},{10,... | collective-permute-start | bytes 1769480 | tf_op jit(solution)/shard_map/ppermute | solution.py:679
  52.4 9.4 %collective-permute-start.10 = (bf16[96,1536]{1,0:T(8,128)(2,1)S(1)}, bf16[96,1536]{1,0:T(8,128)(2,1)S(1)}, u32[]{:S(2)}, u32[]{:S(2)}) collective-permute-start(bf16[96,1536]{1,0:T(8,128)(2,1)S(1)} %pad_maximum_fusion.3), channel_id=1, source_target_pairs={{0,8},{1,9},{2,10},{3,11},{4,12},{5,13},{6,14},{7,15},{8,0},{9,1},... | collective-permute-start | bytes 884744 | tf_op jit(solution)/shard_map/ppermute | solution.py:679
  65.3 22.6 %collective-permute-start.15 = (bf16[384,1536]{1,0:T(8,128)(2,1)S(1)}, bf16[384,1536]{1,0:T(8,128)(2,1)S(1)}, u32[]{:S(2)}, u32[]{:S(2)}) collective-permute-start(bf16[384,1536]{1,0:T(8,128)(2,1)S(1)} %constant_dynamic-update-slice_fusion.2.a_ref.b_ref.refs_4_.refs_5_), channel_id=1, source_target_pairs={{0,2},{1,5},{2,0},{3,7},{4,6},{5,1},{6,4},{7,3},{8,10},{9,13},{10,... | collective-permute-start | bytes 3538952 | tf_op jit(solution)/shard_map/ppermute | solution.py:679
  66.1 19.3 %collective-permute-start.16 = (bf16[192,1536]{1,0:T(8,128)(2,1)S(1)}, bf16[192,1536]{1,0:T(8,128)(2,1)S(1)}, u32[]{:S(2)}, u32[]{:S(2)}) collective-permute-start(bf16[192,1536]{1,0:T(8,128)(2,1)S(1)} %get-tuple-element.277), channel_id=1, source_target_pairs={{0,4},{1,3},{2,6},{3,1},{4,0},{5,7},{6,2},{7,5},{8,12},{9,11},{10,... | collective-permute-start | bytes 1769480 | tf_op jit(solution)/shard_map/ppermute | solution.py:679
  67.7 26.2 %collective-permute-start.17 = (bf16[384,1536]{1,0:T(8,128)(2,1)S(1)}, bf16[384,1536]{1,0:T(8,128)(2,1)S(1)}, u32[]{:S(2)}, u32[]{:S(2)}) collective-permute-start(bf16[384,1536]{1,0:T(8,128)(2,1)S(1)} %constant_dynamic-update-slice_fusion.2.a_ref.b_ref.refs_4_.refs_5_), channel_id=1, source_target_pairs={{0,1},{1,0},{2,3},{3,2},{4,5},{5,4},{6,7},{7,6},{8,9},{9,8},{10,11... | collective-permute-start | bytes 3538952 | tf_op jit(solution)/shard_map/ppermute | solution.py:28
  87.9 6.0 %collective-permute-start.18 = (bf16[384,1536]{1,0:T(8,128)(2,1)S(1)}, bf16[384,1536]{1,0:T(8,128)(2,1)S(1)}, u32[]{:S(2)}, u32[]{:S(2)}) collective-permute-start(bf16[384,1536]{1,0:T(8,128)(2,1)S(1)} %collective-permute-done.15.c_ref.d_ref.refs_6_.refs_7_), channel_id=1, source_target_pairs={{0,1},{1,0},{2,3},{3,2},{4,5},{5,4},{6,7},{7,6},{8,9},{9,8},{10,11... | collective-permute-start | bytes 3538952 | tf_op jit(solution)/shard_map/ppermute | solution.py:28
  87.9 16.3 %collective-permute-start.20 = (bf16[384,1536]{1,0:T(8,128)(2,1)S(1)}, bf16[384,1536]{1,0:T(8,128)(2,1)S(1)}, u32[]{:S(2)}, u32[]{:S(2)}) collective-permute-start(bf16[384,1536]{1,0:T(8,128)(2,1)S(1)} %constant_dynamic-update-slice_fusion.9.refs_0_.refs_1_), channel_id=1, source_target_pairs={{0,2},{1,5},{2,0},{3,7},{4,6},{5,1},{6,4},{7,3},{8,10},{9,13},{10,... | collective-permute-start | bytes 3538952 | tf_op jit(solution)/shard_map/ppermute | solution.py:679
  88.5 15.7 %collective-permute-start.21 = (bf16[384,1536]{1,0:T(8,128)(2,1)S(1)}, bf16[384,1536]{1,0:T(8,128)(2,1)S(1)}, u32[]{:S(2)}, u32[]{:S(2)}) collective-permute-start(bf16[384,1536]{1,0:T(8,128)(2,1)S(1)} %constant_dynamic-update-slice_fusion.9.refs_0_.refs_1_), channel_id=1, source_target_pairs={{0,1},{1,0},{2,3},{3,2},{4,5},{5,4},{6,7},{7,6},{8,9},{9,8},{10,11... | collective-permute-start | bytes 3538952 | tf_op jit(solution)/shard_map/ppermute | solution.py:28
  104.2 3.1 %collective-permute-start.22 = (bf16[384,1536]{1,0:T(8,128)(2,1)S(1)}, bf16[384,1536]{1,0:T(8,128)(2,1)S(1)}, u32[]{:S(2)}, u32[]{:S(2)}) collective-permute-start(bf16[384,1536]{1,0:T(8,128)(2,1)S(1)} %collective-permute-done.20.refs_2_.refs_3_), channel_id=1, source_target_pairs={{0,1},{1,0},{2,3},{3,2},{4,5},{5,4},{6,7},{7,6},{8,9},{9,8},{10,11... | collective-permute-start | bytes 3538952 | tf_op jit(solution)/shard_map/ppermute | solution.py:28
  104.3 3.0 %collective-permute-start.19 = (f32[256,128]{1,0:T(8,128)S(1)}, f32[256,128]{1,0:T(8,128)S(1)}, u32[]{:S(2)}, u32[]{:S(2)}) collective-permute-start(f32[256,128]{1,0:T(8,128)S(1)} %get-tuple-element.279), channel_id=1, source_target_pairs={{0,1},{1,0},{2,3},{3,2},{4,5},{5,4},{6,7},{7,6},{8,9},{9,8},{10,11... | collective-permute-start | bytes 393224 | tf_op jit(solution)/shard_map/ppermute | solution.py:28
  118.5 2.9 %collective-permute-start.24 = (bf16[384,1536]{1,0:T(8,128)(2,1)S(1)}, bf16[384,1536]{1,0:T(8,128)(2,1)S(1)}, u32[]{:S(2)}, u32[]{:S(2)}) collective-permute-start(bf16[384,1536]{1,0:T(8,128)(2,1)S(1)} %get-tuple-element.198), channel_id=1, source_target_pairs={{0,1},{1,0},{2,3},{3,2},{4,5},{5,4},{6,7},{7,6},{8,9},{9,8},{10,11... | collective-permute-start | bytes 3538952 | tf_op jit(solution)/shard_map/ppermute | solution.py:28
  118.7 4.4 %collective-permute-start.25 = (bf16[384,1536]{1,0:T(8,128)(2,1)S(1)}, bf16[384,1536]{1,0:T(8,128)(2,1)S(1)}, u32[]{:S(2)}, u32[]{:S(2)}) collective-permute-start(bf16[384,1536]{1,0:T(8,128)(2,1)S(1)} %get-tuple-element.201), channel_id=1, source_target_pairs={{0,1},{1,0},{2,3},{3,2},{4,5},{5,4},{6,7},{7,6},{8,9},{9,8},{10,11... | collective-permute-start | bytes 3538952 | tf_op jit(solution)/shard_map/ppermute | solution.py:28
  123.4 16.3 %collective-permute-start.26 = (bf16[384,1536]{1,0:T(8,128)(2,1)S(1)}, bf16[384,1536]{1,0:T(8,128)(2,1)S(1)}, u32[]{:S(2)}, u32[]{:S(2)}) collective-permute-start(bf16[384,1536]{1,0:T(8,128)(2,1)S(1)} %add_convert_fusion.2), channel_id=1, source_target_pairs={{0,2},{1,5},{2,0},{3,7},{4,6},{5,1},{6,4},{7,3},{8,10},{9,13},{10,... | collective-permute-start | bytes 3538952 | tf_op jit(solution)/shard_map/ppermute | solution.py:679
  132.7 16.5 %collective-permute-start.28 = (bf16[384,1536]{1,0:T(8,128)(2,1)S(1)}, bf16[384,1536]{1,0:T(8,128)(2,1)S(1)}, u32[]{:S(2)}, u32[]{:S(2)}) collective-permute-start(bf16[384,1536]{1,0:T(8,128)(2,1)S(1)} %get-tuple-element.207), channel_id=1, source_target_pairs={{0,1},{1,0},{2,3},{3,2},{4,5},{5,4},{6,7},{7,6},{8,9},{9,8},{10,11... | collective-permute-start | bytes 3538952 | tf_op jit(solution)/shard_map/ppermute | solution.py:28
  132.8 16.5 %collective-permute-start.29 = (bf16[384,1536]{1,0:T(8,128)(2,1)S(1)}, bf16[384,1536]{1,0:T(8,128)(2,1)S(1)}, u32[]{:S(2)}, u32[]{:S(2)}) collective-permute-start(bf16[384,1536]{1,0:T(8,128)(2,1)S(1)} %get-tuple-element.216), channel_id=1, source_target_pairs={{0,1},{1,0},{2,3},{3,2},{4,5},{5,4},{6,7},{7,6},{8,9},{9,8},{10,11... | collective-permute-start | bytes 3538952 | tf_op jit(solution)/shard_map/ppermute | solution.py:28
  140.0 9.9 %collective-permute-start.27 = (bf16[192,1536]{1,0:T(8,128)(2,1)S(1)}, bf16[192,1536]{1,0:T(8,128)(2,1)S(1)}, u32[]{:S(2)}, u32[]{:S(2)}) collective-permute-start(bf16[192,1536]{1,0:T(8,128)(2,1)S(1)} %add_convert_fusion.4), channel_id=1, source_target_pairs={{0,4},{1,3},{2,6},{3,1},{4,0},{5,7},{6,2},{7,5},{8,12},{9,11},{10,... | collective-permute-start | bytes 1769480 | tf_op jit(solution)/shard_map/ppermute | solution.py:679
  150.5 24.2 %collective-permute-start.33 = (bf16[384,1536]{1,0:T(8,128)(2,1)S(1)}, bf16[384,1536]{1,0:T(8,128)(2,1)S(1)}, u32[]{:S(2)}, u32[]{:S(2)}) collective-permute-start(bf16[384,1536]{1,0:T(8,128)(2,1)S(1)} %add_convert_fusion.1), channel_id=1, source_target_pairs={{0,2},{1,5},{2,0},{3,7},{4,6},{5,1},{6,4},{7,3},{8,10},{9,13},{10,... | collective-permute-start | bytes 3538952 | tf_op jit(solution)/shard_map/ppermute | solution.py:679
  164.0 7.0 %collective-permute-start.30 = (bf16[384,1152]{1,0:T(8,128)(2,1)S(1)}, bf16[384,1152]{1,0:T(8,128)(2,1)S(1)}, u32[]{:S(2)}, u32[]{:S(2)}) collective-permute-start(bf16[384,1152]{1,0:T(8,128)(2,1)S(1)} %get-tuple-element.229), channel_id=1, source_target_pairs={{0,1},{1,0},{2,3},{3,2},{4,5},{5,4},{6,7},{7,6},{8,9},{9,8},{10,11... | collective-permute-start | bytes 2654216 | tf_op jit(solution)/shard_map/ppermute | solution.py:28
  164.0 7.0 %collective-permute-start.31 = (bf16[384,1152]{1,0:T(8,128)(2,1)S(1)}, bf16[384,1152]{1,0:T(8,128)(2,1)S(1)}, u32[]{:S(2)}, u32[]{:S(2)}) collective-permute-start(bf16[384,1152]{1,0:T(8,128)(2,1)S(1)} %get-tuple-element.232), channel_id=1, source_target_pairs={{0,1},{1,0},{2,3},{3,2},{4,5},{5,4},{6,7},{7,6},{8,9},{9,8},{10,11... | collective-permute-start | bytes 2654216 | tf_op jit(solution)/shard_map/ppermute | solution.py:28
  164.5 10.1 %collective-permute-start.32 = (bf16[96,1536]{1,0:T(8,128)(2,1)S(1)}, bf16[96,1536]{1,0:T(8,128)(2,1)S(1)}, u32[]{:S(2)}, u32[]{:S(2)}) collective-permute-start(bf16[96,1536]{1,0:T(8,128)(2,1)S(1)} %slice.213), channel_id=1, source_target_pairs={{0,8},{1,9},{2,10},{3,11},{4,12},{5,13},{6,14},{7,15},{8,0},{9,1},... | collective-permute-start | bytes 884744 | tf_op jit(solution)/shard_map/ppermute | solution.py:679
  173.2 27.1 %collective-permute-start.39 = (bf16[384,1152]{1,0:T(8,128)(2,1)}, bf16[384,1152]{1,0:T(8,128)(2,1)}, u32[]{:S(2)}, u32[]{:S(2)}) collective-permute-start(bf16[384,1152]{1,0:T(8,128)(2,1)} %get-tuple-element.235), channel_id=1, source_target_pairs={{0,2},{1,5},{2,0},{3,7},{4,6},{5,1},{6,4},{7,3},{8,10},{9,13},{10,... | collective-permute-start | bytes 2654216 | tf_op jit(solution)/shard_map/ppermute | solution.py:679
  175.9 24.3 %collective-permute-start.38 = (bf16[192,1536]{1,0:T(8,128)(2,1)}, bf16[192,1536]{1,0:T(8,128)(2,1)}, u32[]{:S(2)}, u32[]{:S(2)}) collective-permute-start(bf16[192,1536]{1,0:T(8,128)(2,1)} %add_convert_fusion.3), channel_id=1, source_target_pairs={{0,4},{1,3},{2,6},{3,1},{4,0},{5,7},{6,2},{7,5},{8,12},{9,11},{10,... | collective-permute-start | bytes 1769480 | tf_op jit(solution)/shard_map/ppermute | solution.py:679
  179.6 12.1 %collective-permute-start.34 = (bf16[384,384]{1,0:T(8,128)(2,1)}, bf16[384,384]{1,0:T(8,128)(2,1)}, u32[]{:S(2)}, u32[]{:S(2)}) collective-permute-start(bf16[384,384]{1,0:T(8,128)(2,1)} %get-tuple-element.241), channel_id=1, source_target_pairs={{0,1},{1,0},{2,3},{3,2},{4,5},{5,4},{6,7},{7,6},{8,9},{9,8},{10,11... | collective-permute-start | bytes 884744 | tf_op jit(solution)/shard_map/ppermute | solution.py:28
  180.3 9.6 %collective-permute-start.23 = (f32[256,128]{1,0:T(8,128)}, f32[256,128]{1,0:T(8,128)}, u32[]{:S(2)}, u32[]{:S(2)}) collective-permute-start(f32[256,128]{1,0:T(8,128)} %constant_dynamic-slice_fusion), channel_id=1, source_target_pairs={{0,1},{1,0},{2,3},{3,2},{4,5},{5,4},{6,7},{7,6},{8,9},{9,8},{10,11... | collective-permute-start | bytes 393224 | tf_op jit(solution)/shard_map/ppermute | solution.py:28
  180.8 12.0 %collective-permute-start.35 = (bf16[384,384]{1,0:T(8,128)(2,1)}, bf16[384,384]{1,0:T(8,128)(2,1)S(1)}, u32[]{:S(2)}, u32[]{:S(2)}) collective-permute-start(bf16[384,384]{1,0:T(8,128)(2,1)} %copy-done.39), channel_id=1, source_target_pairs={{0,1},{1,0},{2,3},{3,2},{4,5},{5,4},{6,7},{7,6},{8,9},{9,8},{10,11... | collective-permute-start | bytes 884744 | tf_op jit(solution)/shard_map/ppermute | solution.py:28
  189.9 10.4 %collective-permute-start.37 = (bf16[48,1536]{1,0:T(8,128)(2,1)S(1)}, bf16[48,1536]{1,0:T(8,128)(2,1)S(1)}, u32[]{:S(2)}, u32[]{:S(2)}) collective-permute-start(bf16[48,1536]{1,0:T(8,128)(2,1)S(1)} %copy-done.47), channel_id=1, source_target_pairs={{0,16},{1,17},{2,18},{3,19},{4,20},{5,21},{6,22},{7,23},{8,24},{9,... | collective-permute-start | bytes 442376 | tf_op jit(solution)/shard_map/ppermute | solution.py:679
  194.9 16.5 %collective-permute-start.42 = (bf16[384,512]{1,0:T(8,128)(2,1)S(1)}, bf16[384,512]{1,0:T(8,128)(2,1)S(1)}, u32[]{:S(2)}, u32[]{:S(2)}) collective-permute-start(bf16[384,512]{1,0:T(8,128)(2,1)S(1)} %get-tuple-element.255), channel_id=1, source_target_pairs={{0,2},{1,5},{2,0},{3,7},{4,6},{5,1},{6,4},{7,3},{8,10},{9,13},{10,... | collective-permute-start | bytes 1179656 | tf_op jit(solution)/shard_map/ppermute | solution.py:679
  202.2 9.2 %collective-permute-start.43 = (bf16[96,1536]{1,0:T(8,128)(2,1)S(1)}, bf16[96,1536]{1,0:T(8,128)(2,1)S(1)}, u32[]{:S(2)}, u32[]{:S(2)}) collective-permute-start(bf16[96,1536]{1,0:T(8,128)(2,1)S(1)} %slice.212), channel_id=1, source_target_pairs={{0,8},{1,9},{2,10},{3,11},{4,12},{5,13},{6,14},{7,15},{8,0},{9,1},... | collective-permute-start | bytes 884744 | tf_op jit(solution)/shard_map/ppermute | solution.py:679
  203.5 8.4 %collective-permute-start.41 = (bf16[192,1152]{1,0:T(8,128)(2,1)S(1)}, bf16[192,1152]{1,0:T(8,128)(2,1)S(1)}, u32[]{:S(2)}, u32[]{:S(2)}) collective-permute-start(bf16[192,1152]{1,0:T(8,128)(2,1)S(1)} %add_convert_fusion.5), channel_id=1, source_target_pairs={{0,4},{1,3},{2,6},{3,1},{4,0},{5,7},{6,2},{7,5},{8,12},{9,11},{10,... | collective-permute-start | bytes 1327112 | tf_op jit(solution)/shard_map/ppermute | solution.py:679
  211.2 19.1 %collective-permute-start.40 = (f32[256,768]{1,0:T(8,128)S(1)}, f32[256,768]{1,0:T(8,128)S(1)}, u32[]{:S(2)}, u32[]{:S(2)}) collective-permute-start(f32[256,768]{1,0:T(8,128)S(1)} %constant_dynamic-slice_fusion.1), channel_id=1, source_target_pairs={{0,1},{1,0},{2,3},{3,2},{4,5},{5,4},{6,7},{7,6},{8,9},{9,8},{10,11... | collective-permute-start | bytes 2359304 | tf_op jit(solution)/shard_map/ppermute | solution.py:28
  212.0 10.3 %collective-permute-start.49 = (bf16[48,1536]{1,0:T(8,128)(2,1)S(1)}, bf16[48,1536]{1,0:T(8,128)(2,1)S(1)}, u32[]{:S(2)}, u32[]{:S(2)}) collective-permute-start(bf16[48,1536]{1,0:T(8,128)(2,1)S(1)} %slice.215), channel_id=1, source_target_pairs={{0,16},{1,17},{2,18},{3,19},{4,20},{5,21},{6,22},{7,23},{8,24},{9,... | collective-permute-start | bytes 442376 | tf_op jit(solution)/shard_map/ppermute | solution.py:679
  215.0 8.0 %collective-permute-start.46 = (bf16[192,512]{1,0:T(8,128)(2,1)S(1)}, bf16[192,512]{1,0:T(8,128)(2,1)S(1)}, u32[]{:S(2)}, u32[]{:S(2)}) collective-permute-start(bf16[192,512]{1,0:T(8,128)(2,1)S(1)} %add_convert_fusion.7), channel_id=1, source_target_pairs={{0,4},{1,3},{2,6},{3,1},{4,0},{5,7},{6,2},{7,5},{8,12},{9,11},{10,... | collective-permute-start | bytes 589832 | tf_op jit(solution)/shard_map/ppermute | solution.py:679
  217.3 9.7 %collective-permute-start.44 = (bf16[96,1152]{1,0:T(8,128)(2,1)S(1)}, bf16[96,1152]{1,0:T(8,128)(2,1)S(1)}, u32[]{:S(2)}, u32[]{:S(2)}) collective-permute-start(bf16[96,1152]{1,0:T(8,128)(2,1)S(1)} %slice.214), channel_id=1, source_target_pairs={{0,8},{1,9},{2,10},{3,11},{4,12},{5,13},{6,14},{7,15},{8,0},{9,1},... | collective-permute-start | bytes 663560 | tf_op jit(solution)/shard_map/ppermute | solution.py:679
  223.1 5.6 %collective-permute-start.47 = (bf16[96,512]{1,0:T(8,128)(2,1)S(1)}, bf16[96,512]{1,0:T(8,128)(2,1)S(1)}, u32[]{:S(2)}, u32[]{:S(2)}) collective-permute-start(bf16[96,512]{1,0:T(8,128)(2,1)S(1)} %slice.218), channel_id=1, source_target_pairs={{0,8},{1,9},{2,10},{3,11},{4,12},{5,13},{6,14},{7,15},{8,0},{9,1},... | collective-permute-start | bytes 294920 | tf_op jit(solution)/shard_map/ppermute | solution.py:679
  227.1 8.1 %collective-permute-start.45 = (bf16[48,1152]{1,0:T(8,128)(2,1)S(1)}, bf16[48,1152]{1,0:T(8,128)(2,1)S(1)}, u32[]{:S(2)}, u32[]{:S(2)}) collective-permute-start(bf16[48,1152]{1,0:T(8,128)(2,1)S(1)} %slice.217), channel_id=1, source_target_pairs={{0,16},{1,17},{2,18},{3,19},{4,20},{5,21},{6,22},{7,23},{8,24},{9,... | collective-permute-start | bytes 331784 | tf_op jit(solution)/shard_map/ppermute | solution.py:679
  228.7 7.0 %collective-permute-start.48 = (bf16[48,512]{1,0:T(8,128)(2,1)S(1)}, bf16[48,512]{1,0:T(8,128)(2,1)S(1)}, u32[]{:S(2)}, u32[]{:S(2)}) collective-permute-start(bf16[48,512]{1,0:T(8,128)(2,1)S(1)} %slice.219), channel_id=1, source_target_pairs={{0,16},{1,17},{2,18},{3,19},{4,20},{5,21},{6,22},{7,23},{8,24},{9,... | collective-permute-start | bytes 147464 | tf_op jit(solution)/shard_map/ppermute | solution.py:679
  (56 other events, 492.6 us)

commit v2 on v1

--- a/solution.py
+++ b/solution.py
@@ -54,7 +54,9 @@
     lax.fori_loop(0, width // block, run, 0)
 
 
-def call(body, outs, args, grid=None, in_specs=None, out_specs=None, scratch=(), flops=0):
+def call(
+    body, outs, args, grid=None, in_specs=None, out_specs=None, scratch=(), flops=0, grant=VMEM_LIMIT
+):
     whole = pl.BlockSpec(memory_space=pltpu.VMEM)
     return pl.pallas_call(
         body,
@@ -63,7 +65,7 @@
         in_specs=in_specs or [whole] * len(args),
         out_specs=out_specs or jax.tree.map(lambda _: whole, outs),
         scratch_shapes=scratch,
-        compiler_params=pltpu.CompilerParams(vmem_limit_bytes=VMEM_LIMIT),
+        compiler_params=pltpu.CompilerParams(vmem_limit_bytes=grant),
         cost_estimate=pl.CostEstimate(flops=flops, bytes_accessed=1 << 20, transcendentals=0),
     )(*args)
 
@@ -275,21 +277,19 @@
 
 
 def down_kernel(
-    at, len_ref, h0_ref, h1_ref, first_ref, vec_ref, proj_ref, cot_ref, *refs
+    len_ref, h0_ref, h1_ref, first_ref, vec_ref, proj_ref, cot_ref, *refs
 ):
-    pieces, refs = refs[:8], refs[8:]
+    both_ref, more_ref, both_other, more_other, *refs = refs
     emb_ref, low_ref, lowt_ref, res_ref, pgrad_ref, sums_ref = refs[:6]
-    ffn_ref, norm_ref, sec_ref, gp_ref, gs_ref, inv_ref, prj_ref, w_ref, sems = refs[6:]
-    copies = load_weights(pieces, w_ref, sems, at=at)
+    ffn_ref, norm_ref, sec_ref, gp_ref, gs_ref, inv_ref, prj_ref, w_ref = refs[6:]
     tokens = first_ref.shape[0]
     length = len_ref[0]
-    for copy in copies:
-        copy.wait()
-
-    def matmul(span):
-        ffn_ref[:, span] = nt(h0_ref[...], w_ref[0, span]) + nt(h1_ref[...], w_ref[1, span])
-
-    columns_of(ffn_ref.shape[1], matmul)
+    quarter = w_ref.shape[0] // 4
+    for place, ref, part in ((0, both_other, 0), (1, more_other, 0), (2, both_other, 1), (3, more_other, 1)):
+        w_ref[place * quarter : (place + 1) * quarter] = ref[part * quarter : (part + 1) * quarter]
+    for ref, first in ((both_ref, 0), (more_ref, 2 * quarter)):
+        span = slice(first, first + 2 * quarter)
+        ffn_ref[:, span] = nt(h0_ref[...], ref[...]) + nt(h1_ref[...], w_ref[span])
 
     def norm(rows):
         value = first_ref[rows, :] + ffn_ref[rows, :] + vec_ref[6:7, :]
@@ -353,13 +353,12 @@
         shaped((width, embed), F32),
         shaped((24, width), F32),
     )
-    pieces, at = zip(*pieces)
     args = (length, *hidden, first, vec, proj, cot, *pieces)
     return call(
-        functools.partial(down_kernel, at),
+        down_kernel,
         outs,
         args,
-        in_specs=[pl.BlockSpec(memory_space=pltpu.SMEM)] + [WHOLE] * 6 + [ANY] * 8,
+        in_specs=[pl.BlockSpec(memory_space=pltpu.SMEM)] + [WHOLE] * 10,
         scratch=[
             pltpu.VMEM((tokens, width), F32),
             pltpu.VMEM((tokens, width), F32),
@@ -368,8 +367,7 @@
             pltpu.VMEM((tokens, width), F32),
             pltpu.VMEM((tokens, LANES), F32),
             pltpu.VMEM((tokens, embed), F32),
-            pltpu.VMEM((2, width, hidden[0].shape[1]), BF16),
-            pltpu.SemaphoreType.DMA((2, 4)),
+            pltpu.VMEM((width, hidden[0].shape[1]), BF16),
         ],
         flops=2 * tokens * width * hidden[0].shape[1] * 2,
     )
@@ -399,27 +397,31 @@
     )
 
 
-def up_grad(g_low, low_t, slope, down, up, start, swapped):
+def up_grad(g_low, low_t, slope, down, up, start, swapped, biases):
     tokens, width = g_low.shape
     pieces, at = zip(*down, *up)
     hidden = slope.shape[1]
     block = column_block(hidden)
 
     def kernel(g_ref, lowt_ref, slope_ref, start_ref, *refs):
-        join_rows(refs[:4], wd_ref := refs[-2], swapped)
-        join_rows(refs[4:8], wu_ref := refs[-1], swapped)
-        keep_ref, send_ref, bias_ref, first_ref, gh_ref, gin_ref = refs[8:-2]
+        wd_ref, wu_ref = refs[-2:]
+        join_rows(refs[:4], wd_ref, swapped)
+        join_rows(refs[4:8], wu_ref, swapped)
+        more, refs = refs[8 : 8 + len(biases)], refs[8 + len(biases) :]
+        keep_ref, send_ref, bias_ref, first_ref, gh_ref, gin_ref = refs[:-2]
         def matmul(span):
             gh_ref[:, span] = nn(g_ref[...], wd_ref[:, span])
 
         columns_of(block, matmul)
         bias_ref[...] = jnp.zeros_like(bias_ref)
+        for ref in more:
+            bias_ref[8:16, :] = ref[...]
 
         def act(rows):
             grad = (gh_ref[rows, :] * slope_ref[rows, :].astype(F32)).astype(BF16)
             gin_ref[rows, :] = grad
             wide = grad.astype(F32)
-            bias_ref[...] += jnp.sum(wide.reshape(STRIP // 8, 8, wide.shape[1]), axis=0)
+            bias_ref[0:8, :] += jnp.sum(wide.reshape(STRIP // 8, 8, wide.shape[1]), axis=0)
 
         strips(tokens, STRIP, act)
         split_rows(nn(lowt_ref[...], gin_ref[...]).astype(BF16), keep_ref, send_ref, swapped)
@@ -437,14 +439,20 @@
     act = pl.BlockSpec((tokens, block), lambda i: (0, i))
     piece = pl.BlockSpec((width // 2, block), lambda i: (0, i))
     parts = [pl.BlockSpec((width // 4, block), lambda i, row=row: (row, i)) for row in at]
+    thin = pl.BlockSpec((8, block), lambda i: (0, i))
     out = shaped((width // 2, hidden), BF16)
     return call(
         kernel,
-        (out, out, shaped((8, hidden), F32), shaped((tokens, width), F32)),
-        (g_low, low_t, slope, start, *pieces),
+        (out, out, shaped((8 * (1 + len(biases)), hidden), F32), shaped((tokens, width), F32)),
+        (g_low, low_t, slope, start, *pieces, *biases),
         grid=(hidden // block,),
-        in_specs=[row, turned, act, row] + parts,
-        out_specs=(piece, piece, pl.BlockSpec((8, block), lambda i: (0, i)), row),
+        in_specs=[row, turned, act, row] + parts + [thin] * len(biases),
+        out_specs=(
+            piece,
+            piece,
+            pl.BlockSpec((8 * (1 + len(biases)), block), lambda i: (0, i)),
+            row,
+        ),
         scratch=[
             pltpu.VMEM((tokens, block), F32),
             pltpu.VMEM((tokens, block), BF16),
@@ -455,13 +463,14 @@
     )
 
 
-def norm_back(g_first, res, vec, weights, cols):
+def norm_back(g_first, res, vec, weights, sums_two, cols):
     tokens, width = g_first.shape
 
     def kernel(
-        gf_ref, res_ref, vec_ref, w_ref, gres_ref, turn_ref, gatt_ref, sums_ref, low_ref
+        gf_ref, res_ref, vec_ref, w_ref, two_ref, gres_ref, turn_ref, gatt_ref, sums_ref, low_ref
     ):
-        sums_ref[...] = jnp.zeros_like(sums_ref)
+        sums_ref[0:24, :] = jnp.zeros((24, width), F32)
+        sums_ref[24:48, :] = two_ref[...]
 
         def back(rows):
             value = res_ref[rows, :]
@@ -494,23 +503,28 @@
         shaped((tokens, width), F32),
         shaped((width, tokens), BF16),
         shaped((2, tokens, cols), BF16),
-        shaped((24, width), F32),
+        shaped((48, width), F32),
     )
     return call(
         kernel,
         outs,
-        (g_first, res, vec, weights),
+        (g_first, res, vec, weights, sums_two),
         scratch=[pltpu.VMEM((tokens, width), BF16)],
         flops=4 * tokens * width * cols,
     )
 
 
-def attention_back(pairs, g_att, att, qkv, lse, mask):
+def attention_back(pairs, g_att, att, qkv, lse, mask, earlier=()):
     tokens, cols = att.shape[1:]
     wide = len(pairs) * LANES
     scale = HD ** (-0.5)
 
-    def kernel(gatt_ref, att_ref, qkv_ref, lse_ref, mask_ref, gqkv_ref, sums_ref, col_ref):
+    before = sum(part.shape[3] for part in earlier)
+
+    def kernel(gatt_ref, att_ref, qkv_ref, lse_ref, mask_ref, *refs):
+        gqkv_ref, sums_ref, col_ref = refs[len(earlier) :]
+        for ref in refs[: len(earlier)]:
+            sums_ref[:, :, :, 0:before] = ref[...]
         col_ref[...] = jnp.broadcast_to(mask_ref[...], (LANES, tokens)).T
         lane = lax.broadcasted_iota(jnp.int32, (tokens, LANES), 1) < HD
 
@@ -550,15 +564,16 @@
             gqkv_ref[half, :, pl.ds(pl.multiple_of(2 * wide + to, LANES), LANES)] = g_v
             for row, grads in ((0, g_q), (1, g_v)):
                 total = jnp.sum(grads.astype(F32).reshape(-1, 8, LANES), axis=0)
-                sums_ref[half, row, :, pl.ds(to, LANES)] = total
+                place_to = pl.ds(pl.multiple_of(before + to, LANES), LANES)
+                sums_ref[half, row, :, place_to] = total
             return carry
 
         lax.fori_loop(0, 2 * len(pairs), pair, 0)
 
     return call(
         kernel,
-        (shaped((2, tokens, 3 * wide), BF16), shaped((2, 2, 8, wide), F32)),
-        (g_att, att, qkv, lse, mask),
+        (shaped((2, tokens, 3 * wide), BF16), shaped((2, 2, 8, before + wide), F32)),
+        (g_att, att, qkv, lse, mask, *earlier),
         scratch=[pltpu.VMEM((tokens, LANES), F32)],
         flops=20 * tokens * tokens * wide * 2,
     )
@@ -753,6 +768,7 @@
         in_specs=[pl.BlockSpec(memory_space=pltpu.HBM)] * 6,
         scratch=[pltpu.VMEM(arg.shape, arg.dtype) for arg in args]
         + [pltpu.VMEM((8, LANES), F32), pltpu.SemaphoreType.DMA((6,))],
+        grant=60 * 1024 * 1024,
     )
 
 
@@ -829,15 +845,14 @@
 
 
 def pack_grads(
-    core, thin, broad, rel, absolute, up_rel, sums_one, sums_two, up_own, up_other, qkv_a, qkv_b,
-    proj_grad,
+    core, thin, broad, rel, absolute, up_rel, sums, up_sums, head_sums, proj_grad,
 ):
     width, hidden = thin.shape[2], broad.shape[2]
     count = width // SMALL
 
     def kernel(
-        core_ref, thin_ref, broad_ref, rel_ref, abs_ref, up_ref, one_ref, two_ref, uo_ref, ux_ref,
-        qa_ref, qb_ref, pg_ref, own_ref, other_ref,
+        core_ref, thin_ref, broad_ref, rel_ref, abs_ref, up_ref, sums_ref, ups_ref, heads_ref,
+        pg_ref, own_ref, other_ref,
     ):
         first = core_ref[0] == 0
         fold = lambda v: jnp.sum(v, axis=0, keepdims=True)
@@ -847,17 +862,17 @@
             return jnp.concatenate([low, high], axis=1)
 
         def heads(half, kind):
-            return jnp.concatenate([fold(qa_ref[half, kind]), fold(qb_ref[half, kind])], axis=1)
+            return fold(heads_ref[half, kind])
 
         rows = [
-            fold(one_ref[0:8]),
-            fold(two_ref[0:8]),
+            fold(sums_ref[0:8]),
+            fold(sums_ref[24:32]),
             ordered(heads(0, 0), heads(1, 0)),
             ordered(heads(0, 1), heads(1, 1)),
-            fold(one_ref[16:24]),
-            fold(one_ref[8:16]),
-            fold(two_ref[16:24]),
-            fold(two_ref[8:16]),
+            fold(sums_ref[16:24]),
+            fold(sums_ref[8:16]),
+            fold(sums_ref[40:48]),
+            fold(sums_ref[32:40]),
         ]
         grads = jnp.concatenate(rows, axis=0)
         row = lax.broadcasted_iota(jnp.int32, (8, width), 0)
@@ -866,7 +881,7 @@
         spread = jnp.concatenate(spread, axis=0)
         high = spread.astype(BF16)
         rest = (spread - high.astype(F32)).astype(BF16)
-        up = ordered(fold(uo_ref[...]), fold(ux_ref[...]))
+        up = ordered(fold(ups_ref[0:8]), fold(ups_ref[8:16]))
         index = lax.broadcasted_iota(jnp.int32, (count, hidden), 0)
         up = jnp.where(up_ref[...] == index, up, 0.0)
         up_high = up.astype(BF16)
@@ -895,34 +910,31 @@
         kernel,
         (out, out),
         (
-            core[None], thin, broad, rel, absolute, up_rel, sums_one, sums_two, up_own, up_other,
-            qkv_a, qkv_b, proj_grad,
+            core[None], thin, broad, rel, absolute, up_rel, sums, up_sums, head_sums, proj_grad,
         ),
-        in_specs=[pl.BlockSpec(memory_space=pltpu.SMEM)] + [WHOLE] * 12,
-    )
-
-
-def finish(a_kept, a_came, b_kept, b_came, cols, chunk, up_chunk, emb_shape):
-    rows = a_kept.shape[0]
-    a_wide = (a_kept.shape[1] - cols) // 3
+        in_specs=[pl.BlockSpec(memory_space=pltpu.SMEM)] + [WHOLE] * 9,
+    )
+
+
+def finish(kept, came, a_wide, cols, chunk, up_chunk, emb_shape):
+    rows = kept.shape[0]
     b_wide = cols - a_wide
-
-    def kernel(
-        ak_ref, ac_ref, bk_ref, bc_ref, qkv_ref, out_ref, emb_ref, gain_ref, bias_ref, up_ref,
-        a_ref, b_ref,
-    ):
-        a_ref[...] = ak_ref[...] + ac_ref[...].astype(F32)
-        b_ref[...] = bk_ref[...] + bc_ref[...].astype(F32)
+    beside = 3 * a_wide
+    second = beside + cols
+
+    def kernel(kept_ref, came_ref, qkv_ref, out_ref, emb_ref, gain_ref, bias_ref, up_ref, sum_ref):
+        sum_ref[...] = kept_ref[...] + came_ref[...].astype(F32)
         for part in range(3):
-            qkv_ref[part, :, :a_wide] = a_ref[:, part * a_wide : (part + 1) * a_wide]
-            qkv_ref[part, :, a_wide:] = b_ref[:, part * b_wide : (part + 1) * b_wide]
-        out_ref[...] = a_ref[:, 3 * a_wide :]
-        first = 3 * b_wide
+            qkv_ref[part, :, :a_wide] = sum_ref[:, part * a_wide : (part + 1) * a_wide]
+            start = second + part * b_wide
+            qkv_ref[part, :, a_wide:] = sum_ref[:, start : start + b_wide]
+        out_ref[...] = sum_ref[:, beside:second]
+        first = second + 3 * b_wide
         half = SMALL // 2
-        emb_ref[...] = b_ref[0:half, first:]
-        gain_ref[...] = b_ref[half : half + 2, first : first + chunk]
-        bias_ref[...] = b_ref[half + 2 : half + 8, first : first + chunk]
-        up_ref[...] = b_ref[half : half + 1, first + UP : first + UP + up_chunk]
+        emb_ref[...] = sum_ref[0:half, first:]
+        gain_ref[...] = sum_ref[half : half + 2, first : first + chunk]
+        bias_ref[...] = sum_ref[half + 2 : half + 8, first : first + chunk]
+        up_ref[...] = sum_ref[half : half + 1, first + UP : first + UP + up_chunk]
 
     outs = (
         shaped((3, rows, cols), F32),
@@ -932,12 +944,7 @@
         shaped((6, chunk), F32),
         shaped((1, up_chunk), F32),
     )
-    return call(
-        kernel,
-        outs,
-        (a_kept, a_came, b_kept, b_came),
-        scratch=[pltpu.VMEM(a_kept.shape, F32), pltpu.VMEM(b_kept.shape, F32)],
-    )
+    return call(kernel, outs, (kept, came), scratch=[pltpu.VMEM(kept.shape, F32)])
 
 
 def pack_plain(qkv_w, out_w, emb_w, gains, biases, up_bias):
@@ -984,7 +991,7 @@
 
 
 def pack_grads_plain(
-    core, blocks, sizes, sums_one, sums_two, up_own, up_other, qkv_a, qkv_b, proj_grad
+    core, blocks, sizes, sums, up_sums, head_sums, proj_grad
 ):
     rows, extra, emb_size, chunk, up_chunk, pad_to = sizes
     size = blocks.shape[0]
@@ -1000,9 +1007,10 @@
     def relative(value):
         return value.reshape(size, 2, -1)[blocks]
 
-    gain_two, shift_two, ffn_bias = (row.reshape(size, 2, chunk) for row in fold(sums_two))
-    gain_one, shift_one, out_bias = (row.reshape(size, 2, chunk) for row in fold(sums_one))
-    own, other = jnp.sum(jnp.concatenate([qkv_a, qkv_b], axis=3), axis=2)
+    gain_one, shift_one, out_bias, gain_two, shift_two, ffn_bias = (
+        row.reshape(size, 2, chunk) for row in fold(sums)
+    )
+    own, other = jnp.sum(head_sums, axis=2)
     small = jnp.concatenate(
         [
             proj_grad.reshape(size, 2, emb_size),
@@ -1014,7 +1022,7 @@
             shift_one,
             ffn_bias,
             shift_two,
-            relative(absolute(fold(up_own)[0], fold(up_other)[0])),
+            relative(absolute(*fold(up_sums))),
         ],
         axis=2,
     ).astype(BF16)
@@ -1163,15 +1171,22 @@
     )
     two_other = quarters(*after(two_other, hid_own))
     three_both_other = swap_cores(three_both)
-    hid_other, slope_other = up_forward(first_low, two_other, side_bias[1], True)
-    three_more, three_both_other = after((three_more, three_both_other), hid_other)
     cot_mine = lax.dynamic_index_in_dim(cotangent, core, 0, keepdims=False)
     cot_other = lax.dynamic_index_in_dim(cotangent, 1 - core, 0, keepdims=False)
-    cot = in_order(cot_mine, after(swap_cores(cot_other), hid_other))
+    cot = in_order(cot_mine, after(swap_cores(after(cot_other, first_low)), hid_own))
+    hid_other, slope_other = up_forward(after(first_low, cot), two_other, side_bias[1], True)
+    three_more, three_both_other = after((three_more, three_both_other), hid_other)
+    three_more_other = swap_cores(three_more)
     three_own = quarters(three_both, three_more)
-    three_other = quarters(three_both_other, swap_cores(three_more))
+    three_other = quarters(three_both_other, three_more_other)
     emb, g_ffn, g_ffn_t, g_res_two, proj_grad, sums_two = down_both(
-        seq_len[None], (hid_own, hid_other), (*three_own, *three_other), first, vec, proj, cot
+        seq_len[None],
+        (hid_own, hid_other),
+        (three_both, three_more, three_both_other, three_more_other),
+        first,
+        vec,
+        proj,
+        cot,
     )
 
     def low(*values):
@@ -1184,39 +1199,41 @@
     dk_other, ds_other = down_grad(g_ffn_t, hid_other, True)
     ds_came, dk_came = swap_cores(ds_other), swap_cores(dk_other)
     dk, ds = down_grad(g_ffn_t, after(hid_own, ds_other), False)
-    ds_came, dk_came = after((ds_came, dk_came), ds)
-    d_sent = low(ds, ds_came)
-    d_came = ways.flip(d_sent, lasts)
+    ds_came = after(ds_came, ds)
+    d_high = low(halves(ds)[1], halves(ds_came)[1])
+    d_low = low(halves(ds)[0], halves(ds_came)[0])
+    d_came_high = ways.flip(d_high, lasts)
     uk_other, us_other, up_bias_other, part = up_grad(
-        after(g_ffn, d_sent),
+        after(g_ffn, d_high, d_low),
         first_low_t,
         slope_other,
         three_other,
         two_other,
         g_res_two,
         True,
+        (),
     )
     us_came, uk_came = swap_cores(us_other), swap_cores(uk_other)
-    d_came = after(d_came, us_other)
-    d_sent = low(halves(dk)[1], halves(dk_came)[1], halves(d_came)[1])
-    d_held = added(halves(dk)[0], halves(dk_came)[0], halves(d_came)[0])
-    d_came = ways.flip(d_sent, seconds)
-    uk, us, up_bias_own, g_first = up_grad(
-        after(g_ffn, us_other, d_sent),
+    d_came_high, dk_came, d_low = after((d_came_high, dk_came, d_low), us_other)
+    d_came_low = ways.flip(d_low, lasts)
+    uk, us, up_bias, g_first = up_grad(
+        after(g_ffn, us_other, d_came_high),
         first_low_t,
         slope_own,
         three_own,
         two_own,
         part,
         False,
-    )
-    d_came, us_came, uk_came = after((d_came, us_came, uk_came), us)
+        (up_bias_other,),
+    )
+    d_came_low, us_came, uk_came = after((d_came_low, us_came, uk_came), us)
     u_sent = low(us, us_came)
     u_came = ways.flip(u_sent, lasts)
-    d_held, d_sent = spread(d_held + d_came.astype(F32))
-    d_came = ways.flip(d_sent, depth - 3)
-    g_res_one, g_branch_t, g_att, sums_one = norm_back(
-        after(g_first, u_sent, d_sent), res_one, vec, weights, cols
+    d_sent = low(halves(dk)[1], halves(dk_came)[1], d_came_high)
+    d_held = added(halves(dk)[0], halves(dk_came)[0], d_came_low)
+    d_came = ways.flip(d_sent, seconds)
+    g_res_one, g_branch_t, g_att, sums = norm_back(
+        after(g_first, u_sent, d_sent), res_one, vec, weights, sums_two, cols
     )
     pairs = list(range(cols // LANES))
     split = (len(pairs) + 1) // 2
@@ -1224,7 +1241,9 @@
     beside = (g_branch_t, att)
     ak_other, as_other = project_other(here_t, g_a, beside)
     as_came, ak_came = swap_cores(as_other), swap_cores(ak_other)
-    g_b, bias_b = attention_back(pairs[split:], after(g_att, as_other), att, qkv, lse, mask)
+    g_b, head_sums = attention_back(
+        pairs[split:], after(g_att, as_other), att, qkv, lse, mask, (bias_a,)
+    )
     as_came, ak_came = after((as_came, ak_came), g_b)
     a_keep, a_send = project_own(here_t, g_a, beside, (), ak_came, as_came)
     d_came, u_came = after((d_came, u_came), a_send)
@@ -1233,18 +1252,16 @@
     u_held = added(halves(uk)[0], halves(uk_came)[0], halves(u_came)[0])
     u_came = ways.flip(u_sent, seconds)
     d_held, d_sent = spread(d_held + d_came.astype(F32))
-    d_came = ways.flip(d_sent, depth - 4)
+    d_came = ways.flip(d_sent, depth - 3)
     bk_other, bs_other = project_other(here_t, after(g_b, a_send, u_sent, d_sent), ())
     bs_came, bk_came = swap_cores(bs_other), swap_cores(bk_other)
     if fast:
         small_own, small_other = pack_grads(
-            *tables, sums_one, after(sums_two, bs_other), up_bias_own, up_bias_other, bias_a,
-            bias_b, proj_grad,
+            *tables, after(sums, bs_other), up_bias, head_sums, proj_grad
         )
     else:
         small_own, small_other = pack_grads_plain(
-            core, blocks, small_sizes, sums_one, sums_two, up_bias_own, up_bias_other, bias_a,
-            bias_b, proj_grad,
+            core, blocks, small_sizes, sums, up_bias, head_sums, proj_grad
         )
     small_came = swap_cores(small_other)
     bs_came, bk_came = after((bs_came, bk_came), small_other)
@@ -1254,49 +1271,43 @@
     a_sent = low(halves(a_keep)[1], halves(a_came)[1])
     a_held = added(halves(a_keep)[0], halves(a_came)[0])
     a_came = ways.flip(a_sent, seconds)
-    u_held, u_sent = spread(u_held + u_came.astype(F32))
+    u_held, u_sent = spread(after(u_held, a_sent) + u_came.astype(F32))
     u_came = ways.flip(u_sent, depth - 3)
-    d_held = d_held + d_came.astype(F32)
-    g_here = token_back(
-        (after(g_a, b_send, a_sent, u_sent), g_b), g_res_one, perm, weights, cols
-    )
-    a_came, b_came, u_came = after((a_came, b_came, u_came), g_here)
+    d_held, d_sent = spread(after(d_held, a_sent) + d_came.astype(F32))
+    d_came = ways.flip(d_sent, depth - 4)
+    b_came = after(b_came, u_sent, d_sent)
     b_sent = low(halves(b_keep)[1], halves(b_came)[1])
     b_held = added(halves(b_keep)[0], halves(b_came)[0])
     b_came = ways.flip(b_sent, seconds)
-    a_held, a_sent = spread(a_held + a_came.astype(F32))
-    a_came = ways.flip(a_sent, depth - 3)
-    u_held, u_sent = spread(u_held + u_came.astype(F32))
-    u_came = ways.flip(u_sent, depth - 4)
+    g_here = token_back(
+        (after(g_a, b_send, a_sent, u_sent, b_sent), g_b), g_res_one, perm, weights, cols
+    )
+    a_came, b_came, u_came, d_came, emb = after((a_came, b_came, u_came, d_came, emb), g_here)
+    held = jnp.concatenate([a_held + a_came.astype(F32), b_held + b_came.astype(F32)], axis=1)
+    for step in range(depth - 3, -1, -1):
+        held, sent = spread(held)
+        came = ways.flip(sent, step)
+        if step == depth - 3:
+            u_held, u_sent = spread(u_held + after(u_came, sent).astype(F32))
+            u_came = ways.flip(u_sent, depth - 4)
+        if step:
+            held = held + came.astype(F32)
+    d_held = d_held + after(d_came, u_sent).astype(F32)
     for step in range(depth - 5, -1, -1):
         d_held, sent = spread(d_held)
         d_held = d_held + ways.flip(sent, step).astype(F32)
         u_held, sent = spread(u_held + u_came.astype(F32))
         u_came = ways.flip(sent, step)
     down_shard, up_shard = d_held, u_held + u_came.astype(F32)
-    b_held, b_sent = spread(b_held + b_came.astype(F32))
-    b_came = ways.flip(b_sent, depth - 3)
-    for step in range(depth - 4, -1, -1):
-        a_held, sent = spread(a_held + a_came.astype(F32))
-        a_came = ways.flip(sent, step)
-        b_held, sent = spread(b_held + b_came.astype(F32))
-        b_came = ways.flip(sent, step)
+    a_wide, b_wide = split * LANES, (len(pairs) - split) * LANES
     if fast:
         qkv_shard, out_shard, emb_shard, gain_shard, bias_shard, up_bias_shard = finish(
-            a_held,
-            a_came,
-            b_held,
-            b_came,
-            cols,
-            chunk,
-            up_bias_vector.size,
-            embedding_projection_weight.shape,
+            held, came, a_wide, cols, chunk, up_bias_vector.size, embedding_projection_weight.shape
         )
         out_shard, up_bias_shard = out_shard.T, up_bias_shard[0]
     else:
-        a_shard = a_held + a_came.astype(F32)
-        b_shard = b_held + b_came.astype(F32)
-        a_wide, b_wide = split * LANES, (len(pairs) - split) * LANES
+        shard = held + came.astype(F32)
+        a_shard, b_shard = shard[:, : 3 * a_wide + cols], shard[:, 3 * a_wide + cols :]
         qkv_shard = jnp.stack(
             [
                 jnp.concatenate(

time: 237 us -> 223 us (0.941)
  local copies, waits for them, and re-layouts: 22.6 us -> 14.2 us
  waiting for transfers between devices: 61.9 us -> 56 us
    unnamed x114 -> x76, local copies, waits for them, and re-layouts: 16.8 us -> 8.82 us
    ppermute x29 -> x28, waiting for transfers between devices: 56.8 us -> 51.5 us  [flip(): return lax.ppermute(value, ('dp', 'tensor'), pairs)]
    add x6 -> x7, other arithmetic: 3.2 us -> 5.68 us  [the longest x1 1.69 us: body(): u_held, u_sent = spread(after(u_held, a_sent) + u_came.astype(F32))]
    ppermute x29 -> x28, starting transfers between devices: 40.8 us -> 40.2 us  [flip(): return lax.ppermute(value, ('dp', 'tensor'), pairs)]
  transfers between devices with their start and end apart: 50 -> 49, of which waited for: 22 -> 21; matrix products, arithmetic and copies ran while one was open for 9% -> 10% of each run, Pallas kernels for 31% -> 33%
where the time goes in v2:
time: 223 us
  Pallas kernels  86.8 us (39%)
  waiting for transfers between devices  56 us (25%)
  starting transfers between devices  43.6 us (20%)
  other arithmetic  16.7 us (7%)
  local copies, waits for them, and re-layouts  14.2 us (6%)
  between operations  5.5 us (2%)
    pallas_call x20, Pallas kernels, call(): pl.pallas_call(body, out_shape=outs, grid=grid or (), in_specs=in_specs o...  86.8 us
    ppermute x28, waiting for transfers between devices, flip(): return lax.ppermute(value, ('dp', 'tensor'), pairs)  51.5 us
    ppermute x28, starting transfers between devices, flip(): return lax.ppermute(value, ('dp', 'tensor'), pairs)  40.2 us
    unnamed x76, local copies, waits for them, and re-layouts  8.82 us
  transfers between devices with their start and end apart: 49, of which 21 were waited for; matrix products, arithmetic and copies ran while one was open for 10% of the time, Pallas kernels for 33%

profile of v2, /device:TPU:0, one launch (start us, length us, event | category | flops | bytes accessed | tf_op | source)
XLA Modules:
  0.0 222.7 jit_solution(16055283308549277563)
XLA Ops:
  0.6 1.7 shard_map.222
  2.4 4.1 %collective-permute-start = (bf16[48,1664]{1,0:T(8,128)(2,1)}, bf16[48,1664]{1,0:T(8,128)(2,1)S(1)}, u32[]{:S(2)}, u32[]{:S(2)}) collective-permute-start(bf16[48,1664]{1,0:T(8,128)(2,1)} %shard_map.222), channel_id=1, source_target_pairs={{0,16},{1,17},{2,18},{3,19},{4,20},{5,21},{6,22},{7,23},{8,24},{9,... | collective-permute-start | bytes 479240 | tf_op jit(solution)/shard_map/ppermute | solution.py:694
  10.0 4.2 %collective-permute-done = bf16[48,1664]{1,0:T(8,128)(2,1)S(1)} collective-permute-done((bf16[48,1664]{1,0:T(8,128)(2,1)}, bf16[48,1664]{1,0:T(8,128)(2,1)S(1)}, u32[]{:S(2)}, u32[]{:S(2)}) %collective-permute-start) | collective-permute-done | bytes 159776 | tf_op jit(solution)/shard_map/ppermute | solution.py:694
  15.8 3.3 %collective-permute-start.2 = (bf16[48,1536]{1,0:T(8,128)(2,1)}, bf16[48,1536]{1,0:T(8,128)(2,1)}, u32[]{:S(2)}, u32[]{:S(2)}) collective-permute-start(bf16[48,1536]{1,0:T(8,128)(2,1)} %param.21), channel_id=1, source_target_pairs={{0,16},{1,17},{2,18},{3,19},{4,20},{5,21},{6,22},{7,23},{8,24},{9,... | collective-permute-start | bytes 442376 | tf_op jit(solution)/shard_map/ppermute | solution.py:694
  19.1 1.6 constant_dynamic-update-slice_fusion.5
  28.2 1.4 collective-permute-start.3
  29.6 1.5 collective-permute-start.4
  32.0 3.3 %collective-permute-start.5 = (bf16[96,1536]{1,0:T(8,128)(2,1)S(1)}, bf16[96,1536]{1,0:T(8,128)(2,1)S(1)}, u32[]{:S(2)}, u32[]{:S(2)}) collective-permute-start(bf16[96,1536]{1,0:T(8,128)(2,1)S(1)} %get-tuple-element.309), channel_id=1, source_target_pairs={{0,8},{1,9},{2,10},{3,11},{4,12},{5,13},{6,14},{7,15},{8,0},{9,1},... | collective-permute-start | bytes 884744 | tf_op jit(solution)/shard_map/ppermute | solution.py:694
  36.5 1.7 collective-permute-start.6
  39.3 6.2 %collective-permute-done.6 = bf16[48,1536]{1,0:T(8,128)(2,1)S(1)} collective-permute-done((bf16[48,1536]{1,0:T(8,128)(2,1)S(1)}, bf16[48,1536]{1,0:T(8,128)(2,1)S(1)}, u32[]{:S(2)}, u32[]{:S(2)}) %collective-permute-start.6) | collective-permute-done | bytes 147488 | tf_op jit(solution)/shard_map/ppermute | solution.py:694
  48.0 1.6 collective-permute-start.9
  49.6 2.2 collective-permute-start.10
  51.8 7.2 %collective-permute-done.10 = bf16[96,1536]{1,0:T(8,128)(2,1)S(1)} collective-permute-done((bf16[96,1536]{1,0:T(8,128)(2,1)S(1)}, bf16[96,1536]{1,0:T(8,128)(2,1)S(1)}, u32[]{:S(2)}, u32[]{:S(2)}) %collective-permute-start.10) | collective-permute-done | bytes 294944 | tf_op jit(solution)/shard_map/ppermute | solution.py:694
  58.9 3.5 %collective-permute-done.9 = bf16[192,1536]{1,0:T(8,128)(2,1)S(1)} collective-permute-done((bf16[192,1536]{1,0:T(8,128)(2,1)S(1)}, bf16[192,1536]{1,0:T(8,128)(2,1)S(1)}, u32[]{:S(2)}, u32[]{:S(2)}) %collective-permute-start.9) | collective-permute-done | bytes 589856 | tf_op jit(solution)/shard_map/ppermute | solution.py:694
  63.3 1.6 collective-permute-start.16
  65.3 1.7 shard_map.223
  67.0 15.8 %shard_map.224 = (bf16[2,512,1152]{2,1,0:T(8,128)(2,1)S(1)}, f32[2,6,512]{2,1,0:T(8,128)S(1)}, bf16[2,512,384]{2,1,0:T(8,128)(2,1)S(1)}, f32[512,768]{1,0:T(8,12...) custom-call(bf16[512,768]{1,0:T(8,128)(2,1)S(1)} %maximum_select_fus, ...), custom_call_target="tpu_custom_call" | custom-call | flops 2415919104 | bytes 1048576 | tf_op jit(solution)/shard_map/pallas_call | solution.py:61
  82.8 2.3 %collective-permute-done.15.c_ref.d_ref.refs_6_.refs_7_ = bf16[384,1536]{1,0:T(8,128)(2,1)S(1)} collective-permute-done((bf16[384,1536]{1,0:T(8,128)(2,1)S(1)}, bf16[384,1536]{1,0:T(8,128)(2,1)S(1)}, u32[]{:S(2)}, u32[]{:S(2)}) %collective-permute-start.15) | collective-permute-done | bytes 1179680 | tf_op jit(solution)/shard_map/ppermute | solution.py:694
  86.4 5.1 %shard_map.225 = (bf16[512,1536]{1,0:T(8,128)(2,1)S(1)}, bf16[512,1536]{1,0:T(8,128)(2,1)S(1)}) custom-call(bf16[512,768]{1,0:T(8,128)(2,1)S(1)} %get-tuple-element.200.low_ref, bf16[384,1536]{1,0:T(8,128)(2,1)S(1)} %constant_dynamic-update-slice_fusion.2.a_ref.b_ref.refs_4_.refs_5_, ...), custom_call_target="tpu_custom_call" | custom-call | flops 1207959552 | bytes 1048576 | tf_op jit(solution)/shard_map/pallas_call | solution.py:61
  91.5 5.1 %shard_map.226 = (bf16[512,1536]{1,0:T(8,128)(2,1)S(1)}, bf16[512,1536]{1,0:T(8,128)(2,1)S(1)}) custom-call(bf16[512,768]{1,0:T(8,128)(2,1)S(1)} %get-tuple-element.200.low_ref, bf16[384,1536]{1,0:T(8,128)(2,1)S(1)} %collective-permute-done.18.a_ref.b_ref.refs_4_.refs_5_, bf16[384,1536]{1,0:T(8,128)(2,1)S(1)} %collective-permute-done.18.a_ref.b_ref.refs_4_.refs_5_, ...), custom_call_target="tpu_custom_call" | custom-call | flops 1207959552 | bytes 1048576 | tf_op jit(solution)/shard_map/pallas_call | solution.py:61
  96.7 4.8 %collective-permute-done.20.refs_1_.refs_2_.refs_3_ = bf16[384,1536]{1,0:T(8,128)(2,1)S(1)} collective-permute-done((bf16[384,1536]{1,0:T(8,128)(2,1)S(1)}, bf16[384,1536]{1,0:T(8,128)(2,1)S(1)}, u32[]{:S(2)}, u32[]{:S(2)}) %collective-permute-start.20) | collective-permute-done | bytes 1179680 | tf_op jit(solution)/shard_map/ppermute | solution.py:694
  101.4 2.8 %collective-permute-done.22.refs_3_.refs_2_ = bf16[384,1536]{1,0:T(8,128)(2,1)S(1)} collective-permute-done((bf16[384,1536]{1,0:T(8,128)(2,1)S(1)}, bf16[384,1536]{1,0:T(8,128)(2,1)S(1)}, u32[]{:S(2)}, u32[]{:S(2)}) %collective-permute-start.22) | collective-permute-done | bytes 1179680 | tf_op jit(solution)/shard_map/ppermute | solution.py:28
  104.3 8.4 %shard_map.227 = (f32[512,128]{1,0:T(8,128)S(1)}, bf16[512,768]{1,0:T(8,128)(2,1)S(1)}, bf16[768,512]{1,0:T(8,128)(2,1)S(1)}, f32[512,768]{1,0:T(8,128)S(1)}, f3...) custom-call(s32[1]{0:T(128)} %dynamic_slice.43.len_ref, bf16[512,1536]{1,0:T(8,128)(2,1)S(1)} %get-tuple-element.211.h0_ref.hid_ref, ...), custom_call_target="tpu_custom_call" | custom-call | flops 2415919104 | bytes 1048576 | tf_op jit(solution)/shard_map/pallas_call | solution.py:61
  112.7 2.0 shard_map.228
  115.3 2.0 shard_map.229
  118.5 8.6 %shard_map.230 = (bf16[384,1536]{1,0:T(8,128)(2,1)S(1)}, bf16[384,1536]{1,0:T(8,128)(2,1)S(1)}, f32[8,1536]{1,0:T(8,128)S(1)}, f32[512,768]{1,0:T(8,128)S(1)}) custom-call(bf16[512,768]{1,0:T(8,128)(2,1)S(1)} %get-tuple-element.221.g_ref, bf16[768,512]{1,0:T(8,128)(2,1)S(1)} %get-tuple-element.215.lowt_ref, ...), custom_call_target="tpu_custom_call" | custom-call | flops 3623878656 | bytes 1048576 | tf_op jit(solution)/shard_map/pallas_call | solution.py:61
  127.9 1.4 collective-permute-start.26
  129.2 8.7 %shard_map.231 = (bf16[384,1536]{1,0:T(8,128)(2,1)S(1)}, bf16[384,1536]{1,0:T(8,128)(2,1)S(1)}, f32[16,1536]{1,0:T(8,128)S(1)}, f32[512,768]{1,0:T(8,128)S(1)}) custom-call(bf16[512,768]{1,0:T(8,128)(2,1)S(1)} %get-tuple-element.221.g_ref, bf16[768,512]{1,0:T(8,128)(2,1)S(1)} %get-tuple-element.215.lowt_ref, ...), custom_call_target="tpu_custom_call" | custom-call | flops 3623878656 | bytes 1048576 | tf_op jit(solution)/shard_map/pallas_call | solution.py:61
  139.5 2.4 %shard_map.232 = (f32[512,768]{1,0:T(8,128)S(1)}, bf16[768,512]{1,0:T(8,128)(2,1)S(1)}, bf16[2,512,384]{2,1,0:T(8,128)(2,1)S(1)}, f32[48,768]{1,0:T(8,128)S(1)}) custom-call(f32[512,768]{1,0:T(8,128)S(1)} %get-tuple-element.232.gf_ref, f32[512,768]{1,0:T(8,128)S(1)} %get-tuple-element.233.res_ref, f32[8,768]{1,0:T(8,128)S(1)} %get-tuple-element.190.vec_ref, ...), custom_call_target="tpu_custom_call" | custom-call | flops 603979776 | bytes 1048576 | tf_op jit(solution)/shard_map/pallas_call | solution.py:61
  143.0 6.8 %shard_map.233 = (bf16[2,512,768]{2,1,0:T(8,128)(2,1)S(1)}, f32[2,2,8,256]{3,2,1,0:T(8,128)S(1)}) custom-call(bf16[2,512,384]{2,1,0:T(8,128)(2,1)S(1)} %get-tuple-element.244.gatt_ref, bf16[2,512,384]{2,1,0:T(8,128)(2,1)S(1)} %get-tuple-element.237.att_ref.refs_1_, bf16[2,512,1152]{2,1,0:T(8,128)(2,1)S(1)} %get-tuple-element.238.qkv_ref, ...), custom_call_target="tpu_custom_call" | custom-call | flops 2684354560 | bytes 1048576 | tf_op jit(solution)/shard_map/pallas_call | solution.py:61
  152.1 3.7 %shard_map.235 = (bf16[2,512,384]{2,1,0:T(8,128)(2,1)S(1)}, f32[2,2,8,384]{3,2,1,0:T(8,128)S(1)}) custom-call(bf16[2,512,384]{2,1,0:T(8,128)(2,1)S(1)} %get-tuple-element.244.gatt_ref, bf16[2,512,384]{2,1,0:T(8,128)(2,1)S(1)} %get-tuple-element.237.att_ref.refs_1_, bf16[2,512,1152]{2,1,0:T(8,128)(2,1)S(1)} %get-tuple-element.238.qkv_ref, ...), custom_call_target="tpu_custom_call" | custom-call | flops 1342177280 | bytes 1048576 | tf_op jit(solution)/shard_map/pallas_call | solution.py:61
  155.9 2.2 shard_map.236
  159.1 2.5 %collective-permute-done.31 = bf16[192,1536]{1,0:T(8,128)(2,1)S(1)} collective-permute-done((bf16[192,1536]{1,0:T(8,128)(2,1)S(1)}, bf16[192,1536]{1,0:T(8,128)(2,1)S(1)}, u32[]{:S(2)}, u32[]{:S(2)}) %collective-permute-start.31) | collective-permute-done | bytes 589856 | tf_op jit(solution)/shard_map/ppermute | solution.py:694
  161.7 1.6 convert_add_fusion.1
  166.6 3.1 %collective-permute-start.33 = (bf16[96,1536]{1,0:T(8,128)(2,1)}, bf16[96,1536]{1,0:T(8,128)(2,1)}, u32[]{:S(2)}, u32[]{:S(2)}) collective-permute-start(bf16[96,1536]{1,0:T(8,128)(2,1)} %slice.203), channel_id=1, source_target_pairs={{0,8},{1,9},{2,10},{3,11},{4,12},{5,13},{6,14},{7,15},{8,0},{9,1},... | collective-permute-start | bytes 884744 | tf_op jit(solution)/shard_map/ppermute | solution.py:694
  169.8 3.1 %shard_map.238 = (bf16[768,128]{1,0:T(8,128)(2,1)S(1)}, bf16[768,128]{1,0:T(8,128)(2,1)}) custom-call(s32[1]{0:T(128)} %bitcast.8.core_ref, bf16[2,128,768]{2,1,0:T(8,128)(2,1)S(1)} %copy-done.8, bf16[2,128,3072]{2,1,0:T(8,128)(2,1)S(1)} %add_convert_fusion.broad_ref, s32[1,768]{1,0:T(1,128)S(1)} %and_select_fusion.rel_ref, s32[1,768]{1,0:T(1,128)S(1)} %copy-done.22, ...), custom_call_target="tpu_custom_call" | custom-call | bytes 1048576 | tf_op jit(solution)/shard_map/pallas_call | solution.py:61
  179.4 1.7 shard_map.239
  181.1 1.4 collective-permute-start.40
  185.3 1.7 convert_add_fusion
  187.0 1.5 collective-permute-start.43
  189.7 2.9 %collective-permute-done.40 = bf16[384,512]{1,0:T(8,128)(2,1)S(1)} collective-permute-done((bf16[384,512]{1,0:T(8,128)(2,1)S(1)}, bf16[384,512]{1,0:T(8,128)(2,1)S(1)}, u32[]{:S(2)}, u32[]{:S(2)}) %collective-permute-start.40) | collective-permute-done | bytes 393248 | tf_op jit(solution)/shard_map/ppermute | solution.py:694
  192.8 4.7 %shard_map.240 = f32[512,768]{1,0:T(8,128)S(1)} custom-call(bf16[2,512,768]{2,1,0:T(8,128)(2,1)S(1)} %copy-done.2, bf16[2,512,384]{2,1,0:T(8,128)(2,1)S(1)} %copy-done.4, f32[512,768]{1,0:T(8,128)S(1)} %copy-done.10, bf16[768,768]{1,0:T(8,128)(2,1)S(1)} %copy-done.6, bf16[2,768,1536]{2,1,0:T(8,128)(2,1)S(1)} %bitcast.28), custom_call_target="tpu_custom_call" | custom-call | flops 2415919104 | bytes 1048576 | tf_op jit(solution)/shard_map/pallas_call | solution.py:61
  198.4 1.5 collective-permute-done.42
  201.6 1.5 collective-permute-start.48
  204.6 5.8 %collective-permute-done.48 = bf16[48,1536]{1,0:T(8,128)(2,1)S(1)} collective-permute-done((bf16[48,1536]{1,0:T(8,128)(2,1)S(1)}, bf16[48,1536]{1,0:T(8,128)(2,1)S(1)}, u32[]{:S(2)}, u32[]{:S(2)}) %collective-permute-start.48) | collective-permute-done | bytes 147488 | tf_op jit(solution)/shard_map/ppermute | solution.py:694
  211.1 1.4 collective-permute-done.46
  212.7 2.1 collective-permute-start.47
  214.8 7.1 %collective-permute-done.47.came_ref = bf16[48,1664]{1,0:T(8,128)(2,1)S(1)} collective-permute-done((bf16[48,1664]{1,0:T(8,128)(2,1)S(1)}, bf16[48,1664]{1,0:T(8,128)(2,1)S(1)}, u32[]{:S(2)}, u32[]{:S(2)}) %collective-permute-start.47) | collective-permute-done | bytes 159776 | tf_op jit(solution)/shard_map/ppermute | solution.py:694
  (213 shorter events, 44.9 us)
Async XLA Ops:
  2.4 11.8 %collective-permute-start = (bf16[48,1664]{1,0:T(8,128)(2,1)}, bf16[48,1664]{1,0:T(8,128)(2,1)S(1)}, u32[]{:S(2)}, u32[]{:S(2)}) collective-permute-start(bf16[48,1664]{1,0:T(8,128)(2,1)} %shard_map.222), channel_id=1, source_target_pairs={{0,16},{1,17},{2,18},{3,19},{4,20},{5,21},{6,22},{7,23},{8,24},{9,... | collective-permute-start | bytes 479240 | tf_op jit(solution)/shard_map/ppermute | solution.py:694
  15.0 12.2 %collective-permute-start.1 = (bf16[96,1664]{1,0:T(8,128)(2,1)}, bf16[96,1664]{1,0:T(8,128)(2,1)}, u32[]{:S(2)}, u32[]{:S(2)}) collective-permute-start(bf16[96,1664]{1,0:T(8,128)(2,1)} %pad_maximum_fusion.3), channel_id=1, source_target_pairs={{0,8},{1,9},{2,10},{3,11},{4,12},{5,13},{6,14},{7,15},{8,0},{9,1},... | collective-permute-start | bytes 958472 | tf_op jit(solution)/shard_map/ppermute | solution.py:694
  15.8 11.4 %collective-permute-start.2 = (bf16[48,1536]{1,0:T(8,128)(2,1)}, bf16[48,1536]{1,0:T(8,128)(2,1)}, u32[]{:S(2)}, u32[]{:S(2)}) collective-permute-start(bf16[48,1536]{1,0:T(8,128)(2,1)} %param.21), channel_id=1, source_target_pairs={{0,16},{1,17},{2,18},{3,19},{4,20},{5,21},{6,22},{7,23},{8,24},{9,... | collective-permute-start | bytes 442376 | tf_op jit(solution)/shard_map/ppermute | solution.py:694
  28.2 18.0 %collective-permute-start.3 = (bf16[192,1664]{1,0:T(8,128)(2,1)S(1)}, bf16[192,1664]{1,0:T(8,128)(2,1)S(1)}, u32[]{:S(2)}, u32[]{:S(2)}) collective-permute-start(bf16[192,1664]{1,0:T(8,128)(2,1)S(1)} %pad_maximum_fusion.1.refs_0_), channel_id=1, source_target_pairs={{0,4},{1,3},{2,6},{3,1},{4,0},{5,7},{6,2},{7,5},{8,12},{9,11},{10,... | collective-permute-start | bytes 1916936 | tf_op jit(solution)/shard_map/ppermute | solution.py:694
  29.6 16.6 %collective-permute-start.4 = (bf16[192,1664]{1,0:T(8,128)(2,1)S(1)}, bf16[192,1664]{1,0:T(8,128)(2,1)S(1)}, u32[]{:S(2)}, u32[]{:S(2)}) collective-permute-start(bf16[192,1664]{1,0:T(8,128)(2,1)S(1)} %pad_maximum_fusion.1.refs_0_), channel_id=1, source_target_pairs={{0,2},{1,5},{2,0},{3,7},{4,6},{5,1},{6,4},{7,3},{8,10},{9,13},{10,... | collective-permute-start | bytes 1916936 | tf_op jit(solution)/shard_map/ppermute | solution.py:694
  31.1 7.8 %collective-permute-start.7 = (bf16[256,768]{1,0:T(8,128)(2,1)S(1)}, bf16[256,768]{1,0:T(8,128)(2,1)S(1)}, u32[]{:S(2)}, u32[]{:S(2)}) collective-permute-start(bf16[256,768]{1,0:T(8,128)(2,1)S(1)} %get-tuple-element.160), channel_id=1, source_target_pairs={{0,1},{1,0},{2,3},{3,2},{4,5},{5,4},{6,7},{7,6},{8,9},{9,8},{10,11... | collective-permute-start | bytes 1179656 | tf_op jit(solution)/shard_map/ppermute | solution.py:28
  32.0 14.2 %collective-permute-start.5 = (bf16[96,1536]{1,0:T(8,128)(2,1)S(1)}, bf16[96,1536]{1,0:T(8,128)(2,1)S(1)}, u32[]{:S(2)}, u32[]{:S(2)}) collective-permute-start(bf16[96,1536]{1,0:T(8,128)(2,1)S(1)} %get-tuple-element.309), channel_id=1, source_target_pairs={{0,8},{1,9},{2,10},{3,11},{4,12},{5,13},{6,14},{7,15},{8,0},{9,1},... | collective-permute-start | bytes 884744 | tf_op jit(solution)/shard_map/ppermute | solution.py:694
  36.5 9.0 %collective-permute-start.6 = (bf16[48,1536]{1,0:T(8,128)(2,1)S(1)}, bf16[48,1536]{1,0:T(8,128)(2,1)S(1)}, u32[]{:S(2)}, u32[]{:S(2)}) collective-permute-start(bf16[48,1536]{1,0:T(8,128)(2,1)S(1)} %bitcast.29), channel_id=1, source_target_pairs={{0,16},{1,17},{2,18},{3,19},{4,20},{5,21},{6,22},{7,23},{8,24},{9,... | collective-permute-start | bytes 442376 | tf_op jit(solution)/shard_map/ppermute | solution.py:694
  38.9 10.7 %collective-permute-start.11 = (bf16[192,1664]{1,0:T(8,128)(2,1)S(1)}, bf16[192,1664]{1,0:T(8,128)(2,1)S(1)}, u32[]{:S(2)}, u32[]{:S(2)}) collective-permute-start(bf16[192,1664]{1,0:T(8,128)(2,1)S(1)} %pad_maximum_fusion.1.refs_0_), channel_id=1, source_target_pairs={{0,1},{1,0},{2,3},{3,2},{4,5},{5,4},{6,7},{7,6},{8,9},{9,8},{10,11... | collective-permute-start | bytes 1916936 | tf_op jit(solution)/shard_map/ppermute | solution.py:28
  46.2 16.3 %collective-permute-start.12 = (bf16[192,1664]{1,0:T(8,128)(2,1)S(1)}, bf16[192,1664]{1,0:T(8,128)(2,1)S(1)}, u32[]{:S(2)}, u32[]{:S(2)}) collective-permute-start(bf16[192,1664]{1,0:T(8,128)(2,1)S(1)} %collective-permute-done.3.refs_1_), channel_id=1, source_target_pairs={{0,1},{1,0},{2,3},{3,2},{4,5},{5,4},{6,7},{7,6},{8,9},{9,8},{10,11... | collective-permute-start | bytes 1916936 | tf_op jit(solution)/shard_map/ppermute | solution.py:28
  46.2 16.3 %collective-permute-start.8 = (bf16[192,1664]{1,0:T(8,128)(2,1)S(1)}, bf16[192,1664]{1,0:T(8,128)(2,1)S(1)}, u32[]{:S(2)}, u32[]{:S(2)}) collective-permute-start(bf16[192,1664]{1,0:T(8,128)(2,1)S(1)} %collective-permute-done.3.refs_1_), channel_id=1, source_target_pairs={{0,2},{1,5},{2,0},{3,7},{4,6},{5,1},{6,4},{7,3},{8,10},{9,13},{10,... | collective-permute-start | bytes 1916936 | tf_op jit(solution)/shard_map/ppermute | solution.py:694
  46.8 15.7 %collective-permute-start.13 = (bf16[192,1664]{1,0:T(8,128)(2,1)S(1)}, bf16[192,1664]{1,0:T(8,128)(2,1)S(1)}, u32[]{:S(2)}, u32[]{:S(2)}) collective-permute-start(bf16[192,1664]{1,0:T(8,128)(2,1)S(1)} %collective-permute-done.4.refs_2_), channel_id=1, source_target_pairs={{0,1},{1,0},{2,3},{3,2},{4,5},{5,4},{6,7},{7,6},{8,9},{9,8},{10,11... | collective-permute-start | bytes 1916936 | tf_op jit(solution)/shard_map/ppermute | solution.py:28
  48.0 14.5 %collective-permute-start.9 = (bf16[192,1536]{1,0:T(8,128)(2,1)S(1)}, bf16[192,1536]{1,0:T(8,128)(2,1)S(1)}, u32[]{:S(2)}, u32[]{:S(2)}) collective-permute-start(bf16[192,1536]{1,0:T(8,128)(2,1)S(1)} %pad_maximum_fusion.2), channel_id=1, source_target_pairs={{0,4},{1,3},{2,6},{3,1},{4,0},{5,7},{6,2},{7,5},{8,12},{9,11},{10,... | collective-permute-start | bytes 1769480 | tf_op jit(solution)/shard_map/ppermute | solution.py:694
  49.6 9.4 %collective-permute-start.10 = (bf16[96,1536]{1,0:T(8,128)(2,1)S(1)}, bf16[96,1536]{1,0:T(8,128)(2,1)S(1)}, u32[]{:S(2)}, u32[]{:S(2)}) collective-permute-start(bf16[96,1536]{1,0:T(8,128)(2,1)S(1)} %pad_maximum_fusion.4), channel_id=1, source_target_pairs={{0,8},{1,9},{2,10},{3,11},{4,12},{5,13},{6,14},{7,15},{8,0},{9,1},... | collective-permute-start | bytes 884744 | tf_op jit(solution)/shard_map/ppermute | solution.py:694
  62.5 22.6 %collective-permute-start.15 = (bf16[384,1536]{1,0:T(8,128)(2,1)S(1)}, bf16[384,1536]{1,0:T(8,128)(2,1)S(1)}, u32[]{:S(2)}, u32[]{:S(2)}) collective-permute-start(bf16[384,1536]{1,0:T(8,128)(2,1)S(1)} %constant_dynamic-update-slice_fusion.2.a_ref.b_ref.refs_4_.refs_5_), channel_id=1, source_target_pairs={{0,2},{1,5},{2,0},{3,7},{4,6},{5,1},{6,4},{7,3},{8,10},{9,13},{10,... | collective-permute-start | bytes 3538952 | tf_op jit(solution)/shard_map/ppermute | solution.py:694
  63.2 2.1 collective-permute-start.14
  63.3 19.5 %collective-permute-start.16 = (bf16[192,1536]{1,0:T(8,128)(2,1)S(1)}, bf16[192,1536]{1,0:T(8,128)(2,1)S(1)}, u32[]{:S(2)}, u32[]{:S(2)}) collective-permute-start(bf16[192,1536]{1,0:T(8,128)(2,1)S(1)} %get-tuple-element.301), channel_id=1, source_target_pairs={{0,4},{1,3},{2,6},{3,1},{4,0},{5,7},{6,2},{7,5},{8,12},{9,11},{10,... | collective-permute-start | bytes 1769480 | tf_op jit(solution)/shard_map/ppermute | solution.py:694
  64.9 26.6 %collective-permute-start.18 = (bf16[384,1536]{1,0:T(8,128)(2,1)S(1)}, bf16[384,1536]{1,0:T(8,128)(2,1)S(1)}, u32[]{:S(2)}, u32[]{:S(2)}) collective-permute-start(bf16[384,1536]{1,0:T(8,128)(2,1)S(1)} %constant_dynamic-update-slice_fusion.2.a_ref.b_ref.refs_4_.refs_5_), channel_id=1, source_target_pairs={{0,1},{1,0},{2,3},{3,2},{4,5},{5,4},{6,7},{7,6},{8,9},{9,8},{10,11... | collective-permute-start | bytes 3538952 | tf_op jit(solution)/shard_map/ppermute | solution.py:28
  85.1 6.4 %collective-permute-start.19 = (bf16[384,1536]{1,0:T(8,128)(2,1)S(1)}, bf16[384,1536]{1,0:T(8,128)(2,1)S(1)}, u32[]{:S(2)}, u32[]{:S(2)}) collective-permute-start(bf16[384,1536]{1,0:T(8,128)(2,1)S(1)} %collective-permute-done.15.c_ref.d_ref.refs_6_.refs_7_), channel_id=1, source_target_pairs={{0,1},{1,0},{2,3},{3,2},{4,5},{5,4},{6,7},{7,6},{8,9},{9,8},{10,11... | collective-permute-start | bytes 3538952 | tf_op jit(solution)/shard_map/ppermute | solution.py:28
  85.2 16.3 %collective-permute-start.20 = (bf16[384,1536]{1,0:T(8,128)(2,1)S(1)}, bf16[384,1536]{1,0:T(8,128)(2,1)S(1)}, u32[]{:S(2)}, u32[]{:S(2)}) collective-permute-start(bf16[384,1536]{1,0:T(8,128)(2,1)S(1)} %constant_dynamic-update-slice_fusion.9.refs_0_.refs_1_), channel_id=1, source_target_pairs={{0,2},{1,5},{2,0},{3,7},{4,6},{5,1},{6,4},{7,3},{8,10},{9,13},{10,... | collective-permute-start | bytes 3538952 | tf_op jit(solution)/shard_map/ppermute | solution.py:694
  85.8 15.7 %collective-permute-start.21 = (bf16[384,1536]{1,0:T(8,128)(2,1)S(1)}, bf16[384,1536]{1,0:T(8,128)(2,1)S(1)}, u32[]{:S(2)}, u32[]{:S(2)}) collective-permute-start(bf16[384,1536]{1,0:T(8,128)(2,1)S(1)} %constant_dynamic-update-slice_fusion.9.refs_0_.refs_1_), channel_id=1, source_target_pairs={{0,1},{1,0},{2,3},{3,2},{4,5},{5,4},{6,7},{7,6},{8,9},{9,8},{10,11... | collective-permute-start | bytes 3538952 | tf_op jit(solution)/shard_map/ppermute | solution.py:28
  86.0 5.5 %collective-permute-start.17 = (f32[256,128]{1,0:T(8,128)S(1)}, f32[256,128]{1,0:T(8,128)S(1)}, u32[]{:S(2)}, u32[]{:S(2)}) collective-permute-start(f32[256,128]{1,0:T(8,128)S(1)} %get-tuple-element.198), channel_id=1, source_target_pairs={{0,1},{1,0},{2,3},{3,2},{4,5},{5,4},{6,7},{7,6},{8,9},{9,8},{10,11... | collective-permute-start | bytes 393224 | tf_op jit(solution)/shard_map/ppermute | solution.py:28
  101.4 2.8 %collective-permute-start.22 = (bf16[384,1536]{1,0:T(8,128)(2,1)S(1)}, bf16[384,1536]{1,0:T(8,128)(2,1)S(1)}, u32[]{:S(2)}, u32[]{:S(2)}) collective-permute-start(bf16[384,1536]{1,0:T(8,128)(2,1)S(1)} %collective-permute-done.20.refs_1_.refs_2_.refs_3_), channel_id=1, source_target_pairs={{0,1},{1,0},{2,3},{3,2},{4,5},{5,4},{6,7},{7,6},{8,9},{9,8},{10,11... | collective-permute-start | bytes 3538952 | tf_op jit(solution)/shard_map/ppermute | solution.py:28
  114.7 2.9 %collective-permute-start.23 = (bf16[384,1536]{1,0:T(8,128)(2,1)S(1)}, bf16[384,1536]{1,0:T(8,128)(2,1)S(1)}, u32[]{:S(2)}, u32[]{:S(2)}) collective-permute-start(bf16[384,1536]{1,0:T(8,128)(2,1)S(1)} %get-tuple-element.210), channel_id=1, source_target_pairs={{0,1},{1,0},{2,3},{3,2},{4,5},{5,4},{6,7},{7,6},{8,9},{9,8},{10,11... | collective-permute-start | bytes 3538952 | tf_op jit(solution)/shard_map/ppermute | solution.py:28
  114.9 12.8 %collective-permute-start.25 = (bf16[384,1536]{1,0:T(8,128)(2,1)S(1)}, bf16[384,1536]{1,0:T(8,128)(2,1)S(1)}, u32[]{:S(2)}, u32[]{:S(2)}) collective-permute-start(bf16[384,1536]{1,0:T(8,128)(2,1)S(1)} %get-tuple-element.219), channel_id=1, source_target_pairs={{0,1},{1,0},{2,3},{3,2},{4,5},{5,4},{6,7},{7,6},{8,9},{9,8},{10,11... | collective-permute-start | bytes 3538952 | tf_op jit(solution)/shard_map/ppermute | solution.py:28
  117.9 9.9 %collective-permute-start.24 = (bf16[192,1536]{1,0:T(8,128)(2,1)S(1)}, bf16[192,1536]{1,0:T(8,128)(2,1)S(1)}, u32[]{:S(2)}, u32[]{:S(2)}) collective-permute-start(bf16[192,1536]{1,0:T(8,128)(2,1)S(1)} %get-tuple-element.297), channel_id=1, source_target_pairs={{0,2},{1,5},{2,0},{3,7},{4,6},{5,1},{6,4},{7,3},{8,10},{9,13},{10,... | collective-permute-start | bytes 1769480 | tf_op jit(solution)/shard_map/ppermute | solution.py:694
  127.2 11.0 %collective-permute-start.27 = (bf16[384,1536]{1,0:T(8,128)(2,1)S(1)}, bf16[384,1536]{1,0:T(8,128)(2,1)S(1)}, u32[]{:S(2)}, u32[]{:S(2)}) collective-permute-start(bf16[384,1536]{1,0:T(8,128)(2,1)S(1)} %get-tuple-element.218), channel_id=1, source_target_pairs={{0,1},{1,0},{2,3},{3,2},{4,5},{5,4},{6,7},{7,6},{8,9},{9,8},{10,11... | collective-permute-start | bytes 3538952 | tf_op jit(solution)/shard_map/ppermute | solution.py:28
  127.2 10.9 %collective-permute-start.28 = (bf16[384,1536]{1,0:T(8,128)(2,1)S(1)}, bf16[384,1536]{1,0:T(8,128)(2,1)S(1)}, u32[]{:S(2)}, u32[]{:S(2)}) collective-permute-start(bf16[384,1536]{1,0:T(8,128)(2,1)S(1)} %get-tuple-element.228), channel_id=1, source_target_pairs={{0,1},{1,0},{2,3},{3,2},{4,5},{5,4},{6,7},{7,6},{8,9},{9,8},{10,11... | collective-permute-start | bytes 3538952 | tf_op jit(solution)/shard_map/ppermute | solution.py:28
  127.9 10.3 %collective-permute-start.26 = (bf16[192,1536]{1,0:T(8,128)(2,1)S(1)}, bf16[192,1536]{1,0:T(8,128)(2,1)S(1)}, u32[]{:S(2)}, u32[]{:S(2)}) collective-permute-start(bf16[192,1536]{1,0:T(8,128)(2,1)S(1)} %get-tuple-element.227), channel_id=1, source_target_pairs={{0,2},{1,5},{2,0},{3,7},{4,6},{5,1},{6,4},{7,3},{8,10},{9,13},{10,... | collective-permute-start | bytes 1769480 | tf_op jit(solution)/shard_map/ppermute | solution.py:694
  138.5 23.2 %collective-permute-start.32 = (bf16[384,1536]{1,0:T(8,128)(2,1)S(1)}, bf16[384,1536]{1,0:T(8,128)(2,1)S(1)}, u32[]{:S(2)}, u32[]{:S(2)}) collective-permute-start(bf16[384,1536]{1,0:T(8,128)(2,1)S(1)} %add_convert_fusion.1), channel_id=1, source_target_pairs={{0,2},{1,5},{2,0},{3,7},{4,6},{5,1},{6,4},{7,3},{8,10},{9,13},{10,... | collective-permute-start | bytes 3538952 | tf_op jit(solution)/shard_map/ppermute | solution.py:694
  151.0 4.8 %collective-permute-start.29 = (bf16[384,1152]{1,0:T(8,128)(2,1)S(1)}, bf16[384,1152]{1,0:T(8,128)(2,1)S(1)}, u32[]{:S(2)}, u32[]{:S(2)}) collective-permute-start(bf16[384,1152]{1,0:T(8,128)(2,1)S(1)} %get-tuple-element.242), channel_id=1, source_target_pairs={{0,1},{1,0},{2,3},{3,2},{4,5},{5,4},{6,7},{7,6},{8,9},{9,8},{10,11... | collective-permute-start | bytes 2654216 | tf_op jit(solution)/shard_map/ppermute | solution.py:28
  151.1 4.8 %collective-permute-start.30 = (bf16[384,1152]{1,0:T(8,128)(2,1)S(1)}, bf16[384,1152]{1,0:T(8,128)(2,1)S(1)}, u32[]{:S(2)}, u32[]{:S(2)}) collective-permute-start(bf16[384,1152]{1,0:T(8,128)(2,1)S(1)} %get-tuple-element.243), channel_id=1, source_target_pairs={{0,1},{1,0},{2,3},{3,2},{4,5},{5,4},{6,7},{7,6},{8,9},{9,8},{10,11... | collective-permute-start | bytes 2654216 | tf_op jit(solution)/shard_map/ppermute | solution.py:28
  151.6 10.1 %collective-permute-start.31 = (bf16[192,1536]{1,0:T(8,128)(2,1)S(1)}, bf16[192,1536]{1,0:T(8,128)(2,1)S(1)}, u32[]{:S(2)}, u32[]{:S(2)}) collective-permute-start(bf16[192,1536]{1,0:T(8,128)(2,1)S(1)} %add_convert_fusion.3), channel_id=1, source_target_pairs={{0,4},{1,3},{2,6},{3,1},{4,0},{5,7},{6,2},{7,5},{8,12},{9,11},{10,... | collective-permute-start | bytes 1769480 | tf_op jit(solution)/shard_map/ppermute | solution.py:694
  158.0 24.5 %collective-permute-start.35 = (bf16[384,1152]{1,0:T(8,128)(2,1)}, bf16[384,1152]{1,0:T(8,128)(2,1)}, u32[]{:S(2)}, u32[]{:S(2)}) collective-permute-start(bf16[384,1152]{1,0:T(8,128)(2,1)} %get-tuple-element.251), channel_id=1, source_target_pairs={{0,2},{1,5},{2,0},{3,7},{4,6},{5,1},{6,4},{7,3},{8,10},{9,13},{10,... | collective-permute-start | bytes 2654216 | tf_op jit(solution)/shard_map/ppermute | solution.py:694
  163.3 19.2 %collective-permute-start.34 = (bf16[192,1536]{1,0:T(8,128)(2,1)}, bf16[192,1536]{1,0:T(8,128)(2,1)}, u32[]{:S(2)}, u32[]{:S(2)}) collective-permute-start(bf16[192,1536]{1,0:T(8,128)(2,1)} %get-tuple-element.295), channel_id=1, source_target_pairs={{0,4},{1,3},{2,6},{3,1},{4,0},{5,7},{6,2},{7,5},{8,12},{9,11},{10,... | collective-permute-start | bytes 1769480 | tf_op jit(solution)/shard_map/ppermute | solution.py:694
  166.1 7.4 %collective-permute-start.36 = (bf16[384,384]{1,0:T(8,128)(2,1)S(1)}, bf16[384,384]{1,0:T(8,128)(2,1)S(1)}, u32[]{:S(2)}, u32[]{:S(2)}) collective-permute-start(bf16[384,384]{1,0:T(8,128)(2,1)S(1)} %get-tuple-element.257), channel_id=1, source_target_pairs={{0,1},{1,0},{2,3},{3,2},{4,5},{5,4},{6,7},{7,6},{8,9},{9,8},{10,11... | collective-permute-start | bytes 884744 | tf_op jit(solution)/shard_map/ppermute | solution.py:28
  166.1 9.3 %collective-permute-start.37 = (bf16[384,384]{1,0:T(8,128)(2,1)}, bf16[384,384]{1,0:T(8,128)(2,1)}, u32[]{:S(2)}, u32[]{:S(2)}) collective-permute-start(bf16[384,384]{1,0:T(8,128)(2,1)} %get-tuple-element.258), channel_id=1, source_target_pairs={{0,1},{1,0},{2,3},{3,2},{4,5},{5,4},{6,7},{7,6},{8,9},{9,8},{10,11... | collective-permute-start | bytes 884744 | tf_op jit(solution)/shard_map/ppermute | solution.py:28
  166.6 15.9 %collective-permute-start.33 = (bf16[96,1536]{1,0:T(8,128)(2,1)}, bf16[96,1536]{1,0:T(8,128)(2,1)}, u32[]{:S(2)}, u32[]{:S(2)}) collective-permute-start(bf16[96,1536]{1,0:T(8,128)(2,1)} %slice.203), channel_id=1, source_target_pairs={{0,8},{1,9},{2,10},{3,11},{4,12},{5,13},{6,14},{7,15},{8,0},{9,1},... | collective-permute-start | bytes 884744 | tf_op jit(solution)/shard_map/ppermute | solution.py:694
  174.3 1.7 collective-permute-start.38
  181.1 11.4 %collective-permute-start.40 = (bf16[384,512]{1,0:T(8,128)(2,1)S(1)}, bf16[384,512]{1,0:T(8,128)(2,1)S(1)}, u32[]{:S(2)}, u32[]{:S(2)}) collective-permute-start(bf16[384,512]{1,0:T(8,128)(2,1)S(1)} %get-tuple-element.268), channel_id=1, source_target_pairs={{0,2},{1,5},{2,0},{3,7},{4,6},{5,1},{6,4},{7,3},{8,10},{9,13},{10,... | collective-permute-start | bytes 1179656 | tf_op jit(solution)/shard_map/ppermute | solution.py:694
  183.6 16.2 %collective-permute-start.39 = (bf16[192,1152]{1,0:T(8,128)(2,1)S(1)}, bf16[192,1152]{1,0:T(8,128)(2,1)S(1)}, u32[]{:S(2)}, u32[]{:S(2)}) collective-permute-start(bf16[192,1152]{1,0:T(8,128)(2,1)S(1)} %add_convert_fusion.6), channel_id=1, source_target_pairs={{0,4},{1,3},{2,6},{3,1},{4,0},{5,7},{6,2},{7,5},{8,12},{9,11},{10,... | collective-permute-start | bytes 1327112 | tf_op jit(solution)/shard_map/ppermute | solution.py:694
  187.0 10.8 %collective-permute-start.43 = (bf16[48,1536]{1,0:T(8,128)(2,1)S(1)}, bf16[48,1536]{1,0:T(8,128)(2,1)S(1)}, u32[]{:S(2)}, u32[]{:S(2)}) collective-permute-start(bf16[48,1536]{1,0:T(8,128)(2,1)S(1)} %slice.206), channel_id=1, source_target_pairs={{0,16},{1,17},{2,18},{3,19},{4,20},{5,21},{6,22},{7,23},{8,24},{9,... | collective-permute-start | bytes 442376 | tf_op jit(solution)/shard_map/ppermute | solution.py:694
  188.5 11.3 %collective-permute-start.42 = (bf16[96,1536]{1,0:T(8,128)(2,1)S(1)}, bf16[96,1536]{1,0:T(8,128)(2,1)S(1)}, u32[]{:S(2)}, u32[]{:S(2)}) collective-permute-start(bf16[96,1536]{1,0:T(8,128)(2,1)S(1)} %slice.202), channel_id=1, source_target_pairs={{0,8},{1,9},{2,10},{3,11},{4,12},{5,13},{6,14},{7,15},{8,0},{9,1},... | collective-permute-start | bytes 884744 | tf_op jit(solution)/shard_map/ppermute | solution.py:694
  192.6 5.7 %collective-permute-start.41 = (bf16[192,512]{1,0:T(8,128)(2,1)S(1)}, bf16[192,512]{1,0:T(8,128)(2,1)S(1)}, u32[]{:S(2)}, u32[]{:S(2)}) collective-permute-start(bf16[192,512]{1,0:T(8,128)(2,1)S(1)} %add_convert_fusion.8), channel_id=1, source_target_pairs={{0,4},{1,3},{2,6},{3,1},{4,0},{5,7},{6,2},{7,5},{8,12},{9,11},{10,... | collective-permute-start | bytes 589832 | tf_op jit(solution)/shard_map/ppermute | solution.py:694
  197.5 17.2 %collective-permute-start.45 = (f32[256,768]{1,0:T(8,128)S(1)}, f32[256,768]{1,0:T(8,128)S(1)}, u32[]{:S(2)}, u32[]{:S(2)}) collective-permute-start(f32[256,768]{1,0:T(8,128)S(1)} %constant_dynamic-slice_fusion.1), channel_id=1, source_target_pairs={{0,1},{1,0},{2,3},{3,2},{4,5},{5,4},{6,7},{7,6},{8,9},{9,8},{10,11... | collective-permute-start | bytes 2359304 | tf_op jit(solution)/shard_map/ppermute | solution.py:28
  201.2 11.4 %collective-permute-start.46 = (bf16[96,1664]{1,0:T(8,128)(2,1)S(1)}, bf16[96,1664]{1,0:T(8,128)(2,1)S(1)}, u32[]{:S(2)}, u32[]{:S(2)}) collective-permute-start(bf16[96,1664]{1,0:T(8,128)(2,1)S(1)} %fusion.3), channel_id=1, source_target_pairs={{0,8},{1,9},{2,10},{3,11},{4,12},{5,13},{6,14},{7,15},{8,0},{9,1},... | collective-permute-start | bytes 958472 | tf_op jit(solution)/shard_map/ppermute | solution.py:694
  201.6 8.7 %collective-permute-start.48 = (bf16[48,1536]{1,0:T(8,128)(2,1)S(1)}, bf16[48,1536]{1,0:T(8,128)(2,1)S(1)}, u32[]{:S(2)}, u32[]{:S(2)}) collective-permute-start(bf16[48,1536]{1,0:T(8,128)(2,1)S(1)} %slice.205), channel_id=1, source_target_pairs={{0,16},{1,17},{2,18},{3,19},{4,20},{5,21},{6,22},{7,23},{8,24},{9,... | collective-permute-start | bytes 442376 | tf_op jit(solution)/shard_map/ppermute | solution.py:694
  212.7 9.2 %collective-permute-start.47 = (bf16[48,1664]{1,0:T(8,128)(2,1)S(1)}, bf16[48,1664]{1,0:T(8,128)(2,1)S(1)}, u32[]{:S(2)}, u32[]{:S(2)}) collective-permute-start(bf16[48,1664]{1,0:T(8,128)(2,1)S(1)} %slice.204), channel_id=1, source_target_pairs={{0,16},{1,17},{2,18},{3,19},{4,20},{5,21},{6,22},{7,23},{8,24},{9,... | collective-permute-start | bytes 479240 | tf_op jit(solution)/shard_map/ppermute | solution.py:694
  (36 other events, 399.6 us)

commit v3 on v2

--- a/solution.py
+++ b/solution.py
@@ -686,12 +686,22 @@
         outer = list(range(self.depth - 1, 1, -1))
         self.bits = (outer + [1, 0], outer + [0, 1])
 
-    def flip(self, value, step):
+    def flip(self, value, *steps):
         pairs = []
         for i in range(self.size):
             for core in range(2):
-                pairs.append((i * 2 + core, (i ^ (1 << self.bits[core][step])) * 2 + core))
+                to = i
+                for step in steps:
+                    to ^= 1 << self.bits[core][step]
+                pairs.append((i * 2 + core, to * 2 + core))
         return lax.ppermute(value, ("dp", "tensor"), pairs)
+
+    def last_outer(self):
+        low, high = self.depth - 4, self.depth - 3
+        return (low,), (high,), (low, high)
+
+    def flip_three(self, values):
+        return [self.flip(value, *steps) for value, steps in zip(values, self.last_outer())]
 
     def blocks(self):
         tables = []
@@ -706,8 +716,8 @@
         return jnp.where(self.core == 0, table[0], table[1]) ^ self.rank
 
 
-def join(held, came):
-    return jnp.concatenate([held, came], axis=0)
+def join(*parts):
+    return jnp.concatenate(parts, axis=0)
 
 
 def added(*values):
@@ -922,8 +932,12 @@
     beside = 3 * a_wide
     second = beside + cols
 
-    def kernel(kept_ref, came_ref, qkv_ref, out_ref, emb_ref, gain_ref, bias_ref, up_ref, sum_ref):
-        sum_ref[...] = kept_ref[...] + came_ref[...].astype(F32)
+    def kernel(kept_ref, *refs):
+        qkv_ref, out_ref, emb_ref, gain_ref, bias_ref, up_ref, sum_ref = refs[len(came) :]
+        total = kept_ref[...]
+        for ref in refs[: len(came)]:
+            total = total + ref[...].astype(F32)
+        sum_ref[...] = total
         for part in range(3):
             qkv_ref[part, :, :a_wide] = sum_ref[:, part * a_wide : (part + 1) * a_wide]
             start = second + part * b_wide
@@ -944,7 +958,7 @@
         shaped((6, chunk), F32),
         shaped((1, up_chunk), F32),
     )
-    return call(kernel, outs, (kept, came), scratch=[pltpu.VMEM(kept.shape, F32)])
+    return call(kernel, outs, (kept, *came), scratch=[pltpu.VMEM(kept.shape, F32)])
 
 
 def pack_plain(qkv_w, out_w, emb_w, gains, biases, up_bias):
@@ -1078,7 +1092,7 @@
 
     wide = 4 * cols
     seconds, lasts = depth - 2, depth - 1
-    for step in range(depth - 3):
+    for step in range(depth - 4):
         one = join(one, ways.flip(one, step))
     tokens, order, lengths, key_mask = after((tokens, order, lengths, key_mask), one)
     mine = order[0, core]
@@ -1086,15 +1100,15 @@
     my_half = lax.dynamic_index_in_dim(tokens, mine, 0, keepdims=False)
     their_half = lax.dynamic_index_in_dim(tokens, theirs, 0, keepdims=False)
     blocks = ways.blocks()
-    one_came = ways.flip(one, depth - 3)
+    one_came = ways.flip_three([one] * 3)
     if fast:
         thin, broad = spreads(sides, width, 2 * ff_local, chunk, up_bias_vector.size)
         places_of = jnp.argsort(blocks)
         rel = (jnp.arange(width, dtype=jnp.int32) // rows)[None]
         absolute = jnp.repeat(places_of, rows)[None].astype(jnp.int32)
         up_rel = jnp.repeat(places_of, 2 * up_bias_vector.size)[None].astype(jnp.int32)
-        one_came, thin, broad, rel, absolute, up_rel = together(
-            one_came, thin, broad, rel, absolute, up_rel
+        *one_came, thin, broad, rel, absolute, up_rel = together(
+            *one_came, thin, broad, rel, absolute, up_rel
         )
         tables = (core, thin, broad, rel, absolute, up_rel)
 
@@ -1117,31 +1131,19 @@
     for step in range(depth - 4):
         two = join(two, ways.flip(two, step))
         three = join(three, ways.flip(three, step))
-    two_came = ways.flip(two, depth - 4)
-    one_came, two_came = together(one_came, two_came)
-    one = join(one, one_came)
-    two = join(two, two_came)
+    one = join(one, *one_came)
     here = in_order(my_half, swap_cores(after(their_half, one)))
-    one_b, one_c, two_came, three_came, here, mask, perm = together(
-        ways.flip(one, seconds),
-        ways.flip(one, lasts),
-        ways.flip(two, depth - 3),
-        ways.flip(after(three, two), depth - 4),
-        here,
-        mask,
-        perm,
-    )
-    two = join(two, two_came)
-    three = join(three, three_came)
-    one_d, two_b, three_came, *one_other = together(
-        ways.flip(one_b, lasts),
-        ways.flip(two, seconds),
-        ways.flip(three, depth - 3),
-        swap_cores(one),
-        swap_cores(one_b),
-        swap_cores(one_c),
-    )
-    three = join(three, three_came)
+    two_came = ways.flip_three([after(two, one)] * 3)
+    one_b, one_c, here, mask, perm, *two_came = together(
+        ways.flip(one, seconds), ways.flip(one, lasts), here, mask, perm, *two_came
+    )
+    two = join(two, *two_came)
+    one_other = together(swap_cores(one), swap_cores(one_b), swap_cores(one_c))
+    three_came = ways.flip_three([after(three, two, *one_other)] * 3)
+    one_d, two_b, *three_came = together(
+        ways.flip(one_b, lasts), ways.flip(two, seconds), *three_came
+    )
+    three = join(three, *three_came)
     two_both = join(two, two_b)
     one_pieces = (one, one_b, one_c, one_d, *one_other, swap_cores(one_d))
     two_more, three_b = ways.flip(two_both, lasts), ways.flip(three, seconds)
@@ -1196,6 +1198,10 @@
         kept, sent = halves(value)
         return kept, sent.astype(BF16)
 
+    def quarter_out(value):
+        kept, *sent = jnp.split(value, 4)
+        return kept, [part.astype(BF16) for part in sent]
+
     dk_other, ds_other = down_grad(g_ffn_t, hid_other, True)
     ds_came, dk_came = swap_cores(ds_other), swap_cores(dk_other)
     dk, ds = down_grad(g_ffn_t, after(hid_own, ds_other), False)
@@ -1251,8 +1257,8 @@
     u_sent = low(halves(uk)[1], halves(uk_came)[1], halves(u_came)[1])
     u_held = added(halves(uk)[0], halves(uk_came)[0], halves(u_came)[0])
     u_came = ways.flip(u_sent, seconds)
-    d_held, d_sent = spread(d_held + d_came.astype(F32))
-    d_came = ways.flip(d_sent, depth - 3)
+    d_held, d_sent = quarter_out(d_held + d_came.astype(F32))
+    d_came = ways.flip_three(d_sent)
     bk_other, bs_other = project_other(here_t, after(g_b, a_send, u_sent, d_sent), ())
     bs_came, bk_came = swap_cores(bs_other), swap_cores(bk_other)
     if fast:
@@ -1266,39 +1272,34 @@
     small_came = swap_cores(small_other)
     bs_came, bk_came = after((bs_came, bk_came), small_other)
     b_keep, b_send = project_own(here_t, g_b, (), (small_own, small_came), bk_came, bs_came)
-    d_came, u_came, a_came = after((d_came, u_came, a_came), b_send)
+    u_came, a_came = after((u_came, a_came), b_send)
     b_came = ways.flip(b_send, lasts)
     a_sent = low(halves(a_keep)[1], halves(a_came)[1])
     a_held = added(halves(a_keep)[0], halves(a_came)[0])
     a_came = ways.flip(a_sent, seconds)
-    u_held, u_sent = spread(after(u_held, a_sent) + u_came.astype(F32))
-    u_came = ways.flip(u_sent, depth - 3)
-    d_held, d_sent = spread(after(d_held, a_sent) + d_came.astype(F32))
-    d_came = ways.flip(d_sent, depth - 4)
-    b_came = after(b_came, u_sent, d_sent)
+    u_held, u_sent = quarter_out(after(u_held, a_sent) + u_came.astype(F32))
+    u_came = ways.flip_three(u_sent)
+    b_came = after(b_came, *u_sent)
     b_sent = low(halves(b_keep)[1], halves(b_came)[1])
     b_held = added(halves(b_keep)[0], halves(b_came)[0])
     b_came = ways.flip(b_sent, seconds)
     g_here = token_back(
-        (after(g_a, b_send, a_sent, u_sent, b_sent), g_b), g_res_one, perm, weights, cols
-    )
-    a_came, b_came, u_came, d_came, emb = after((a_came, b_came, u_came, d_came, emb), g_here)
+        (after(g_a, b_send, a_sent, b_sent, *u_sent, *d_came), g_b), g_res_one, perm, weights, cols
+    )
+    a_came, b_came, u_came, emb = after((a_came, b_came, u_came, emb), g_here)
     held = jnp.concatenate([a_held + a_came.astype(F32), b_held + b_came.astype(F32)], axis=1)
-    for step in range(depth - 3, -1, -1):
-        held, sent = spread(held)
-        came = ways.flip(sent, step)
-        if step == depth - 3:
-            u_held, u_sent = spread(u_held + after(u_came, sent).astype(F32))
-            u_came = ways.flip(u_sent, depth - 4)
-        if step:
-            held = held + came.astype(F32)
-    d_held = d_held + after(d_came, u_sent).astype(F32)
+    held, sent = quarter_out(held)
+    came = ways.flip_three(sent)
+    d_came, u_came, u_held = after((d_came, u_came, u_held), *sent)
+    d_held, u_held = added(d_held, *d_came), added(u_held, *u_came)
     for step in range(depth - 5, -1, -1):
+        held, sent = spread(added(held, *came))
+        came = [ways.flip(sent, step)]
         d_held, sent = spread(d_held)
         d_held = d_held + ways.flip(sent, step).astype(F32)
-        u_held, sent = spread(u_held + u_came.astype(F32))
-        u_came = ways.flip(sent, step)
-    down_shard, up_shard = d_held, u_held + u_came.astype(F32)
+        u_held, sent = spread(u_held)
+        u_held = u_held + ways.flip(sent, step).astype(F32)
+    down_shard, up_shard = d_held, u_held
     a_wide, b_wide = split * LANES, (len(pairs) - split) * LANES
     if fast:
         qkv_shard, out_shard, emb_shard, gain_shard, bias_shard, up_bias_shard = finish(
@@ -1306,7 +1307,7 @@
         )
         out_shard, up_bias_shard = out_shard.T, up_bias_shard[0]
     else:
-        shard = held + came.astype(F32)
+        shard = added(held, *came)
         a_shard, b_shard = shard[:, : 3 * a_wide + cols], shard[:, 3 * a_wide + cols :]
         qkv_shard = jnp.stack(
             [

time: 223 us -> 215 us (0.964)
  waiting for transfers between devices: 56 us -> 44.8 us
  starting transfers between devices: 43.6 us -> 52.1 us
  local copies, waits for them, and re-layouts: 14.2 us -> 9.53 us
    ppermute x28 -> x34, waiting for transfers between devices: 51.5 us -> 40.9 us  [flip(): return lax.ppermute(value, ('dp', 'tensor'), pairs)]
    ppermute x28 -> x34, starting transfers between devices: 40.2 us -> 49 us  [flip(): return lax.ppermute(value, ('dp', 'tensor'), pairs)]
    add x6 -> x0, other arithmetic: 3.83 us -> none  [the longest x1 1.69 us: body(): u_held, u_sent = spread(after(u_held, a_sent) + u_came.astype(F32))]
    unnamed x76 -> x62, local copies, waits for them, and re-layouts: 8.82 us -> 5.46 us
    another operation x1 -> x3, other arithmetic: 0.04 us -> 3.12 us
    concatenate x4 -> x2, other arithmetic: 2.81 us -> 0.07 us  [the longest x1 0.05 us: join(): return jnp.concatenate(parts, axis=0)]
  transfers between devices with their start and end apart: 49 -> 55, of which waited for: 21 -> 19; matrix products, arithmetic and copies ran while one was open for 10% -> 9% of each run, Pallas kernels for 33% -> 35%
where the time goes in v3:
time: 215 us; the launch traced here: 214 us
  Pallas kernels  87.1 us (41%)
  starting transfers between devices  52.1 us (24%)
  waiting for transfers between devices  44.8 us (21%)
  other arithmetic  15.1 us (7%)
  local copies, waits for them, and re-layouts  9.53 us (4%)
  between operations  5.4 us (3%)
    pallas_call x20, Pallas kernels, call(): pl.pallas_call(body, out_shape=outs, grid=grid or (), in_specs=in_specs o...  87.1 us
    ppermute x34, starting transfers between devices, flip(): return lax.ppermute(value, ('dp', 'tensor'), pairs)  49 us
    ppermute x34, waiting for transfers between devices, flip(): return lax.ppermute(value, ('dp', 'tensor'), pairs)  40.9 us
    unnamed x62, local copies, waits for them, and re-layouts  5.46 us
  transfers between devices with their start and end apart: 55, of which 19 were waited for; matrix products, arithmetic and copies ran while one was open for 9% of the time, Pallas kernels for 35%

profile of v3, /device:TPU:0, one launch (start us, length us, event | category | flops | bytes accessed | tf_op | source)
XLA Modules:
  0.0 214.1 jit_solution(3675340648926198818)
XLA Ops:
  0.6 1.7 shard_map.222
  2.4 4.1 %collective-permute-start = (bf16[48,1664]{1,0:T(8,128)(2,1)}, bf16[48,1664]{1,0:T(8,128)(2,1)S(1)}, u32[]{:S(2)}, u32[]{:S(2)}) collective-permute-start(bf16[48,1664]{1,0:T(8,128)(2,1)} %shard_map.222), channel_id=1, source_target_pairs={{0,16},{1,17},{2,18},{3,19},{4,20},{5,21},{6,22},{7,23},{8,24},{9,... | collective-permute-start | bytes 479240 | tf_op jit(solution)/shard_map/ppermute | solution.py:697
  6.5 1.6 collective-permute-start.1
  18.9 1.6 collective-permute-start.3
  20.5 1.5 collective-permute-start.4
  22.4 4.9 %collective-permute-start.6 = (bf16[48,1536]{1,0:T(8,128)(2,1)S(1)}, bf16[48,1536]{1,0:T(8,128)(2,1)S(1)}, u32[]{:S(2)}, u32[]{:S(2)}) collective-permute-start(bf16[48,1536]{1,0:T(8,128)(2,1)S(1)} %copy-done.20), channel_id=1, source_target_pairs={{0,16},{1,17},{2,18},{3,19},{4,20},{5,21},{6,22},{7,23},{8,24},{9,... | collective-permute-start | bytes 442376 | tf_op jit(solution)/shard_map/ppermute | solution.py:697
  27.3 1.5 collective-permute-start.8
  29.9 5.7 %collective-permute-done.6 = bf16[48,1536]{1,0:T(8,128)(2,1)S(1)} collective-permute-done((bf16[48,1536]{1,0:T(8,128)(2,1)S(1)}, bf16[48,1536]{1,0:T(8,128)(2,1)S(1)}, u32[]{:S(2)}, u32[]{:S(2)}) %collective-permute-start.6) | collective-permute-done | bytes 147488 | tf_op jit(solution)/shard_map/ppermute | solution.py:697
  35.6 3.7 %collective-permute-done.7 = bf16[48,1536]{1,0:T(8,128)(2,1)S(1)} collective-permute-done((bf16[48,1536]{1,0:T(8,128)(2,1)S(1)}, bf16[48,1536]{1,0:T(8,128)(2,1)S(1)}, u32[]{:S(2)}, u32[]{:S(2)}) %collective-permute-start.7) | collective-permute-done | bytes 147488 | tf_op jit(solution)/shard_map/ppermute | solution.py:697
  40.2 1.6 collective-permute-start.10
  42.4 2.0 collective-permute-start.14
  45.4 1.9 collective-permute-start.16
  47.3 8.3 %collective-permute-done.10 = bf16[192,1536]{1,0:T(8,128)(2,1)S(1)} collective-permute-done((bf16[192,1536]{1,0:T(8,128)(2,1)S(1)}, bf16[192,1536]{1,0:T(8,128)(2,1)S(1)}, u32[]{:S(2)}, u32[]{:S(2)}) %collective-permute-start.10) | collective-permute-done | bytes 589856 | tf_op jit(solution)/shard_map/ppermute | solution.py:697
  56.2 1.5 collective-permute-done.16
  59.7 1.7 shard_map.223
  61.4 15.8 %shard_map.224 = (bf16[2,512,1152]{2,1,0:T(8,128)(2,1)S(1)}, f32[2,6,512]{2,1,0:T(8,128)S(1)}, bf16[2,512,384]{2,1,0:T(8,128)(2,1)S(1)}, f32[512,768]{1,0:T(8,12...) custom-call(bf16[512,768]{1,0:T(8,128)(2,1)S(1)} %maximum_select_fus, ...), custom_call_target="tpu_custom_call" | custom-call | flops 2415919104 | bytes 1048576 | tf_op jit(solution)/shard_map/pallas_call | solution.py:61
  77.3 3.0 %collective-permute-done.18.c_ref.d_ref.refs_6_.refs_7_ = bf16[384,1536]{1,0:T(8,128)(2,1)S(1)} collective-permute-done((bf16[384,1536]{1,0:T(8,128)(2,1)S(1)}, bf16[384,1536]{1,0:T(8,128)(2,1)S(1)}, u32[]{:S(2)}, u32[]{:S(2)}) %collective-permute-start.18) | collective-permute-done | bytes 1179680 | tf_op jit(solution)/shard_map/ppermute | solution.py:697
  82.2 5.1 %shard_map.225 = (bf16[512,1536]{1,0:T(8,128)(2,1)S(1)}, bf16[512,1536]{1,0:T(8,128)(2,1)S(1)}) custom-call(bf16[512,768]{1,0:T(8,128)(2,1)S(1)} %get-tuple-element.212.low_ref, bf16[384,1536]{1,0:T(8,128)(2,1)S(1)} %constant_dynamic-update-slice_fusion.4.a_ref.b_ref.refs_4_.refs_5_, ...), custom_call_target="tpu_custom_call" | custom-call | flops 1207959552 | bytes 1048576 | tf_op jit(solution)/shard_map/pallas_call | solution.py:61
  87.3 5.1 %shard_map.226 = (bf16[512,1536]{1,0:T(8,128)(2,1)S(1)}, bf16[512,1536]{1,0:T(8,128)(2,1)S(1)}) custom-call(bf16[512,768]{1,0:T(8,128)(2,1)S(1)} %get-tuple-element.212.low_ref, bf16[384,1536]{1,0:T(8,128)(2,1)S(1)} %collective-permute-done.21.a_ref.b_ref.refs_4_.refs_5_, bf16[384,1536]{1,0:T(8,128)(2,1)S(1)} %collective-permute-done.21.a_ref.b_ref.refs_4_.refs_5_, ...), custom_call_target="tpu_custom_call" | custom-call | flops 1207959552 | bytes 1048576 | tf_op jit(solution)/shard_map/pallas_call | solution.py:61
  92.4 4.2 %collective-permute-done.23.refs_1_.refs_2_.refs_3_ = bf16[384,1536]{1,0:T(8,128)(2,1)S(1)} collective-permute-done((bf16[384,1536]{1,0:T(8,128)(2,1)S(1)}, bf16[384,1536]{1,0:T(8,128)(2,1)S(1)}, u32[]{:S(2)}, u32[]{:S(2)}) %collective-permute-start.23) | collective-permute-done | bytes 1179680 | tf_op jit(solution)/shard_map/ppermute | solution.py:697
  96.6 2.8 %collective-permute-done.25.refs_3_.refs_2_ = bf16[384,1536]{1,0:T(8,128)(2,1)S(1)} collective-permute-done((bf16[384,1536]{1,0:T(8,128)(2,1)S(1)}, bf16[384,1536]{1,0:T(8,128)(2,1)S(1)}, u32[]{:S(2)}, u32[]{:S(2)}) %collective-permute-start.25) | collective-permute-done | bytes 1179680 | tf_op jit(solution)/shard_map/ppermute | solution.py:28
  99.5 8.4 %shard_map.227 = (f32[512,128]{1,0:T(8,128)S(1)}, bf16[512,768]{1,0:T(8,128)(2,1)S(1)}, bf16[768,512]{1,0:T(8,128)(2,1)S(1)}, f32[512,768]{1,0:T(8,128)S(1)}, f3...) custom-call(s32[1]{0:T(128)} %dynamic_slice.43.len_ref, bf16[512,1536]{1,0:T(8,128)(2,1)S(1)} %get-tuple-element.223.h0_ref.hid_ref, ...), custom_call_target="tpu_custom_call" | custom-call | flops 2415919104 | bytes 1048576 | tf_op jit(solution)/shard_map/pallas_call | solution.py:61
  107.9 2.0 shard_map.228
  110.5 2.0 shard_map.229
  114.3 8.6 %shard_map.230 = (bf16[384,1536]{1,0:T(8,128)(2,1)S(1)}, bf16[384,1536]{1,0:T(8,128)(2,1)S(1)}, f32[8,1536]{1,0:T(8,128)S(1)}, f32[512,768]{1,0:T(8,128)S(1)}) custom-call(bf16[512,768]{1,0:T(8,128)(2,1)S(1)} %get-tuple-element.233.g_ref, bf16[768,512]{1,0:T(8,128)(2,1)S(1)} %get-tuple-element.227.lowt_ref, ...), custom_call_target="tpu_custom_call" | custom-call | flops 3623878656 | bytes 1048576 | tf_op jit(solution)/shard_map/pallas_call | solution.py:61
  124.4 8.7 %shard_map.231 = (bf16[384,1536]{1,0:T(8,128)(2,1)S(1)}, bf16[384,1536]{1,0:T(8,128)(2,1)S(1)}, f32[16,1536]{1,0:T(8,128)S(1)}, f32[512,768]{1,0:T(8,128)S(1)}) custom-call(bf16[512,768]{1,0:T(8,128)(2,1)S(1)} %get-tuple-element.233.g_ref, bf16[768,512]{1,0:T(8,128)(2,1)S(1)} %get-tuple-element.227.lowt_ref, ...), custom_call_target="tpu_custom_call" | custom-call | flops 3623878656 | bytes 1048576 | tf_op jit(solution)/shard_map/pallas_call | solution.py:61
  134.9 2.4 %shard_map.232 = (f32[512,768]{1,0:T(8,128)S(1)}, bf16[768,512]{1,0:T(8,128)(2,1)S(1)}, bf16[2,512,384]{2,1,0:T(8,128)(2,1)S(1)}, f32[48,768]{1,0:T(8,128)S(1)}) custom-call(f32[512,768]{1,0:T(8,128)S(1)} %get-tuple-element.244.gf_ref, f32[512,768]{1,0:T(8,128)S(1)} %get-tuple-element.245.res_ref, f32[8,768]{1,0:T(8,128)S(1)} %get-tuple-element.202.vec_ref, ...), custom_call_target="tpu_custom_call" | custom-call | flops 603979776 | bytes 1048576 | tf_op jit(solution)/shard_map/pallas_call | solution.py:61
  138.5 6.8 %shard_map.233 = (bf16[2,512,768]{2,1,0:T(8,128)(2,1)S(1)}, f32[2,2,8,256]{3,2,1,0:T(8,128)S(1)}) custom-call(bf16[2,512,384]{2,1,0:T(8,128)(2,1)S(1)} %get-tuple-element.256.gatt_ref, bf16[2,512,384]{2,1,0:T(8,128)(2,1)S(1)} %get-tuple-element.249.att_ref.refs_1_, bf16[2,512,1152]{2,1,0:T(8,128)(2,1)S(1)} %get-tuple-element.250.qkv_ref, ...), custom_call_target="tpu_custom_call" | custom-call | flops 2684354560 | bytes 1048576 | tf_op jit(solution)/shard_map/pallas_call | solution.py:61
  148.0 3.7 %shard_map.235 = (bf16[2,512,384]{2,1,0:T(8,128)(2,1)S(1)}, f32[2,2,8,384]{3,2,1,0:T(8,128)S(1)}) custom-call(bf16[2,512,384]{2,1,0:T(8,128)(2,1)S(1)} %get-tuple-element.256.gatt_ref, bf16[2,512,384]{2,1,0:T(8,128)(2,1)S(1)} %get-tuple-element.249.att_ref.refs_1_, bf16[2,512,1152]{2,1,0:T(8,128)(2,1)S(1)} %get-tuple-element.250.qkv_ref, ...), custom_call_target="tpu_custom_call" | custom-call | flops 1342177280 | bytes 1048576 | tf_op jit(solution)/shard_map/pallas_call | solution.py:61
  151.8 2.1 %shard_map.236 = (bf16[384,1152]{1,0:T(8,128)(2,1)S(1)}, bf16[384,1152]{1,0:T(8,128)(2,1)}) custom-call(bf16[768,512]{1,0:T(8,128)(2,1)S(1)} %get-tuple-element.203.xt_ref, bf16[2,512,768]{2,1,0:T(8,128)(2,1)S(1)} %get-tuple-element.287.g_ref.a_ref, bf16[384,1152]{1,0:T(8,128)(2,1)S(1)} %collective-permute-done.33.kc_ref, ...), custom_call_target="tpu_custom_call" | custom-call | flops 905969664 | bytes 1048576 | tf_op jit(solution)/shard_map/pallas_call | solution.py:61
  155.1 2.2 %collective-permute-done.34 = bf16[192,1536]{1,0:T(8,128)(2,1)S(1)} collective-permute-done((bf16[192,1536]{1,0:T(8,128)(2,1)S(1)}, bf16[192,1536]{1,0:T(8,128)(2,1)S(1)}, u32[]{:S(2)}, u32[]{:S(2)}) %collective-permute-start.34) | collective-permute-done | bytes 589856 | tf_op jit(solution)/shard_map/ppermute | solution.py:697
  157.3 1.6 convert_add_fusion.1
  163.6 3.1 %shard_map.238 = (bf16[768,128]{1,0:T(8,128)(2,1)S(1)}, bf16[768,128]{1,0:T(8,128)(2,1)}) custom-call(s32[1]{0:T(128)} %bitcast.8.core_ref, bf16[2,128,768]{2,1,0:T(8,128)(2,1)S(1)} %add_convert_fusion.7.thin_ref, bf16[2,128,3072]{2,1,0:T(8,128)(2,1)S(1)} %add_convert_fusion.broad_ref, s32[1,768]{1,0:T(1,128)S(1)} %and_select_fusion.rel_ref, ...), custom_call_target="tpu_custom_call" | custom-call | bytes 1048576 | tf_op jit(solution)/shard_map/pallas_call | solution.py:61
  167.4 2.6 %collective-permute-start.47 = (bf16[48,1536]{1,0:T(8,128)(2,1)}, bf16[48,1536]{1,0:T(8,128)(2,1)S(1)}, u32[]{:S(2)}, u32[]{:S(2)}) collective-permute-start(bf16[48,1536]{1,0:T(8,128)(2,1)} %get-tuple-element.328), channel_id=1, source_target_pairs={{0,16},{1,17},{2,18},{3,19},{4,20},{5,21},{6,22},{7,23},{8,24},{9,... | collective-permute-start | bytes 442376 | tf_op jit(solution)/shard_map/ppermute | solution.py:697
  170.0 1.7 collective-permute-start.49
  173.8 1.8 shard_map.239
  175.7 1.5 collective-permute-start.42
  178.4 1.7 fusion.13
  180.2 1.8 collective-permute-start.44
  182.1 1.4 collective-permute-done.42
  184.2 2.6 %collective-permute-start.46 = (bf16[48,1536]{1,0:T(8,128)(2,1)S(1)}, bf16[48,1536]{1,0:T(8,128)(2,1)S(1)}, u32[]{:S(2)}, u32[]{:S(2)}) collective-permute-start(bf16[48,1536]{1,0:T(8,128)(2,1)S(1)} %get-tuple-element.323), channel_id=1, source_target_pairs={{0,24},{1,25},{2,26},{3,27},{4,28},{5,29},{6,30},{7,31},{8,16},{9,... | collective-permute-start | bytes 442376 | tf_op jit(solution)/shard_map/ppermute | solution.py:697
  188.9 4.7 %shard_map.240 = f32[512,768]{1,0:T(8,128)S(1)} custom-call(bf16[2,512,768]{2,1,0:T(8,128)(2,1)S(1)} %copy-done.2, bf16[2,512,384]{2,1,0:T(8,128)(2,1)S(1)} %copy-done.5, f32[512,768]{1,0:T(8,128)S(1)} %copy-done.9, bf16[768,768]{1,0:T(8,128)(2,1)S(1)} %copy-done.7, bf16[2,768,1536]{2,1,0:T(8,128)(2,1)S(1)} %bitcast.28), custom_call_target="tpu_custom_call" | custom-call | flops 2415919104 | bytes 1048576 | tf_op jit(solution)/shard_map/pallas_call | solution.py:61
  195.0 2.3 %collective-permute-done.43 = bf16[192,512]{1,0:T(8,128)(2,1)S(1)} collective-permute-done((bf16[192,512]{1,0:T(8,128)(2,1)S(1)}, bf16[192,512]{1,0:T(8,128)(2,1)S(1)}, u32[]{:S(2)}, u32[]{:S(2)}) %collective-permute-start.43) | collective-permute-done | bytes 196640 | tf_op jit(solution)/shard_map/ppermute | solution.py:697
  199.0 1.5 collective-permute-start.53
  200.5 2.6 %collective-permute-start.54 = (bf16[48,1664]{1,0:T(8,128)(2,1)S(1)}, bf16[48,1664]{1,0:T(8,128)(2,1)S(1)}, u32[]{:S(2)}, u32[]{:S(2)}) collective-permute-start(bf16[48,1664]{1,0:T(8,128)(2,1)S(1)} %get-tuple-element.320), channel_id=1, source_target_pairs={{0,24},{1,25},{2,26},{3,27},{4,28},{5,29},{6,30},{7,31},{8,16},{9,... | collective-permute-start | bytes 479240 | tf_op jit(solution)/shard_map/ppermute | solution.py:697
  203.2 1.7 fusion.5
  205.8 3.9 %collective-permute-done.52.refs_0_ = bf16[48,1664]{1,0:T(8,128)(2,1)S(1)} collective-permute-done((bf16[48,1664]{1,0:T(8,128)(2,1)S(1)}, bf16[48,1664]{1,0:T(8,128)(2,1)S(1)}, u32[]{:S(2)}, u32[]{:S(2)}) %collective-permute-start.52) | collective-permute-done | bytes 159776 | tf_op jit(solution)/shard_map/ppermute | solution.py:697
  209.7 2.3 %collective-permute-done.54.refs_2_ = bf16[48,1664]{1,0:T(8,128)(2,1)S(1)} collective-permute-done((bf16[48,1664]{1,0:T(8,128)(2,1)S(1)}, bf16[48,1664]{1,0:T(8,128)(2,1)S(1)}, u32[]{:S(2)}, u32[]{:S(2)}) %collective-permute-start.54) | collective-permute-done | bytes 159776 | tf_op jit(solution)/shard_map/ppermute | solution.py:697
  (203 shorter events, 43.5 us)
Async XLA Ops:
  2.4 15.7 %collective-permute-start = (bf16[48,1664]{1,0:T(8,128)(2,1)}, bf16[48,1664]{1,0:T(8,128)(2,1)S(1)}, u32[]{:S(2)}, u32[]{:S(2)}) collective-permute-start(bf16[48,1664]{1,0:T(8,128)(2,1)} %shard_map.222), channel_id=1, source_target_pairs={{0,16},{1,17},{2,18},{3,19},{4,20},{5,21},{6,22},{7,23},{8,24},{9,... | collective-permute-start | bytes 479240 | tf_op jit(solution)/shard_map/ppermute | solution.py:697
  6.5 11.6 %collective-permute-start.1 = (bf16[48,1664]{1,0:T(8,128)(2,1)}, bf16[48,1664]{1,0:T(8,128)(2,1)S(1)}, u32[]{:S(2)}, u32[]{:S(2)}) collective-permute-start(bf16[48,1664]{1,0:T(8,128)(2,1)} %shard_map.222), channel_id=1, source_target_pairs={{0,8},{1,9},{2,10},{3,11},{4,12},{5,13},{6,14},{7,15},{8,0},{9,1},... | collective-permute-start | bytes 479240 | tf_op jit(solution)/shard_map/ppermute | solution.py:697
  8.0 10.8 %collective-permute-start.2 = (bf16[48,1664]{1,0:T(8,128)(2,1)}, bf16[48,1664]{1,0:T(8,128)(2,1)S(1)}, u32[]{:S(2)}, u32[]{:S(2)}) collective-permute-start(bf16[48,1664]{1,0:T(8,128)(2,1)} %shard_map.222), channel_id=1, source_target_pairs={{0,24},{1,25},{2,26},{3,27},{4,28},{5,29},{6,30},{7,31},{8,16},{9,... | collective-permute-start | bytes 479240 | tf_op jit(solution)/shard_map/ppermute | solution.py:697
  18.9 20.4 %collective-permute-start.3 = (bf16[192,1664]{1,0:T(8,128)(2,1)S(1)}, bf16[192,1664]{1,0:T(8,128)(2,1)S(1)}, u32[]{:S(2)}, u32[]{:S(2)}) collective-permute-start(bf16[192,1664]{1,0:T(8,128)(2,1)S(1)} %pad_maximum_fusion.1.refs_0_), channel_id=1, source_target_pairs={{0,4},{1,3},{2,6},{3,1},{4,0},{5,7},{6,2},{7,5},{8,12},{9,11},{10,... | collective-permute-start | bytes 1916936 | tf_op jit(solution)/shard_map/ppermute | solution.py:697
  20.5 18.8 %collective-permute-start.4 = (bf16[192,1664]{1,0:T(8,128)(2,1)S(1)}, bf16[192,1664]{1,0:T(8,128)(2,1)S(1)}, u32[]{:S(2)}, u32[]{:S(2)}) collective-permute-start(bf16[192,1664]{1,0:T(8,128)(2,1)S(1)} %pad_maximum_fusion.1.refs_0_), channel_id=1, source_target_pairs={{0,2},{1,5},{2,0},{3,7},{4,6},{5,1},{6,4},{7,3},{8,10},{9,13},{10,... | collective-permute-start | bytes 1916936 | tf_op jit(solution)/shard_map/ppermute | solution.py:697
  22.0 5.4 %collective-permute-start.5 = (bf16[256,768]{1,0:T(8,128)(2,1)S(1)}, bf16[256,768]{1,0:T(8,128)(2,1)S(1)}, u32[]{:S(2)}, u32[]{:S(2)}) collective-permute-start(bf16[256,768]{1,0:T(8,128)(2,1)S(1)} %get-tuple-element.165), channel_id=1, source_target_pairs={{0,1},{1,0},{2,3},{3,2},{4,5},{5,4},{6,7},{7,6},{8,9},{9,8},{10,11... | collective-permute-start | bytes 1179656 | tf_op jit(solution)/shard_map/ppermute | solution.py:28
  22.4 13.1 %collective-permute-start.6 = (bf16[48,1536]{1,0:T(8,128)(2,1)S(1)}, bf16[48,1536]{1,0:T(8,128)(2,1)S(1)}, u32[]{:S(2)}, u32[]{:S(2)}) collective-permute-start(bf16[48,1536]{1,0:T(8,128)(2,1)S(1)} %copy-done.20), channel_id=1, source_target_pairs={{0,16},{1,17},{2,18},{3,19},{4,20},{5,21},{6,22},{7,23},{8,24},{9,... | collective-permute-start | bytes 442376 | tf_op jit(solution)/shard_map/ppermute | solution.py:697
  27.3 11.9 %collective-permute-start.7 = (bf16[48,1536]{1,0:T(8,128)(2,1)S(1)}, bf16[48,1536]{1,0:T(8,128)(2,1)S(1)}, u32[]{:S(2)}, u32[]{:S(2)}) collective-permute-start(bf16[48,1536]{1,0:T(8,128)(2,1)S(1)} %copy-done.20), channel_id=1, source_target_pairs={{0,8},{1,9},{2,10},{3,11},{4,12},{5,13},{6,14},{7,15},{8,0},{9,1},... | collective-permute-start | bytes 442376 | tf_op jit(solution)/shard_map/ppermute | solution.py:697
  27.3 11.9 %collective-permute-start.8 = (bf16[48,1536]{1,0:T(8,128)(2,1)S(1)}, bf16[48,1536]{1,0:T(8,128)(2,1)S(1)}, u32[]{:S(2)}, u32[]{:S(2)}) collective-permute-start(bf16[48,1536]{1,0:T(8,128)(2,1)S(1)} %copy-done.20), channel_id=1, source_target_pairs={{0,24},{1,25},{2,26},{3,27},{4,28},{5,29},{6,30},{7,31},{8,16},{9,... | collective-permute-start | bytes 442376 | tf_op jit(solution)/shard_map/ppermute | solution.py:697
  35.6 6.2 %collective-permute-start.11 = (bf16[192,1664]{1,0:T(8,128)(2,1)S(1)}, bf16[192,1664]{1,0:T(8,128)(2,1)S(1)}, u32[]{:S(2)}, u32[]{:S(2)}) collective-permute-start(bf16[192,1664]{1,0:T(8,128)(2,1)S(1)} %pad_maximum_fusion.1.refs_0_), channel_id=1, source_target_pairs={{0,1},{1,0},{2,3},{3,2},{4,5},{5,4},{6,7},{7,6},{8,9},{9,8},{10,11... | collective-permute-start | bytes 1916936 | tf_op jit(solution)/shard_map/ppermute | solution.py:28
  39.4 16.8 %collective-permute-start.9 = (bf16[192,1664]{1,0:T(8,128)(2,1)S(1)}, bf16[192,1664]{1,0:T(8,128)(2,1)S(1)}, u32[]{:S(2)}, u32[]{:S(2)}) collective-permute-start(bf16[192,1664]{1,0:T(8,128)(2,1)S(1)} %collective-permute-done.3.refs_1_), channel_id=1, source_target_pairs={{0,2},{1,5},{2,0},{3,7},{4,6},{5,1},{6,4},{7,3},{8,10},{9,13},{10,... | collective-permute-start | bytes 1916936 | tf_op jit(solution)/shard_map/ppermute | solution.py:697
  40.2 15.4 %collective-permute-start.10 = (bf16[192,1536]{1,0:T(8,128)(2,1)S(1)}, bf16[192,1536]{1,0:T(8,128)(2,1)S(1)}, u32[]{:S(2)}, u32[]{:S(2)}) collective-permute-start(bf16[192,1536]{1,0:T(8,128)(2,1)S(1)} %get-tuple-element.340), channel_id=1, source_target_pairs={{0,4},{1,3},{2,6},{3,1},{4,0},{5,7},{6,2},{7,5},{8,12},{9,11},{10,... | collective-permute-start | bytes 1769480 | tf_op jit(solution)/shard_map/ppermute | solution.py:697
  42.4 13.8 %collective-permute-start.14 = (bf16[48,1536]{1,0:T(8,128)(2,1)S(1)}, bf16[48,1536]{1,0:T(8,128)(2,1)S(1)}, u32[]{:S(2)}, u32[]{:S(2)}) collective-permute-start(bf16[48,1536]{1,0:T(8,128)(2,1)S(1)} %bitcast.29), channel_id=1, source_target_pairs={{0,16},{1,17},{2,18},{3,19},{4,20},{5,21},{6,22},{7,23},{8,24},{9,... | collective-permute-start | bytes 442376 | tf_op jit(solution)/shard_map/ppermute | solution.py:697
  44.3 11.9 %collective-permute-start.15 = (bf16[48,1536]{1,0:T(8,128)(2,1)S(1)}, bf16[48,1536]{1,0:T(8,128)(2,1)S(1)}, u32[]{:S(2)}, u32[]{:S(2)}) collective-permute-start(bf16[48,1536]{1,0:T(8,128)(2,1)S(1)} %bitcast.30), channel_id=1, source_target_pairs={{0,8},{1,9},{2,10},{3,11},{4,12},{5,13},{6,14},{7,15},{8,0},{9,1},... | collective-permute-start | bytes 442376 | tf_op jit(solution)/shard_map/ppermute | solution.py:697
  45.4 12.2 %collective-permute-start.16 = (bf16[48,1536]{1,0:T(8,128)(2,1)S(1)}, bf16[48,1536]{1,0:T(8,128)(2,1)S(1)}, u32[]{:S(2)}, u32[]{:S(2)}) collective-permute-start(bf16[48,1536]{1,0:T(8,128)(2,1)S(1)} %bitcast.31), channel_id=1, source_target_pairs={{0,24},{1,25},{2,26},{3,27},{4,28},{5,29},{6,30},{7,31},{8,16},{9,... | collective-permute-start | bytes 442376 | tf_op jit(solution)/shard_map/ppermute | solution.py:697
  57.7 22.6 %collective-permute-start.18 = (bf16[384,1536]{1,0:T(8,128)(2,1)S(1)}, bf16[384,1536]{1,0:T(8,128)(2,1)S(1)}, u32[]{:S(2)}, u32[]{:S(2)}) collective-permute-start(bf16[384,1536]{1,0:T(8,128)(2,1)S(1)} %constant_dynamic-update-slice_fusion.4.a_ref.b_ref.refs_4_.refs_5_), channel_id=1, source_target_pairs={{0,2},{1,5},{2,0},{3,7},{4,6},{5,1},{6,4},{7,3},{8,10},{9,13},{10,... | collective-permute-start | bytes 3538952 | tf_op jit(solution)/shard_map/ppermute | solution.py:697
  59.0 18.2 %collective-permute-start.19 = (bf16[192,1536]{1,0:T(8,128)(2,1)S(1)}, bf16[192,1536]{1,0:T(8,128)(2,1)S(1)}, u32[]{:S(2)}, u32[]{:S(2)}) collective-permute-start(bf16[192,1536]{1,0:T(8,128)(2,1)S(1)} %get-tuple-element.332), channel_id=1, source_target_pairs={{0,4},{1,3},{2,6},{3,1},{4,0},{5,7},{6,2},{7,5},{8,12},{9,11},{10,... | collective-permute-start | bytes 1769480 | tf_op jit(solution)/shard_map/ppermute | solution.py:697
  59.7 27.7 %collective-permute-start.21 = (bf16[384,1536]{1,0:T(8,128)(2,1)S(1)}, bf16[384,1536]{1,0:T(8,128)(2,1)S(1)}, u32[]{:S(2)}, u32[]{:S(2)}) collective-permute-start(bf16[384,1536]{1,0:T(8,128)(2,1)S(1)} %constant_dynamic-update-slice_fusion.4.a_ref.b_ref.refs_4_.refs_5_), channel_id=1, source_target_pairs={{0,1},{1,0},{2,3},{3,2},{4,5},{5,4},{6,7},{7,6},{8,9},{9,8},{10,11... | collective-permute-start | bytes 3538952 | tf_op jit(solution)/shard_map/ppermute | solution.py:28
  80.3 7.0 %collective-permute-start.22 = (bf16[384,1536]{1,0:T(8,128)(2,1)S(1)}, bf16[384,1536]{1,0:T(8,128)(2,1)S(1)}, u32[]{:S(2)}, u32[]{:S(2)}) collective-permute-start(bf16[384,1536]{1,0:T(8,128)(2,1)S(1)} %collective-permute-done.18.c_ref.d_ref.refs_6_.refs_7_), channel_id=1, source_target_pairs={{0,1},{1,0},{2,3},{3,2},{4,5},{5,4},{6,7},{7,6},{8,9},{9,8},{10,11... | collective-permute-start | bytes 3538952 | tf_op jit(solution)/shard_map/ppermute | solution.py:28
  80.3 16.3 %collective-permute-start.23 = (bf16[384,1536]{1,0:T(8,128)(2,1)S(1)}, bf16[384,1536]{1,0:T(8,128)(2,1)S(1)}, u32[]{:S(2)}, u32[]{:S(2)}) collective-permute-start(bf16[384,1536]{1,0:T(8,128)(2,1)S(1)} %constant_dynamic-update-slice_fusion.13.refs_0_.refs_1_), channel_id=1, source_target_pairs={{0,2},{1,5},{2,0},{3,7},{4,6},{5,1},{6,4},{7,3},{8,10},{9,13},{10,... | collective-permute-start | bytes 3538952 | tf_op jit(solution)/shard_map/ppermute | solution.py:697
  81.5 15.1 %collective-permute-start.24 = (bf16[384,1536]{1,0:T(8,128)(2,1)S(1)}, bf16[384,1536]{1,0:T(8,128)(2,1)S(1)}, u32[]{:S(2)}, u32[]{:S(2)}) collective-permute-start(bf16[384,1536]{1,0:T(8,128)(2,1)S(1)} %constant_dynamic-update-slice_fusion.13.refs_0_.refs_1_), channel_id=1, source_target_pairs={{0,1},{1,0},{2,3},{3,2},{4,5},{5,4},{6,7},{7,6},{8,9},{9,8},{10,11... | collective-permute-start | bytes 3538952 | tf_op jit(solution)/shard_map/ppermute | solution.py:28
  81.9 5.4 %collective-permute-start.20 = (f32[256,128]{1,0:T(8,128)S(1)}, f32[256,128]{1,0:T(8,128)S(1)}, u32[]{:S(2)}, u32[]{:S(2)}) collective-permute-start(f32[256,128]{1,0:T(8,128)S(1)} %get-tuple-element.210), channel_id=1, source_target_pairs={{0,1},{1,0},{2,3},{3,2},{4,5},{5,4},{6,7},{7,6},{8,9},{9,8},{10,11... | collective-permute-start | bytes 393224 | tf_op jit(solution)/shard_map/ppermute | solution.py:28
  110.1 13.4 %collective-permute-start.28 = (bf16[384,1536]{1,0:T(8,128)(2,1)S(1)}, bf16[384,1536]{1,0:T(8,128)(2,1)S(1)}, u32[]{:S(2)}, u32[]{:S(2)}) collective-permute-start(bf16[384,1536]{1,0:T(8,128)(2,1)S(1)} %get-tuple-element.231), channel_id=1, source_target_pairs={{0,1},{1,0},{2,3},{3,2},{4,5},{5,4},{6,7},{7,6},{8,9},{9,8},{10,11... | collective-permute-start | bytes 3538952 | tf_op jit(solution)/shard_map/ppermute | solution.py:28
  113.1 10.4 %collective-permute-start.27 = (bf16[192,1536]{1,0:T(8,128)(2,1)S(1)}, bf16[192,1536]{1,0:T(8,128)(2,1)S(1)}, u32[]{:S(2)}, u32[]{:S(2)}) collective-permute-start(bf16[192,1536]{1,0:T(8,128)(2,1)S(1)} %get-tuple-element.317), channel_id=1, source_target_pairs={{0,2},{1,5},{2,0},{3,7},{4,6},{5,1},{6,4},{7,3},{8,10},{9,13},{10,... | collective-permute-start | bytes 1769480 | tf_op jit(solution)/shard_map/ppermute | solution.py:697
  122.9 10.4 %collective-permute-start.30 = (bf16[384,1536]{1,0:T(8,128)(2,1)S(1)}, bf16[384,1536]{1,0:T(8,128)(2,1)S(1)}, u32[]{:S(2)}, u32[]{:S(2)}) collective-permute-start(bf16[384,1536]{1,0:T(8,128)(2,1)S(1)} %get-tuple-element.230), channel_id=1, source_target_pairs={{0,1},{1,0},{2,3},{3,2},{4,5},{5,4},{6,7},{7,6},{8,9},{9,8},{10,11... | collective-permute-start | bytes 3538952 | tf_op jit(solution)/shard_map/ppermute | solution.py:28
  123.0 10.4 %collective-permute-start.31 = (bf16[384,1536]{1,0:T(8,128)(2,1)S(1)}, bf16[384,1536]{1,0:T(8,128)(2,1)S(1)}, u32[]{:S(2)}, u32[]{:S(2)}) collective-permute-start(bf16[384,1536]{1,0:T(8,128)(2,1)S(1)} %get-tuple-element.240), channel_id=1, source_target_pairs={{0,1},{1,0},{2,3},{3,2},{4,5},{5,4},{6,7},{7,6},{8,9},{9,8},{10,11... | collective-permute-start | bytes 3538952 | tf_op jit(solution)/shard_map/ppermute | solution.py:28
  123.5 9.9 %collective-permute-start.29 = (bf16[192,1536]{1,0:T(8,128)(2,1)S(1)}, bf16[192,1536]{1,0:T(8,128)(2,1)S(1)}, u32[]{:S(2)}, u32[]{:S(2)}) collective-permute-start(bf16[192,1536]{1,0:T(8,128)(2,1)S(1)} %get-tuple-element.239), channel_id=1, source_target_pairs={{0,2},{1,5},{2,0},{3,7},{4,6},{5,1},{6,4},{7,3},{8,10},{9,13},{10,... | collective-permute-start | bytes 1769480 | tf_op jit(solution)/shard_map/ppermute | solution.py:697
  133.7 23.6 %collective-permute-start.35 = (bf16[384,1536]{1,0:T(8,128)(2,1)S(1)}, bf16[384,1536]{1,0:T(8,128)(2,1)S(1)}, u32[]{:S(2)}, u32[]{:S(2)}) collective-permute-start(bf16[384,1536]{1,0:T(8,128)(2,1)S(1)} %add_convert_fusion.1), channel_id=1, source_target_pairs={{0,2},{1,5},{2,0},{3,7},{4,6},{5,1},{6,4},{7,3},{8,10},{9,13},{10,... | collective-permute-start | bytes 3538952 | tf_op jit(solution)/shard_map/ppermute | solution.py:697
  146.5 5.3 %collective-permute-start.32 = (bf16[384,1152]{1,0:T(8,128)(2,1)S(1)}, bf16[384,1152]{1,0:T(8,128)(2,1)S(1)}, u32[]{:S(2)}, u32[]{:S(2)}) collective-permute-start(bf16[384,1152]{1,0:T(8,128)(2,1)S(1)} %get-tuple-element.254), channel_id=1, source_target_pairs={{0,1},{1,0},{2,3},{3,2},{4,5},{5,4},{6,7},{7,6},{8,9},{9,8},{10,11... | collective-permute-start | bytes 2654216 | tf_op jit(solution)/shard_map/ppermute | solution.py:28
  146.6 5.2 %collective-permute-start.33 = (bf16[384,1152]{1,0:T(8,128)(2,1)S(1)}, bf16[384,1152]{1,0:T(8,128)(2,1)S(1)}, u32[]{:S(2)}, u32[]{:S(2)}) collective-permute-start(bf16[384,1152]{1,0:T(8,128)(2,1)S(1)} %get-tuple-element.255), channel_id=1, source_target_pairs={{0,1},{1,0},{2,3},{3,2},{4,5},{5,4},{6,7},{7,6},{8,9},{9,8},{10,11... | collective-permute-start | bytes 2654216 | tf_op jit(solution)/shard_map/ppermute | solution.py:28
  147.1 10.2 %collective-permute-start.34 = (bf16[192,1536]{1,0:T(8,128)(2,1)S(1)}, bf16[192,1536]{1,0:T(8,128)(2,1)S(1)}, u32[]{:S(2)}, u32[]{:S(2)}) collective-permute-start(bf16[192,1536]{1,0:T(8,128)(2,1)S(1)} %add_convert_fusion.3), channel_id=1, source_target_pairs={{0,4},{1,3},{2,6},{3,1},{4,0},{5,7},{6,2},{7,5},{8,12},{9,11},{10,... | collective-permute-start | bytes 1769480 | tf_op jit(solution)/shard_map/ppermute | solution.py:697
  154.0 23.2 %collective-permute-start.37 = (bf16[384,1152]{1,0:T(8,128)(2,1)}, bf16[384,1152]{1,0:T(8,128)(2,1)}, u32[]{:S(2)}, u32[]{:S(2)}) collective-permute-start(bf16[384,1152]{1,0:T(8,128)(2,1)} %get-tuple-element.264), channel_id=1, source_target_pairs={{0,2},{1,5},{2,0},{3,7},{4,6},{5,1},{6,4},{7,3},{8,10},{9,13},{10,... | collective-permute-start | bytes 2654216 | tf_op jit(solution)/shard_map/ppermute | solution.py:697
  158.9 16.7 %collective-permute-start.36 = (bf16[192,1536]{1,0:T(8,128)(2,1)}, bf16[192,1536]{1,0:T(8,128)(2,1)}, u32[]{:S(2)}, u32[]{:S(2)}) collective-permute-start(bf16[192,1536]{1,0:T(8,128)(2,1)} %get-tuple-element.315), channel_id=1, source_target_pairs={{0,4},{1,3},{2,6},{3,1},{4,0},{5,7},{6,2},{7,5},{8,12},{9,11},{10,... | collective-permute-start | bytes 1769480 | tf_op jit(solution)/shard_map/ppermute | solution.py:697
  163.1 4.3 %collective-permute-start.38 = (bf16[384,384]{1,0:T(8,128)(2,1)}, bf16[384,384]{1,0:T(8,128)(2,1)}, u32[]{:S(2)}, u32[]{:S(2)}) collective-permute-start(bf16[384,384]{1,0:T(8,128)(2,1)} %get-tuple-element.269), channel_id=1, source_target_pairs={{0,1},{1,0},{2,3},{3,2},{4,5},{5,4},{6,7},{7,6},{8,9},{9,8},{10,11... | collective-permute-start | bytes 884744 | tf_op jit(solution)/shard_map/ppermute | solution.py:28
  163.1 6.9 %collective-permute-start.39 = (bf16[384,384]{1,0:T(8,128)(2,1)}, bf16[384,384]{1,0:T(8,128)(2,1)}, u32[]{:S(2)}, u32[]{:S(2)}) collective-permute-start(bf16[384,384]{1,0:T(8,128)(2,1)} %get-tuple-element.270), channel_id=1, source_target_pairs={{0,1},{1,0},{2,3},{3,2},{4,5},{5,4},{6,7},{7,6},{8,9},{9,8},{10,11... | collective-permute-start | bytes 884744 | tf_op jit(solution)/shard_map/ppermute | solution.py:28
  167.4 16.8 %collective-permute-start.47 = (bf16[48,1536]{1,0:T(8,128)(2,1)}, bf16[48,1536]{1,0:T(8,128)(2,1)S(1)}, u32[]{:S(2)}, u32[]{:S(2)}) collective-permute-start(bf16[48,1536]{1,0:T(8,128)(2,1)} %get-tuple-element.328), channel_id=1, source_target_pairs={{0,16},{1,17},{2,18},{3,19},{4,20},{5,21},{6,22},{7,23},{8,24},{9,... | collective-permute-start | bytes 442376 | tf_op jit(solution)/shard_map/ppermute | solution.py:697
  170.0 16.8 %collective-permute-start.48 = (bf16[48,1536]{1,0:T(8,128)(2,1)}, bf16[48,1536]{1,0:T(8,128)(2,1)S(1)}, u32[]{:S(2)}, u32[]{:S(2)}) collective-permute-start(bf16[48,1536]{1,0:T(8,128)(2,1)} %get-tuple-element.327), channel_id=1, source_target_pairs={{0,8},{1,9},{2,10},{3,11},{4,12},{5,13},{6,14},{7,15},{8,0},{9,1},... | collective-permute-start | bytes 442376 | tf_op jit(solution)/shard_map/ppermute | solution.py:697
  170.0 18.0 %collective-permute-start.49 = (bf16[48,1536]{1,0:T(8,128)(2,1)}, bf16[48,1536]{1,0:T(8,128)(2,1)S(1)}, u32[]{:S(2)}, u32[]{:S(2)}) collective-permute-start(bf16[48,1536]{1,0:T(8,128)(2,1)} %get-tuple-element.326), channel_id=1, source_target_pairs={{0,24},{1,25},{2,26},{3,27},{4,28},{5,29},{6,30},{7,31},{8,16},{9,... | collective-permute-start | bytes 442376 | tf_op jit(solution)/shard_map/ppermute | solution.py:697
  175.7 7.8 %collective-permute-start.42 = (bf16[384,512]{1,0:T(8,128)(2,1)S(1)}, bf16[384,512]{1,0:T(8,128)(2,1)S(1)}, u32[]{:S(2)}, u32[]{:S(2)}) collective-permute-start(bf16[384,512]{1,0:T(8,128)(2,1)S(1)} %get-tuple-element.280), channel_id=1, source_target_pairs={{0,2},{1,5},{2,0},{3,7},{4,6},{5,1},{6,4},{7,3},{8,10},{9,13},{10,... | collective-permute-start | bytes 1179656 | tf_op jit(solution)/shard_map/ppermute | solution.py:697
  180.2 13.9 %collective-permute-start.44 = (bf16[48,1536]{1,0:T(8,128)(2,1)S(1)}, bf16[48,1536]{1,0:T(8,128)(2,1)S(1)}, u32[]{:S(2)}, u32[]{:S(2)}) collective-permute-start(bf16[48,1536]{1,0:T(8,128)(2,1)S(1)} %get-tuple-element.325), channel_id=1, source_target_pairs={{0,16},{1,17},{2,18},{3,19},{4,20},{5,21},{6,22},{7,23},{8,24},{9,... | collective-permute-start | bytes 442376 | tf_op jit(solution)/shard_map/ppermute | solution.py:697
  183.5 11.5 %collective-permute-start.45 = (bf16[48,1536]{1,0:T(8,128)(2,1)S(1)}, bf16[48,1536]{1,0:T(8,128)(2,1)S(1)}, u32[]{:S(2)}, u32[]{:S(2)}) collective-permute-start(bf16[48,1536]{1,0:T(8,128)(2,1)S(1)} %get-tuple-element.324), channel_id=1, source_target_pairs={{0,8},{1,9},{2,10},{3,11},{4,12},{5,13},{6,14},{7,15},{8,0},{9,1},... | collective-permute-start | bytes 442376 | tf_op jit(solution)/shard_map/ppermute | solution.py:697
  184.2 10.8 %collective-permute-start.46 = (bf16[48,1536]{1,0:T(8,128)(2,1)S(1)}, bf16[48,1536]{1,0:T(8,128)(2,1)S(1)}, u32[]{:S(2)}, u32[]{:S(2)}) collective-permute-start(bf16[48,1536]{1,0:T(8,128)(2,1)S(1)} %get-tuple-element.323), channel_id=1, source_target_pairs={{0,24},{1,25},{2,26},{3,27},{4,28},{5,29},{6,30},{7,31},{8,16},{9,... | collective-permute-start | bytes 442376 | tf_op jit(solution)/shard_map/ppermute | solution.py:697
  186.8 10.4 %collective-permute-start.41 = (bf16[192,1152]{1,0:T(8,128)(2,1)S(1)}, bf16[192,1152]{1,0:T(8,128)(2,1)S(1)}, u32[]{:S(2)}, u32[]{:S(2)}) collective-permute-start(bf16[192,1152]{1,0:T(8,128)(2,1)S(1)} %add_convert_fusion.6), channel_id=1, source_target_pairs={{0,4},{1,3},{2,6},{3,1},{4,0},{5,7},{6,2},{7,5},{8,12},{9,11},{10,... | collective-permute-start | bytes 1327112 | tf_op jit(solution)/shard_map/ppermute | solution.py:697
  188.1 9.2 %collective-permute-start.43 = (bf16[192,512]{1,0:T(8,128)(2,1)S(1)}, bf16[192,512]{1,0:T(8,128)(2,1)S(1)}, u32[]{:S(2)}, u32[]{:S(2)}) collective-permute-start(bf16[192,512]{1,0:T(8,128)(2,1)S(1)} %add_convert_fusion.8), channel_id=1, source_target_pairs={{0,4},{1,3},{2,6},{3,1},{4,0},{5,7},{6,2},{7,5},{8,12},{9,11},{10,... | collective-permute-start | bytes 589832 | tf_op jit(solution)/shard_map/ppermute | solution.py:697
  194.2 18.7 %collective-permute-start.51 = (f32[256,768]{1,0:T(8,128)S(1)}, f32[256,768]{1,0:T(8,128)S(1)}, u32[]{:S(2)}, u32[]{:S(2)}) collective-permute-start(f32[256,768]{1,0:T(8,128)S(1)} %constant_dynamic-slice_fusion.1), channel_id=1, source_target_pairs={{0,1},{1,0},{2,3},{3,2},{4,5},{5,4},{6,7},{7,6},{8,9},{9,8},{10,11... | collective-permute-start | bytes 2359304 | tf_op jit(solution)/shard_map/ppermute | solution.py:28
  198.6 11.1 %collective-permute-start.52 = (bf16[48,1664]{1,0:T(8,128)(2,1)S(1)}, bf16[48,1664]{1,0:T(8,128)(2,1)S(1)}, u32[]{:S(2)}, u32[]{:S(2)}) collective-permute-start(bf16[48,1664]{1,0:T(8,128)(2,1)S(1)} %get-tuple-element.322), channel_id=1, source_target_pairs={{0,16},{1,17},{2,18},{3,19},{4,20},{5,21},{6,22},{7,23},{8,24},{9,... | collective-permute-start | bytes 479240 | tf_op jit(solution)/shard_map/ppermute | solution.py:697
  199.0 10.7 %collective-permute-start.53 = (bf16[48,1664]{1,0:T(8,128)(2,1)S(1)}, bf16[48,1664]{1,0:T(8,128)(2,1)S(1)}, u32[]{:S(2)}, u32[]{:S(2)}) collective-permute-start(bf16[48,1664]{1,0:T(8,128)(2,1)S(1)} %get-tuple-element.321), channel_id=1, source_target_pairs={{0,8},{1,9},{2,10},{3,11},{4,12},{5,13},{6,14},{7,15},{8,0},{9,1},... | collective-permute-start | bytes 479240 | tf_op jit(solution)/shard_map/ppermute | solution.py:697
  200.5 11.5 %collective-permute-start.54 = (bf16[48,1664]{1,0:T(8,128)(2,1)S(1)}, bf16[48,1664]{1,0:T(8,128)(2,1)S(1)}, u32[]{:S(2)}, u32[]{:S(2)}) collective-permute-start(bf16[48,1664]{1,0:T(8,128)(2,1)S(1)} %get-tuple-element.320), channel_id=1, source_target_pairs={{0,24},{1,25},{2,26},{3,27},{4,28},{5,29},{6,30},{7,31},{8,16},{9,... | collective-permute-start | bytes 479240 | tf_op jit(solution)/shard_map/ppermute | solution.py:697
  (34 other events, 334.3 us)

commit v4 on v3

--- a/solution.py
+++ b/solution.py
@@ -13,7 +13,7 @@
 STRIP = 128
 F32 = jnp.float32
 BF16 = jnp.bfloat16
-VMEM_LIMIT = 18 * 1024 * 1024
+VMEM_LIMIT = 15 * 1024 * 1024
 
 
 def nn(left, right):
@@ -399,60 +399,57 @@
 
 def up_grad(g_low, low_t, slope, down, up, start, swapped, biases):
     tokens, width = g_low.shape
-    pieces, at = zip(*down, *up)
     hidden = slope.shape[1]
     block = column_block(hidden)
-
-    def kernel(g_ref, lowt_ref, slope_ref, start_ref, *refs):
-        wd_ref, wu_ref = refs[-2:]
-        join_rows(refs[:4], wd_ref, swapped)
-        join_rows(refs[4:8], wu_ref, swapped)
-        more, refs = refs[8 : 8 + len(biases)], refs[8 + len(biases) :]
-        keep_ref, send_ref, bias_ref, first_ref, gh_ref, gin_ref = refs[:-2]
-        def matmul(span):
-            gh_ref[:, span] = nn(g_ref[...], wd_ref[:, span])
-
-        columns_of(block, matmul)
+    quarter = width // 4
+    count = 8 * (1 + len(biases))
+
+    def kernel(g_ref, lowt_ref, slope_ref, start_ref, db_ref, dm_ref, ub_ref, um_ref, *refs):
+        more, refs = refs[: len(biases)], refs[len(biases) :]
+        keep_ref, send_ref, bias_ref, first_ref, gh_ref, gin_ref, wd_ref, wu_ref = refs
+        first_ref[...] = start_ref[...]
         bias_ref[...] = jnp.zeros_like(bias_ref)
         for ref in more:
             bias_ref[8:16, :] = ref[...]
 
-        def act(rows):
-            grad = (gh_ref[rows, :] * slope_ref[rows, :].astype(F32)).astype(BF16)
-            gin_ref[rows, :] = grad
-            wide = grad.astype(F32)
-            bias_ref[0:8, :] += jnp.sum(wide.reshape(STRIP // 8, 8, wide.shape[1]), axis=0)
-
-        strips(tokens, STRIP, act)
-        split_rows(nn(lowt_ref[...], gin_ref[...]).astype(BF16), keep_ref, send_ref, swapped)
-        @pl.when(pl.program_id(0) == 0)
-        def _():
-            first_ref[...] = start_ref[...]
-
-        def add(span):
-            first_ref[:, span] += nt(gin_ref[...], wu_ref[span, :])
-
-        columns_of(width, add)
-
-    row = pl.BlockSpec((tokens, width), lambda i: (0, 0))
-    turned = pl.BlockSpec((width, tokens), lambda i: (0, 0))
-    act = pl.BlockSpec((tokens, block), lambda i: (0, i))
-    piece = pl.BlockSpec((width // 2, block), lambda i: (0, i))
-    parts = [pl.BlockSpec((width // 4, block), lambda i, row=row: (row, i)) for row in at]
-    thin = pl.BlockSpec((8, block), lambda i: (0, i))
+        def chunk(i, carry):
+            here = pl.ds(pl.multiple_of(i * block, block), block)
+            for target, both_ref, more_ref in ((wd_ref, db_ref, dm_ref), (wu_ref, ub_ref, um_ref)):
+                for place in range(4):
+                    source = OTHER[place] if swapped else place
+                    ref = (both_ref, more_ref)[source // 2]
+                    rows = slice((source % 2) * quarter, (source % 2 + 1) * quarter)
+                    target[place * quarter : (place + 1) * quarter, :] = ref[rows, here]
+
+            def matmul(span):
+                gh_ref[:, span] = nn(g_ref[...], wd_ref[:, span])
+
+            columns_of(block, matmul)
+
+            def act(rows):
+                grad = (gh_ref[rows, :] * slope_ref[rows, here].astype(F32)).astype(BF16)
+                gin_ref[rows, :] = grad
+                wide = grad.astype(F32)
+                total = jnp.sum(wide.reshape(STRIP // 8, 8, wide.shape[1]), axis=0)
+                bias_ref[0:8, here] += total
+
+            strips(tokens, STRIP, act)
+            made = nn(lowt_ref[...], gin_ref[...]).astype(BF16)
+            split_rows(made, keep_ref.at[:, here], send_ref.at[:, here], swapped)
+
+            def add(span):
+                first_ref[:, span] += nt(gin_ref[...], wu_ref[span, :])
+
+            columns_of(width, add)
+            return carry
+
+        lax.fori_loop(0, hidden // block, chunk, 0)
+
     out = shaped((width // 2, hidden), BF16)
     return call(
         kernel,
-        (out, out, shaped((8 * (1 + len(biases)), hidden), F32), shaped((tokens, width), F32)),
-        (g_low, low_t, slope, start, *pieces, *biases),
-        grid=(hidden // block,),
-        in_specs=[row, turned, act, row] + parts + [thin] * len(biases),
-        out_specs=(
-            piece,
-            piece,
-            pl.BlockSpec((8 * (1 + len(biases)), block), lambda i: (0, i)),
-            row,
-        ),
+        (out, out, shaped((count, hidden), F32), shaped((tokens, width), F32)),
+        (g_low, low_t, slope, start, *down, *up, *biases),
         scratch=[
             pltpu.VMEM((tokens, block), F32),
             pltpu.VMEM((tokens, block), BF16),
@@ -1167,20 +1164,20 @@
     def quarters(both, more):
         return ((both, 0), (both, 1), (more, 0), (more, 1))
 
-    two_own = quarters(two_both, two_more)
+    two_own = (two_both, two_more)
     hid_own, slope_own = up_forward(
-        after(first_low, three_both, two_more), two_own, side_bias[0], False
-    )
-    two_other = quarters(*after(two_other, hid_own))
+        after(first_low, three_both, two_more), quarters(*two_own), side_bias[0], False
+    )
+    two_other = after(two_other, hid_own)
     three_both_other = swap_cores(three_both)
     cot_mine = lax.dynamic_index_in_dim(cotangent, core, 0, keepdims=False)
     cot_other = lax.dynamic_index_in_dim(cotangent, 1 - core, 0, keepdims=False)
     cot = in_order(cot_mine, after(swap_cores(after(cot_other, first_low)), hid_own))
-    hid_other, slope_other = up_forward(after(first_low, cot), two_other, side_bias[1], True)
+    hid_other, slope_other = up_forward(after(first_low, cot), quarters(*two_other), side_bias[1], True)
     three_more, three_both_other = after((three_more, three_both_other), hid_other)
     three_more_other = swap_cores(three_more)
-    three_own = quarters(three_both, three_more)
-    three_other = quarters(three_both_other, three_more_other)
+    three_own = (three_both, three_more)
+    three_other = (three_both_other, three_more_other)
     emb, g_ffn, g_ffn_t, g_res_two, proj_grad, sums_two = down_both(
         seq_len[None],
         (hid_own, hid_other),
@@ -1252,18 +1249,19 @@
     )
     as_came, ak_came = after((as_came, ak_came), g_b)
     a_keep, a_send = project_own(here_t, g_a, beside, (), ak_came, as_came)
-    d_came, u_came = after((d_came, u_came), a_send)
+    u_came = after(u_came, a_send)
     a_came = ways.flip(a_send, lasts)
     u_sent = low(halves(uk)[1], halves(uk_came)[1], halves(u_came)[1])
     u_held = added(halves(uk)[0], halves(uk_came)[0], halves(u_came)[0])
     u_came = ways.flip(u_sent, seconds)
+    bk_other, bs_other = project_other(here_t, after(g_b, a_send, u_sent), ())
+    bs_came, bk_came = swap_cores(bs_other), swap_cores(bk_other)
+    d_came = after(d_came, bs_other)
     d_held, d_sent = quarter_out(d_held + d_came.astype(F32))
     d_came = ways.flip_three(d_sent)
-    bk_other, bs_other = project_other(here_t, after(g_b, a_send, u_sent, d_sent), ())
-    bs_came, bk_came = swap_cores(bs_other), swap_cores(bk_other)
     if fast:
         small_own, small_other = pack_grads(
-            *tables, after(sums, bs_other), up_bias, head_sums, proj_grad
+            *tables, after(sums, bs_other, *d_sent), up_bias, head_sums, proj_grad
         )
     else:
         small_own, small_other = pack_grads_plain(

time: 215 us -> 211 us (0.981)
  no operation moved by 1% of the time
where the time goes in v4:
time: 211 us
  Pallas kernels  85.6 us (41%)
  starting transfers between devices  52.7 us (25%)
  waiting for transfers between devices  42.7 us (20%)
  other arithmetic  15.1 us (7%)
  local copies, waits for them, and re-layouts  9.53 us (5%)
  between operations  5.41 us (3%)
    pallas_call x20, Pallas kernels, call(): pl.pallas_call(body, out_shape=outs, grid=grid or (), in_specs=in_specs o...  85.6 us
    ppermute x34, starting transfers between devices, flip(): return lax.ppermute(value, ('dp', 'tensor'), pairs)  49.5 us
    ppermute x34, waiting for transfers between devices, flip(): return lax.ppermute(value, ('dp', 'tensor'), pairs)  38.8 us
    unnamed x62, local copies, waits for them, and re-layouts  5.46 us
  transfers between devices with their start and end apart: 55, of which 19 were waited for; matrix products, arithmetic and copies ran while one was open for 9% of the time, Pallas kernels for 35%

profile of v4, /device:TPU:0, one launch (start us, length us, event | category | flops | bytes accessed | tf_op | source)
XLA Modules:
  0.0 211.1 jit_solution(7588628132227384215)
XLA Ops:
  0.6 1.7 shard_map.222
  2.4 4.1 %collective-permute-start = (bf16[48,1664]{1,0:T(8,128)(2,1)}, bf16[48,1664]{1,0:T(8,128)(2,1)S(1)}, u32[]{:S(2)}, u32[]{:S(2)}) collective-permute-start(bf16[48,1664]{1,0:T(8,128)(2,1)} %shard_map.222), channel_id=1, source_target_pairs={{0,16},{1,17},{2,18},{3,19},{4,20},{5,21},{6,22},{7,23},{8,24},{9,... | collective-permute-start | bytes 479240 | tf_op jit(solution)/shard_map/ppermute | solution.py:694
  6.5 1.6 collective-permute-start.1
  18.9 1.6 collective-permute-start.3
  20.5 1.5 collective-permute-start.4
  22.4 4.9 %collective-permute-start.6 = (bf16[48,1536]{1,0:T(8,128)(2,1)S(1)}, bf16[48,1536]{1,0:T(8,128)(2,1)S(1)}, u32[]{:S(2)}, u32[]{:S(2)}) collective-permute-start(bf16[48,1536]{1,0:T(8,128)(2,1)S(1)} %copy-done.20), channel_id=1, source_target_pairs={{0,16},{1,17},{2,18},{3,19},{4,20},{5,21},{6,22},{7,23},{8,24},{9,... | collective-permute-start | bytes 442376 | tf_op jit(solution)/shard_map/ppermute | solution.py:694
  27.3 1.5 collective-permute-start.8
  29.9 5.7 %collective-permute-done.6 = bf16[48,1536]{1,0:T(8,128)(2,1)S(1)} collective-permute-done((bf16[48,1536]{1,0:T(8,128)(2,1)S(1)}, bf16[48,1536]{1,0:T(8,128)(2,1)S(1)}, u32[]{:S(2)}, u32[]{:S(2)}) %collective-permute-start.6) | collective-permute-done | bytes 147488 | tf_op jit(solution)/shard_map/ppermute | solution.py:694
  35.6 3.7 %collective-permute-done.7 = bf16[48,1536]{1,0:T(8,128)(2,1)S(1)} collective-permute-done((bf16[48,1536]{1,0:T(8,128)(2,1)S(1)}, bf16[48,1536]{1,0:T(8,128)(2,1)S(1)}, u32[]{:S(2)}, u32[]{:S(2)}) %collective-permute-start.7) | collective-permute-done | bytes 147488 | tf_op jit(solution)/shard_map/ppermute | solution.py:694
  40.2 1.6 collective-permute-start.10
  42.4 2.0 collective-permute-start.14
  45.4 1.9 collective-permute-start.16
  47.3 8.3 %collective-permute-done.10 = bf16[192,1536]{1,0:T(8,128)(2,1)S(1)} collective-permute-done((bf16[192,1536]{1,0:T(8,128)(2,1)S(1)}, bf16[192,1536]{1,0:T(8,128)(2,1)S(1)}, u32[]{:S(2)}, u32[]{:S(2)}) %collective-permute-start.10) | collective-permute-done | bytes 589856 | tf_op jit(solution)/shard_map/ppermute | solution.py:694
  56.2 1.5 collective-permute-done.16
  59.7 1.7 shard_map.223
  61.4 15.8 %shard_map.224 = (bf16[2,512,1152]{2,1,0:T(8,128)(2,1)S(1)}, f32[2,6,512]{2,1,0:T(8,128)S(1)}, bf16[2,512,384]{2,1,0:T(8,128)(2,1)S(1)}, f32[512,768]{1,0:T(8,12...) custom-call(bf16[512,768]{1,0:T(8,128)(2,1)S(1)} %maximum_select_fus, ...), custom_call_target="tpu_custom_call" | custom-call | flops 2415919104 | bytes 1048576 | tf_op jit(solution)/shard_map/pallas_call | solution.py:61
  77.3 3.0 %collective-permute-done.18.c_ref.d_ref.um_ref = bf16[384,1536]{1,0:T(8,128)(2,1)S(1)} collective-permute-done((bf16[384,1536]{1,0:T(8,128)(2,1)S(1)}, bf16[384,1536]{1,0:T(8,128)(2,1)S(1)}, u32[]{:S(2)}, u32[]{:S(2)}) %collective-permute-start.18) | collective-permute-done | bytes 1179680 | tf_op jit(solution)/shard_map/ppermute | solution.py:694
  82.2 5.1 %shard_map.225 = (bf16[512,1536]{1,0:T(8,128)(2,1)S(1)}, bf16[512,1536]{1,0:T(8,128)(2,1)S(1)}) custom-call(bf16[512,768]{1,0:T(8,128)(2,1)S(1)} %get-tuple-element.212.low_ref, bf16[384,1536]{1,0:T(8,128)(2,1)S(1)} %constant_dynamic-update-slice_fusion.4.a_ref.b_ref.ub_ref, bf16[384,1536]{1,0:T(8,128)(2,1)S(1)} %constant_dynamic-update-slice_fusion.4.a_ref.b_ref.ub_ref, ...), custom_call_target="tpu_custom_call" | custom-call | flops 1207959552 | bytes 1048576 | tf_op jit(solution)/shard_map/pallas_call | solution.py:61
  87.3 5.1 %shard_map.226 = (bf16[512,1536]{1,0:T(8,128)(2,1)S(1)}, bf16[512,1536]{1,0:T(8,128)(2,1)S(1)}) custom-call(bf16[512,768]{1,0:T(8,128)(2,1)S(1)} %get-tuple-element.212.low_ref, bf16[384,1536]{1,0:T(8,128)(2,1)S(1)} %collective-permute-done.21.a_ref.b_ref.ub_ref, bf16[384,1536]{1,0:T(8,128)(2,1)S(1)} %collective-permute-done.21.a_ref.b_ref.ub_ref, ...), custom_call_target="tpu_custom_call" | custom-call | flops 1207959552 | bytes 1048576 | tf_op jit(solution)/shard_map/pallas_call | solution.py:61
  92.4 4.2 %collective-permute-done.23.refs_1_.dm_ref = bf16[384,1536]{1,0:T(8,128)(2,1)S(1)} collective-permute-done((bf16[384,1536]{1,0:T(8,128)(2,1)S(1)}, bf16[384,1536]{1,0:T(8,128)(2,1)S(1)}, u32[]{:S(2)}, u32[]{:S(2)}) %collective-permute-start.23) | collective-permute-done | bytes 1179680 | tf_op jit(solution)/shard_map/ppermute | solution.py:694
  96.6 2.8 %collective-permute-done.25.refs_3_.dm_ref = bf16[384,1536]{1,0:T(8,128)(2,1)S(1)} collective-permute-done((bf16[384,1536]{1,0:T(8,128)(2,1)S(1)}, bf16[384,1536]{1,0:T(8,128)(2,1)S(1)}, u32[]{:S(2)}, u32[]{:S(2)}) %collective-permute-start.25) | collective-permute-done | bytes 1179680 | tf_op jit(solution)/shard_map/ppermute | solution.py:28
  99.5 8.4 %shard_map.227 = (f32[512,128]{1,0:T(8,128)S(1)}, bf16[512,768]{1,0:T(8,128)(2,1)S(1)}, bf16[768,512]{1,0:T(8,128)(2,1)S(1)}, f32[512,768]{1,0:T(8,128)S(1)}, f3...) custom-call(s32[1]{0:T(128)} %dynamic_slice.43.len_ref, bf16[512,1536]{1,0:T(8,128)(2,1)S(1)} %get-tuple-element.223.h0_ref.hid_ref, ...), custom_call_target="tpu_custom_call" | custom-call | flops 2415919104 | bytes 1048576 | tf_op jit(solution)/shard_map/pallas_call | solution.py:61
  107.9 2.0 shard_map.228
  110.5 2.0 shard_map.229
  114.3 8.0 %shard_map.230 = (bf16[384,1536]{1,0:T(8,128)(2,1)S(1)}, bf16[384,1536]{1,0:T(8,128)(2,1)S(1)}, f32[8,1536]{1,0:T(8,128)S(1)}, f32[512,768]{1,0:T(8,128)S(1)}) custom-call(bf16[512,768]{1,0:T(8,128)(2,1)S(1)} %get-tuple-element.233.g_ref, bf16[768,512]{1,0:T(8,128)(2,1)S(1)} %get-tuple-element.227.lowt_ref, ...), custom_call_target="tpu_custom_call" | custom-call | flops 3623878656 | bytes 1048576 | tf_op jit(solution)/shard_map/pallas_call | solution.py:61
  124.2 8.2 %shard_map.231 = (bf16[384,1536]{1,0:T(8,128)(2,1)S(1)}, bf16[384,1536]{1,0:T(8,128)(2,1)S(1)}, f32[16,1536]{1,0:T(8,128)S(1)}, f32[512,768]{1,0:T(8,128)S(1)}) custom-call(bf16[512,768]{1,0:T(8,128)(2,1)S(1)} %get-tuple-element.233.g_ref, bf16[768,512]{1,0:T(8,128)(2,1)S(1)} %get-tuple-element.227.lowt_ref, ...), custom_call_target="tpu_custom_call" | custom-call | flops 3623878656 | bytes 1048576 | tf_op jit(solution)/shard_map/pallas_call | solution.py:61
  134.4 2.4 %shard_map.232 = (f32[512,768]{1,0:T(8,128)S(1)}, bf16[768,512]{1,0:T(8,128)(2,1)S(1)}, bf16[2,512,384]{2,1,0:T(8,128)(2,1)S(1)}, f32[48,768]{1,0:T(8,128)S(1)}) custom-call(f32[512,768]{1,0:T(8,128)S(1)} %get-tuple-element.244.gf_ref, f32[512,768]{1,0:T(8,128)S(1)} %get-tuple-element.245.res_ref, f32[8,768]{1,0:T(8,128)S(1)} %get-tuple-element.202.vec_ref, ...), custom_call_target="tpu_custom_call" | custom-call | flops 603979776 | bytes 1048576 | tf_op jit(solution)/shard_map/pallas_call | solution.py:61
  138.0 6.8 %shard_map.233 = (bf16[2,512,768]{2,1,0:T(8,128)(2,1)S(1)}, f32[2,2,8,256]{3,2,1,0:T(8,128)S(1)}) custom-call(bf16[2,512,384]{2,1,0:T(8,128)(2,1)S(1)} %get-tuple-element.256.gatt_ref, bf16[2,512,384]{2,1,0:T(8,128)(2,1)S(1)} %get-tuple-element.249.att_ref.refs_1_, bf16[2,512,1152]{2,1,0:T(8,128)(2,1)S(1)} %get-tuple-element.250.qkv_ref, ...), custom_call_target="tpu_custom_call" | custom-call | flops 2684354560 | bytes 1048576 | tf_op jit(solution)/shard_map/pallas_call | solution.py:61
  147.3 3.5 %shard_map.235 = (bf16[2,512,384]{2,1,0:T(8,128)(2,1)S(1)}, f32[2,2,8,384]{3,2,1,0:T(8,128)S(1)}) custom-call(bf16[2,512,384]{2,1,0:T(8,128)(2,1)S(1)} %get-tuple-element.256.gatt_ref, bf16[2,512,384]{2,1,0:T(8,128)(2,1)S(1)} %get-tuple-element.249.att_ref.refs_1_, bf16[2,512,1152]{2,1,0:T(8,128)(2,1)S(1)} %get-tuple-element.250.qkv_ref, ...), custom_call_target="tpu_custom_call" | custom-call | flops 1342177280 | bytes 1048576 | tf_op jit(solution)/shard_map/pallas_call | solution.py:61
  150.8 2.1 %shard_map.236 = (bf16[384,1152]{1,0:T(8,128)(2,1)S(1)}, bf16[384,1152]{1,0:T(8,128)(2,1)}) custom-call(bf16[768,512]{1,0:T(8,128)(2,1)S(1)} %get-tuple-element.203.xt_ref, bf16[2,512,768]{2,1,0:T(8,128)(2,1)S(1)} %get-tuple-element.287.g_ref.a_ref, bf16[384,1152]{1,0:T(8,128)(2,1)S(1)} %collective-permute-done.33.kc_ref, ...), custom_call_target="tpu_custom_call" | custom-call | flops 905969664 | bytes 1048576 | tf_op jit(solution)/shard_map/pallas_call | solution.py:61
  153.0 1.3 collective-permute-start.36
  154.3 1.6 convert_add_fusion.1
  156.8 1.3 shard_map.237
  160.7 3.1 %shard_map.238 = (bf16[768,128]{1,0:T(8,128)(2,1)S(1)}, bf16[768,128]{1,0:T(8,128)(2,1)}) custom-call(s32[1]{0:T(128)} %bitcast.8.core_ref, bf16[2,128,768]{2,1,0:T(8,128)(2,1)S(1)} %add_convert_fusion.7.thin_ref, bf16[2,128,3072]{2,1,0:T(8,128)(2,1)S(1)} %add_convert_fusion.broad_ref, s32[1,768]{1,0:T(1,128)S(1)} %and_select_fusion.rel_ref, ...), custom_call_target="tpu_custom_call" | custom-call | bytes 1048576 | tf_op jit(solution)/shard_map/pallas_call | solution.py:61
  164.5 2.6 %collective-permute-start.47 = (bf16[48,1536]{1,0:T(8,128)(2,1)}, bf16[48,1536]{1,0:T(8,128)(2,1)S(1)}, u32[]{:S(2)}, u32[]{:S(2)}) collective-permute-start(bf16[48,1536]{1,0:T(8,128)(2,1)} %get-tuple-element.328), channel_id=1, source_target_pairs={{0,16},{1,17},{2,18},{3,19},{4,20},{5,21},{6,22},{7,23},{8,24},{9,... | collective-permute-start | bytes 442376 | tf_op jit(solution)/shard_map/ppermute | solution.py:694
  167.2 1.8 collective-permute-start.49
  171.0 1.8 shard_map.239
  175.3 1.8 fusion.13
  177.1 1.9 collective-permute-start.44
  179.1 1.6 collective-permute-done.42
  181.7 2.6 %collective-permute-start.46 = (bf16[48,1536]{1,0:T(8,128)(2,1)S(1)}, bf16[48,1536]{1,0:T(8,128)(2,1)S(1)}, u32[]{:S(2)}, u32[]{:S(2)}) collective-permute-start(bf16[48,1536]{1,0:T(8,128)(2,1)S(1)} %get-tuple-element.323), channel_id=1, source_target_pairs={{0,24},{1,25},{2,26},{3,27},{4,28},{5,29},{6,30},{7,31},{8,16},{9,... | collective-permute-start | bytes 442376 | tf_op jit(solution)/shard_map/ppermute | solution.py:694
  186.4 4.7 %shard_map.240 = f32[512,768]{1,0:T(8,128)S(1)} custom-call(bf16[2,512,768]{2,1,0:T(8,128)(2,1)S(1)} %copy-done.2, bf16[2,512,384]{2,1,0:T(8,128)(2,1)S(1)} %copy-done.5, f32[512,768]{1,0:T(8,128)S(1)} %copy-done.9, bf16[768,768]{1,0:T(8,128)(2,1)S(1)} %copy-done.7, bf16[2,768,1536]{2,1,0:T(8,128)(2,1)S(1)} %bitcast.28), custom_call_target="tpu_custom_call" | custom-call | flops 2415919104 | bytes 1048576 | tf_op jit(solution)/shard_map/pallas_call | solution.py:61
  192.0 2.7 %collective-permute-done.43 = bf16[192,512]{1,0:T(8,128)(2,1)S(1)} collective-permute-done((bf16[192,512]{1,0:T(8,128)(2,1)S(1)}, bf16[192,512]{1,0:T(8,128)(2,1)S(1)}, u32[]{:S(2)}, u32[]{:S(2)}) %collective-permute-start.43) | collective-permute-done | bytes 196640 | tf_op jit(solution)/shard_map/ppermute | solution.py:694
  196.2 1.9 collective-permute-start.53
  198.0 2.5 %collective-permute-start.54 = (bf16[48,1664]{1,0:T(8,128)(2,1)S(1)}, bf16[48,1664]{1,0:T(8,128)(2,1)S(1)}, u32[]{:S(2)}, u32[]{:S(2)}) collective-permute-start(bf16[48,1664]{1,0:T(8,128)(2,1)S(1)} %get-tuple-element.320), channel_id=1, source_target_pairs={{0,24},{1,25},{2,26},{3,27},{4,28},{5,29},{6,30},{7,31},{8,16},{9,... | collective-permute-start | bytes 479240 | tf_op jit(solution)/shard_map/ppermute | solution.py:694
  200.7 1.7 fusion.5
  203.3 3.6 %collective-permute-done.52.refs_0_ = bf16[48,1664]{1,0:T(8,128)(2,1)S(1)} collective-permute-done((bf16[48,1664]{1,0:T(8,128)(2,1)S(1)}, bf16[48,1664]{1,0:T(8,128)(2,1)S(1)}, u32[]{:S(2)}, u32[]{:S(2)}) %collective-permute-start.52) | collective-permute-done | bytes 159776 | tf_op jit(solution)/shard_map/ppermute | solution.py:694
  206.9 2.2 %collective-permute-done.54.refs_2_ = bf16[48,1664]{1,0:T(8,128)(2,1)S(1)} collective-permute-done((bf16[48,1664]{1,0:T(8,128)(2,1)S(1)}, bf16[48,1664]{1,0:T(8,128)(2,1)S(1)}, u32[]{:S(2)}, u32[]{:S(2)}) %collective-permute-start.54) | collective-permute-done | bytes 159776 | tf_op jit(solution)/shard_map/ppermute | solution.py:694
  (203 shorter events, 42.5 us)
Async XLA Ops:
  2.4 15.7 %collective-permute-start = (bf16[48,1664]{1,0:T(8,128)(2,1)}, bf16[48,1664]{1,0:T(8,128)(2,1)S(1)}, u32[]{:S(2)}, u32[]{:S(2)}) collective-permute-start(bf16[48,1664]{1,0:T(8,128)(2,1)} %shard_map.222), channel_id=1, source_target_pairs={{0,16},{1,17},{2,18},{3,19},{4,20},{5,21},{6,22},{7,23},{8,24},{9,... | collective-permute-start | bytes 479240 | tf_op jit(solution)/shard_map/ppermute | solution.py:694
  6.5 11.6 %collective-permute-start.1 = (bf16[48,1664]{1,0:T(8,128)(2,1)}, bf16[48,1664]{1,0:T(8,128)(2,1)S(1)}, u32[]{:S(2)}, u32[]{:S(2)}) collective-permute-start(bf16[48,1664]{1,0:T(8,128)(2,1)} %shard_map.222), channel_id=1, source_target_pairs={{0,8},{1,9},{2,10},{3,11},{4,12},{5,13},{6,14},{7,15},{8,0},{9,1},... | collective-permute-start | bytes 479240 | tf_op jit(solution)/shard_map/ppermute | solution.py:694
  8.0 10.8 %collective-permute-start.2 = (bf16[48,1664]{1,0:T(8,128)(2,1)}, bf16[48,1664]{1,0:T(8,128)(2,1)S(1)}, u32[]{:S(2)}, u32[]{:S(2)}) collective-permute-start(bf16[48,1664]{1,0:T(8,128)(2,1)} %shard_map.222), channel_id=1, source_target_pairs={{0,24},{1,25},{2,26},{3,27},{4,28},{5,29},{6,30},{7,31},{8,16},{9,... | collective-permute-start | bytes 479240 | tf_op jit(solution)/shard_map/ppermute | solution.py:694
  18.9 20.4 %collective-permute-start.3 = (bf16[192,1664]{1,0:T(8,128)(2,1)S(1)}, bf16[192,1664]{1,0:T(8,128)(2,1)S(1)}, u32[]{:S(2)}, u32[]{:S(2)}) collective-permute-start(bf16[192,1664]{1,0:T(8,128)(2,1)S(1)} %pad_maximum_fusion.1.refs_0_), channel_id=1, source_target_pairs={{0,4},{1,3},{2,6},{3,1},{4,0},{5,7},{6,2},{7,5},{8,12},{9,11},{10,... | collective-permute-start | bytes 1916936 | tf_op jit(solution)/shard_map/ppermute | solution.py:694
  20.5 18.8 %collective-permute-start.4 = (bf16[192,1664]{1,0:T(8,128)(2,1)S(1)}, bf16[192,1664]{1,0:T(8,128)(2,1)S(1)}, u32[]{:S(2)}, u32[]{:S(2)}) collective-permute-start(bf16[192,1664]{1,0:T(8,128)(2,1)S(1)} %pad_maximum_fusion.1.refs_0_), channel_id=1, source_target_pairs={{0,2},{1,5},{2,0},{3,7},{4,6},{5,1},{6,4},{7,3},{8,10},{9,13},{10,... | collective-permute-start | bytes 1916936 | tf_op jit(solution)/shard_map/ppermute | solution.py:694
  22.0 5.4 %collective-permute-start.5 = (bf16[256,768]{1,0:T(8,128)(2,1)S(1)}, bf16[256,768]{1,0:T(8,128)(2,1)S(1)}, u32[]{:S(2)}, u32[]{:S(2)}) collective-permute-start(bf16[256,768]{1,0:T(8,128)(2,1)S(1)} %get-tuple-element.165), channel_id=1, source_target_pairs={{0,1},{1,0},{2,3},{3,2},{4,5},{5,4},{6,7},{7,6},{8,9},{9,8},{10,11... | collective-permute-start | bytes 1179656 | tf_op jit(solution)/shard_map/ppermute | solution.py:28
  22.4 13.1 %collective-permute-start.6 = (bf16[48,1536]{1,0:T(8,128)(2,1)S(1)}, bf16[48,1536]{1,0:T(8,128)(2,1)S(1)}, u32[]{:S(2)}, u32[]{:S(2)}) collective-permute-start(bf16[48,1536]{1,0:T(8,128)(2,1)S(1)} %copy-done.20), channel_id=1, source_target_pairs={{0,16},{1,17},{2,18},{3,19},{4,20},{5,21},{6,22},{7,23},{8,24},{9,... | collective-permute-start | bytes 442376 | tf_op jit(solution)/shard_map/ppermute | solution.py:694
  27.3 11.9 %collective-permute-start.7 = (bf16[48,1536]{1,0:T(8,128)(2,1)S(1)}, bf16[48,1536]{1,0:T(8,128)(2,1)S(1)}, u32[]{:S(2)}, u32[]{:S(2)}) collective-permute-start(bf16[48,1536]{1,0:T(8,128)(2,1)S(1)} %copy-done.20), channel_id=1, source_target_pairs={{0,8},{1,9},{2,10},{3,11},{4,12},{5,13},{6,14},{7,15},{8,0},{9,1},... | collective-permute-start | bytes 442376 | tf_op jit(solution)/shard_map/ppermute | solution.py:694
  27.3 11.9 %collective-permute-start.8 = (bf16[48,1536]{1,0:T(8,128)(2,1)S(1)}, bf16[48,1536]{1,0:T(8,128)(2,1)S(1)}, u32[]{:S(2)}, u32[]{:S(2)}) collective-permute-start(bf16[48,1536]{1,0:T(8,128)(2,1)S(1)} %copy-done.20), channel_id=1, source_target_pairs={{0,24},{1,25},{2,26},{3,27},{4,28},{5,29},{6,30},{7,31},{8,16},{9,... | collective-permute-start | bytes 442376 | tf_op jit(solution)/shard_map/ppermute | solution.py:694
  35.6 6.2 %collective-permute-start.11 = (bf16[192,1664]{1,0:T(8,128)(2,1)S(1)}, bf16[192,1664]{1,0:T(8,128)(2,1)S(1)}, u32[]{:S(2)}, u32[]{:S(2)}) collective-permute-start(bf16[192,1664]{1,0:T(8,128)(2,1)S(1)} %pad_maximum_fusion.1.refs_0_), channel_id=1, source_target_pairs={{0,1},{1,0},{2,3},{3,2},{4,5},{5,4},{6,7},{7,6},{8,9},{9,8},{10,11... | collective-permute-start | bytes 1916936 | tf_op jit(solution)/shard_map/ppermute | solution.py:28
  39.4 16.8 %collective-permute-start.9 = (bf16[192,1664]{1,0:T(8,128)(2,1)S(1)}, bf16[192,1664]{1,0:T(8,128)(2,1)S(1)}, u32[]{:S(2)}, u32[]{:S(2)}) collective-permute-start(bf16[192,1664]{1,0:T(8,128)(2,1)S(1)} %collective-permute-done.3.refs_1_), channel_id=1, source_target_pairs={{0,2},{1,5},{2,0},{3,7},{4,6},{5,1},{6,4},{7,3},{8,10},{9,13},{10,... | collective-permute-start | bytes 1916936 | tf_op jit(solution)/shard_map/ppermute | solution.py:694
  40.2 15.4 %collective-permute-start.10 = (bf16[192,1536]{1,0:T(8,128)(2,1)S(1)}, bf16[192,1536]{1,0:T(8,128)(2,1)S(1)}, u32[]{:S(2)}, u32[]{:S(2)}) collective-permute-start(bf16[192,1536]{1,0:T(8,128)(2,1)S(1)} %get-tuple-element.340), channel_id=1, source_target_pairs={{0,4},{1,3},{2,6},{3,1},{4,0},{5,7},{6,2},{7,5},{8,12},{9,11},{10,... | collective-permute-start | bytes 1769480 | tf_op jit(solution)/shard_map/ppermute | solution.py:694
  42.4 13.8 %collective-permute-start.14 = (bf16[48,1536]{1,0:T(8,128)(2,1)S(1)}, bf16[48,1536]{1,0:T(8,128)(2,1)S(1)}, u32[]{:S(2)}, u32[]{:S(2)}) collective-permute-start(bf16[48,1536]{1,0:T(8,128)(2,1)S(1)} %bitcast.29), channel_id=1, source_target_pairs={{0,16},{1,17},{2,18},{3,19},{4,20},{5,21},{6,22},{7,23},{8,24},{9,... | collective-permute-start | bytes 442376 | tf_op jit(solution)/shard_map/ppermute | solution.py:694
  44.3 11.9 %collective-permute-start.15 = (bf16[48,1536]{1,0:T(8,128)(2,1)S(1)}, bf16[48,1536]{1,0:T(8,128)(2,1)S(1)}, u32[]{:S(2)}, u32[]{:S(2)}) collective-permute-start(bf16[48,1536]{1,0:T(8,128)(2,1)S(1)} %bitcast.30), channel_id=1, source_target_pairs={{0,8},{1,9},{2,10},{3,11},{4,12},{5,13},{6,14},{7,15},{8,0},{9,1},... | collective-permute-start | bytes 442376 | tf_op jit(solution)/shard_map/ppermute | solution.py:694
  45.4 12.2 %collective-permute-start.16 = (bf16[48,1536]{1,0:T(8,128)(2,1)S(1)}, bf16[48,1536]{1,0:T(8,128)(2,1)S(1)}, u32[]{:S(2)}, u32[]{:S(2)}) collective-permute-start(bf16[48,1536]{1,0:T(8,128)(2,1)S(1)} %bitcast.31), channel_id=1, source_target_pairs={{0,24},{1,25},{2,26},{3,27},{4,28},{5,29},{6,30},{7,31},{8,16},{9,... | collective-permute-start | bytes 442376 | tf_op jit(solution)/shard_map/ppermute | solution.py:694
  57.7 22.6 %collective-permute-start.18 = (bf16[384,1536]{1,0:T(8,128)(2,1)S(1)}, bf16[384,1536]{1,0:T(8,128)(2,1)S(1)}, u32[]{:S(2)}, u32[]{:S(2)}) collective-permute-start(bf16[384,1536]{1,0:T(8,128)(2,1)S(1)} %constant_dynamic-update-slice_fusion.4.a_ref.b_ref.ub_ref), channel_id=1, source_target_pairs={{0,2},{1,5},{2,0},{3,7},{4,6},{5,1},{6,4},{7,3},{8,10},{9,13},{10,... | collective-permute-start | bytes 3538952 | tf_op jit(solution)/shard_map/ppermute | solution.py:694
  59.0 18.2 %collective-permute-start.19 = (bf16[192,1536]{1,0:T(8,128)(2,1)S(1)}, bf16[192,1536]{1,0:T(8,128)(2,1)S(1)}, u32[]{:S(2)}, u32[]{:S(2)}) collective-permute-start(bf16[192,1536]{1,0:T(8,128)(2,1)S(1)} %get-tuple-element.332), channel_id=1, source_target_pairs={{0,4},{1,3},{2,6},{3,1},{4,0},{5,7},{6,2},{7,5},{8,12},{9,11},{10,... | collective-permute-start | bytes 1769480 | tf_op jit(solution)/shard_map/ppermute | solution.py:694
  59.7 27.7 %collective-permute-start.21 = (bf16[384,1536]{1,0:T(8,128)(2,1)S(1)}, bf16[384,1536]{1,0:T(8,128)(2,1)S(1)}, u32[]{:S(2)}, u32[]{:S(2)}) collective-permute-start(bf16[384,1536]{1,0:T(8,128)(2,1)S(1)} %constant_dynamic-update-slice_fusion.4.a_ref.b_ref.ub_ref), channel_id=1, source_target_pairs={{0,1},{1,0},{2,3},{3,2},{4,5},{5,4},{6,7},{7,6},{8,9},{9,8},{10,11... | collective-permute-start | bytes 3538952 | tf_op jit(solution)/shard_map/ppermute | solution.py:28
  80.3 7.0 %collective-permute-start.22 = (bf16[384,1536]{1,0:T(8,128)(2,1)S(1)}, bf16[384,1536]{1,0:T(8,128)(2,1)S(1)}, u32[]{:S(2)}, u32[]{:S(2)}) collective-permute-start(bf16[384,1536]{1,0:T(8,128)(2,1)S(1)} %collective-permute-done.18.c_ref.d_ref.um_ref), channel_id=1, source_target_pairs={{0,1},{1,0},{2,3},{3,2},{4,5},{5,4},{6,7},{7,6},{8,9},{9,8},{10,11... | collective-permute-start | bytes 3538952 | tf_op jit(solution)/shard_map/ppermute | solution.py:28
  80.3 16.3 %collective-permute-start.23 = (bf16[384,1536]{1,0:T(8,128)(2,1)S(1)}, bf16[384,1536]{1,0:T(8,128)(2,1)S(1)}, u32[]{:S(2)}, u32[]{:S(2)}) collective-permute-start(bf16[384,1536]{1,0:T(8,128)(2,1)S(1)} %constant_dynamic-update-slice_fusion.13.refs_0_.db_ref), channel_id=1, source_target_pairs={{0,2},{1,5},{2,0},{3,7},{4,6},{5,1},{6,4},{7,3},{8,10},{9,13},{10,... | collective-permute-start | bytes 3538952 | tf_op jit(solution)/shard_map/ppermute | solution.py:694
  81.5 15.1 %collective-permute-start.24 = (bf16[384,1536]{1,0:T(8,128)(2,1)S(1)}, bf16[384,1536]{1,0:T(8,128)(2,1)S(1)}, u32[]{:S(2)}, u32[]{:S(2)}) collective-permute-start(bf16[384,1536]{1,0:T(8,128)(2,1)S(1)} %constant_dynamic-update-slice_fusion.13.refs_0_.db_ref), channel_id=1, source_target_pairs={{0,1},{1,0},{2,3},{3,2},{4,5},{5,4},{6,7},{7,6},{8,9},{9,8},{10,11... | collective-permute-start | bytes 3538952 | tf_op jit(solution)/shard_map/ppermute | solution.py:28
  81.9 5.4 %collective-permute-start.20 = (f32[256,128]{1,0:T(8,128)S(1)}, f32[256,128]{1,0:T(8,128)S(1)}, u32[]{:S(2)}, u32[]{:S(2)}) collective-permute-start(f32[256,128]{1,0:T(8,128)S(1)} %get-tuple-element.210), channel_id=1, source_target_pairs={{0,1},{1,0},{2,3},{3,2},{4,5},{5,4},{6,7},{7,6},{8,9},{9,8},{10,11... | collective-permute-start | bytes 393224 | tf_op jit(solution)/shard_map/ppermute | solution.py:28
  110.1 12.8 %collective-permute-start.28 = (bf16[384,1536]{1,0:T(8,128)(2,1)S(1)}, bf16[384,1536]{1,0:T(8,128)(2,1)S(1)}, u32[]{:S(2)}, u32[]{:S(2)}) collective-permute-start(bf16[384,1536]{1,0:T(8,128)(2,1)S(1)} %get-tuple-element.231), channel_id=1, source_target_pairs={{0,1},{1,0},{2,3},{3,2},{4,5},{5,4},{6,7},{7,6},{8,9},{9,8},{10,11... | collective-permute-start | bytes 3538952 | tf_op jit(solution)/shard_map/ppermute | solution.py:28
  113.1 9.9 %collective-permute-start.27 = (bf16[192,1536]{1,0:T(8,128)(2,1)S(1)}, bf16[192,1536]{1,0:T(8,128)(2,1)S(1)}, u32[]{:S(2)}, u32[]{:S(2)}) collective-permute-start(bf16[192,1536]{1,0:T(8,128)(2,1)S(1)} %get-tuple-element.317), channel_id=1, source_target_pairs={{0,2},{1,5},{2,0},{3,7},{4,6},{5,1},{6,4},{7,3},{8,10},{9,13},{10,... | collective-permute-start | bytes 1769480 | tf_op jit(solution)/shard_map/ppermute | solution.py:694
  122.3 10.4 %collective-permute-start.30 = (bf16[384,1536]{1,0:T(8,128)(2,1)S(1)}, bf16[384,1536]{1,0:T(8,128)(2,1)S(1)}, u32[]{:S(2)}, u32[]{:S(2)}) collective-permute-start(bf16[384,1536]{1,0:T(8,128)(2,1)S(1)} %get-tuple-element.230), channel_id=1, source_target_pairs={{0,1},{1,0},{2,3},{3,2},{4,5},{5,4},{6,7},{7,6},{8,9},{9,8},{10,11... | collective-permute-start | bytes 3538952 | tf_op jit(solution)/shard_map/ppermute | solution.py:28
  122.4 10.3 %collective-permute-start.31 = (bf16[384,1536]{1,0:T(8,128)(2,1)S(1)}, bf16[384,1536]{1,0:T(8,128)(2,1)S(1)}, u32[]{:S(2)}, u32[]{:S(2)}) collective-permute-start(bf16[384,1536]{1,0:T(8,128)(2,1)S(1)} %get-tuple-element.240), channel_id=1, source_target_pairs={{0,1},{1,0},{2,3},{3,2},{4,5},{5,4},{6,7},{7,6},{8,9},{9,8},{10,11... | collective-permute-start | bytes 3538952 | tf_op jit(solution)/shard_map/ppermute | solution.py:28
  123.0 9.9 %collective-permute-start.29 = (bf16[192,1536]{1,0:T(8,128)(2,1)S(1)}, bf16[192,1536]{1,0:T(8,128)(2,1)S(1)}, u32[]{:S(2)}, u32[]{:S(2)}) collective-permute-start(bf16[192,1536]{1,0:T(8,128)(2,1)S(1)} %get-tuple-element.239), channel_id=1, source_target_pairs={{0,2},{1,5},{2,0},{3,7},{4,6},{5,1},{6,4},{7,3},{8,10},{9,13},{10,... | collective-permute-start | bytes 1769480 | tf_op jit(solution)/shard_map/ppermute | solution.py:694
  133.2 21.1 %collective-permute-start.34 = (bf16[384,1536]{1,0:T(8,128)(2,1)S(1)}, bf16[384,1536]{1,0:T(8,128)(2,1)S(1)}, u32[]{:S(2)}, u32[]{:S(2)}) collective-permute-start(bf16[384,1536]{1,0:T(8,128)(2,1)S(1)} %add_convert_fusion.1), channel_id=1, source_target_pairs={{0,2},{1,5},{2,0},{3,7},{4,6},{5,1},{6,4},{7,3},{8,10},{9,13},{10,... | collective-permute-start | bytes 3538952 | tf_op jit(solution)/shard_map/ppermute | solution.py:694
  146.0 4.8 %collective-permute-start.32 = (bf16[384,1152]{1,0:T(8,128)(2,1)S(1)}, bf16[384,1152]{1,0:T(8,128)(2,1)S(1)}, u32[]{:S(2)}, u32[]{:S(2)}) collective-permute-start(bf16[384,1152]{1,0:T(8,128)(2,1)S(1)} %get-tuple-element.254), channel_id=1, source_target_pairs={{0,1},{1,0},{2,3},{3,2},{4,5},{5,4},{6,7},{7,6},{8,9},{9,8},{10,11... | collective-permute-start | bytes 2654216 | tf_op jit(solution)/shard_map/ppermute | solution.py:28
  146.1 4.8 %collective-permute-start.33 = (bf16[384,1152]{1,0:T(8,128)(2,1)S(1)}, bf16[384,1152]{1,0:T(8,128)(2,1)S(1)}, u32[]{:S(2)}, u32[]{:S(2)}) collective-permute-start(bf16[384,1152]{1,0:T(8,128)(2,1)S(1)} %get-tuple-element.255), channel_id=1, source_target_pairs={{0,1},{1,0},{2,3},{3,2},{4,5},{5,4},{6,7},{7,6},{8,9},{9,8},{10,11... | collective-permute-start | bytes 2654216 | tf_op jit(solution)/shard_map/ppermute | solution.py:28
  146.6 11.5 %collective-permute-start.39 = (bf16[192,1536]{1,0:T(8,128)(2,1)S(1)}, bf16[192,1536]{1,0:T(8,128)(2,1)S(1)}, u32[]{:S(2)}, u32[]{:S(2)}) collective-permute-start(bf16[192,1536]{1,0:T(8,128)(2,1)S(1)} %add_convert_fusion.3), channel_id=1, source_target_pairs={{0,4},{1,3},{2,6},{3,1},{4,0},{5,7},{6,2},{7,5},{8,12},{9,11},{10,... | collective-permute-start | bytes 1769480 | tf_op jit(solution)/shard_map/ppermute | solution.py:694
  153.0 21.0 %collective-permute-start.36 = (bf16[384,1152]{1,0:T(8,128)(2,1)}, bf16[384,1152]{1,0:T(8,128)(2,1)}, u32[]{:S(2)}, u32[]{:S(2)}) collective-permute-start(bf16[384,1152]{1,0:T(8,128)(2,1)} %get-tuple-element.264), channel_id=1, source_target_pairs={{0,2},{1,5},{2,0},{3,7},{4,6},{5,1},{6,4},{7,3},{8,10},{9,13},{10,... | collective-permute-start | bytes 2654216 | tf_op jit(solution)/shard_map/ppermute | solution.py:694
  155.9 16.9 %collective-permute-start.35 = (bf16[192,1536]{1,0:T(8,128)(2,1)}, bf16[192,1536]{1,0:T(8,128)(2,1)}, u32[]{:S(2)}, u32[]{:S(2)}) collective-permute-start(bf16[192,1536]{1,0:T(8,128)(2,1)} %get-tuple-element.315), channel_id=1, source_target_pairs={{0,4},{1,3},{2,6},{3,1},{4,0},{5,7},{6,2},{7,5},{8,12},{9,11},{10,... | collective-permute-start | bytes 1769480 | tf_op jit(solution)/shard_map/ppermute | solution.py:694
  158.1 6.4 %collective-permute-start.37 = (bf16[384,384]{1,0:T(8,128)(2,1)}, bf16[384,384]{1,0:T(8,128)(2,1)}, u32[]{:S(2)}, u32[]{:S(2)}) collective-permute-start(bf16[384,384]{1,0:T(8,128)(2,1)} %get-tuple-element.267), channel_id=1, source_target_pairs={{0,1},{1,0},{2,3},{3,2},{4,5},{5,4},{6,7},{7,6},{8,9},{9,8},{10,11... | collective-permute-start | bytes 884744 | tf_op jit(solution)/shard_map/ppermute | solution.py:28
  158.1 9.1 %collective-permute-start.38 = (bf16[384,384]{1,0:T(8,128)(2,1)}, bf16[384,384]{1,0:T(8,128)(2,1)}, u32[]{:S(2)}, u32[]{:S(2)}) collective-permute-start(bf16[384,384]{1,0:T(8,128)(2,1)} %get-tuple-element.268), channel_id=1, source_target_pairs={{0,1},{1,0},{2,3},{3,2},{4,5},{5,4},{6,7},{7,6},{8,9},{9,8},{10,11... | collective-permute-start | bytes 884744 | tf_op jit(solution)/shard_map/ppermute | solution.py:28
  164.5 17.2 %collective-permute-start.47 = (bf16[48,1536]{1,0:T(8,128)(2,1)}, bf16[48,1536]{1,0:T(8,128)(2,1)S(1)}, u32[]{:S(2)}, u32[]{:S(2)}) collective-permute-start(bf16[48,1536]{1,0:T(8,128)(2,1)} %get-tuple-element.328), channel_id=1, source_target_pairs={{0,16},{1,17},{2,18},{3,19},{4,20},{5,21},{6,22},{7,23},{8,24},{9,... | collective-permute-start | bytes 442376 | tf_op jit(solution)/shard_map/ppermute | solution.py:694
  167.2 17.2 %collective-permute-start.48 = (bf16[48,1536]{1,0:T(8,128)(2,1)}, bf16[48,1536]{1,0:T(8,128)(2,1)S(1)}, u32[]{:S(2)}, u32[]{:S(2)}) collective-permute-start(bf16[48,1536]{1,0:T(8,128)(2,1)} %get-tuple-element.327), channel_id=1, source_target_pairs={{0,8},{1,9},{2,10},{3,11},{4,12},{5,13},{6,14},{7,15},{8,0},{9,1},... | collective-permute-start | bytes 442376 | tf_op jit(solution)/shard_map/ppermute | solution.py:694
  167.2 18.0 %collective-permute-start.49 = (bf16[48,1536]{1,0:T(8,128)(2,1)}, bf16[48,1536]{1,0:T(8,128)(2,1)S(1)}, u32[]{:S(2)}, u32[]{:S(2)}) collective-permute-start(bf16[48,1536]{1,0:T(8,128)(2,1)} %get-tuple-element.326), channel_id=1, source_target_pairs={{0,24},{1,25},{2,26},{3,27},{4,28},{5,29},{6,30},{7,31},{8,16},{9,... | collective-permute-start | bytes 442376 | tf_op jit(solution)/shard_map/ppermute | solution.py:694
  172.8 7.8 %collective-permute-start.42 = (bf16[384,512]{1,0:T(8,128)(2,1)S(1)}, bf16[384,512]{1,0:T(8,128)(2,1)S(1)}, u32[]{:S(2)}, u32[]{:S(2)}) collective-permute-start(bf16[384,512]{1,0:T(8,128)(2,1)S(1)} %get-tuple-element.280), channel_id=1, source_target_pairs={{0,2},{1,5},{2,0},{3,7},{4,6},{5,1},{6,4},{7,3},{8,10},{9,13},{10,... | collective-permute-start | bytes 1179656 | tf_op jit(solution)/shard_map/ppermute | solution.py:694
  177.1 14.2 %collective-permute-start.44 = (bf16[48,1536]{1,0:T(8,128)(2,1)S(1)}, bf16[48,1536]{1,0:T(8,128)(2,1)S(1)}, u32[]{:S(2)}, u32[]{:S(2)}) collective-permute-start(bf16[48,1536]{1,0:T(8,128)(2,1)S(1)} %get-tuple-element.325), channel_id=1, source_target_pairs={{0,16},{1,17},{2,18},{3,19},{4,20},{5,21},{6,22},{7,23},{8,24},{9,... | collective-permute-start | bytes 442376 | tf_op jit(solution)/shard_map/ppermute | solution.py:694
  180.7 11.4 %collective-permute-start.45 = (bf16[48,1536]{1,0:T(8,128)(2,1)S(1)}, bf16[48,1536]{1,0:T(8,128)(2,1)S(1)}, u32[]{:S(2)}, u32[]{:S(2)}) collective-permute-start(bf16[48,1536]{1,0:T(8,128)(2,1)S(1)} %get-tuple-element.324), channel_id=1, source_target_pairs={{0,8},{1,9},{2,10},{3,11},{4,12},{5,13},{6,14},{7,15},{8,0},{9,1},... | collective-permute-start | bytes 442376 | tf_op jit(solution)/shard_map/ppermute | solution.py:694
  181.7 10.3 %collective-permute-start.46 = (bf16[48,1536]{1,0:T(8,128)(2,1)S(1)}, bf16[48,1536]{1,0:T(8,128)(2,1)S(1)}, u32[]{:S(2)}, u32[]{:S(2)}) collective-permute-start(bf16[48,1536]{1,0:T(8,128)(2,1)S(1)} %get-tuple-element.323), channel_id=1, source_target_pairs={{0,24},{1,25},{2,26},{3,27},{4,28},{5,29},{6,30},{7,31},{8,16},{9,... | collective-permute-start | bytes 442376 | tf_op jit(solution)/shard_map/ppermute | solution.py:694
  184.3 10.4 %collective-permute-start.41 = (bf16[192,1152]{1,0:T(8,128)(2,1)S(1)}, bf16[192,1152]{1,0:T(8,128)(2,1)S(1)}, u32[]{:S(2)}, u32[]{:S(2)}) collective-permute-start(bf16[192,1152]{1,0:T(8,128)(2,1)S(1)} %add_convert_fusion.6), channel_id=1, source_target_pairs={{0,4},{1,3},{2,6},{3,1},{4,0},{5,7},{6,2},{7,5},{8,12},{9,11},{10,... | collective-permute-start | bytes 1327112 | tf_op jit(solution)/shard_map/ppermute | solution.py:694
  185.2 9.5 %collective-permute-start.43 = (bf16[192,512]{1,0:T(8,128)(2,1)S(1)}, bf16[192,512]{1,0:T(8,128)(2,1)S(1)}, u32[]{:S(2)}, u32[]{:S(2)}) collective-permute-start(bf16[192,512]{1,0:T(8,128)(2,1)S(1)} %add_convert_fusion.8), channel_id=1, source_target_pairs={{0,4},{1,3},{2,6},{3,1},{4,0},{5,7},{6,2},{7,5},{8,12},{9,11},{10,... | collective-permute-start | bytes 589832 | tf_op jit(solution)/shard_map/ppermute | solution.py:694
  191.4 18.5 %collective-permute-start.51 = (f32[256,768]{1,0:T(8,128)S(1)}, f32[256,768]{1,0:T(8,128)S(1)}, u32[]{:S(2)}, u32[]{:S(2)}) collective-permute-start(f32[256,768]{1,0:T(8,128)S(1)} %constant_dynamic-slice_fusion.1), channel_id=1, source_target_pairs={{0,1},{1,0},{2,3},{3,2},{4,5},{5,4},{6,7},{7,6},{8,9},{9,8},{10,11... | collective-permute-start | bytes 2359304 | tf_op jit(solution)/shard_map/ppermute | solution.py:28
  196.1 10.7 %collective-permute-start.52 = (bf16[48,1664]{1,0:T(8,128)(2,1)S(1)}, bf16[48,1664]{1,0:T(8,128)(2,1)S(1)}, u32[]{:S(2)}, u32[]{:S(2)}) collective-permute-start(bf16[48,1664]{1,0:T(8,128)(2,1)S(1)} %get-tuple-element.322), channel_id=1, source_target_pairs={{0,16},{1,17},{2,18},{3,19},{4,20},{5,21},{6,22},{7,23},{8,24},{9,... | collective-permute-start | bytes 479240 | tf_op jit(solution)/shard_map/ppermute | solution.py:694
  196.2 10.7 %collective-permute-start.53 = (bf16[48,1664]{1,0:T(8,128)(2,1)S(1)}, bf16[48,1664]{1,0:T(8,128)(2,1)S(1)}, u32[]{:S(2)}, u32[]{:S(2)}) collective-permute-start(bf16[48,1664]{1,0:T(8,128)(2,1)S(1)} %get-tuple-element.321), channel_id=1, source_target_pairs={{0,8},{1,9},{2,10},{3,11},{4,12},{5,13},{6,14},{7,15},{8,0},{9,1},... | collective-permute-start | bytes 479240 | tf_op jit(solution)/shard_map/ppermute | solution.py:694
  198.0 11.0 %collective-permute-start.54 = (bf16[48,1664]{1,0:T(8,128)(2,1)S(1)}, bf16[48,1664]{1,0:T(8,128)(2,1)S(1)}, u32[]{:S(2)}, u32[]{:S(2)}) collective-permute-start(bf16[48,1664]{1,0:T(8,128)(2,1)S(1)} %get-tuple-element.320), channel_id=1, source_target_pairs={{0,24},{1,25},{2,26},{3,27},{4,28},{5,29},{6,30},{7,31},{8,16},{9,... | collective-permute-start | bytes 479240 | tf_op jit(solution)/shard_map/ppermute | solution.py:694
  (34 other events, 331.3 us)

commit v5 on v4

--- a/solution.py
+++ b/solution.py
@@ -10,7 +10,7 @@
 
 HD = 64
 LANES = 128
-STRIP = 128
+STRIP = 256
 F32 = jnp.float32
 BF16 = jnp.bfloat16
 VMEM_LIMIT = 15 * 1024 * 1024

time: 211 us -> 211 us (level)
  no operation moved by 1% of the time
where the time goes in v5:
time: 211 us; the launch traced here: 210 us
  Pallas kernels  84.4 us (40%)
  starting transfers between devices  52.2 us (25%)
  waiting for transfers between devices  43.6 us (21%)
  other arithmetic  15.1 us (7%)
  local copies, waits for them, and re-layouts  9.53 us (5%)
  between operations  5.4 us (3%)
    pallas_call x20, Pallas kernels, call(): pl.pallas_call(body, out_shape=outs, grid=grid or (), in_specs=in_specs o...  84.4 us
    ppermute x34, starting transfers between devices, flip(): return lax.ppermute(value, ('dp', 'tensor'), pairs)  49.1 us
    ppermute x34, waiting for transfers between devices, flip(): return lax.ppermute(value, ('dp', 'tensor'), pairs)  39.7 us
    unnamed x62, local copies, waits for them, and re-layouts  5.46 us
  transfers between devices with their start and end apart: 55, of which 19 were waited for; matrix products, arithmetic and copies ran while one was open for 9% of the time, Pallas kernels for 35%

profile of v5, /device:TPU:0, one launch (start us, length us, event | category | flops | bytes accessed | tf_op | source)
XLA Modules:
  0.0 210.2 jit_solution(1405761364804454164)
XLA Ops:
  0.6 1.7 shard_map.222
  2.4 4.1 %collective-permute-start = (bf16[48,1664]{1,0:T(8,128)(2,1)}, bf16[48,1664]{1,0:T(8,128)(2,1)S(1)}, u32[]{:S(2)}, u32[]{:S(2)}) collective-permute-start(bf16[48,1664]{1,0:T(8,128)(2,1)} %shard_map.222), channel_id=1, source_target_pairs={{0,16},{1,17},{2,18},{3,19},{4,20},{5,21},{6,22},{7,23},{8,24},{9,... | collective-permute-start | bytes 479240 | tf_op jit(solution)/shard_map/ppermute | solution.py:694
  6.5 1.6 collective-permute-start.1
  18.9 1.6 collective-permute-start.3
  20.5 1.5 collective-permute-start.4
  22.4 4.9 %collective-permute-start.6 = (bf16[48,1536]{1,0:T(8,128)(2,1)S(1)}, bf16[48,1536]{1,0:T(8,128)(2,1)S(1)}, u32[]{:S(2)}, u32[]{:S(2)}) collective-permute-start(bf16[48,1536]{1,0:T(8,128)(2,1)S(1)} %copy-done.20), channel_id=1, source_target_pairs={{0,16},{1,17},{2,18},{3,19},{4,20},{5,21},{6,22},{7,23},{8,24},{9,... | collective-permute-start | bytes 442376 | tf_op jit(solution)/shard_map/ppermute | solution.py:694
  27.3 1.5 collective-permute-start.8
  29.9 5.7 %collective-permute-done.6 = bf16[48,1536]{1,0:T(8,128)(2,1)S(1)} collective-permute-done((bf16[48,1536]{1,0:T(8,128)(2,1)S(1)}, bf16[48,1536]{1,0:T(8,128)(2,1)S(1)}, u32[]{:S(2)}, u32[]{:S(2)}) %collective-permute-start.6) | collective-permute-done | bytes 147488 | tf_op jit(solution)/shard_map/ppermute | solution.py:694
  35.6 3.7 %collective-permute-done.7 = bf16[48,1536]{1,0:T(8,128)(2,1)S(1)} collective-permute-done((bf16[48,1536]{1,0:T(8,128)(2,1)S(1)}, bf16[48,1536]{1,0:T(8,128)(2,1)S(1)}, u32[]{:S(2)}, u32[]{:S(2)}) %collective-permute-start.7) | collective-permute-done | bytes 147488 | tf_op jit(solution)/shard_map/ppermute | solution.py:694
  40.2 1.6 collective-permute-start.10
  42.4 2.0 collective-permute-start.14
  45.4 1.9 collective-permute-start.16
  47.3 8.3 %collective-permute-done.10 = bf16[192,1536]{1,0:T(8,128)(2,1)S(1)} collective-permute-done((bf16[192,1536]{1,0:T(8,128)(2,1)S(1)}, bf16[192,1536]{1,0:T(8,128)(2,1)S(1)}, u32[]{:S(2)}, u32[]{:S(2)}) %collective-permute-start.10) | collective-permute-done | bytes 589856 | tf_op jit(solution)/shard_map/ppermute | solution.py:694
  56.2 1.5 collective-permute-done.16
  59.7 1.7 shard_map.223
  61.4 15.4 %shard_map.224 = (bf16[2,512,1152]{2,1,0:T(8,128)(2,1)S(1)}, f32[2,6,512]{2,1,0:T(8,128)S(1)}, bf16[2,512,384]{2,1,0:T(8,128)(2,1)S(1)}, f32[512,768]{1,0:T(8,12...) custom-call(bf16[512,768]{1,0:T(8,128)(2,1)S(1)} %maximum_select_fus, ...), custom_call_target="tpu_custom_call" | custom-call | flops 2415919104 | bytes 1048576 | tf_op jit(solution)/shard_map/pallas_call | solution.py:61
  76.9 3.4 %collective-permute-done.18.c_ref.d_ref.um_ref = bf16[384,1536]{1,0:T(8,128)(2,1)S(1)} collective-permute-done((bf16[384,1536]{1,0:T(8,128)(2,1)S(1)}, bf16[384,1536]{1,0:T(8,128)(2,1)S(1)}, u32[]{:S(2)}, u32[]{:S(2)}) %collective-permute-start.18) | collective-permute-done | bytes 1179680 | tf_op jit(solution)/shard_map/ppermute | solution.py:694
  82.2 5.1 %shard_map.225 = (bf16[512,1536]{1,0:T(8,128)(2,1)S(1)}, bf16[512,1536]{1,0:T(8,128)(2,1)S(1)}) custom-call(bf16[512,768]{1,0:T(8,128)(2,1)S(1)} %get-tuple-element.212.low_ref, bf16[384,1536]{1,0:T(8,128)(2,1)S(1)} %constant_dynamic-update-slice_fusion.4.a_ref.b_ref.ub_ref, bf16[384,1536]{1,0:T(8,128)(2,1)S(1)} %constant_dynamic-update-slice_fusion.4.a_ref.b_ref.ub_ref, ...), custom_call_target="tpu_custom_call" | custom-call | flops 1207959552 | bytes 1048576 | tf_op jit(solution)/shard_map/pallas_call | solution.py:61
  87.3 5.1 %shard_map.226 = (bf16[512,1536]{1,0:T(8,128)(2,1)S(1)}, bf16[512,1536]{1,0:T(8,128)(2,1)S(1)}) custom-call(bf16[512,768]{1,0:T(8,128)(2,1)S(1)} %get-tuple-element.212.low_ref, bf16[384,1536]{1,0:T(8,128)(2,1)S(1)} %collective-permute-done.21.a_ref.b_ref.ub_ref, bf16[384,1536]{1,0:T(8,128)(2,1)S(1)} %collective-permute-done.21.a_ref.b_ref.ub_ref, ...), custom_call_target="tpu_custom_call" | custom-call | flops 1207959552 | bytes 1048576 | tf_op jit(solution)/shard_map/pallas_call | solution.py:61
  92.4 4.2 %collective-permute-done.23.refs_1_.dm_ref = bf16[384,1536]{1,0:T(8,128)(2,1)S(1)} collective-permute-done((bf16[384,1536]{1,0:T(8,128)(2,1)S(1)}, bf16[384,1536]{1,0:T(8,128)(2,1)S(1)}, u32[]{:S(2)}, u32[]{:S(2)}) %collective-permute-start.23) | collective-permute-done | bytes 1179680 | tf_op jit(solution)/shard_map/ppermute | solution.py:694
  96.6 2.8 %collective-permute-done.25.refs_3_.dm_ref = bf16[384,1536]{1,0:T(8,128)(2,1)S(1)} collective-permute-done((bf16[384,1536]{1,0:T(8,128)(2,1)S(1)}, bf16[384,1536]{1,0:T(8,128)(2,1)S(1)}, u32[]{:S(2)}, u32[]{:S(2)}) %collective-permute-start.25) | collective-permute-done | bytes 1179680 | tf_op jit(solution)/shard_map/ppermute | solution.py:28
  99.5 7.6 %shard_map.227 = (f32[512,128]{1,0:T(8,128)S(1)}, bf16[512,768]{1,0:T(8,128)(2,1)S(1)}, bf16[768,512]{1,0:T(8,128)(2,1)S(1)}, f32[512,768]{1,0:T(8,128)S(1)}, f3...) custom-call(s32[1]{0:T(128)} %dynamic_slice.43.len_ref, bf16[512,1536]{1,0:T(8,128)(2,1)S(1)} %get-tuple-element.223.h0_ref.hid_ref, ...), custom_call_target="tpu_custom_call" | custom-call | flops 2415919104 | bytes 1048576 | tf_op jit(solution)/shard_map/pallas_call | solution.py:61
  107.1 2.0 shard_map.228
  109.6 2.0 shard_map.229
  113.5 8.1 %shard_map.230 = (bf16[384,1536]{1,0:T(8,128)(2,1)S(1)}, bf16[384,1536]{1,0:T(8,128)(2,1)S(1)}, f32[8,1536]{1,0:T(8,128)S(1)}, f32[512,768]{1,0:T(8,128)S(1)}) custom-call(bf16[512,768]{1,0:T(8,128)(2,1)S(1)} %get-tuple-element.233.g_ref, bf16[768,512]{1,0:T(8,128)(2,1)S(1)} %get-tuple-element.227.lowt_ref, ...), custom_call_target="tpu_custom_call" | custom-call | flops 3623878656 | bytes 1048576 | tf_op jit(solution)/shard_map/pallas_call | solution.py:61
  123.4 7.9 %shard_map.231 = (bf16[384,1536]{1,0:T(8,128)(2,1)S(1)}, bf16[384,1536]{1,0:T(8,128)(2,1)S(1)}, f32[16,1536]{1,0:T(8,128)S(1)}, f32[512,768]{1,0:T(8,128)S(1)}) custom-call(bf16[512,768]{1,0:T(8,128)(2,1)S(1)} %get-tuple-element.233.g_ref, bf16[768,512]{1,0:T(8,128)(2,1)S(1)} %get-tuple-element.227.lowt_ref, ...), custom_call_target="tpu_custom_call" | custom-call | flops 3623878656 | bytes 1048576 | tf_op jit(solution)/shard_map/pallas_call | solution.py:61
  133.6 2.2 %shard_map.232 = (f32[512,768]{1,0:T(8,128)S(1)}, bf16[768,512]{1,0:T(8,128)(2,1)S(1)}, bf16[2,512,384]{2,1,0:T(8,128)(2,1)S(1)}, f32[48,768]{1,0:T(8,128)S(1)}) custom-call(f32[512,768]{1,0:T(8,128)S(1)} %get-tuple-element.244.gf_ref, f32[512,768]{1,0:T(8,128)S(1)} %get-tuple-element.245.res_ref, f32[8,768]{1,0:T(8,128)S(1)} %get-tuple-element.202.vec_ref, ...), custom_call_target="tpu_custom_call" | custom-call | flops 603979776 | bytes 1048576 | tf_op jit(solution)/shard_map/pallas_call | solution.py:61
  136.9 6.8 %shard_map.233 = (bf16[2,512,768]{2,1,0:T(8,128)(2,1)S(1)}, f32[2,2,8,256]{3,2,1,0:T(8,128)S(1)}) custom-call(bf16[2,512,384]{2,1,0:T(8,128)(2,1)S(1)} %get-tuple-element.256.gatt_ref, bf16[2,512,384]{2,1,0:T(8,128)(2,1)S(1)} %get-tuple-element.249.att_ref.refs_1_, bf16[2,512,1152]{2,1,0:T(8,128)(2,1)S(1)} %get-tuple-element.250.qkv_ref, ...), custom_call_target="tpu_custom_call" | custom-call | flops 2684354560 | bytes 1048576 | tf_op jit(solution)/shard_map/pallas_call | solution.py:61
  146.4 3.7 %shard_map.235 = (bf16[2,512,384]{2,1,0:T(8,128)(2,1)S(1)}, f32[2,2,8,384]{3,2,1,0:T(8,128)S(1)}) custom-call(bf16[2,512,384]{2,1,0:T(8,128)(2,1)S(1)} %get-tuple-element.256.gatt_ref, bf16[2,512,384]{2,1,0:T(8,128)(2,1)S(1)} %get-tuple-element.249.att_ref.refs_1_, bf16[2,512,1152]{2,1,0:T(8,128)(2,1)S(1)} %get-tuple-element.250.qkv_ref, ...), custom_call_target="tpu_custom_call" | custom-call | flops 1342177280 | bytes 1048576 | tf_op jit(solution)/shard_map/pallas_call | solution.py:61
  150.2 2.1 %shard_map.236 = (bf16[384,1152]{1,0:T(8,128)(2,1)S(1)}, bf16[384,1152]{1,0:T(8,128)(2,1)}) custom-call(bf16[768,512]{1,0:T(8,128)(2,1)S(1)} %get-tuple-element.203.xt_ref, bf16[2,512,768]{2,1,0:T(8,128)(2,1)S(1)} %get-tuple-element.287.g_ref.a_ref, bf16[384,1152]{1,0:T(8,128)(2,1)S(1)} %collective-permute-done.33.kc_ref, ...), custom_call_target="tpu_custom_call" | custom-call | flops 905969664 | bytes 1048576 | tf_op jit(solution)/shard_map/pallas_call | solution.py:61
  153.5 1.6 convert_add_fusion.1
  156.0 1.3 shard_map.237
  157.8 1.3 fusion.14
  159.9 3.1 %shard_map.238 = (bf16[768,128]{1,0:T(8,128)(2,1)S(1)}, bf16[768,128]{1,0:T(8,128)(2,1)}) custom-call(s32[1]{0:T(128)} %bitcast.8.core_ref, bf16[2,128,768]{2,1,0:T(8,128)(2,1)S(1)} %add_convert_fusion.7.thin_ref, bf16[2,128,3072]{2,1,0:T(8,128)(2,1)S(1)} %add_convert_fusion.broad_ref, s32[1,768]{1,0:T(1,128)S(1)} %and_select_fusion.rel_ref, ...), custom_call_target="tpu_custom_call" | custom-call | bytes 1048576 | tf_op jit(solution)/shard_map/pallas_call | solution.py:61
  163.7 2.6 %collective-permute-start.47 = (bf16[48,1536]{1,0:T(8,128)(2,1)}, bf16[48,1536]{1,0:T(8,128)(2,1)S(1)}, u32[]{:S(2)}, u32[]{:S(2)}) collective-permute-start(bf16[48,1536]{1,0:T(8,128)(2,1)} %get-tuple-element.328), channel_id=1, source_target_pairs={{0,16},{1,17},{2,18},{3,19},{4,20},{5,21},{6,22},{7,23},{8,24},{9,... | collective-permute-start | bytes 442376 | tf_op jit(solution)/shard_map/ppermute | solution.py:694
  166.4 1.7 collective-permute-start.49
  170.2 1.8 shard_map.239
  174.5 1.8 fusion.13
  176.3 1.8 collective-permute-start.44
  178.1 1.8 collective-permute-done.42
  180.7 2.6 %collective-permute-start.46 = (bf16[48,1536]{1,0:T(8,128)(2,1)S(1)}, bf16[48,1536]{1,0:T(8,128)(2,1)S(1)}, u32[]{:S(2)}, u32[]{:S(2)}) collective-permute-start(bf16[48,1536]{1,0:T(8,128)(2,1)S(1)} %get-tuple-element.323), channel_id=1, source_target_pairs={{0,24},{1,25},{2,26},{3,27},{4,28},{5,29},{6,30},{7,31},{8,16},{9,... | collective-permute-start | bytes 442376 | tf_op jit(solution)/shard_map/ppermute | solution.py:694
  185.3 4.7 %shard_map.240 = f32[512,768]{1,0:T(8,128)S(1)} custom-call(bf16[2,512,768]{2,1,0:T(8,128)(2,1)S(1)} %copy-done.2, bf16[2,512,384]{2,1,0:T(8,128)(2,1)S(1)} %copy-done.5, f32[512,768]{1,0:T(8,128)S(1)} %copy-done.9, bf16[768,768]{1,0:T(8,128)(2,1)S(1)} %copy-done.7, bf16[2,768,1536]{2,1,0:T(8,128)(2,1)S(1)} %bitcast.28), custom_call_target="tpu_custom_call" | custom-call | flops 2415919104 | bytes 1048576 | tf_op jit(solution)/shard_map/pallas_call | solution.py:61
  191.2 2.4 %collective-permute-done.43 = bf16[192,512]{1,0:T(8,128)(2,1)S(1)} collective-permute-done((bf16[192,512]{1,0:T(8,128)(2,1)S(1)}, bf16[192,512]{1,0:T(8,128)(2,1)S(1)}, u32[]{:S(2)}, u32[]{:S(2)}) %collective-permute-start.43) | collective-permute-done | bytes 196640 | tf_op jit(solution)/shard_map/ppermute | solution.py:694
  195.3 1.7 collective-permute-start.53
  197.0 2.5 %collective-permute-start.54 = (bf16[48,1664]{1,0:T(8,128)(2,1)S(1)}, bf16[48,1664]{1,0:T(8,128)(2,1)S(1)}, u32[]{:S(2)}, u32[]{:S(2)}) collective-permute-start(bf16[48,1664]{1,0:T(8,128)(2,1)S(1)} %get-tuple-element.320), channel_id=1, source_target_pairs={{0,24},{1,25},{2,26},{3,27},{4,28},{5,29},{6,30},{7,31},{8,16},{9,... | collective-permute-start | bytes 479240 | tf_op jit(solution)/shard_map/ppermute | solution.py:694
  199.6 1.7 fusion.5
  202.2 3.8 %collective-permute-done.52.refs_0_ = bf16[48,1664]{1,0:T(8,128)(2,1)S(1)} collective-permute-done((bf16[48,1664]{1,0:T(8,128)(2,1)S(1)}, bf16[48,1664]{1,0:T(8,128)(2,1)S(1)}, u32[]{:S(2)}, u32[]{:S(2)}) %collective-permute-start.52) | collective-permute-done | bytes 159776 | tf_op jit(solution)/shard_map/ppermute | solution.py:694
  206.0 2.2 %collective-permute-done.54.refs_2_ = bf16[48,1664]{1,0:T(8,128)(2,1)S(1)} collective-permute-done((bf16[48,1664]{1,0:T(8,128)(2,1)S(1)}, bf16[48,1664]{1,0:T(8,128)(2,1)S(1)}, u32[]{:S(2)}, u32[]{:S(2)}) %collective-permute-start.54) | collective-permute-done | bytes 159776 | tf_op jit(solution)/shard_map/ppermute | solution.py:694
  (203 shorter events, 42.9 us)
Async XLA Ops:
  2.4 15.7 %collective-permute-start = (bf16[48,1664]{1,0:T(8,128)(2,1)}, bf16[48,1664]{1,0:T(8,128)(2,1)S(1)}, u32[]{:S(2)}, u32[]{:S(2)}) collective-permute-start(bf16[48,1664]{1,0:T(8,128)(2,1)} %shard_map.222), channel_id=1, source_target_pairs={{0,16},{1,17},{2,18},{3,19},{4,20},{5,21},{6,22},{7,23},{8,24},{9,... | collective-permute-start | bytes 479240 | tf_op jit(solution)/shard_map/ppermute | solution.py:694
  6.5 11.6 %collective-permute-start.1 = (bf16[48,1664]{1,0:T(8,128)(2,1)}, bf16[48,1664]{1,0:T(8,128)(2,1)S(1)}, u32[]{:S(2)}, u32[]{:S(2)}) collective-permute-start(bf16[48,1664]{1,0:T(8,128)(2,1)} %shard_map.222), channel_id=1, source_target_pairs={{0,8},{1,9},{2,10},{3,11},{4,12},{5,13},{6,14},{7,15},{8,0},{9,1},... | collective-permute-start | bytes 479240 | tf_op jit(solution)/shard_map/ppermute | solution.py:694
  8.0 10.8 %collective-permute-start.2 = (bf16[48,1664]{1,0:T(8,128)(2,1)}, bf16[48,1664]{1,0:T(8,128)(2,1)S(1)}, u32[]{:S(2)}, u32[]{:S(2)}) collective-permute-start(bf16[48,1664]{1,0:T(8,128)(2,1)} %shard_map.222), channel_id=1, source_target_pairs={{0,24},{1,25},{2,26},{3,27},{4,28},{5,29},{6,30},{7,31},{8,16},{9,... | collective-permute-start | bytes 479240 | tf_op jit(solution)/shard_map/ppermute | solution.py:694
  18.9 20.4 %collective-permute-start.3 = (bf16[192,1664]{1,0:T(8,128)(2,1)S(1)}, bf16[192,1664]{1,0:T(8,128)(2,1)S(1)}, u32[]{:S(2)}, u32[]{:S(2)}) collective-permute-start(bf16[192,1664]{1,0:T(8,128)(2,1)S(1)} %pad_maximum_fusion.1.refs_0_), channel_id=1, source_target_pairs={{0,4},{1,3},{2,6},{3,1},{4,0},{5,7},{6,2},{7,5},{8,12},{9,11},{10,... | collective-permute-start | bytes 1916936 | tf_op jit(solution)/shard_map/ppermute | solution.py:694
  20.5 18.8 %collective-permute-start.4 = (bf16[192,1664]{1,0:T(8,128)(2,1)S(1)}, bf16[192,1664]{1,0:T(8,128)(2,1)S(1)}, u32[]{:S(2)}, u32[]{:S(2)}) collective-permute-start(bf16[192,1664]{1,0:T(8,128)(2,1)S(1)} %pad_maximum_fusion.1.refs_0_), channel_id=1, source_target_pairs={{0,2},{1,5},{2,0},{3,7},{4,6},{5,1},{6,4},{7,3},{8,10},{9,13},{10,... | collective-permute-start | bytes 1916936 | tf_op jit(solution)/shard_map/ppermute | solution.py:694
  22.0 5.4 %collective-permute-start.5 = (bf16[256,768]{1,0:T(8,128)(2,1)S(1)}, bf16[256,768]{1,0:T(8,128)(2,1)S(1)}, u32[]{:S(2)}, u32[]{:S(2)}) collective-permute-start(bf16[256,768]{1,0:T(8,128)(2,1)S(1)} %get-tuple-element.165), channel_id=1, source_target_pairs={{0,1},{1,0},{2,3},{3,2},{4,5},{5,4},{6,7},{7,6},{8,9},{9,8},{10,11... | collective-permute-start | bytes 1179656 | tf_op jit(solution)/shard_map/ppermute | solution.py:28
  22.4 13.1 %collective-permute-start.6 = (bf16[48,1536]{1,0:T(8,128)(2,1)S(1)}, bf16[48,1536]{1,0:T(8,128)(2,1)S(1)}, u32[]{:S(2)}, u32[]{:S(2)}) collective-permute-start(bf16[48,1536]{1,0:T(8,128)(2,1)S(1)} %copy-done.20), channel_id=1, source_target_pairs={{0,16},{1,17},{2,18},{3,19},{4,20},{5,21},{6,22},{7,23},{8,24},{9,... | collective-permute-start | bytes 442376 | tf_op jit(solution)/shard_map/ppermute | solution.py:694
  27.3 11.9 %collective-permute-start.7 = (bf16[48,1536]{1,0:T(8,128)(2,1)S(1)}, bf16[48,1536]{1,0:T(8,128)(2,1)S(1)}, u32[]{:S(2)}, u32[]{:S(2)}) collective-permute-start(bf16[48,1536]{1,0:T(8,128)(2,1)S(1)} %copy-done.20), channel_id=1, source_target_pairs={{0,8},{1,9},{2,10},{3,11},{4,12},{5,13},{6,14},{7,15},{8,0},{9,1},... | collective-permute-start | bytes 442376 | tf_op jit(solution)/shard_map/ppermute | solution.py:694
  27.3 11.9 %collective-permute-start.8 = (bf16[48,1536]{1,0:T(8,128)(2,1)S(1)}, bf16[48,1536]{1,0:T(8,128)(2,1)S(1)}, u32[]{:S(2)}, u32[]{:S(2)}) collective-permute-start(bf16[48,1536]{1,0:T(8,128)(2,1)S(1)} %copy-done.20), channel_id=1, source_target_pairs={{0,24},{1,25},{2,26},{3,27},{4,28},{5,29},{6,30},{7,31},{8,16},{9,... | collective-permute-start | bytes 442376 | tf_op jit(solution)/shard_map/ppermute | solution.py:694
  35.6 6.2 %collective-permute-start.11 = (bf16[192,1664]{1,0:T(8,128)(2,1)S(1)}, bf16[192,1664]{1,0:T(8,128)(2,1)S(1)}, u32[]{:S(2)}, u32[]{:S(2)}) collective-permute-start(bf16[192,1664]{1,0:T(8,128)(2,1)S(1)} %pad_maximum_fusion.1.refs_0_), channel_id=1, source_target_pairs={{0,1},{1,0},{2,3},{3,2},{4,5},{5,4},{6,7},{7,6},{8,9},{9,8},{10,11... | collective-permute-start | bytes 1916936 | tf_op jit(solution)/shard_map/ppermute | solution.py:28
  39.4 16.8 %collective-permute-start.9 = (bf16[192,1664]{1,0:T(8,128)(2,1)S(1)}, bf16[192,1664]{1,0:T(8,128)(2,1)S(1)}, u32[]{:S(2)}, u32[]{:S(2)}) collective-permute-start(bf16[192,1664]{1,0:T(8,128)(2,1)S(1)} %collective-permute-done.3.refs_1_), channel_id=1, source_target_pairs={{0,2},{1,5},{2,0},{3,7},{4,6},{5,1},{6,4},{7,3},{8,10},{9,13},{10,... | collective-permute-start | bytes 1916936 | tf_op jit(solution)/shard_map/ppermute | solution.py:694
  40.2 15.4 %collective-permute-start.10 = (bf16[192,1536]{1,0:T(8,128)(2,1)S(1)}, bf16[192,1536]{1,0:T(8,128)(2,1)S(1)}, u32[]{:S(2)}, u32[]{:S(2)}) collective-permute-start(bf16[192,1536]{1,0:T(8,128)(2,1)S(1)} %get-tuple-element.340), channel_id=1, source_target_pairs={{0,4},{1,3},{2,6},{3,1},{4,0},{5,7},{6,2},{7,5},{8,12},{9,11},{10,... | collective-permute-start | bytes 1769480 | tf_op jit(solution)/shard_map/ppermute | solution.py:694
  42.4 13.8 %collective-permute-start.14 = (bf16[48,1536]{1,0:T(8,128)(2,1)S(1)}, bf16[48,1536]{1,0:T(8,128)(2,1)S(1)}, u32[]{:S(2)}, u32[]{:S(2)}) collective-permute-start(bf16[48,1536]{1,0:T(8,128)(2,1)S(1)} %bitcast.29), channel_id=1, source_target_pairs={{0,16},{1,17},{2,18},{3,19},{4,20},{5,21},{6,22},{7,23},{8,24},{9,... | collective-permute-start | bytes 442376 | tf_op jit(solution)/shard_map/ppermute | solution.py:694
  44.3 11.9 %collective-permute-start.15 = (bf16[48,1536]{1,0:T(8,128)(2,1)S(1)}, bf16[48,1536]{1,0:T(8,128)(2,1)S(1)}, u32[]{:S(2)}, u32[]{:S(2)}) collective-permute-start(bf16[48,1536]{1,0:T(8,128)(2,1)S(1)} %bitcast.30), channel_id=1, source_target_pairs={{0,8},{1,9},{2,10},{3,11},{4,12},{5,13},{6,14},{7,15},{8,0},{9,1},... | collective-permute-start | bytes 442376 | tf_op jit(solution)/shard_map/ppermute | solution.py:694
  45.4 12.2 %collective-permute-start.16 = (bf16[48,1536]{1,0:T(8,128)(2,1)S(1)}, bf16[48,1536]{1,0:T(8,128)(2,1)S(1)}, u32[]{:S(2)}, u32[]{:S(2)}) collective-permute-start(bf16[48,1536]{1,0:T(8,128)(2,1)S(1)} %bitcast.31), channel_id=1, source_target_pairs={{0,24},{1,25},{2,26},{3,27},{4,28},{5,29},{6,30},{7,31},{8,16},{9,... | collective-permute-start | bytes 442376 | tf_op jit(solution)/shard_map/ppermute | solution.py:694
  57.7 22.6 %collective-permute-start.18 = (bf16[384,1536]{1,0:T(8,128)(2,1)S(1)}, bf16[384,1536]{1,0:T(8,128)(2,1)S(1)}, u32[]{:S(2)}, u32[]{:S(2)}) collective-permute-start(bf16[384,1536]{1,0:T(8,128)(2,1)S(1)} %constant_dynamic-update-slice_fusion.4.a_ref.b_ref.ub_ref), channel_id=1, source_target_pairs={{0,2},{1,5},{2,0},{3,7},{4,6},{5,1},{6,4},{7,3},{8,10},{9,13},{10,... | collective-permute-start | bytes 3538952 | tf_op jit(solution)/shard_map/ppermute | solution.py:694
  59.0 17.9 %collective-permute-start.19 = (bf16[192,1536]{1,0:T(8,128)(2,1)S(1)}, bf16[192,1536]{1,0:T(8,128)(2,1)S(1)}, u32[]{:S(2)}, u32[]{:S(2)}) collective-permute-start(bf16[192,1536]{1,0:T(8,128)(2,1)S(1)} %get-tuple-element.332), channel_id=1, source_target_pairs={{0,4},{1,3},{2,6},{3,1},{4,0},{5,7},{6,2},{7,5},{8,12},{9,11},{10,... | collective-permute-start | bytes 1769480 | tf_op jit(solution)/shard_map/ppermute | solution.py:694
  59.7 27.6 %collective-permute-start.21 = (bf16[384,1536]{1,0:T(8,128)(2,1)S(1)}, bf16[384,1536]{1,0:T(8,128)(2,1)S(1)}, u32[]{:S(2)}, u32[]{:S(2)}) collective-permute-start(bf16[384,1536]{1,0:T(8,128)(2,1)S(1)} %constant_dynamic-update-slice_fusion.4.a_ref.b_ref.ub_ref), channel_id=1, source_target_pairs={{0,1},{1,0},{2,3},{3,2},{4,5},{5,4},{6,7},{7,6},{8,9},{9,8},{10,11... | collective-permute-start | bytes 3538952 | tf_op jit(solution)/shard_map/ppermute | solution.py:28
  80.3 7.0 %collective-permute-start.22 = (bf16[384,1536]{1,0:T(8,128)(2,1)S(1)}, bf16[384,1536]{1,0:T(8,128)(2,1)S(1)}, u32[]{:S(2)}, u32[]{:S(2)}) collective-permute-start(bf16[384,1536]{1,0:T(8,128)(2,1)S(1)} %collective-permute-done.18.c_ref.d_ref.um_ref), channel_id=1, source_target_pairs={{0,1},{1,0},{2,3},{3,2},{4,5},{5,4},{6,7},{7,6},{8,9},{9,8},{10,11... | collective-permute-start | bytes 3538952 | tf_op jit(solution)/shard_map/ppermute | solution.py:28
  80.3 16.3 %collective-permute-start.23 = (bf16[384,1536]{1,0:T(8,128)(2,1)S(1)}, bf16[384,1536]{1,0:T(8,128)(2,1)S(1)}, u32[]{:S(2)}, u32[]{:S(2)}) collective-permute-start(bf16[384,1536]{1,0:T(8,128)(2,1)S(1)} %constant_dynamic-update-slice_fusion.13.refs_0_.db_ref), channel_id=1, source_target_pairs={{0,2},{1,5},{2,0},{3,7},{4,6},{5,1},{6,4},{7,3},{8,10},{9,13},{10,... | collective-permute-start | bytes 3538952 | tf_op jit(solution)/shard_map/ppermute | solution.py:694
  81.5 15.1 %collective-permute-start.24 = (bf16[384,1536]{1,0:T(8,128)(2,1)S(1)}, bf16[384,1536]{1,0:T(8,128)(2,1)S(1)}, u32[]{:S(2)}, u32[]{:S(2)}) collective-permute-start(bf16[384,1536]{1,0:T(8,128)(2,1)S(1)} %constant_dynamic-update-slice_fusion.13.refs_0_.db_ref), channel_id=1, source_target_pairs={{0,1},{1,0},{2,3},{3,2},{4,5},{5,4},{6,7},{7,6},{8,9},{9,8},{10,11... | collective-permute-start | bytes 3538952 | tf_op jit(solution)/shard_map/ppermute | solution.py:28
  81.9 5.4 %collective-permute-start.20 = (f32[256,128]{1,0:T(8,128)S(1)}, f32[256,128]{1,0:T(8,128)S(1)}, u32[]{:S(2)}, u32[]{:S(2)}) collective-permute-start(f32[256,128]{1,0:T(8,128)S(1)} %get-tuple-element.210), channel_id=1, source_target_pairs={{0,1},{1,0},{2,3},{3,2},{4,5},{5,4},{6,7},{7,6},{8,9},{9,8},{10,11... | collective-permute-start | bytes 393224 | tf_op jit(solution)/shard_map/ppermute | solution.py:28
  109.3 12.9 %collective-permute-start.28 = (bf16[384,1536]{1,0:T(8,128)(2,1)S(1)}, bf16[384,1536]{1,0:T(8,128)(2,1)S(1)}, u32[]{:S(2)}, u32[]{:S(2)}) collective-permute-start(bf16[384,1536]{1,0:T(8,128)(2,1)S(1)} %get-tuple-element.231), channel_id=1, source_target_pairs={{0,1},{1,0},{2,3},{3,2},{4,5},{5,4},{6,7},{7,6},{8,9},{9,8},{10,11... | collective-permute-start | bytes 3538952 | tf_op jit(solution)/shard_map/ppermute | solution.py:28
  112.3 9.9 %collective-permute-start.27 = (bf16[192,1536]{1,0:T(8,128)(2,1)S(1)}, bf16[192,1536]{1,0:T(8,128)(2,1)S(1)}, u32[]{:S(2)}, u32[]{:S(2)}) collective-permute-start(bf16[192,1536]{1,0:T(8,128)(2,1)S(1)} %get-tuple-element.317), channel_id=1, source_target_pairs={{0,2},{1,5},{2,0},{3,7},{4,6},{5,1},{6,4},{7,3},{8,10},{9,13},{10,... | collective-permute-start | bytes 1769480 | tf_op jit(solution)/shard_map/ppermute | solution.py:694
  121.6 9.9 %collective-permute-start.30 = (bf16[384,1536]{1,0:T(8,128)(2,1)S(1)}, bf16[384,1536]{1,0:T(8,128)(2,1)S(1)}, u32[]{:S(2)}, u32[]{:S(2)}) collective-permute-start(bf16[384,1536]{1,0:T(8,128)(2,1)S(1)} %get-tuple-element.230), channel_id=1, source_target_pairs={{0,1},{1,0},{2,3},{3,2},{4,5},{5,4},{6,7},{7,6},{8,9},{9,8},{10,11... | collective-permute-start | bytes 3538952 | tf_op jit(solution)/shard_map/ppermute | solution.py:28
  121.7 9.9 %collective-permute-start.31 = (bf16[384,1536]{1,0:T(8,128)(2,1)S(1)}, bf16[384,1536]{1,0:T(8,128)(2,1)S(1)}, u32[]{:S(2)}, u32[]{:S(2)}) collective-permute-start(bf16[384,1536]{1,0:T(8,128)(2,1)S(1)} %get-tuple-element.240), channel_id=1, source_target_pairs={{0,1},{1,0},{2,3},{3,2},{4,5},{5,4},{6,7},{7,6},{8,9},{9,8},{10,11... | collective-permute-start | bytes 3538952 | tf_op jit(solution)/shard_map/ppermute | solution.py:28
  122.2 9.9 %collective-permute-start.29 = (bf16[192,1536]{1,0:T(8,128)(2,1)S(1)}, bf16[192,1536]{1,0:T(8,128)(2,1)S(1)}, u32[]{:S(2)}, u32[]{:S(2)}) collective-permute-start(bf16[192,1536]{1,0:T(8,128)(2,1)S(1)} %get-tuple-element.239), channel_id=1, source_target_pairs={{0,2},{1,5},{2,0},{3,7},{4,6},{5,1},{6,4},{7,3},{8,10},{9,13},{10,... | collective-permute-start | bytes 1769480 | tf_op jit(solution)/shard_map/ppermute | solution.py:694
  132.4 21.1 %collective-permute-start.34 = (bf16[384,1536]{1,0:T(8,128)(2,1)S(1)}, bf16[384,1536]{1,0:T(8,128)(2,1)S(1)}, u32[]{:S(2)}, u32[]{:S(2)}) collective-permute-start(bf16[384,1536]{1,0:T(8,128)(2,1)S(1)} %add_convert_fusion.1), channel_id=1, source_target_pairs={{0,2},{1,5},{2,0},{3,7},{4,6},{5,1},{6,4},{7,3},{8,10},{9,13},{10,... | collective-permute-start | bytes 3538952 | tf_op jit(solution)/shard_map/ppermute | solution.py:694
  144.9 5.3 %collective-permute-start.32 = (bf16[384,1152]{1,0:T(8,128)(2,1)S(1)}, bf16[384,1152]{1,0:T(8,128)(2,1)S(1)}, u32[]{:S(2)}, u32[]{:S(2)}) collective-permute-start(bf16[384,1152]{1,0:T(8,128)(2,1)S(1)} %get-tuple-element.254), channel_id=1, source_target_pairs={{0,1},{1,0},{2,3},{3,2},{4,5},{5,4},{6,7},{7,6},{8,9},{9,8},{10,11... | collective-permute-start | bytes 2654216 | tf_op jit(solution)/shard_map/ppermute | solution.py:28
  145.0 5.2 %collective-permute-start.33 = (bf16[384,1152]{1,0:T(8,128)(2,1)S(1)}, bf16[384,1152]{1,0:T(8,128)(2,1)S(1)}, u32[]{:S(2)}, u32[]{:S(2)}) collective-permute-start(bf16[384,1152]{1,0:T(8,128)(2,1)S(1)} %get-tuple-element.255), channel_id=1, source_target_pairs={{0,1},{1,0},{2,3},{3,2},{4,5},{5,4},{6,7},{7,6},{8,9},{9,8},{10,11... | collective-permute-start | bytes 2654216 | tf_op jit(solution)/shard_map/ppermute | solution.py:28
  145.5 11.8 %collective-permute-start.39 = (bf16[192,1536]{1,0:T(8,128)(2,1)S(1)}, bf16[192,1536]{1,0:T(8,128)(2,1)S(1)}, u32[]{:S(2)}, u32[]{:S(2)}) collective-permute-start(bf16[192,1536]{1,0:T(8,128)(2,1)S(1)} %add_convert_fusion.3), channel_id=1, source_target_pairs={{0,4},{1,3},{2,6},{3,1},{4,0},{5,7},{6,2},{7,5},{8,12},{9,11},{10,... | collective-permute-start | bytes 1769480 | tf_op jit(solution)/shard_map/ppermute | solution.py:694
  152.4 20.9 %collective-permute-start.36 = (bf16[384,1152]{1,0:T(8,128)(2,1)}, bf16[384,1152]{1,0:T(8,128)(2,1)}, u32[]{:S(2)}, u32[]{:S(2)}) collective-permute-start(bf16[384,1152]{1,0:T(8,128)(2,1)} %get-tuple-element.264), channel_id=1, source_target_pairs={{0,2},{1,5},{2,0},{3,7},{4,6},{5,1},{6,4},{7,3},{8,10},{9,13},{10,... | collective-permute-start | bytes 2654216 | tf_op jit(solution)/shard_map/ppermute | solution.py:694
  155.1 16.9 %collective-permute-start.35 = (bf16[192,1536]{1,0:T(8,128)(2,1)}, bf16[192,1536]{1,0:T(8,128)(2,1)}, u32[]{:S(2)}, u32[]{:S(2)}) collective-permute-start(bf16[192,1536]{1,0:T(8,128)(2,1)} %get-tuple-element.315), channel_id=1, source_target_pairs={{0,4},{1,3},{2,6},{3,1},{4,0},{5,7},{6,2},{7,5},{8,12},{9,11},{10,... | collective-permute-start | bytes 1769480 | tf_op jit(solution)/shard_map/ppermute | solution.py:694
  157.3 6.4 %collective-permute-start.37 = (bf16[384,384]{1,0:T(8,128)(2,1)}, bf16[384,384]{1,0:T(8,128)(2,1)}, u32[]{:S(2)}, u32[]{:S(2)}) collective-permute-start(bf16[384,384]{1,0:T(8,128)(2,1)} %get-tuple-element.267), channel_id=1, source_target_pairs={{0,1},{1,0},{2,3},{3,2},{4,5},{5,4},{6,7},{7,6},{8,9},{9,8},{10,11... | collective-permute-start | bytes 884744 | tf_op jit(solution)/shard_map/ppermute | solution.py:28
  157.3 9.1 %collective-permute-start.38 = (bf16[384,384]{1,0:T(8,128)(2,1)}, bf16[384,384]{1,0:T(8,128)(2,1)}, u32[]{:S(2)}, u32[]{:S(2)}) collective-permute-start(bf16[384,384]{1,0:T(8,128)(2,1)} %get-tuple-element.268), channel_id=1, source_target_pairs={{0,1},{1,0},{2,3},{3,2},{4,5},{5,4},{6,7},{7,6},{8,9},{9,8},{10,11... | collective-permute-start | bytes 884744 | tf_op jit(solution)/shard_map/ppermute | solution.py:28
  163.7 16.9 %collective-permute-start.47 = (bf16[48,1536]{1,0:T(8,128)(2,1)}, bf16[48,1536]{1,0:T(8,128)(2,1)S(1)}, u32[]{:S(2)}, u32[]{:S(2)}) collective-permute-start(bf16[48,1536]{1,0:T(8,128)(2,1)} %get-tuple-element.328), channel_id=1, source_target_pairs={{0,16},{1,17},{2,18},{3,19},{4,20},{5,21},{6,22},{7,23},{8,24},{9,... | collective-permute-start | bytes 442376 | tf_op jit(solution)/shard_map/ppermute | solution.py:694
  166.4 16.9 %collective-permute-start.48 = (bf16[48,1536]{1,0:T(8,128)(2,1)}, bf16[48,1536]{1,0:T(8,128)(2,1)S(1)}, u32[]{:S(2)}, u32[]{:S(2)}) collective-permute-start(bf16[48,1536]{1,0:T(8,128)(2,1)} %get-tuple-element.327), channel_id=1, source_target_pairs={{0,8},{1,9},{2,10},{3,11},{4,12},{5,13},{6,14},{7,15},{8,0},{9,1},... | collective-permute-start | bytes 442376 | tf_op jit(solution)/shard_map/ppermute | solution.py:694
  166.4 18.0 %collective-permute-start.49 = (bf16[48,1536]{1,0:T(8,128)(2,1)}, bf16[48,1536]{1,0:T(8,128)(2,1)S(1)}, u32[]{:S(2)}, u32[]{:S(2)}) collective-permute-start(bf16[48,1536]{1,0:T(8,128)(2,1)} %get-tuple-element.326), channel_id=1, source_target_pairs={{0,24},{1,25},{2,26},{3,27},{4,28},{5,29},{6,30},{7,31},{8,16},{9,... | collective-permute-start | bytes 442376 | tf_op jit(solution)/shard_map/ppermute | solution.py:694
  172.0 7.8 %collective-permute-start.42 = (bf16[384,512]{1,0:T(8,128)(2,1)S(1)}, bf16[384,512]{1,0:T(8,128)(2,1)S(1)}, u32[]{:S(2)}, u32[]{:S(2)}) collective-permute-start(bf16[384,512]{1,0:T(8,128)(2,1)S(1)} %get-tuple-element.280), channel_id=1, source_target_pairs={{0,2},{1,5},{2,0},{3,7},{4,6},{5,1},{6,4},{7,3},{8,10},{9,13},{10,... | collective-permute-start | bytes 1179656 | tf_op jit(solution)/shard_map/ppermute | solution.py:694
  176.3 14.2 %collective-permute-start.44 = (bf16[48,1536]{1,0:T(8,128)(2,1)S(1)}, bf16[48,1536]{1,0:T(8,128)(2,1)S(1)}, u32[]{:S(2)}, u32[]{:S(2)}) collective-permute-start(bf16[48,1536]{1,0:T(8,128)(2,1)S(1)} %get-tuple-element.325), channel_id=1, source_target_pairs={{0,16},{1,17},{2,18},{3,19},{4,20},{5,21},{6,22},{7,23},{8,24},{9,... | collective-permute-start | bytes 442376 | tf_op jit(solution)/shard_map/ppermute | solution.py:694
  179.9 11.4 %collective-permute-start.45 = (bf16[48,1536]{1,0:T(8,128)(2,1)S(1)}, bf16[48,1536]{1,0:T(8,128)(2,1)S(1)}, u32[]{:S(2)}, u32[]{:S(2)}) collective-permute-start(bf16[48,1536]{1,0:T(8,128)(2,1)S(1)} %get-tuple-element.324), channel_id=1, source_target_pairs={{0,8},{1,9},{2,10},{3,11},{4,12},{5,13},{6,14},{7,15},{8,0},{9,1},... | collective-permute-start | bytes 442376 | tf_op jit(solution)/shard_map/ppermute | solution.py:694
  180.7 10.6 %collective-permute-start.46 = (bf16[48,1536]{1,0:T(8,128)(2,1)S(1)}, bf16[48,1536]{1,0:T(8,128)(2,1)S(1)}, u32[]{:S(2)}, u32[]{:S(2)}) collective-permute-start(bf16[48,1536]{1,0:T(8,128)(2,1)S(1)} %get-tuple-element.323), channel_id=1, source_target_pairs={{0,24},{1,25},{2,26},{3,27},{4,28},{5,29},{6,30},{7,31},{8,16},{9,... | collective-permute-start | bytes 442376 | tf_op jit(solution)/shard_map/ppermute | solution.py:694
  183.3 10.4 %collective-permute-start.41 = (bf16[192,1152]{1,0:T(8,128)(2,1)S(1)}, bf16[192,1152]{1,0:T(8,128)(2,1)S(1)}, u32[]{:S(2)}, u32[]{:S(2)}) collective-permute-start(bf16[192,1152]{1,0:T(8,128)(2,1)S(1)} %add_convert_fusion.6), channel_id=1, source_target_pairs={{0,4},{1,3},{2,6},{3,1},{4,0},{5,7},{6,2},{7,5},{8,12},{9,11},{10,... | collective-permute-start | bytes 1327112 | tf_op jit(solution)/shard_map/ppermute | solution.py:694
  184.4 9.3 %collective-permute-start.43 = (bf16[192,512]{1,0:T(8,128)(2,1)S(1)}, bf16[192,512]{1,0:T(8,128)(2,1)S(1)}, u32[]{:S(2)}, u32[]{:S(2)}) collective-permute-start(bf16[192,512]{1,0:T(8,128)(2,1)S(1)} %add_convert_fusion.8), channel_id=1, source_target_pairs={{0,4},{1,3},{2,6},{3,1},{4,0},{5,7},{6,2},{7,5},{8,12},{9,11},{10,... | collective-permute-start | bytes 589832 | tf_op jit(solution)/shard_map/ppermute | solution.py:694
  190.5 18.5 %collective-permute-start.51 = (f32[256,768]{1,0:T(8,128)S(1)}, f32[256,768]{1,0:T(8,128)S(1)}, u32[]{:S(2)}, u32[]{:S(2)}) collective-permute-start(f32[256,768]{1,0:T(8,128)S(1)} %constant_dynamic-slice_fusion.1), channel_id=1, source_target_pairs={{0,1},{1,0},{2,3},{3,2},{4,5},{5,4},{6,7},{7,6},{8,9},{9,8},{10,11... | collective-permute-start | bytes 2359304 | tf_op jit(solution)/shard_map/ppermute | solution.py:28
  195.1 11.0 %collective-permute-start.52 = (bf16[48,1664]{1,0:T(8,128)(2,1)S(1)}, bf16[48,1664]{1,0:T(8,128)(2,1)S(1)}, u32[]{:S(2)}, u32[]{:S(2)}) collective-permute-start(bf16[48,1664]{1,0:T(8,128)(2,1)S(1)} %get-tuple-element.322), channel_id=1, source_target_pairs={{0,16},{1,17},{2,18},{3,19},{4,20},{5,21},{6,22},{7,23},{8,24},{9,... | collective-permute-start | bytes 479240 | tf_op jit(solution)/shard_map/ppermute | solution.py:694
  195.3 10.7 %collective-permute-start.53 = (bf16[48,1664]{1,0:T(8,128)(2,1)S(1)}, bf16[48,1664]{1,0:T(8,128)(2,1)S(1)}, u32[]{:S(2)}, u32[]{:S(2)}) collective-permute-start(bf16[48,1664]{1,0:T(8,128)(2,1)S(1)} %get-tuple-element.321), channel_id=1, source_target_pairs={{0,8},{1,9},{2,10},{3,11},{4,12},{5,13},{6,14},{7,15},{8,0},{9,1},... | collective-permute-start | bytes 479240 | tf_op jit(solution)/shard_map/ppermute | solution.py:694
  197.0 11.2 %collective-permute-start.54 = (bf16[48,1664]{1,0:T(8,128)(2,1)S(1)}, bf16[48,1664]{1,0:T(8,128)(2,1)S(1)}, u32[]{:S(2)}, u32[]{:S(2)}) collective-permute-start(bf16[48,1664]{1,0:T(8,128)(2,1)S(1)} %get-tuple-element.320), channel_id=1, source_target_pairs={{0,24},{1,25},{2,26},{3,27},{4,28},{5,29},{6,30},{7,31},{8,16},{9,... | collective-permute-start | bytes 479240 | tf_op jit(solution)/shard_map/ppermute | solution.py:694
  (34 other events, 329.9 us)
